TPU v7x, 512 devices: a whole 4x8x8 slice. The times are simulated.
512 devices in a mesh: seq: 128 (over z_lo, x, y, core), head: 4 (over z_hi).
Axes of the slice: x: 4, y: 8, z: 8 (z_hi: 4, z_lo: 2; z = z_hi * 2 + z_lo), core: 2. Of those that a mesh axis runs over, the one named last changes fastest.
Arguments:
- queries: bfloat16 [65536, 1024], P('seq', 'head'), may hold values from -6 to 6
- keys: bfloat16 [65536, 1024], P('seq', 'head'), may hold values from -6 to 6
- values: bfloat16 [65536, 1024], P('seq', 'head'), may hold values from -6 to 6
- block_keep: int32 [256], replicated, may hold values 0 or 1
- w_out: bfloat16 [1024, 1024], P('head'), may hold values from -0.75 to 0.75
Outputs:
- projected: bfloat16 [65536, 1024], P('seq', 'head')
All inputs are finite; a program needn't handle non-finite values.
Results may differ from a plain program's by a relative error of at most 0.015.
Values may be sent and summed in bfloat16 or wider, within the bound.
No kernel may reach another device: no remote copies, remote signals or barrier semaphores. Data moves between devices by JAX's collectives and lax.ppermute only.
A program may use at most 64 MiB of HBM per device.

v0:
```python
import math

import jax
import jax.numpy as jnp
from jax import lax
from jax.sharding import PartitionSpec as P

HD = 64
BLOCK = 256


def extended(block, sides, width):
    for axis, dim in sides:
        count = lax.axis_size(axis)
        forward = [(i, i + 1) for i in range(count - 1)]
        backward = [(target, source) for source, target in forward]
        low = lax.ppermute(
            lax.slice_in_dim(block, block.shape[dim] - width, None, axis=dim), axis, forward
        )
        high = lax.ppermute(lax.slice_in_dim(block, 0, width, axis=dim), axis, backward)
        block = jnp.concatenate([low, block, high], axis=dim)
    return block


def partner(value, axis, distance):
    mask = 2**distance
    pairs = [(source, source ^ mask) for source in range(lax.axis_size(axis))]
    return lax.ppermute(value, axis, pairs)


def allowed_blocks(block_ids, block_keep, count):
    inside = (block_ids >= 0) & (block_ids < count)
    safe_ids = jnp.clip(block_ids, 0, count - 1)
    matches = safe_ids[:, None] == jnp.arange(count, dtype=jnp.int32)[None, :]
    kept = jnp.any(matches & (block_keep[None, :] == 1), axis=1)
    return inside & kept


def per_device(queries, keys, values, block_keep, w_out):
    rows = queries.shape[0]
    width = queries.shape[1]
    local_blocks = rows // BLOCK
    head_count = width // HD
    seq_count = lax.axis_size("seq")
    seq_bits = seq_count.bit_length() - 1
    local_bits = local_blocks.bit_length() - 1
    count = local_blocks * seq_count
    factor = 1.0 / math.sqrt(HD)
    paired = jnp.stack([keys, values]).reshape(2, local_blocks, BLOCK, width)
    first = lax.axis_index("seq") * local_blocks
    block_ids = first + jnp.arange(local_blocks, dtype=jnp.int32)
    sources = [paired]
    validity = [jnp.ones((local_blocks,), dtype=bool)]
    padded = extended(paired, (("seq", 1),), 1)
    sources.append(padded[:, :local_blocks])
    validity.append(allowed_blocks(block_ids - 1, block_keep, count))
    sources.append(padded[:, 2:])
    validity.append(allowed_blocks(block_ids + 1, block_keep, count))
    far_levels = list(range(max(1, local_bits), local_bits + seq_bits))
    for level in far_levels:
        arrived = partner(paired, "seq", level - local_bits)
        sources.append(arrived)
        validity.append(allowed_blocks(jnp.bitwise_xor(block_ids, 1 << level), block_keep, count))
    source_count = len(sources)
    stacked = jnp.stack(sources, 2)
    live_all = jnp.stack(validity, 1)
    pieces = []
    for local in range(local_blocks):
        query_now = queries[local * BLOCK : (local + 1) * BLOCK].reshape(BLOCK, head_count, HD)
        key_now = stacked[0, local].reshape(source_count, BLOCK, head_count, HD)
        value_now = stacked[1, local].reshape(source_count, BLOCK, head_count, HD)
        scores = (
            jnp.einsum("qhd,skhd->hqsk", query_now, key_now, preferred_element_type=jnp.float32)
            * factor
        )
        masked = jnp.where(live_all[local][None, None, :, None], scores, -jnp.inf)
        top = jnp.max(masked, axis=(2, 3), keepdims=True)
        expo = jnp.exp(masked - top)
        total = jnp.sum(expo, axis=(2, 3))
        weights = expo.astype(jnp.bfloat16)
        mixed = jnp.einsum("hqsk,skhd->qhd", weights, value_now, preferred_element_type=jnp.float32)
        mixed = mixed / jnp.transpose(total)[:, :, None]
        pieces.append(mixed.reshape(BLOCK, width).astype(jnp.bfloat16))
    attended = jnp.concatenate(pieces, 0)
    partial_out = jnp.dot(attended, w_out, preferred_element_type=jnp.float32)
    result = lax.psum_scatter(
        partial_out.astype(jnp.bfloat16), "head", scatter_dimension=1, tiled=True
    )
    return result


def solution(mesh):
    placed = (P("seq", "head"), P("seq", "head"), P("seq", "head"), P(), P("head", None))
    return jax.shard_map(
        per_device, mesh=mesh, in_specs=placed, out_specs=P("seq", "head"), check_vma=False
    )
```

profile of v0, /device:TPU:56, one launch (start us, length us, event | category | flops | bytes accessed | tf_op | source)
XLA Modules:
  0.0 157.8 jit_solution(14093863268204586965)
XLA Ops:
  6.5 1.2 pad_maximum_fusion
  7.7 4.0 %collective-permute-start.4 = (bf16[2,2,256,256]{3,2,1,0:T(8,128)(2,1)S(1)}, bf16[2,2,256,256]{3,2,1,0:T(8,128)(2,1)S(1)}, u32[]{:S(2)}, u32[]{:S(2)}) collective-permute-start(bf16[2,2,256,256]{3,2,1,0:T(8,128)(2,1)S(1)} %pad_maximum_fusion), channel_id=1, source_target_pairs={{0,16},{4,20},{8,24},{12,28},{16,0},{20,4},{24,8},{28,12},{32,48},... | collective-permute-start | bytes 1572872 | tf_op jit(solution)/shard_map/ppermute | solution.py:28
  11.8 3.3 %collective-permute-start.3 = (bf16[2,2,256,256]{3,2,1,0:T(8,128)(2,1)S(1)}, bf16[2,2,256,256]{3,2,1,0:T(8,128)(2,1)S(1)}, u32[]{:S(2)}, u32[]{:S(2)}) collective-permute-start(bf16[2,2,256,256]{3,2,1,0:T(8,128)(2,1)S(1)} %pad_maximum_fusion), channel_id=1, source_target_pairs={{0,8},{4,12},{8,0},{12,4},{16,24},{20,28},{24,16},{28,20},{32,40},... | collective-permute-start | bytes 1572872 | tf_op jit(solution)/shard_map/ppermute | solution.py:28
  15.0 1.9 %collective-permute-start.2 = (bf16[2,2,256,256]{3,2,1,0:T(8,128)(2,1)S(1)}, bf16[2,2,256,256]{3,2,1,0:T(8,128)(2,1)S(1)}, u32[]{:S(2)}, u32[]{:S(2)}) collective-permute-start(bf16[2,2,256,256]{3,2,1,0:T(8,128)(2,1)S(1)} %pad_maximum_fusion), channel_id=1, source_target_pairs={{0,4},{4,0},{8,12},{12,8},{16,20},{20,16},{24,28},{28,24},{32,36},... | collective-permute-start | bytes 1572872 | tf_op jit(solution)/shard_map/ppermute | solution.py:28
  17.0 2.0 %fusion.37 = (bf16[2,1,256,256]{3,2,1,0:T(8,128)(2,1)}, bf16[2,1,256,256]{3,2,1,0:T(8,128)(2,1)}) fusion(bf16[1,2,256,256]{3,2,1,0:T(8,128)(2,1)} %bitcast.129, bf16[1,2,256,256]{3,2,1,0:T(8,128)(2,1)} %bitcast.124), kind=kLoop, calls=%fused_computation.49 | loop fusion | flops 262144 | bytes 1048576 | tf_op jit(solution)/shard_map/stack | solution.py:49
  18.9 2.7 %collective-permute-start.1 = (bf16[2,1,256,256]{3,2,1,0:T(8,128)(2,1)}, bf16[2,1,256,256]{3,2,1,0:T(8,128)(2,1)}, u32[]{:S(2)}, u32[]{:S(2)}) collective-permute-start(bf16[2,1,256,256]{3,2,1,0:T(8,128)(2,1)} %get-tuple-element.22), channel_id=1, source_target_pairs={{4,0},{8,4},{12,8},{16,12},{20,16},{24,20},{28,24},{32,28},{36,32}... | collective-permute-start | bytes 786440 | tf_op jit(solution)/shard_map/ppermute | solution.py:20
  21.6 1.9 %collective-permute-start = (bf16[2,1,256,256]{3,2,1,0:T(8,128)(2,1)}, bf16[2,1,256,256]{3,2,1,0:T(8,128)(2,1)}, u32[]{:S(2)}, u32[]{:S(2)}) collective-permute-start(bf16[2,1,256,256]{3,2,1,0:T(8,128)(2,1)} %get-tuple-element.23), channel_id=1, source_target_pairs={{0,4},{4,8},{8,12},{12,16},{16,20},{20,24},{24,28},{28,32},{32,36}... | collective-permute-start | bytes 786440 | tf_op jit(solution)/shard_map/ppermute | solution.py:17
  23.7 0.7 broadcast_compare_fusion
  24.3 0.3 and_reduce_fusion
  24.7 0.1 copy.90
  24.8 0.1 copy.89
  24.9 0.1 copy.82
  25.0 0.1 copy.84
  25.1 0.1 copy.83
  25.3 0.1 copy.88
  25.4 0.1 copy.86
  25.7 1.0 fusion.43
  26.8 1.9 %maximum_dynamic-update-slice_fusion = bf16[2,2,10,256,256]{4,3,1,2,0:T(8,128)(2,1)} fusion(bf16[1,2,1,256,256]{4,3,1,2,0:T(8,128)(2,1)} %bitcast.125, bf16[1,2,1,256,256]{4,3,1,2,0:T(8,128)(2,1)} %bitcast.130), kind=kLoop, calls=%fused_computation.40 | loop fusion | flops 1048575 | bytes 1048576
  28.9 11.4 %collective-permute-done = bf16[2,1,256,256]{3,2,1,0:T(8,128)(2,1)} collective-permute-done((bf16[2,1,256,256]{3,2,1,0:T(8,128)(2,1)}, bf16[2,1,256,256]{3,2,1,0:T(8,128)(2,1)}, u32[]{:S(2)}, u32[]{:S(2)}) %collective-permute-start) | collective-permute-done | bytes 262176 | tf_op jit(solution)/shard_map/ppermute | solution.py:17
  40.3 4.3 %collective-permute-start.8 = (bf16[2,2,256,256]{3,2,1,0:T(8,128)(2,1)S(1)}, bf16[2,2,256,256]{3,2,1,0:T(8,128)(2,1)S(1)}, u32[]{:S(2)}, u32[]{:S(2)}) collective-permute-start(bf16[2,2,256,256]{3,2,1,0:T(8,128)(2,1)S(1)} %pad_maximum_fusion), channel_id=1, source_target_pairs={{0,256},{4,260},{8,264},{12,268},{16,272},{20,276},{24,280},{28,28... | collective-permute-start | bytes 1572872 | tf_op jit(solution)/shard_map/ppermute | solution.py:28
  44.6 1.9 %fusion.35 = bf16[2,2,10,256,256]{4,3,1,2,0:T(8,128)(2,1)} fusion(bf16[2,2,10,256,256]{4,3,1,2,0:T(8,128)(2,1)} %maximum_dynamic-update-slice_fusion, bf16[2,1,256,256]{3,2,1,0:T(8,128)(2,1)} %collective-permute-done, bf16[1,2,256,256]{3,2,1,0:T(8,128)(2,1)} %bitcast.126, bf16[1,2,256,256]{3,2,1,0:T(8,128)(2,1)} %bitcast.131), kind=kLoop, calls=%fused_computation.38 | loop fusion | flops 1572864 | bytes 1310720
  46.5 3.7 %collective-permute-start.5 = (bf16[2,2,256,256]{3,2,1,0:T(8,128)(2,1)S(1)}, bf16[2,2,256,256]{3,2,1,0:T(8,128)(2,1)S(1)}, u32[]{:S(2)}, u32[]{:S(2)}) collective-permute-start(bf16[2,2,256,256]{3,2,1,0:T(8,128)(2,1)S(1)} %pad_maximum_fusion), channel_id=1, source_target_pairs={{0,32},{4,36},{8,40},{12,44},{16,48},{20,52},{24,56},{28,60},{32,0... | collective-permute-start | bytes 1572872 | tf_op jit(solution)/shard_map/ppermute | solution.py:28
  50.2 1.8 %fusion.33 = bf16[2,2,10,256,256]{4,3,1,2,0:T(8,128)(2,1)} fusion(bf16[2,2,10,256,256]{4,3,1,2,0:T(8,128)(2,1)} %fusion.35, bf16[2,1,256,256]{3,2,1,0:T(8,128)(2,1)} %collective-permute-done.1, bf16[1,2,256,256]{3,2,1,0:T(8,128)(2,1)S(1)} %bitcast.127, bf16[1,2,256,256]{3,2,1,0:T(8,128)(2,1)S(1)} %bitcast.132), kind=kLoop, calls=%fused_computation.34 | loop fusion | flops 1572864 | bytes 1310720
  52.0 4.9 %collective-permute-start.7 = (bf16[2,2,256,256]{3,2,1,0:T(8,128)(2,1)S(1)}, bf16[2,2,256,256]{3,2,1,0:T(8,128)(2,1)S(1)}, u32[]{:S(2)}, u32[]{:S(2)}) collective-permute-start(bf16[2,2,256,256]{3,2,1,0:T(8,128)(2,1)S(1)} %pad_maximum_fusion), channel_id=1, source_target_pairs={{0,128},{4,132},{8,136},{12,140},{16,144},{20,148},{24,152},{28,15... | collective-permute-start | bytes 1572872 | tf_op jit(solution)/shard_map/ppermute | solution.py:28
  56.9 0.8 bitcast_dynamic-update-slice_fusion.5
  57.8 2.5 %collective-permute-start.6 = (bf16[2,2,256,256]{3,2,1,0:T(8,128)(2,1)S(1)}, bf16[2,2,256,256]{3,2,1,0:T(8,128)(2,1)S(1)}, u32[]{:S(2)}, u32[]{:S(2)}) collective-permute-start(bf16[2,2,256,256]{3,2,1,0:T(8,128)(2,1)S(1)} %pad_maximum_fusion), channel_id=1, source_target_pairs={{0,64},{4,68},{8,72},{12,76},{16,80},{20,84},{24,88},{28,92},{32,9... | collective-permute-start | bytes 1572872 | tf_op jit(solution)/shard_map/ppermute | solution.py:28
  60.3 0.8 bitcast_dynamic-update-slice_fusion.4
  61.1 0.9 bitcast_dynamic-update-slice_fusion.3
  62.0 9.2 %collective-permute-done.5 = bf16[2,2,256,256]{3,2,1,0:T(8,128)(2,1)S(1)} collective-permute-done((bf16[2,2,256,256]{3,2,1,0:T(8,128)(2,1)S(1)}, bf16[2,2,256,256]{3,2,1,0:T(8,128)(2,1)S(1)}, u32[]{:S(2)}, u32[]{:S(2)}) %collective-permute-start.5) | collective-permute-done | bytes 524320 | tf_op jit(solution)/shard_map/ppermute | solution.py:28
  71.2 0.8 bitcast_dynamic-update-slice_fusion.2
  72.0 0.8 bitcast_dynamic-update-slice_fusion.1
  72.9 0.8 bitcast_dynamic-update-slice_fusion
  73.7 0.9 bitcast_dynamic-update-slice_fusion.6
  74.6 4.5 %fusion.42 = (bf16[1,1,10,256,256]{4,3,1,2,0:T(8,128)(2,1)S(1)}, bf16[1,1,10,256,256]{4,3,1,2,0:T(8,128)(2,1)}, bf16[1,1,10,256,256]{4,3,1,2,0:T(8,128)(2,1)}, bf16[1,1,10,256,256]{4,3,1,2,0:T(8,128)(2,1)}) fusion(bf16[2,2,10,256,256]{4,3,1,2,0:T(8,128)(2,1)} %bitcast_dynamic-update-slice_fusion.6), kind=kLoop, calls=%fused_computation.86 | loop fusion | bytes 10485760 | tf_op jit(solution)/shard_map/slice | solution.py:70
  79.1 0.6 copy.91
  79.8 1.6 %copy.96 = bf16[1,1,10,256,256]{3,4,2,1,0:T(8,128)(2,1)S(1)} copy(bf16[1,1,10,256,256]{4,3,1,2,0:T(8,128)(2,1)} %get-tuple-element.19) | data formatting | bytes 2621440 | tf_op jit(solution)/shard_map/slice | solution.py:70
  81.4 2.4 %copy.95 = bf16[1,1,10,256,256]{3,4,2,1,0:T(8,128)(2,1)} copy(bf16[1,1,10,256,256]{4,3,1,2,0:T(8,128)(2,1)} %get-tuple-element.20) | data formatting | bytes 2621440 | tf_op jit(solution)/shard_map/slice | solution.py:71
  83.8 2.4 %copy.81 = bf16[1,1,10,256,256]{3,4,2,1,0:T(8,128)(2,1)} copy(bf16[1,1,10,256,256]{4,3,1,2,0:T(8,128)(2,1)} %get-tuple-element.21) | data formatting | bytes 2621440 | tf_op jit(solution)/shard_map/slice | solution.py:71
  86.2 2.2 %bitcast_reduce_fusion = (f32[4,256]{1,0:T(4,128)S(1)}, f32[4,10,256,256]{3,2,1,0:T(8,128)S(1)}) fusion(pred[10]{0:T(512)(128)(4,1)S(1)} %get-tuple-element.27, bf16[256,4,64,1]{0,2,3,1:T(8,128)(2,1)S(1)} %bitcast.136, bf16[10,256,4,64]{1,3,2,0:T(8,128)(2,1)S(1)} %bitcast.122), kind=kOutput, calls=%fused_computation.1 | convolution fusion | flops 343407616 | bytes 11931658 | tf_op jit(solution)/shard_map/qhd,skhd->hqsk/dot_general | solution.py:73
  88.4 4.6 %fusion.4 = (f32[4,256]{1,0:T(4,128)S(1)}, bf16[4,256,10,256]{1,3,2,0:T(8,128)(2,1)}) fusion(f32[4,10,256,256]{3,2,1,0:T(8,128)S(1)} %get-tuple-element.29, f32[4,256]{1,0:T(4,128)S(1)} %get-tuple-element.28, pred[10]{0:T(512)(128)(4,1)S(1)} %get-tuple-element.27), kind=kLoop, calls=%fused_computation.10 | loop fusion | flops 13106176 | bytes 15736842 | tf_op jit(solution)/shard_map/reduce_sum | solution.py:79
  93.0 2.2 %bitcast_reduce_fusion.1 = (f32[4,256]{1,0:T(4,128)S(1)}, f32[4,10,256,256]{3,2,1,0:T(8,128)S(1)}) fusion(pred[10]{0:T(512)(128)(4,1)S(1)} %get-tuple-element.26, bf16[256,4,64,1]{0,2,3,1:T(8,128)(2,1)S(1)} %bitcast.135, bf16[10,256,4,64]{1,3,2,0:T(8,128)(2,1)S(1)} %bitcast.121), kind=kOutput, calls=%fused_computation.4 | convolution fusion | flops 343407616 | bytes 11931658 | tf_op jit(solution)/shard_map/qhd,skhd->hqsk/dot_general | solution.py:73
  95.2 4.7 %fusion.2 = (f32[4,256]{1,0:T(4,128)S(1)}, bf16[4,256,10,256]{1,3,2,0:T(8,128)(2,1)}) fusion(f32[4,10,256,256]{3,2,1,0:T(8,128)S(1)} %get-tuple-element.31, f32[4,256]{1,0:T(4,128)S(1)} %get-tuple-element.30, pred[10]{0:T(512)(128)(4,1)S(1)} %get-tuple-element.26), kind=kLoop, calls=%fused_computation.8 | loop fusion | flops 13106176 | bytes 15736842 | tf_op jit(solution)/shard_map/reduce_sum | solution.py:79
  99.9 3.6 %fusion.23 = bf16[256,4,64]{0,2,1:T(8,128)(2,1)S(1)} fusion(bf16[10,256,4,64]{1,3,2,0:T(8,128)(2,1)S(1)} %bitcast.134, bf16[4,256,10,256]{1,3,2,0:T(8,128)(2,1)} %get-tuple-element.17, f32[256,4]{0,1:T(4,128)S(1)} %bitcast.139), kind=kOutput, calls=%fused_computation.24 | convolution fusion | flops 335675392 | bytes 6688768 | tf_op jit(solution)/shard_map/hqsk,skhd->qhd/dot_general | solution.py:81
  103.5 0.4 copy-done.3
  103.9 0.4 copy-done.4
  104.3 1.0 fusion.29
  105.3 1.5 convolution_convert_fusion
  106.8 44.2 %reduce-scatter.2.cloned.1.call-done = bf16[512,256]{1,0:T(8,128)(2,1)} async-done(((bf16[512,1024]{1,0:T(8,128)(2,1)}), bf16[512,256]{1,0:T(8,128)(2,1)}) %reduce-scatter.2.cloned.1.call-update) | async-done | bytes 262160 | tf_op jit(solution)/shard_map/reduce_scatter | solution.py:86
  (40 shorter events, 0.7 us)
Async XLA Ops:
  6.5 98.8 %copy-start = (bf16[256,1024]{1,0:T(8,128)(2,1)S(1)}, bf16[256,1024]{1,0:T(8,128)(2,1)}, u32[]{:S(2)}) copy-start(bf16[256,1024]{1,0:T(8,128)(2,1)} %param.9) | copy-start | bytes 1572868
  6.5 43.7 %copy-start.1 = (bf16[512,256]{1,0:T(8,128)(2,1)S(1)}, bf16[512,256]{1,0:T(8,128)(2,1)}, u32[]{:S(2)}) copy-start(bf16[512,256]{1,0:T(8,128)(2,1)} %param.7) | copy-start | bytes 786436
  6.5 43.7 %copy-start.2 = (bf16[512,256]{1,0:T(8,128)(2,1)S(1)}, bf16[512,256]{1,0:T(8,128)(2,1)}, u32[]{:S(2)}) copy-start(bf16[512,256]{1,0:T(8,128)(2,1)} %param.6) | copy-start | bytes 786436
  6.5 144.5 %reduce-scatter.2.cloned.1.call-start = ((), (), s32[]{:S(2)}) async-start(), calls=%async_computation.1 | async-start | bytes 1310720 | tf_op jit(solution)/shard_map/reduce_scatter | solution.py:86
  7.7 53.4 %collective-permute-start.4 = (bf16[2,2,256,256]{3,2,1,0:T(8,128)(2,1)S(1)}, bf16[2,2,256,256]{3,2,1,0:T(8,128)(2,1)S(1)}, u32[]{:S(2)}, u32[]{:S(2)}) collective-permute-start(bf16[2,2,256,256]{3,2,1,0:T(8,128)(2,1)S(1)} %pad_maximum_fusion), channel_id=1, source_target_pairs={{0,16},{4,20},{8,24},{12,28},{16,0},{20,4},{24,8},{28,12},{32,48},... | collective-permute-start | bytes 1572872 | tf_op jit(solution)/shard_map/ppermute | solution.py:28
  11.8 46.0 %collective-permute-start.3 = (bf16[2,2,256,256]{3,2,1,0:T(8,128)(2,1)S(1)}, bf16[2,2,256,256]{3,2,1,0:T(8,128)(2,1)S(1)}, u32[]{:S(2)}, u32[]{:S(2)}) collective-permute-start(bf16[2,2,256,256]{3,2,1,0:T(8,128)(2,1)S(1)} %pad_maximum_fusion), channel_id=1, source_target_pairs={{0,8},{4,12},{8,0},{12,4},{16,24},{20,28},{24,16},{28,20},{32,40},... | collective-permute-start | bytes 1572872 | tf_op jit(solution)/shard_map/ppermute | solution.py:28
  15.0 37.0 %collective-permute-start.2 = (bf16[2,2,256,256]{3,2,1,0:T(8,128)(2,1)S(1)}, bf16[2,2,256,256]{3,2,1,0:T(8,128)(2,1)S(1)}, u32[]{:S(2)}, u32[]{:S(2)}) collective-permute-start(bf16[2,2,256,256]{3,2,1,0:T(8,128)(2,1)S(1)} %pad_maximum_fusion), channel_id=1, source_target_pairs={{0,4},{4,0},{8,12},{12,8},{16,20},{20,16},{24,28},{28,24},{32,36},... | collective-permute-start | bytes 1572872 | tf_op jit(solution)/shard_map/ppermute | solution.py:28
  18.9 27.6 %collective-permute-start.1 = (bf16[2,1,256,256]{3,2,1,0:T(8,128)(2,1)}, bf16[2,1,256,256]{3,2,1,0:T(8,128)(2,1)}, u32[]{:S(2)}, u32[]{:S(2)}) collective-permute-start(bf16[2,1,256,256]{3,2,1,0:T(8,128)(2,1)} %get-tuple-element.22), channel_id=1, source_target_pairs={{4,0},{8,4},{12,8},{16,12},{20,16},{24,20},{28,24},{32,28},{36,32}... | collective-permute-start | bytes 786440 | tf_op jit(solution)/shard_map/ppermute | solution.py:20
  21.6 18.7 %collective-permute-start = (bf16[2,1,256,256]{3,2,1,0:T(8,128)(2,1)}, bf16[2,1,256,256]{3,2,1,0:T(8,128)(2,1)}, u32[]{:S(2)}, u32[]{:S(2)}) collective-permute-start(bf16[2,1,256,256]{3,2,1,0:T(8,128)(2,1)} %get-tuple-element.23), channel_id=1, source_target_pairs={{0,4},{4,8},{8,12},{12,16},{16,20},{20,24},{24,28},{28,32},{32,36}... | collective-permute-start | bytes 786440 | tf_op jit(solution)/shard_map/ppermute | solution.py:17
  40.3 33.4 %collective-permute-start.8 = (bf16[2,2,256,256]{3,2,1,0:T(8,128)(2,1)S(1)}, bf16[2,2,256,256]{3,2,1,0:T(8,128)(2,1)S(1)}, u32[]{:S(2)}, u32[]{:S(2)}) collective-permute-start(bf16[2,2,256,256]{3,2,1,0:T(8,128)(2,1)S(1)} %pad_maximum_fusion), channel_id=1, source_target_pairs={{0,256},{4,260},{8,264},{12,268},{16,272},{20,276},{24,280},{28,28... | collective-permute-start | bytes 1572872 | tf_op jit(solution)/shard_map/ppermute | solution.py:28
  46.5 24.7 %collective-permute-start.5 = (bf16[2,2,256,256]{3,2,1,0:T(8,128)(2,1)S(1)}, bf16[2,2,256,256]{3,2,1,0:T(8,128)(2,1)S(1)}, u32[]{:S(2)}, u32[]{:S(2)}) collective-permute-start(bf16[2,2,256,256]{3,2,1,0:T(8,128)(2,1)S(1)} %pad_maximum_fusion), channel_id=1, source_target_pairs={{0,32},{4,36},{8,40},{12,44},{16,48},{20,52},{24,56},{28,60},{32,0... | collective-permute-start | bytes 1572872 | tf_op jit(solution)/shard_map/ppermute | solution.py:28
  52.0 20.9 %collective-permute-start.7 = (bf16[2,2,256,256]{3,2,1,0:T(8,128)(2,1)S(1)}, bf16[2,2,256,256]{3,2,1,0:T(8,128)(2,1)S(1)}, u32[]{:S(2)}, u32[]{:S(2)}) collective-permute-start(bf16[2,2,256,256]{3,2,1,0:T(8,128)(2,1)S(1)} %pad_maximum_fusion), channel_id=1, source_target_pairs={{0,128},{4,132},{8,136},{12,140},{16,144},{20,148},{24,152},{28,15... | collective-permute-start | bytes 1572872 | tf_op jit(solution)/shard_map/ppermute | solution.py:28
  57.8 14.3 %collective-permute-start.6 = (bf16[2,2,256,256]{3,2,1,0:T(8,128)(2,1)S(1)}, bf16[2,2,256,256]{3,2,1,0:T(8,128)(2,1)S(1)}, u32[]{:S(2)}, u32[]{:S(2)}) collective-permute-start(bf16[2,2,256,256]{3,2,1,0:T(8,128)(2,1)S(1)} %pad_maximum_fusion), channel_id=1, source_target_pairs={{0,64},{4,68},{8,72},{12,76},{16,80},{20,84},{24,88},{28,92},{32,9... | collective-permute-start | bytes 1572872 | tf_op jit(solution)/shard_map/ppermute | solution.py:28
  95.2 4.7 %copy-start.5 = (bf16[1,1,10,256,256]{3,4,2,1,0:T(8,128)(2,1)S(1)}, bf16[1,1,10,256,256]{3,4,2,1,0:T(8,128)(2,1)}, u32[]{:S(2)}) copy-start(bf16[1,1,10,256,256]{3,4,2,1,0:T(8,128)(2,1)} %copy.95) | copy-start | bytes 3932164
  99.9 4.0 %copy-start.3 = (bf16[4,256,10,256]{1,3,2,0:T(8,128)(2,1)S(1)}, bf16[4,256,10,256]{1,3,2,0:T(8,128)(2,1)}, u32[]{:S(2)}) copy-start(bf16[4,256,10,256]{1,3,2,0:T(8,128)(2,1)} %get-tuple-element.15) | copy-start | bytes 15728644
  99.9 4.4 %copy-start.4 = (bf16[1,1,10,256,256]{3,4,2,1,0:T(8,128)(2,1)S(1)}, bf16[1,1,10,256,256]{3,4,2,1,0:T(8,128)(2,1)}, u32[]{:S(2)}) copy-start(bf16[1,1,10,256,256]{3,4,2,1,0:T(8,128)(2,1)} %copy.81) | copy-start | bytes 3932164
Sparse Core Ops, SparseCore 0:
  106.9 44.0 reduce-scatter.1
where the time goes:
time: 159 us; the launch traced here: 158 us
  waiting for transfers between devices  64.8 us (41%)
  starting transfers between devices  29.2 us (18%)
  local copies, waits for them, and re-layouts  20.6 us (13%)
  other arithmetic  19.1 us (12%)
  between operations  13.7 us (9%)
  matrix products  10.5 us (7%)
    reduce_scatter x1, waiting for transfers between devices, per_device(): lax.psum_scatter(partial_out.astype(jnp.bfloat16), 'head', scatter_dimens...  44.2 us
    ppermute x7, starting transfers between devices, partner(): return lax.ppermute(value, axis, pairs)  24.6 us
    ppermute x1, waiting for transfers between devices, extended(): lax.ppermute(lax.slice_in_dim(block, block.shape[dim] - width, None, axis...  11.4 us
    reduce_sum x2, other arithmetic, per_device(): total = jnp.sum(expo, axis=(2, 3))  9.27 us
    ppermute x7, waiting for transfers between devices, partner(): return lax.ppermute(value, axis, pairs)  9.23 us
    slice x3, local copies, waits for them, and re-layouts, per_device(): key_now = stacked[0, local].reshape(source_count, BLOCK, head_count, HD)  6.74 us
    unnamed x18, local copies, waits for them, and re-layouts  5.84 us
    unnamed x3, other arithmetic  5.56 us
  transfers between devices with their start and end apart: 10, of which 3 were waited for; matrix products, arithmetic and copies ran while one was open for 10% of the time, Pallas kernels for 0%

commit v1 on v0

v1 whole, which is shorter than its diff:
```python
import math

import jax
import jax.numpy as jnp
from jax import lax
from jax.experimental import pallas as pl
from jax.experimental.pallas import tpu as pltpu
from jax.sharding import PartitionSpec as P

HD = 64
BLOCK = 256
MASKED = -1e30


def flat_exchange(value, axis, mask):
    pairs = [(source, source ^ mask) for source in range(lax.axis_size(axis))]
    return lax.ppermute(value, axis, pairs)


def halo_exchange(value, axis):
    count = lax.axis_size(axis)
    pairs = []
    for source in range(count):
        target = source + 1 if source % 2 else source - 1
        if 0 <= target < count:
            pairs.append((source, target))
    return lax.ppermute(value, axis, pairs)


def stacked_heads(q, heads):
    lane = lax.broadcasted_iota(jnp.int32, q.shape, 1)
    zero = jnp.zeros_like(q)
    return jnp.concatenate(
        [jnp.where((lane >= h * HD) & (lane < (h + 1) * HD), q, zero) for h in range(heads)], axis=0
    )


def fold(pieces, q, scores, scale, heads, m0, l0, acc0):
    qs = stacked_heads(q, heads)
    rows = qs.shape[0]
    half = rows // 2
    part = m0
    for at, (keys, _, bias) in enumerate(pieces):
        s = lax.dot_general(qs, keys(), (((1,), (1,)), ((), ())), preferred_element_type=jnp.float32)
        scores[at] = s
        top = jnp.maximum(s[:, :128], s[:, 128:]) + bias
        part = top if part is None else jnp.maximum(part, top)
    m = jnp.max(part, axis=1, keepdims=True)
    if l0 is None:
        total, acc_low, acc_high = None, None, None
    else:
        shrink = jnp.exp2((m0 - m) * scale)
        total = l0 * shrink
        acc_low = acc0[:half] * shrink[:half]
        acc_high = acc0[half:] * shrink[half:]
    for at, (_, values, bias) in enumerate(pieces):
        p = jnp.exp2((scores[at] - (m - bias)) * scale)
        add = p[:, :128] + p[:, 128:]
        total = add if total is None else total + add
        w = p.astype(jnp.bfloat16)
        v = values()
        low = jnp.dot(w[:half], v[:, :128], preferred_element_type=jnp.float32)
        high = jnp.dot(w[half:], v[:, 128:], preferred_element_type=jnp.float32)
        acc_low = low if acc_low is None else acc_low + low
        acc_high = high if acc_high is None else acc_high + high
    return m, total, jnp.concatenate([acc_low, acc_high], axis=0)


def bias_of(keep_ref, block, count):
    safe = jnp.clip(block, 0, count - 1)
    ok = (block >= 0) & (block < count) & (keep_ref[safe] == 1)
    return jnp.where(ok, 0.0, MASKED)


def early_kernel(scale, heads, bits, keep_ref, q_ref, own_ref, core_ref, halo_ref, *rest):
    far_refs = rest[: len(bits)]
    m_ref, l_ref, acc_ref, near, scores = rest[len(bits) :]
    count = keep_ref.shape[0]
    rank = lax.axis_index("seq")
    side = lax.rem(rank, 2)
    tokens = q_ref.shape[0]
    for local in range(2):
        other = 1 - local

        @pl.when(side == local)
        def _():
            near[local] = halo_ref[...]

        @pl.when(side != local)
        def _():
            near[local, :BLOCK] = core_ref[other * BLOCK : (other + 1) * BLOCK]
            near[local, BLOCK:] = core_ref[tokens + other * BLOCK : tokens + (other + 1) * BLOCK]

    def step(local, _):
        block = rank * 2 + local
        here = pl.multiple_of(local * BLOCK, BLOCK)
        there = pl.multiple_of((1 - local) * BLOCK, BLOCK)

        def of(ref, start):
            return (
                lambda: ref[pl.ds(start, BLOCK)],
                lambda: ref[pl.ds(pl.multiple_of(tokens + start, BLOCK), BLOCK)],
            )

        pieces = [
            (*of(own_ref, here), 0.0),
            (*of(own_ref, there), bias_of(keep_ref, block ^ 1, count)),
            (
                lambda: near[local, :BLOCK],
                lambda: near[local, BLOCK:],
                bias_of(keep_ref, block + 2 * local - 1, count),
            ),
            (*of(core_ref, here), bias_of(keep_ref, block ^ 2, count)),
        ]
        for ref, bit in zip(far_refs, bits, strict=True):
            pieces.append((*of(ref, here), bias_of(keep_ref, block ^ (1 << bit), count)))
        m, total, acc = fold(pieces, q_ref[pl.ds(here, BLOCK)], scores, scale, heads, None, None, None)
        m_ref[local] = jnp.broadcast_to(m, m_ref.shape[1:])
        l_ref[local] = total
        acc_ref[local] = acc
        return 0

    lax.fori_loop(0, 2, step, 0)


def late_kernel(scale, heads, bits, keep_ref, q_ref, m_ref, l_ref, acc_ref, *rest):
    far_refs = rest[: len(bits)]
    out_ref, scores = rest[len(bits) :]
    count = keep_ref.shape[0]
    rank = lax.axis_index("seq")
    tokens = q_ref.shape[0]

    def step(local, _):
        block = rank * 2 + local
        here = pl.multiple_of(local * BLOCK, BLOCK)
        pieces = []
        for ref, bit in zip(far_refs, bits, strict=True):
            pieces.append(
                (
                    lambda ref=ref: ref[pl.ds(here, BLOCK)],
                    lambda ref=ref: ref[pl.ds(pl.multiple_of(tokens + here, BLOCK), BLOCK)],
                    bias_of(keep_ref, block ^ (1 << bit), count),
                )
            )
        _, total, acc = fold(
            pieces, q_ref[pl.ds(here, BLOCK)], scores, scale, heads, m_ref[local], l_ref[local], acc_ref[local]
        )
        mixed = acc / jnp.sum(total, axis=1, keepdims=True)
        lane = lax.broadcasted_iota(jnp.int32, (BLOCK, 128), 1)
        for pair in range(2):
            first = mixed[2 * pair * BLOCK : (2 * pair + 1) * BLOCK]
            second = mixed[(2 * pair + 1) * BLOCK : (2 * pair + 2) * BLOCK]
            joined = jnp.where(lane < HD, first, second)
            out_ref[pl.ds(here, BLOCK), pair * 128 : (pair + 1) * 128] = joined.astype(out_ref.dtype)
        return 0

    lax.fori_loop(0, 2, step, 0)


def per_device(queries, keys, values, block_keep, w_out):
    rows, width = queries.shape
    heads = width // HD
    scale = 1.0 / math.sqrt(HD) * math.log2(math.e)
    packed = jnp.concatenate([keys, values], axis=0)
    far = {bit: flat_exchange(packed, "seq", 1 << (bit - 1)) for bit in (4, 3, 2, 6, 5, 7)}
    core = flat_exchange(packed, "seq", 1)
    side = lax.rem(lax.axis_index("seq"), 2)
    edge = packed.reshape(2, 2, BLOCK, width)
    edge = jnp.where(side == 1, edge[:, 1], edge[:, 0]).reshape(2 * BLOCK, width)
    halo = halo_exchange(edge, "seq")
    columns = lax.all_to_all(w_out, "head", 1, 0, tiled=True)

    vmem = pl.BlockSpec(memory_space=pltpu.VMEM)
    smem = pl.BlockSpec(memory_space=pltpu.SMEM)
    stacked = heads * BLOCK
    state = [jax.ShapeDtypeStruct((2, stacked, 128), jnp.float32)] * 3

    def cost(pieces):
        return pl.CostEstimate(
            flops=pieces * 4 * stacked * BLOCK * width,
            transcendentals=pieces * stacked * BLOCK,
            bytes_accessed=pieces * 2 * BLOCK * width * 2,
        )

    early_bits, late_bits = (5, 6, 7), (2, 3, 4)
    state = pl.pallas_call(
        lambda *refs: early_kernel(scale, heads, early_bits, *refs),
        out_shape=state,
        in_specs=[smem] + [vmem] * (4 + len(early_bits)),
        out_specs=[vmem] * 3,
        scratch_shapes=[
            pltpu.VMEM((2, 2 * BLOCK, width), jnp.bfloat16),
            pltpu.VMEM((4 + len(early_bits), stacked, BLOCK), jnp.float32),
        ],
        compiler_params=pltpu.CompilerParams(vmem_limit_bytes=32 << 20),
        cost_estimate=cost(2 * (4 + len(early_bits))),
        name="early",
    )(block_keep, queries, packed, core, halo, *[far[bit] for bit in early_bits])
    attended = pl.pallas_call(
        lambda *refs: late_kernel(scale, heads, late_bits, *refs),
        out_shape=jax.ShapeDtypeStruct((rows, width), jnp.bfloat16),
        in_specs=[smem] + [vmem] * (4 + len(late_bits)),
        out_specs=vmem,
        scratch_shapes=[pltpu.VMEM((len(late_bits), stacked, BLOCK), jnp.float32)],
        compiler_params=pltpu.CompilerParams(vmem_limit_bytes=32 << 20),
        cost_estimate=cost(2 * len(late_bits)),
        name="late",
    )(block_keep, queries, *state, *[far[bit] for bit in late_bits])
    gathered = lax.all_gather(attended, "head")
    weights = columns.reshape(-1, width, columns.shape[1])
    out = lax.dot_general(
        gathered, weights, (((0, 2), (0, 1)), ((), ())), preferred_element_type=jnp.float32
    )
    return out.astype(jnp.bfloat16)


def solution(mesh):
    placed = (P("seq", "head"), P("seq", "head"), P("seq", "head"), P(), P("head", None))
    return jax.shard_map(
        per_device, mesh=mesh, in_specs=placed, out_specs=P("seq", "head"), check_vma=False
    )
```

time: 159 us -> 142 us (0.89)
  blocking collectives: 0 us -> 31.2 us
  local copies, waits for them, and re-layouts: 20.6 us -> 1.46 us
  other arithmetic: 19.1 us -> 0.03 us
  Pallas kernels: 0 us -> 14.3 us
  waiting for transfers between devices: 64.8 us -> 51.1 us
  matrix products: 10.5 us -> 2.36 us
  starting transfers between devices: 29.2 us -> 27.3 us
    reduce_scatter x1 -> x0, waiting for transfers between devices: 44.2 us -> none  [per_device(): lax.psum_scatter(partial_out.astype(jnp.bfloat16), 'head', scatter_dimens...]
    all_to_all x0 -> x1, blocking collectives: none -> 31.2 us  [per_device(): columns = lax.all_to_all(w_out, 'head', 1, 0, tiled=True)]
    ppermute x9 -> x8, waiting for transfers between devices: 20.6 us -> 40.3 us  [the longest x7 35.1 us: flat_exchange(): return lax.ppermute(value, axis, pairs)]
    pallas_call x0 -> x2, Pallas kernels: none -> 14.3 us  [the longest x1 8.8 us: per_device(): pl.pallas_call(lambda *refs: early_kernel(scale, heads, early_bits, *refs...]
    slice x8 -> x0, local copies, waits for them, and re-layouts: 12.8 us -> none  [the longest x3 6.74 us: per_device(): key_now = stacked[0, local].reshape(source_count, BLOCK, head_count, HD)]
    all_gather x0 -> x1, waiting for transfers between devices: none -> 10.8 us  [per_device(): gathered = lax.all_gather(attended, 'head')]
    reduce_sum x2 -> x0, other arithmetic: 9.27 us -> none  [per_device(): total = jnp.sum(expo, axis=(2, 3))]
    dot_general x5 -> x1, matrix products: 10.5 us -> 2.36 us  [per_device(): lax.dot_general(gathered, weights, (((0, 2), (0, 1)), ((), ())), preferre...]
  transfers between devices with their start and end apart: 10 -> 9, of which waited for: 3 -> 4; matrix products, arithmetic and copies ran while one was open for 10% -> 0% of each run, Pallas kernels for 0% -> 6%
where the time goes in v1:
time: 142 us; the launch traced here: 141 us
  waiting for transfers between devices  51.1 us (36%)
  blocking collectives  31.2 us (22%)
  starting transfers between devices  27.3 us (19%)
  Pallas kernels  14.3 us (10%)
  between operations  13.6 us (10%)
  matrix products  2.36 us (2%)
  local copies, waits for them, and re-layouts  1.46 us (1%)
    ppermute x7, waiting for transfers between devices, flat_exchange(): return lax.ppermute(value, axis, pairs)  35.1 us
    all_to_all x1, blocking collectives, per_device(): columns = lax.all_to_all(w_out, 'head', 1, 0, tiled=True)  31.2 us
    ppermute x7, starting transfers between devices, flat_exchange(): return lax.ppermute(value, axis, pairs)  24.7 us
    all_gather x1, waiting for transfers between devices, per_device(): gathered = lax.all_gather(attended, 'head')  10.8 us
    pallas_call x1, Pallas kernels, per_device(): pl.pallas_call(lambda *refs: early_kernel(scale, heads, early_bits, *refs...  8.8 us
    pallas_call x1, Pallas kernels, per_device(): pl.pallas_call(lambda *refs: late_kernel(scale, heads, late_bits, *refs),...  5.46 us
    ppermute x1, waiting for transfers between devices, halo_exchange(): return lax.ppermute(value, axis, pairs)  5.16 us
  transfers between devices with their start and end apart: 9, of which 4 were waited for; matrix products, arithmetic and copies ran while one was open for 0% of the time, Pallas kernels for 6%

profile of v1, /device:TPU:56, one launch (start us, length us, event | category | flops | bytes accessed | tf_op | source)
XLA Modules:
  0.0 141.3 jit_solution(4821739693846953244)
XLA Ops:
  6.5 0.0 copy-start.3
  6.5 0.0 all-gather.3.cloned.1.call-start
  6.5 1.0 constant_dynamic-update-slice_fusion.1
  7.6 0.0 copy-done.3
  7.6 1.9 %collective-permute-start = (bf16[1024,256]{1,0:T(8,128)(2,1)S(1)}, bf16[1024,256]{1,0:T(8,128)(2,1)S(1)}, u32[]{:S(2)}, u32[]{:S(2)}) collective-permute-start(bf16[1024,256]{1,0:T(8,128)(2,1)S(1)} %constant_dynamic-update-slice_fusion.refs_2_), channel_id=1, source_target_pairs={{0,4},{4,0},{8,12},{12,8},{16,20},{20,16},{24,28},{28,24},{32,36},... | collective-permute-start | bytes 1572872 | tf_op jit(solution)/shard_map/ppermute | solution.py:17
  9.5 3.4 %collective-permute-start.2 = (bf16[1024,256]{1,0:T(8,128)(2,1)S(1)}, bf16[1024,256]{1,0:T(8,128)(2,1)S(1)}, u32[]{:S(2)}, u32[]{:S(2)}) collective-permute-start(bf16[1024,256]{1,0:T(8,128)(2,1)S(1)} %constant_dynamic-update-slice_fusion.refs_2_), channel_id=1, source_target_pairs={{0,64},{4,68},{8,72},{12,76},{16,80},{20,84},{24,88},{28,92},{32,9... | collective-permute-start | bytes 1572872 | tf_op jit(solution)/shard_map/ppermute | solution.py:17
  12.9 4.6 %collective-permute-start.3 = (bf16[1024,256]{1,0:T(8,128)(2,1)S(1)}, bf16[1024,256]{1,0:T(8,128)(2,1)S(1)}, u32[]{:S(2)}, u32[]{:S(2)}) collective-permute-start(bf16[1024,256]{1,0:T(8,128)(2,1)S(1)} %constant_dynamic-update-slice_fusion.refs_2_), channel_id=1, source_target_pairs={{0,128},{4,132},{8,136},{12,140},{16,144},{20,148},{24,152},{28,15... | collective-permute-start | bytes 1572872 | tf_op jit(solution)/shard_map/ppermute | solution.py:17
  17.6 4.3 %collective-permute-start.4 = (bf16[1024,256]{1,0:T(8,128)(2,1)S(1)}, bf16[1024,256]{1,0:T(8,128)(2,1)S(1)}, u32[]{:S(2)}, u32[]{:S(2)}) collective-permute-start(bf16[1024,256]{1,0:T(8,128)(2,1)S(1)} %constant_dynamic-update-slice_fusion.refs_2_), channel_id=1, source_target_pairs={{0,256},{4,260},{8,264},{12,268},{16,272},{20,276},{24,280},{28,28... | collective-permute-start | bytes 1572872 | tf_op jit(solution)/shard_map/ppermute | solution.py:17
  21.9 0.0 copy-start
  21.9 0.0 copy-start.1
  21.9 2.7 %collective-permute-start.1 = (bf16[512,256]{1,0:T(8,128)(2,1)S(1)}, bf16[512,256]{1,0:T(8,128)(2,1)S(1)}, u32[]{:S(2)}, u32[]{:S(2)}) collective-permute-start(bf16[512,256]{1,0:T(8,128)(2,1)S(1)} %bitcast.14), channel_id=1, source_target_pairs={{4,8},{8,4},{12,16},{16,12},{20,24},{24,20},{28,32},{32,28},{36,40... | collective-permute-start | bytes 786440 | tf_op jit(solution)/shard_map/ppermute | solution.py:27
  24.6 5.2 %collective-permute-done.1.refs_4_ = bf16[512,256]{1,0:T(8,128)(2,1)S(1)} collective-permute-done((bf16[512,256]{1,0:T(8,128)(2,1)S(1)}, bf16[512,256]{1,0:T(8,128)(2,1)S(1)}, u32[]{:S(2)}, u32[]{:S(2)}) %collective-permute-start.1) | collective-permute-done | bytes 262176 | tf_op jit(solution)/shard_map/ppermute | solution.py:27
  29.8 3.2 %collective-permute-start.5 = (bf16[1024,256]{1,0:T(8,128)(2,1)S(1)}, bf16[1024,256]{1,0:T(8,128)(2,1)S(1)}, u32[]{:S(2)}, u32[]{:S(2)}) collective-permute-start(bf16[1024,256]{1,0:T(8,128)(2,1)S(1)} %constant_dynamic-update-slice_fusion.refs_2_), channel_id=1, source_target_pairs={{0,8},{4,12},{8,0},{12,4},{16,24},{20,28},{24,16},{28,20},{32,40},... | collective-permute-start | bytes 1572872 | tf_op jit(solution)/shard_map/ppermute | solution.py:17
  33.0 0.0 collective-permute-done.refs_3_
  33.0 5.3 %collective-permute-start.6 = (bf16[1024,256]{1,0:T(8,128)(2,1)S(1)}, bf16[1024,256]{1,0:T(8,128)(2,1)S(1)}, u32[]{:S(2)}, u32[]{:S(2)}) collective-permute-start(bf16[1024,256]{1,0:T(8,128)(2,1)S(1)} %constant_dynamic-update-slice_fusion.refs_2_), channel_id=1, source_target_pairs={{0,16},{4,20},{8,24},{12,28},{16,0},{20,4},{24,8},{28,12},{32,48},... | collective-permute-start | bytes 1572872 | tf_op jit(solution)/shard_map/ppermute | solution.py:17
  38.3 0.0 collective-permute-done.2.refs_5_
  38.3 1.9 %collective-permute-start.7 = (bf16[1024,256]{1,0:T(8,128)(2,1)S(1)}, bf16[1024,256]{1,0:T(8,128)(2,1)S(1)}, u32[]{:S(2)}, u32[]{:S(2)}) collective-permute-start(bf16[1024,256]{1,0:T(8,128)(2,1)S(1)} %constant_dynamic-update-slice_fusion.refs_2_), channel_id=1, source_target_pairs={{0,32},{4,36},{8,40},{12,44},{16,48},{20,52},{24,56},{28,60},{32,0... | collective-permute-start | bytes 1572872 | tf_op jit(solution)/shard_map/ppermute | solution.py:17
  40.2 0.0 collective-permute-done.3.refs_6_
  40.2 0.0 collective-permute-done.4.refs_7_
  40.2 0.0 copy-done
  40.2 0.0 copy-done.1
  40.3 8.8 %early.1 = (f32[2,1024,128]{2,1,0:T(8,128)S(1)}, f32[2,1024,128]{2,1,0:T(8,128)S(1)}, f32[2,1024,128]{2,1,0:T(8,128)S(1)}) custom-call(s32[256]{0:T(256)S(1)} %copy-done.1, bf16[512,256]{1,0:T(8,128)(2,1)S(1)} %copy-done, bf16[1024,256]{1,0:T(8,128)(2,1)S(1)} %constant_dynamic-update-slice_fusion.refs_2_, ...), custom_call_target="tpu_custom_call" | custom-call | flops 3758096384 | bytes 3670016 | tf_op jit(solution)/shard_map/early/pallas_call | solution.py:186
  49.1 4.1 %collective-permute-done.5.refs_5_ = bf16[1024,256]{1,0:T(8,128)(2,1)S(1)} collective-permute-done((bf16[1024,256]{1,0:T(8,128)(2,1)S(1)}, bf16[1024,256]{1,0:T(8,128)(2,1)S(1)}, u32[]{:S(2)}, u32[]{:S(2)}) %collective-permute-start.5) | collective-permute-done | bytes 524320 | tf_op jit(solution)/shard_map/ppermute | solution.py:17
  53.1 31.0 %collective-permute-done.6.refs_6_ = bf16[1024,256]{1,0:T(8,128)(2,1)S(1)} collective-permute-done((bf16[1024,256]{1,0:T(8,128)(2,1)S(1)}, bf16[1024,256]{1,0:T(8,128)(2,1)S(1)}, u32[]{:S(2)}, u32[]{:S(2)}) %collective-permute-start.6) | collective-permute-done | bytes 524320 | tf_op jit(solution)/shard_map/ppermute | solution.py:17
  84.2 0.0 collective-permute-done.7.refs_7_
  84.2 0.0 copy-start.2
  84.2 5.5 %late.1 = bf16[512,256]{1,0:T(8,128)(2,1)} custom-call(s32[256]{0:T(256)S(1)} %copy-done.1, bf16[512,256]{1,0:T(8,128)(2,1)S(1)} %copy-done, f32[2,1024,128]{2,1,0:T(8,128)S(1)} %get-tuple-element.8.refs_2_, f32[2,1024,128]{2,1,0:T(8,128)S(1)} %get-tuple-element.9.refs_3_, f32[2,1024,128]{2,1,0:T(8,128)S(1)} %get-tuple-element.10.refs_4_, ...), custom_call_target="tpu_custom_call" | custom-call | flops 1610612736 | bytes 1572864 | tf_op jit(solution)/shard_map/late/pallas_call | solution.py:199
  89.6 0.0 all-gather.3.cloned.1.call-update
  89.6 0.0 copy-done.2
  89.7 0.2 copy.6
  89.9 0.2 copy.7
  90.1 31.2 %all_to_all.16 = bf16[256,4,256]{2,0,1:T(8,128)(2,1)S(1)} all-to-all(bf16[256,4,256]{2,0,1:T(8,128)(2,1)S(1)} %copy.7), channel_id=1, replica_groups=mesh['seq'=128,'head'=4] {'head'}, dimensions={1} | all-to-all | bytes 1048576 | tf_op jit(solution)/shard_map/all_to_all | solution.py:171
  121.3 10.8 %all-gather.3.cloned.1.call-done = bf16[2048,256]{1,0:T(8,128)(2,1)} async-done(((bf16[512,256]{1,0:T(8,128)(2,1)}), bf16[2048,256]{1,0:T(8,128)(2,1)}) %all-gather.3.cloned.1.call-update) | async-done | bytes 1048592 | tf_op jit(solution)/shard_map/all_gather | solution.py:209
  132.1 2.4 %fusion = bf16[512,256]{1,0:T(8,128)(2,1)} fusion(bf16[4,512,256]{2,1,0:T(8,128)(2,1)} %bitcast.15, bf16[256,4,256]{2,0,1:T(8,128)(2,1)S(1)} %all_to_all.16), kind=kOutput, calls=%fused_computation.1 | convolution fusion | flops 268566528 | bytes 1835008 | tf_op jit(solution)/shard_map/dot_general | solution.py:211
  (2 shorter events, 0.0 us)
Async XLA Ops:
  6.5 1.0 copy-start.3
  6.5 125.5 %all-gather.3.cloned.1.call-start = ((), (), s32[]{:S(2)}) async-start(), calls=%async_computation.1 | async-start | bytes 1310720 | tf_op jit(solution)/shard_map/all_gather | solution.py:209
  7.6 25.4 %collective-permute-start = (bf16[1024,256]{1,0:T(8,128)(2,1)S(1)}, bf16[1024,256]{1,0:T(8,128)(2,1)S(1)}, u32[]{:S(2)}, u32[]{:S(2)}) collective-permute-start(bf16[1024,256]{1,0:T(8,128)(2,1)S(1)} %constant_dynamic-update-slice_fusion.refs_2_), channel_id=1, source_target_pairs={{0,4},{4,0},{8,12},{12,8},{16,20},{20,16},{24,28},{28,24},{32,36},... | collective-permute-start | bytes 1572872 | tf_op jit(solution)/shard_map/ppermute | solution.py:17
  9.5 28.8 %collective-permute-start.2 = (bf16[1024,256]{1,0:T(8,128)(2,1)S(1)}, bf16[1024,256]{1,0:T(8,128)(2,1)S(1)}, u32[]{:S(2)}, u32[]{:S(2)}) collective-permute-start(bf16[1024,256]{1,0:T(8,128)(2,1)S(1)} %constant_dynamic-update-slice_fusion.refs_2_), channel_id=1, source_target_pairs={{0,64},{4,68},{8,72},{12,76},{16,80},{20,84},{24,88},{28,92},{32,9... | collective-permute-start | bytes 1572872 | tf_op jit(solution)/shard_map/ppermute | solution.py:17
  12.9 27.3 %collective-permute-start.3 = (bf16[1024,256]{1,0:T(8,128)(2,1)S(1)}, bf16[1024,256]{1,0:T(8,128)(2,1)S(1)}, u32[]{:S(2)}, u32[]{:S(2)}) collective-permute-start(bf16[1024,256]{1,0:T(8,128)(2,1)S(1)} %constant_dynamic-update-slice_fusion.refs_2_), channel_id=1, source_target_pairs={{0,128},{4,132},{8,136},{12,140},{16,144},{20,148},{24,152},{28,15... | collective-permute-start | bytes 1572872 | tf_op jit(solution)/shard_map/ppermute | solution.py:17
  17.6 22.7 %collective-permute-start.4 = (bf16[1024,256]{1,0:T(8,128)(2,1)S(1)}, bf16[1024,256]{1,0:T(8,128)(2,1)S(1)}, u32[]{:S(2)}, u32[]{:S(2)}) collective-permute-start(bf16[1024,256]{1,0:T(8,128)(2,1)S(1)} %constant_dynamic-update-slice_fusion.refs_2_), channel_id=1, source_target_pairs={{0,256},{4,260},{8,264},{12,268},{16,272},{20,276},{24,280},{28,28... | collective-permute-start | bytes 1572872 | tf_op jit(solution)/shard_map/ppermute | solution.py:17
  21.9 18.4 %copy-start = (bf16[512,256]{1,0:T(8,128)(2,1)S(1)}, bf16[512,256]{1,0:T(8,128)(2,1)}, u32[]{:S(2)}) copy-start(bf16[512,256]{1,0:T(8,128)(2,1)} %refs_1_.3) | copy-start | bytes 786436
  21.9 18.3 %copy-start.1 = (s32[256]{0:T(256)S(1)}, s32[256]{0:T(256)}, u32[]{:S(2)}) copy-start(s32[256]{0:T(256)} %refs_0_.3) | copy-start | bytes 3076
  21.9 7.8 %collective-permute-start.1 = (bf16[512,256]{1,0:T(8,128)(2,1)S(1)}, bf16[512,256]{1,0:T(8,128)(2,1)S(1)}, u32[]{:S(2)}, u32[]{:S(2)}) collective-permute-start(bf16[512,256]{1,0:T(8,128)(2,1)S(1)} %bitcast.14), channel_id=1, source_target_pairs={{4,8},{8,4},{12,16},{16,12},{20,24},{24,20},{28,32},{32,28},{36,40... | collective-permute-start | bytes 786440 | tf_op jit(solution)/shard_map/ppermute | solution.py:27
  29.8 23.4 %collective-permute-start.5 = (bf16[1024,256]{1,0:T(8,128)(2,1)S(1)}, bf16[1024,256]{1,0:T(8,128)(2,1)S(1)}, u32[]{:S(2)}, u32[]{:S(2)}) collective-permute-start(bf16[1024,256]{1,0:T(8,128)(2,1)S(1)} %constant_dynamic-update-slice_fusion.refs_2_), channel_id=1, source_target_pairs={{0,8},{4,12},{8,0},{12,4},{16,24},{20,28},{24,16},{28,20},{32,40},... | collective-permute-start | bytes 1572872 | tf_op jit(solution)/shard_map/ppermute | solution.py:17
  33.0 51.1 %collective-permute-start.6 = (bf16[1024,256]{1,0:T(8,128)(2,1)S(1)}, bf16[1024,256]{1,0:T(8,128)(2,1)S(1)}, u32[]{:S(2)}, u32[]{:S(2)}) collective-permute-start(bf16[1024,256]{1,0:T(8,128)(2,1)S(1)} %constant_dynamic-update-slice_fusion.refs_2_), channel_id=1, source_target_pairs={{0,16},{4,20},{8,24},{12,28},{16,0},{20,4},{24,8},{28,12},{32,48},... | collective-permute-start | bytes 1572872 | tf_op jit(solution)/shard_map/ppermute | solution.py:17
  38.3 45.9 %collective-permute-start.7 = (bf16[1024,256]{1,0:T(8,128)(2,1)S(1)}, bf16[1024,256]{1,0:T(8,128)(2,1)S(1)}, u32[]{:S(2)}, u32[]{:S(2)}) collective-permute-start(bf16[1024,256]{1,0:T(8,128)(2,1)S(1)} %constant_dynamic-update-slice_fusion.refs_2_), channel_id=1, source_target_pairs={{0,32},{4,36},{8,40},{12,44},{16,48},{20,52},{24,56},{28,60},{32,0... | collective-permute-start | bytes 1572872 | tf_op jit(solution)/shard_map/ppermute | solution.py:17
  84.2 5.5 %copy-start.2 = (bf16[256,1024]{1,0:T(8,128)(2,1)S(1)}, bf16[256,1024]{1,0:T(8,128)(2,1)}, u32[]{:S(2)}) copy-start(bf16[256,1024]{1,0:T(8,128)(2,1)} %param.9) | copy-start | bytes 1572868
Sparse Core Ops, SparseCore 0:
  89.8 42.2 all-gather.2

commit v2 on v1

v2 whole, which is shorter than its diff:
```python
import math

import jax
import jax.numpy as jnp
from jax import lax
from jax.experimental import pallas as pl
from jax.experimental.pallas import tpu as pltpu
from jax.sharding import PartitionSpec as P

HD = 64
BLOCK = 256
MASKED = -1e30


def flat_exchange(value, axis, mask):
    pairs = [(source, source ^ mask) for source in range(lax.axis_size(axis))]
    return lax.ppermute(value, axis, pairs)


def halo_exchange(value, axis):
    count = lax.axis_size(axis)
    pairs = []
    for source in range(count):
        target = source + 1 if source % 2 else source - 1
        if 0 <= target < count:
            pairs.append((source, target))
    return lax.ppermute(value, axis, pairs)


def after(value, *others):
    return lax.optimization_barrier((value, *others))[0]


def stacked_heads(q, heads):
    lane = lax.broadcasted_iota(jnp.int32, q.shape, 1)
    zero = jnp.zeros_like(q)
    return jnp.concatenate(
        [jnp.where((lane >= h * HD) & (lane < (h + 1) * HD), q, zero) for h in range(heads)], axis=0
    )


def fold(pieces, q, scores, scale, heads, m0, l0, acc0):
    qs = stacked_heads(q, heads)
    rows = qs.shape[0]
    half = rows // 2
    part = m0
    for at, (keys, _, bias) in enumerate(pieces):
        s = lax.dot_general(qs, keys(), (((1,), (1,)), ((), ())), preferred_element_type=jnp.float32)
        scores[at] = s
        top = jnp.maximum(s[:, :128], s[:, 128:]) + bias
        part = top if part is None else jnp.maximum(part, top)
    m = jnp.max(part, axis=1, keepdims=True)
    if l0 is None:
        total, acc_low, acc_high = None, None, None
    else:
        shrink = jnp.exp2((m0 - m) * scale)
        total = l0 * shrink
        acc_low = acc0[:half] * shrink[:half]
        acc_high = acc0[half:] * shrink[half:]
    for at, (_, values, bias) in enumerate(pieces):
        p = jnp.exp2((scores[at] - (m - bias)) * scale)
        add = p[:, :128] + p[:, 128:]
        total = add if total is None else total + add
        w = p.astype(jnp.bfloat16)
        v = values()
        low = jnp.dot(w[:half], v[:, :128], preferred_element_type=jnp.float32)
        high = jnp.dot(w[half:], v[:, 128:], preferred_element_type=jnp.float32)
        acc_low = low if acc_low is None else acc_low + low
        acc_high = high if acc_high is None else acc_high + high
    return m, total, jnp.concatenate([acc_low, acc_high], axis=0)


def bias_of(keep_ref, block, count):
    safe = jnp.clip(block, 0, count - 1)
    ok = (block >= 0) & (block < count) & (keep_ref[safe] == 1)
    return jnp.where(ok, 0.0, MASKED)


def part_of(ref, start):
    return (
        lambda: ref[pl.ds(start, BLOCK)],
        lambda: ref[pl.ds(pl.multiple_of(start + BLOCK, BLOCK), BLOCK)],
    )


def attend_kernel(scale, heads, local, plan, stateful, finish, keep_ref, q_ref, *refs):
    arrays = 1 + max(max(array) if isinstance(array, tuple) else array for _, array, _, _ in plan)
    sources, refs = refs[:arrays], refs[arrays:]
    m0, l0, acc0 = None, None, None
    if stateful:
        m0, l0, acc0 = (ref[...] for ref in refs[:3])
        refs = refs[3:]
    if finish:
        w_ref, out_ref, scores, near = refs
    else:
        m_ref, l_ref, acc_ref, scores, near = refs
    count = keep_ref.shape[0]
    rank = lax.axis_index("seq")
    block = rank * 2 + local
    pieces = []
    for what, array, start, number in plan:
        if what == "near":
            core_ref, halo_ref = sources[array[0]], sources[array[1]]
            mine = lax.rem(rank, 2) == local

            @pl.when(mine)
            def _():
                near[...] = halo_ref[...]

            @pl.when(jnp.logical_not(mine))
            def _():
                near[...] = core_ref[start : start + 2 * BLOCK]

            pieces.append((*part_of(near, 0), bias_of(keep_ref, block + number, count)))
        elif what == "self":
            pieces.append((*part_of(sources[array], start), 0.0))
        else:
            pieces.append((*part_of(sources[array], start), bias_of(keep_ref, block ^ number, count)))
    q = q_ref[local * BLOCK : (local + 1) * BLOCK]
    m, total, acc = fold(pieces, q, scores, scale, heads, m0, l0, acc0)
    if not finish:
        m_ref[...] = jnp.broadcast_to(m, m_ref.shape)
        l_ref[...] = total
        acc_ref[...] = acc
        return
    mixed = acc / jnp.sum(total, axis=1, keepdims=True)
    lane = lax.broadcasted_iota(jnp.int32, (BLOCK, 128), 1)
    joined = []
    for pair in range(2):
        first = mixed[2 * pair * BLOCK : (2 * pair + 1) * BLOCK]
        second = mixed[(2 * pair + 1) * BLOCK : (2 * pair + 2) * BLOCK]
        joined.append(jnp.where(lane < HD, first, second))
    attended = jnp.concatenate(joined, axis=1).astype(jnp.bfloat16)
    groups, _, columns = out_ref.shape
    for group in range(groups):
        w = w_ref[:, group * columns : (group + 1) * columns]
        out_ref[group] = jnp.dot(attended, w, preferred_element_type=jnp.float32).astype(out_ref.dtype)


def attend(name, block_keep, queries, local, sources, plan, state=None, w_out=None, groups=4):
    width = queries.shape[1]
    heads = width // HD
    stacked = heads * BLOCK
    scale = 1.0 / math.sqrt(HD) * math.log2(math.e)
    vmem = pl.BlockSpec(memory_space=pltpu.VMEM)
    smem = pl.BlockSpec(memory_space=pltpu.SMEM)
    finish = w_out is not None
    if finish:
        shape = jax.ShapeDtypeStruct((groups, BLOCK, w_out.shape[1] // groups), jnp.bfloat16)
        specs = vmem
    else:
        shape = [jax.ShapeDtypeStruct((stacked, 128), jnp.float32)] * 3
        specs = [vmem] * 3
    given = [block_keep, queries, *sources, *(state or ()), *((w_out,) if finish else ())]
    return pl.pallas_call(
        lambda *refs: attend_kernel(scale, heads, local, plan, state is not None, finish, *refs),
        out_shape=shape,
        in_specs=[smem] + [vmem] * (len(given) - 1),
        out_specs=specs,
        scratch_shapes=[
            pltpu.VMEM((len(plan), stacked, BLOCK), jnp.float32),
            pltpu.VMEM((2 * BLOCK, width), jnp.bfloat16),
        ],
        compiler_params=pltpu.CompilerParams(vmem_limit_bytes=18 << 20),
        cost_estimate=pl.CostEstimate(
            flops=len(plan) * 4 * stacked * BLOCK * width,
            transcendentals=len(plan) * stacked * BLOCK,
            bytes_accessed=len(plan) * 2 * BLOCK * width * 2,
        ),
        name=name,
    )(*given)


def per_device(queries, keys, values, block_keep, w_out):
    parts = [
        jnp.concatenate([keys[at : at + BLOCK], values[at : at + BLOCK]], axis=0) for at in (0, BLOCK)
    ]
    packed = jnp.concatenate(parts, axis=0)
    side = lax.rem(lax.axis_index("seq"), 2)
    edge = jnp.where(side == 1, parts[1], parts[0])
    y2 = [flat_exchange(part, "seq", 1 << 2) for part in parts]
    y1 = flat_exchange(packed, "seq", 1 << 1)
    x2 = flat_exchange(packed, "seq", 1 << 5)
    x1 = flat_exchange(packed, "seq", 1 << 4)
    y4 = [flat_exchange(part, "seq", (1 << 2) | (1 << 3)) for part in y2]
    core = flat_exchange(after(packed, x2), "seq", 1)
    z1 = flat_exchange(after(packed, x2), "seq", 1 << 6)
    halo = halo_exchange(after(edge, x1), "seq")

    full = [packed, core, halo, y1, x1, x2, z1]

    def common(local):
        here, there = 2 * BLOCK * local, 2 * BLOCK * (1 - local)
        return [
            ("self", 0, here, 0),
            ("xor", 0, there, 1),
            ("near", (1, 2), there, 2 * local - 1),
            ("xor", 1, here, 2),
            ("xor", 3, here, 4),
            ("xor", 4, here, 32),
            ("xor", 5, here, 64),
            ("xor", 6, here, 128),
        ]

    first = attend(
        "first",
        block_keep,
        after(queries, y2[1]),
        0,
        full + [y2[0], y4[0]],
        common(0) + [("xor", 7, 0, 8), ("xor", 8, 0, 16)],
        w_out=w_out,
    )
    out0 = lax.psum_scatter(first, "head", scatter_dimension=0, tiled=False)
    state = attend(
        "second", block_keep, after(queries, first), 1, full + [y2[1]], common(1) + [("xor", 7, 0, 8)]
    )
    last = attend(
        "last", block_keep, queries, 1, [y4[1]], [("xor", 0, 0, 16)], state=state, w_out=w_out
    )
    spread = lax.all_to_all(last, "head", 0, 0, tiled=False)
    out1 = jnp.sum(spread.astype(jnp.float32), axis=0).astype(jnp.bfloat16)
    return jnp.concatenate([out0, out1], axis=0)


def solution(mesh):
    placed = (P("seq", "head"), P("seq", "head"), P("seq", "head"), P(), P("head", None))
    return jax.shard_map(
        per_device, mesh=mesh, in_specs=placed, out_specs=P("seq", "head"), check_vma=False
    )
```

time: 142 us -> 120 us (0.85)
  the two profiles are of different devices: /device:TPU:56 before, /device:TPU:4 now
where the time goes in v2:
time: 120 us
  starting transfers between devices  35.9 us (30%)
  blocking collectives  33.1 us (28%)
  waiting for transfers between devices  15.6 us (13%)
  between operations  13.6 us (11%)
  Pallas kernels  13.3 us (11%)
  local copies, waits for them, and re-layouts  6.48 us (5%)
  other arithmetic  1.85 us (2%)
    ppermute x9, starting transfers between devices, flat_exchange(): return lax.ppermute(value, axis, pairs)  34 us
    all_to_all x1, blocking collectives, per_device(): spread = lax.all_to_all(last, 'head', 0, 0, tiled=False)  33.1 us
    ppermute x9, waiting for transfers between devices, flat_exchange(): return lax.ppermute(value, axis, pairs)  14.2 us
    pallas_call x3, Pallas kernels, attend(): pl.pallas_call(lambda *refs: attend_kernel(scale, heads, local, plan, sta...  13.3 us
    unnamed x18, local copies, waits for them, and re-layouts  5.36 us
  transfers between devices with their start and end apart: 11, of which 5 were waited for; matrix products, arithmetic and copies ran while one was open for 0% of the time, Pallas kernels for 11%

profile of v2, /device:TPU:4, one launch (start us, length us, event | category | flops | bytes accessed | tf_op | source)
XLA Modules:
  0.0 119.8 jit_solution(1610776761788854602)
XLA Ops:
  6.5 0.0 reduce-scatter.2.cloned.1.call-start
  6.5 1.1 fusion
  7.7 7.8 %collective-permute-start.1 = (bf16[1024,256]{1,0:T(8,128)(2,1)S(1)}, bf16[1024,256]{1,0:T(8,128)(2,1)S(1)}, u32[]{:S(2)}, u32[]{:S(2)}) collective-permute-start(bf16[1024,256]{1,0:T(8,128)(2,1)S(1)} %pad_maximum_fusion.refs_2_), channel_id=1, source_target_pairs={{0,128},{4,132},{8,136},{12,140},{16,144},{20,148},{24,152},{28,15... | collective-permute-start | bytes 1572872 | tf_op jit(solution)/shard_map/ppermute | solution.py:17
  15.5 1.9 %collective-permute-start.3 = (bf16[1024,256]{1,0:T(8,128)(2,1)S(1)}, bf16[1024,256]{1,0:T(8,128)(2,1)S(1)}, u32[]{:S(2)}, u32[]{:S(2)}) collective-permute-start(bf16[1024,256]{1,0:T(8,128)(2,1)S(1)} %pad_maximum_fusion.refs_2_), channel_id=1, source_target_pairs={{0,64},{4,68},{8,72},{12,76},{16,80},{20,84},{24,88},{28,92},{32,9... | collective-permute-start | bytes 1572872 | tf_op jit(solution)/shard_map/ppermute | solution.py:17
  17.4 0.0 copy-start
  17.5 0.0 copy-start.1
  17.5 0.1 pad_maximum_fusion.2
  17.6 2.1 %collective-permute-start.7 = (bf16[512,256]{1,0:T(8,128)(2,1)S(1)}, bf16[512,256]{1,0:T(8,128)(2,1)S(1)}, u32[]{:S(2)}, u32[]{:S(2)}) collective-permute-start(bf16[512,256]{1,0:T(8,128)(2,1)S(1)} %get-tuple-element.19), channel_id=1, source_target_pairs={{0,16},{4,20},{8,24},{12,28},{16,0},{20,4},{24,8},{28,12},{32,48},... | collective-permute-start | bytes 786440 | tf_op jit(solution)/shard_map/ppermute | solution.py:17
  19.6 2.8 %collective-permute-start.5 = (bf16[1024,256]{1,0:T(8,128)(2,1)S(1)}, bf16[1024,256]{1,0:T(8,128)(2,1)S(1)}, u32[]{:S(2)}, u32[]{:S(2)}) collective-permute-start(bf16[1024,256]{1,0:T(8,128)(2,1)S(1)} %pad_maximum_fusion.refs_2_), channel_id=1, source_target_pairs={{0,8},{4,12},{8,0},{12,4},{16,24},{20,28},{24,16},{28,20},{32,40},... | collective-permute-start | bytes 1572872 | tf_op jit(solution)/shard_map/ppermute | solution.py:17
  22.4 0.0 copy-start.2
  22.4 4.0 %collective-permute-start = (bf16[512,256]{1,0:T(8,128)(2,1)S(1)}, bf16[512,256]{1,0:T(8,128)(2,1)S(1)}, u32[]{:S(2)}, u32[]{:S(2)}) collective-permute-start(bf16[512,256]{1,0:T(8,128)(2,1)S(1)} %get-tuple-element.21), channel_id=1, source_target_pairs={{0,16},{4,20},{8,24},{12,28},{16,0},{20,4},{24,8},{28,12},{32,48},... | collective-permute-start | bytes 786440 | tf_op jit(solution)/shard_map/ppermute | solution.py:17
  26.4 1.9 %collective-permute-done.1.refs_7_ = bf16[1024,256]{1,0:T(8,128)(2,1)S(1)} collective-permute-done((bf16[1024,256]{1,0:T(8,128)(2,1)S(1)}, bf16[1024,256]{1,0:T(8,128)(2,1)S(1)}, u32[]{:S(2)}, u32[]{:S(2)}) %collective-permute-start.1) | collective-permute-done | bytes 524320 | tf_op jit(solution)/shard_map/ppermute | solution.py:17
  28.3 1.9 %collective-permute-start.2 = (bf16[1024,256]{1,0:T(8,128)(2,1)S(1)}, bf16[1024,256]{1,0:T(8,128)(2,1)S(1)}, u32[]{:S(2)}, u32[]{:S(2)}) collective-permute-start(bf16[1024,256]{1,0:T(8,128)(2,1)S(1)} %pad_maximum_fusion.refs_2_), channel_id=1, source_target_pairs={{0,4},{4,0},{8,12},{12,8},{16,20},{20,16},{24,28},{28,24},{32,36},... | collective-permute-start | bytes 1572872 | tf_op jit(solution)/shard_map/ppermute | solution.py:17
  30.3 1.3 %collective-permute-done.7.refs_9_ = bf16[512,256]{1,0:T(8,128)(2,1)S(1)} collective-permute-done((bf16[512,256]{1,0:T(8,128)(2,1)S(1)}, bf16[512,256]{1,0:T(8,128)(2,1)S(1)}, u32[]{:S(2)}, u32[]{:S(2)}) %collective-permute-start.7) | collective-permute-done | bytes 262176 | tf_op jit(solution)/shard_map/ppermute | solution.py:17
  31.6 4.3 %collective-permute-start.6 = (bf16[1024,256]{1,0:T(8,128)(2,1)S(1)}, bf16[1024,256]{1,0:T(8,128)(2,1)S(1)}, u32[]{:S(2)}, u32[]{:S(2)}) collective-permute-start(bf16[1024,256]{1,0:T(8,128)(2,1)S(1)} %pad_maximum_fusion.refs_2_), channel_id=1, source_target_pairs={{0,256},{4,260},{8,264},{12,268},{16,272},{20,276},{24,280},{28,28... | collective-permute-start | bytes 1572872 | tf_op jit(solution)/shard_map/ppermute | solution.py:17
  35.9 0.0 collective-permute-done.3.refs_6_
  35.9 5.4 %collective-permute-start.8 = (bf16[512,256]{1,0:T(8,128)(2,1)S(1)}, bf16[512,256]{1,0:T(8,128)(2,1)S(1)}, u32[]{:S(2)}, u32[]{:S(2)}) collective-permute-start(bf16[512,256]{1,0:T(8,128)(2,1)S(1)} %collective-permute-done.7.refs_9_), channel_id=1, source_target_pairs={{0,48},{4,52},{8,56},{12,60},{16,32},{20,36},{24,40},{28,44},{32,1... | collective-permute-start | bytes 786440 | tf_op jit(solution)/shard_map/ppermute | solution.py:17
  41.2 4.1 %collective-permute-done.refs_9_ = bf16[512,256]{1,0:T(8,128)(2,1)S(1)} collective-permute-done((bf16[512,256]{1,0:T(8,128)(2,1)S(1)}, bf16[512,256]{1,0:T(8,128)(2,1)S(1)}, u32[]{:S(2)}, u32[]{:S(2)}) %collective-permute-start) | collective-permute-done | bytes 262176 | tf_op jit(solution)/shard_map/ppermute | solution.py:17
  45.3 1.9 %collective-permute-start.4 = (bf16[512,256]{1,0:T(8,128)(2,1)S(1)}, bf16[512,256]{1,0:T(8,128)(2,1)S(1)}, u32[]{:S(2)}, u32[]{:S(2)}) collective-permute-start(bf16[512,256]{1,0:T(8,128)(2,1)S(1)} %get-tuple-element.14), channel_id=1, source_target_pairs={{4,8},{8,4},{12,16},{16,12},{20,24},{24,20},{28,32},{32,28},{36,40... | collective-permute-start | bytes 786440 | tf_op jit(solution)/shard_map/ppermute | solution.py:27
  47.2 6.9 %collective-permute-done.8.refs_10_ = bf16[512,256]{1,0:T(8,128)(2,1)S(1)} collective-permute-done((bf16[512,256]{1,0:T(8,128)(2,1)S(1)}, bf16[512,256]{1,0:T(8,128)(2,1)S(1)}, u32[]{:S(2)}, u32[]{:S(2)}) %collective-permute-start.8) | collective-permute-done | bytes 262176 | tf_op jit(solution)/shard_map/ppermute | solution.py:17
  54.1 3.9 %collective-permute-start.9 = (bf16[512,256]{1,0:T(8,128)(2,1)S(1)}, bf16[512,256]{1,0:T(8,128)(2,1)S(1)}, u32[]{:S(2)}, u32[]{:S(2)}) collective-permute-start(bf16[512,256]{1,0:T(8,128)(2,1)S(1)} %collective-permute-done.refs_9_), channel_id=1, source_target_pairs={{0,48},{4,52},{8,56},{12,60},{16,32},{20,36},{24,40},{28,44},{32,1... | collective-permute-start | bytes 786440 | tf_op jit(solution)/shard_map/ppermute | solution.py:17
  58.0 0.0 collective-permute-done.5.refs_5_
  58.0 0.0 collective-permute-done.4.refs_4_
  58.0 0.0 collective-permute-done.2.refs_3_
  58.1 0.0 collective-permute-done.6.refs_8_
  58.1 0.0 copy-done
  58.1 0.0 copy-done.1
  58.1 0.0 copy-done.2
  58.1 5.9 %first.1 = bf16[4,256,256]{2,1,0:T(8,128)(2,1)} custom-call(s32[256]{0:T(256)S(1)} %copy-done.2, bf16[512,256]{1,0:T(8,128)(2,1)S(1)} %copy-done.1, bf16[1024,256]{1,0:T(8,128)(2,1)S(1)} %pad_maximum_fusion.refs_2_, bf16[1024,256]{1,0:T(8,128)(2,1)S(1)} %collective-permute-done.2.refs_3_, bf16[512,256]{1,0:T(8,128)(2,1)S(1)} %collective-permute-done.4.refs_4_, ...), custom_call_target="tpu_custom_call" | custom-call | flops 2684354560 | bytes 2621440 | tf_op jit(solution)/shard_map/first/pallas_call | solution.py:155
  64.0 0.0 copy-start.3
  64.0 0.8 copy-done.3
  64.8 0.0 copy-start.5
  64.8 0.8 copy-done.5
  65.6 0.0 copy-start.7
  65.6 0.7 copy-done.7
  66.3 0.0 reduce-scatter.2.cloned.1.call-update
  66.4 0.0 copy-start.4
  66.4 1.0 copy-done.4
  67.4 0.0 copy-start.6
  67.4 1.0 copy-done.6
  68.5 0.9 copy-done.8
  69.4 5.9 %second.1 = (f32[1024,128]{1,0:T(8,128)S(1)}, f32[1024,128]{1,0:T(8,128)S(1)}, f32[1024,128]{1,0:T(8,128)S(1)}) custom-call(s32[256]{0:T(256)S(1)} %copy-done.2, bf16[512,256]{1,0:T(8,128)(2,1)S(1)} %copy-done.1, bf16[1024,256]{1,0:T(8,128)(2,1)S(1)} %pad_maximum_fusion.refs_2_, bf16[1024,256]{1,0:T(8,128)(2,1)S(1)} %copy-done.4, ...), custom_call_target="tpu_custom_call" | custom-call | flops 2415919104 | bytes 2359296 | tf_op jit(solution)/shard_map/second/pallas_call | solution.py:155
  75.3 0.0 collective-permute-done.9.refs_2_
  75.3 1.5 %last.1 = bf16[4,256,256]{2,1,0:T(8,128)(2,1)S(1)} custom-call(s32[256]{0:T(256)S(1)} %copy-done.2, bf16[512,256]{1,0:T(8,128)(2,1)S(1)} %copy-done.1, bf16[512,256]{1,0:T(8,128)(2,1)S(1)} %collective-permute-done.9.refs_2_, f32[1024,128]{1,0:T(8,128)S(1)} %get-tuple-element.16.refs_3_, f32[1024,128]{1,0:T(8,128)S(1)} %get-tuple-element.17.refs_4_, ...), custom_call_target="tpu_custom_call" | custom-call | flops 268435456 | bytes 262144 | tf_op jit(solution)/shard_map/last/pallas_call | solution.py:155
  76.8 33.1 %all_to_all.5 = bf16[4,256,256]{2,1,0:T(8,128)(2,1)S(1)} all-to-all(bf16[4,256,256]{2,1,0:T(8,128)(2,1)S(1)} %last.1), channel_id=1, replica_groups=mesh['seq'=128,'head'=4] {'head'}, dimensions={0} | all-to-all | bytes 1048576 | tf_op jit(solution)/shard_map/all_to_all | solution.py:221
  109.8 0.1 reduce_sum.12
  109.9 1.4 %reduce-scatter.2.cloned.1.call-done = bf16[1,256,256]{2,1,0:T(8,128)(2,1)} async-done(((bf16[4,256,256]{2,1,0:T(8,128)(2,1)}), bf16[1,256,256]{2,1,0:T(8,128)(2,1)}) %reduce-scatter.2.cloned.1.call-update) | async-done | bytes 131088 | tf_op jit(solution)/shard_map/reduce_scatter | solution.py:214
  111.3 1.6 %pad_maximum_fusion.3 = bf16[512,256]{1,0:T(8,128)(2,1)} fusion(bf16[256,256]{1,0:T(8,128)(2,1)S(1)} %reduce_sum.12, bf16[256,256]{1,0:T(8,128)(2,1)} %bitcast.1), kind=kLoop, calls=%fused_computation.3 | loop fusion | flops 524288 | bytes 524288 | tf_op jit(solution)/shard_map/concatenate | solution.py:223
  (2 shorter events, 0.0 us)
Async XLA Ops:
  6.5 104.8 %reduce-scatter.2.cloned.1.call-start = ((), (), s32[]{:S(2)}) async-start(), calls=%async_computation.2 | async-start | bytes 655360 | tf_op jit(solution)/shard_map/reduce_scatter | solution.py:214
  7.7 20.6 %collective-permute-start.1 = (bf16[1024,256]{1,0:T(8,128)(2,1)S(1)}, bf16[1024,256]{1,0:T(8,128)(2,1)S(1)}, u32[]{:S(2)}, u32[]{:S(2)}) collective-permute-start(bf16[1024,256]{1,0:T(8,128)(2,1)S(1)} %pad_maximum_fusion.refs_2_), channel_id=1, source_target_pairs={{0,128},{4,132},{8,136},{12,140},{16,144},{20,148},{24,152},{28,15... | collective-permute-start | bytes 1572872 | tf_op jit(solution)/shard_map/ppermute | solution.py:17
  15.5 20.4 %collective-permute-start.3 = (bf16[1024,256]{1,0:T(8,128)(2,1)S(1)}, bf16[1024,256]{1,0:T(8,128)(2,1)S(1)}, u32[]{:S(2)}, u32[]{:S(2)}) collective-permute-start(bf16[1024,256]{1,0:T(8,128)(2,1)S(1)} %pad_maximum_fusion.refs_2_), channel_id=1, source_target_pairs={{0,64},{4,68},{8,72},{12,76},{16,80},{20,84},{24,88},{28,92},{32,9... | collective-permute-start | bytes 1572872 | tf_op jit(solution)/shard_map/ppermute | solution.py:17
  17.4 40.6 %copy-start = (bf16[256,1024]{1,0:T(8,128)(2,1)S(1)}, bf16[256,1024]{1,0:T(8,128)(2,1)}, u32[]{:S(2)}) copy-start(bf16[256,1024]{1,0:T(8,128)(2,1)} %refs_6_.1) | copy-start | bytes 1572868
  17.5 40.6 %copy-start.1 = (bf16[512,256]{1,0:T(8,128)(2,1)S(1)}, bf16[512,256]{1,0:T(8,128)(2,1)}, u32[]{:S(2)}) copy-start(bf16[512,256]{1,0:T(8,128)(2,1)} %refs_1_.3) | copy-start | bytes 786436
  17.6 14.0 %collective-permute-start.7 = (bf16[512,256]{1,0:T(8,128)(2,1)S(1)}, bf16[512,256]{1,0:T(8,128)(2,1)S(1)}, u32[]{:S(2)}, u32[]{:S(2)}) collective-permute-start(bf16[512,256]{1,0:T(8,128)(2,1)S(1)} %get-tuple-element.19), channel_id=1, source_target_pairs={{0,16},{4,20},{8,24},{12,28},{16,0},{20,4},{24,8},{28,12},{32,48},... | collective-permute-start | bytes 786440 | tf_op jit(solution)/shard_map/ppermute | solution.py:17
  19.6 38.4 %collective-permute-start.5 = (bf16[1024,256]{1,0:T(8,128)(2,1)S(1)}, bf16[1024,256]{1,0:T(8,128)(2,1)S(1)}, u32[]{:S(2)}, u32[]{:S(2)}) collective-permute-start(bf16[1024,256]{1,0:T(8,128)(2,1)S(1)} %pad_maximum_fusion.refs_2_), channel_id=1, source_target_pairs={{0,8},{4,12},{8,0},{12,4},{16,24},{20,28},{24,16},{28,20},{32,40},... | collective-permute-start | bytes 1572872 | tf_op jit(solution)/shard_map/ppermute | solution.py:17
  22.4 35.7 %copy-start.2 = (s32[256]{0:T(256)S(1)}, s32[256]{0:T(256)}, u32[]{:S(2)}) copy-start(s32[256]{0:T(256)} %refs_0_.5) | copy-start | bytes 3076
  22.4 22.9 %collective-permute-start = (bf16[512,256]{1,0:T(8,128)(2,1)S(1)}, bf16[512,256]{1,0:T(8,128)(2,1)S(1)}, u32[]{:S(2)}, u32[]{:S(2)}) collective-permute-start(bf16[512,256]{1,0:T(8,128)(2,1)S(1)} %get-tuple-element.21), channel_id=1, source_target_pairs={{0,16},{4,20},{8,24},{12,28},{16,0},{20,4},{24,8},{28,12},{32,48},... | collective-permute-start | bytes 786440 | tf_op jit(solution)/shard_map/ppermute | solution.py:17
  28.3 29.7 %collective-permute-start.2 = (bf16[1024,256]{1,0:T(8,128)(2,1)S(1)}, bf16[1024,256]{1,0:T(8,128)(2,1)S(1)}, u32[]{:S(2)}, u32[]{:S(2)}) collective-permute-start(bf16[1024,256]{1,0:T(8,128)(2,1)S(1)} %pad_maximum_fusion.refs_2_), channel_id=1, source_target_pairs={{0,4},{4,0},{8,12},{12,8},{16,20},{20,16},{24,28},{28,24},{32,36},... | collective-permute-start | bytes 1572872 | tf_op jit(solution)/shard_map/ppermute | solution.py:17
  31.6 26.5 %collective-permute-start.6 = (bf16[1024,256]{1,0:T(8,128)(2,1)S(1)}, bf16[1024,256]{1,0:T(8,128)(2,1)S(1)}, u32[]{:S(2)}, u32[]{:S(2)}) collective-permute-start(bf16[1024,256]{1,0:T(8,128)(2,1)S(1)} %pad_maximum_fusion.refs_2_), channel_id=1, source_target_pairs={{0,256},{4,260},{8,264},{12,268},{16,272},{20,276},{24,280},{28,28... | collective-permute-start | bytes 1572872 | tf_op jit(solution)/shard_map/ppermute | solution.py:17
  35.9 18.2 %collective-permute-start.8 = (bf16[512,256]{1,0:T(8,128)(2,1)S(1)}, bf16[512,256]{1,0:T(8,128)(2,1)S(1)}, u32[]{:S(2)}, u32[]{:S(2)}) collective-permute-start(bf16[512,256]{1,0:T(8,128)(2,1)S(1)} %collective-permute-done.7.refs_9_), channel_id=1, source_target_pairs={{0,48},{4,52},{8,56},{12,60},{16,32},{20,36},{24,40},{28,44},{32,1... | collective-permute-start | bytes 786440 | tf_op jit(solution)/shard_map/ppermute | solution.py:17
  45.3 12.7 %collective-permute-start.4 = (bf16[512,256]{1,0:T(8,128)(2,1)S(1)}, bf16[512,256]{1,0:T(8,128)(2,1)S(1)}, u32[]{:S(2)}, u32[]{:S(2)}) collective-permute-start(bf16[512,256]{1,0:T(8,128)(2,1)S(1)} %get-tuple-element.14), channel_id=1, source_target_pairs={{4,8},{8,4},{12,16},{16,12},{20,24},{24,20},{28,32},{32,28},{36,40... | collective-permute-start | bytes 786440 | tf_op jit(solution)/shard_map/ppermute | solution.py:27
  54.1 21.2 %collective-permute-start.9 = (bf16[512,256]{1,0:T(8,128)(2,1)S(1)}, bf16[512,256]{1,0:T(8,128)(2,1)S(1)}, u32[]{:S(2)}, u32[]{:S(2)}) collective-permute-start(bf16[512,256]{1,0:T(8,128)(2,1)S(1)} %collective-permute-done.refs_9_), channel_id=1, source_target_pairs={{0,48},{4,52},{8,56},{12,60},{16,32},{20,36},{24,40},{28,44},{32,1... | collective-permute-start | bytes 786440 | tf_op jit(solution)/shard_map/ppermute | solution.py:17
  64.0 0.8 copy-start.3
  64.8 0.8 copy-start.5
  65.6 0.7 copy-start.7
  66.4 1.0 copy-start.4
  67.4 1.0 copy-start.6
  68.5 0.9 copy-start.8
Sparse Core Ops, SparseCore 0:
  66.5 44.7 reduce-scatter.1

commit v3 on v2

--- a/solution.py
+++ b/solution.py
@@ -83,7 +83,7 @@
     )
 
 
-def attend_kernel(scale, heads, local, plan, stateful, finish, keep_ref, q_ref, *refs):
+def attend_kernel(scale, heads, local, plan, stateful, finish, rotated, keep_ref, q_ref, *refs):
     arrays = 1 + max(max(array) if isinstance(array, tuple) else array for _, array, _, _ in plan)
     sources, refs = refs[:arrays], refs[arrays:]
     m0, l0, acc0 = None, None, None
@@ -91,7 +91,8 @@
         m0, l0, acc0 = (ref[...] for ref in refs[:3])
         refs = refs[3:]
     if finish:
-        w_ref, out_ref, scores, near = refs
+        w_ref, *outs, scores, near = refs
+        out_refs = outs if rotated else [outs[0].at[at] for at in range(outs[0].shape[0])]
     else:
         m_ref, l_ref, acc_ref, scores, near = refs
     count = keep_ref.shape[0]
@@ -131,13 +132,17 @@
         second = mixed[(2 * pair + 1) * BLOCK : (2 * pair + 2) * BLOCK]
         joined.append(jnp.where(lane < HD, first, second))
     attended = jnp.concatenate(joined, axis=1).astype(jnp.bfloat16)
-    groups, _, columns = out_ref.shape
-    for group in range(groups):
-        w = w_ref[:, group * columns : (group + 1) * columns]
-        out_ref[group] = jnp.dot(attended, w, preferred_element_type=jnp.float32).astype(out_ref.dtype)
-
-
-def attend(name, block_keep, queries, local, sources, plan, state=None, w_out=None, groups=4):
+    groups = len(out_refs)
+    columns = out_refs[0].shape[1]
+    for group, out_ref in enumerate(out_refs):
+        start = group * columns
+        if rotated:
+            start = pl.multiple_of(lax.rem(lax.axis_index("head") + group, groups) * columns, columns)
+        w = w_ref[:, pl.ds(start, columns)]
+        out_ref[...] = jnp.dot(attended, w, preferred_element_type=jnp.float32).astype(out_ref.dtype)
+
+
+def attend(name, block_keep, queries, local, sources, plan, state=None, w_out=None, rotated=False):
     width = queries.shape[1]
     heads = width // HD
     stacked = heads * BLOCK
@@ -146,14 +151,20 @@
     smem = pl.BlockSpec(memory_space=pltpu.SMEM)
     finish = w_out is not None
     if finish:
-        shape = jax.ShapeDtypeStruct((groups, BLOCK, w_out.shape[1] // groups), jnp.bfloat16)
-        specs = vmem
+        groups = lax.axis_size("head")
+        columns = w_out.shape[1] // groups
+        if rotated:
+            shape = [jax.ShapeDtypeStruct((BLOCK, columns), jnp.bfloat16)] * groups
+            specs = [vmem] * groups
+        else:
+            shape = jax.ShapeDtypeStruct((groups, BLOCK, columns), jnp.bfloat16)
+            specs = vmem
     else:
         shape = [jax.ShapeDtypeStruct((stacked, 128), jnp.float32)] * 3
         specs = [vmem] * 3
     given = [block_keep, queries, *sources, *(state or ()), *((w_out,) if finish else ())]
     return pl.pallas_call(
-        lambda *refs: attend_kernel(scale, heads, local, plan, state is not None, finish, *refs),
+        lambda *refs: attend_kernel(scale, heads, local, plan, state is not None, finish, rotated, *refs),
         out_shape=shape,
         in_specs=[smem] + [vmem] * (len(given) - 1),
         out_specs=specs,
@@ -161,12 +172,8 @@
             pltpu.VMEM((len(plan), stacked, BLOCK), jnp.float32),
             pltpu.VMEM((2 * BLOCK, width), jnp.bfloat16),
         ],
-        compiler_params=pltpu.CompilerParams(vmem_limit_bytes=18 << 20),
-        cost_estimate=pl.CostEstimate(
-            flops=len(plan) * 4 * stacked * BLOCK * width,
-            transcendentals=len(plan) * stacked * BLOCK,
-            bytes_accessed=len(plan) * 2 * BLOCK * width * 2,
-        ),
+        compiler_params=pltpu.CompilerParams(vmem_limit_bytes=(len(plan) + 7) << 20),
+        cost_estimate=pl.CostEstimate(flops=1 << 20, transcendentals=0, bytes_accessed=1 << 14),
         name=name,
     )(*given)
 
@@ -178,49 +185,61 @@
     packed = jnp.concatenate(parts, axis=0)
     side = lax.rem(lax.axis_index("seq"), 2)
     edge = jnp.where(side == 1, parts[1], parts[0])
-    y2 = [flat_exchange(part, "seq", 1 << 2) for part in parts]
+    y2 = flat_exchange(packed, "seq", 1 << 2)
+    y4a = flat_exchange(parts[0], "seq", 1 << 3)
     y1 = flat_exchange(packed, "seq", 1 << 1)
+    core = flat_exchange(packed, "seq", 1)
     x2 = flat_exchange(packed, "seq", 1 << 5)
-    x1 = flat_exchange(packed, "seq", 1 << 4)
-    y4 = [flat_exchange(part, "seq", (1 << 2) | (1 << 3)) for part in y2]
-    core = flat_exchange(after(packed, x2), "seq", 1)
+    x1 = flat_exchange(after(packed, core), "seq", 1 << 4)
     z1 = flat_exchange(after(packed, x2), "seq", 1 << 6)
-    halo = halo_exchange(after(edge, x1), "seq")
-
-    full = [packed, core, halo, y1, x1, x2, z1]
-
-    def common(local):
+    halo = halo_exchange(after(edge, core), "seq")
+    y4b = flat_exchange(after(parts[1], y1), "seq", 1 << 3)
+
+    def early(local, queries):
         here, there = 2 * BLOCK * local, 2 * BLOCK * (1 - local)
-        return [
+        plan = [
             ("self", 0, here, 0),
             ("xor", 0, there, 1),
-            ("near", (1, 2), there, 2 * local - 1),
             ("xor", 1, here, 2),
-            ("xor", 3, here, 4),
+            ("xor", 2, here, 4),
+            ("xor", 3, here, 8),
             ("xor", 4, here, 32),
             ("xor", 5, here, 64),
-            ("xor", 6, here, 128),
         ]
-
-    first = attend(
-        "first",
-        block_keep,
-        after(queries, y2[1]),
-        0,
-        full + [y2[0], y4[0]],
-        common(0) + [("xor", 7, 0, 8), ("xor", 8, 0, 16)],
-        w_out=w_out,
-    )
-    out0 = lax.psum_scatter(first, "head", scatter_dimension=0, tiled=False)
-    state = attend(
-        "second", block_keep, after(queries, first), 1, full + [y2[1]], common(1) + [("xor", 7, 0, 8)]
-    )
-    last = attend(
-        "last", block_keep, queries, 1, [y4[1]], [("xor", 0, 0, 16)], state=state, w_out=w_out
-    )
-    spread = lax.all_to_all(last, "head", 0, 0, tiled=False)
-    out1 = jnp.sum(spread.astype(jnp.float32), axis=0).astype(jnp.bfloat16)
-    return jnp.concatenate([out0, out1], axis=0)
+        sources = [packed, core, y1, y2, x1, x2]
+        return attend(f"early{local}", block_keep, queries, local, sources, plan)
+
+    def late(local, y4, state, queries, rotated):
+        here, there = 2 * BLOCK * local, 2 * BLOCK * (1 - local)
+        plan = [("near", (0, 1), there, 2 * local - 1), ("xor", 2, here, 128), ("xor", 3, 0, 16)]
+        sources = [core, halo, z1, y4]
+        return attend(
+            f"late{local}",
+            block_keep,
+            queries,
+            local,
+            sources,
+            plan,
+            state=state,
+            w_out=w_out,
+            rotated=rotated,
+        )
+
+    state0 = early(0, queries)
+    state1 = early(1, queries)
+    mine, *pieces = late(0, y4a, state0, after(queries, state1[0]), True)
+    groups = 1 + len(pieces)
+    moved = [
+        lax.ppermute(piece, "head", [(h, (h + hop + 1) % groups) for h in range(groups)])
+        for hop, piece in enumerate(pieces)
+    ]
+    shares = late(1, y4b, state1, after(queries, mine), False)
+    spread = lax.all_to_all(after(shares, *moved), "head", 0, 0, tiled=False)
+    total = mine.astype(jnp.float32)
+    for piece in moved:
+        total = total + piece.astype(jnp.float32)
+    outs = [total, jnp.sum(spread.astype(jnp.float32), axis=0)]
+    return jnp.concatenate([out.astype(jnp.bfloat16) for out in outs], axis=0)
 
 
 def solution(mesh):

time: 120 us -> 118 us (0.983)
  the two profiles are of different devices: /device:TPU:4 before, /device:TPU:2 now
where the time goes in v3:
time: 118 us; the launch traced here: 117 us
  starting transfers between devices  62.2 us (53%)
  waiting for transfers between devices  34.2 us (29%)
  Pallas kernels  16.9 us (14%)
  other arithmetic  1.95 us (2%)
  local copies, waits for them, and re-layouts  1.75 us (1%)
    ppermute x8, starting transfers between devices, flat_exchange(): return lax.ppermute(value, axis, pairs)  36 us
    ppermute x3, starting transfers between devices, per_device(): lax.ppermute(piece, 'head', [(h, (h + hop + 1) % groups) for h in range(g...  17.7 us
    pallas_call x4, Pallas kernels, attend(): pl.pallas_call(lambda *refs: attend_kernel(scale, heads, local, plan, sta...  16.9 us
    ppermute x8, waiting for transfers between devices, flat_exchange(): return lax.ppermute(value, axis, pairs)  15.2 us
    all_to_all x1, waiting for transfers between devices, per_device(): spread = lax.all_to_all(after(shares, *moved), 'head', 0, 0, tiled=False)  15 us
    all_to_all x1, starting transfers between devices, per_device(): spread = lax.all_to_all(after(shares, *moved), 'head', 0, 0, tiled=False)  5.61 us
    ppermute x3, waiting for transfers between devices, per_device(): lax.ppermute(piece, 'head', [(h, (h + hop + 1) % groups) for h in range(g...  3.89 us
    ppermute x1, starting transfers between devices, halo_exchange(): return lax.ppermute(value, axis, pairs)  2.98 us
  transfers between devices with their start and end apart: 13, of which 4 were waited for; matrix products, arithmetic and copies ran while one was open for 1% of the time, Pallas kernels for 14%

profile of v3, /device:TPU:2, one launch (start us, length us, event | category | flops | bytes accessed | tf_op | source)
XLA Modules:
  0.0 117.3 jit_solution(2094074047401184030)
XLA Ops:
  0.0 1.1 fusion
  1.1 0.0 copy-start.3
  1.2 0.6 copy-done.3
  1.8 1.9 %collective-permute-start = (bf16[1024,256]{1,0:T(8,128)(2,1)S(1)}, bf16[1024,256]{1,0:T(8,128)(2,1)S(1)}, u32[]{:S(2)}, u32[]{:S(2)}) collective-permute-start(bf16[1024,256]{1,0:T(8,128)(2,1)S(1)} %pad_maximum_fusion.refs_2_), channel_id=1, source_target_pairs={{0,4},{4,0},{8,12},{12,8},{16,20},{20,16},{24,28},{28,24},{32,36},... | collective-permute-start | bytes 1572872 | tf_op jit(solution)/shard_map/ppermute | solution.py:17
  3.7 4.0 %collective-permute-start.4 = (bf16[1024,256]{1,0:T(8,128)(2,1)S(1)}, bf16[1024,256]{1,0:T(8,128)(2,1)S(1)}, u32[]{:S(2)}, u32[]{:S(2)}) collective-permute-start(bf16[1024,256]{1,0:T(8,128)(2,1)S(1)} %pad_maximum_fusion.refs_2_), channel_id=1, source_target_pairs={{0,128},{4,132},{8,136},{12,140},{16,144},{20,148},{24,152},{28,15... | collective-permute-start | bytes 1572872 | tf_op jit(solution)/shard_map/ppermute | solution.py:17
  7.7 3.5 %collective-permute-start.1 = (bf16[1024,256]{1,0:T(8,128)(2,1)S(1)}, bf16[1024,256]{1,0:T(8,128)(2,1)S(1)}, u32[]{:S(2)}, u32[]{:S(2)}) collective-permute-start(bf16[1024,256]{1,0:T(8,128)(2,1)S(1)} %pad_maximum_fusion.refs_2_), channel_id=1, source_target_pairs={{0,8},{4,12},{8,0},{12,4},{16,24},{20,28},{24,16},{28,20},{32,40},... | collective-permute-start | bytes 1572872 | tf_op jit(solution)/shard_map/ppermute | solution.py:17
  11.2 4.5 %collective-permute-start.2 = (bf16[1024,256]{1,0:T(8,128)(2,1)S(1)}, bf16[1024,256]{1,0:T(8,128)(2,1)S(1)}, u32[]{:S(2)}, u32[]{:S(2)}) collective-permute-start(bf16[1024,256]{1,0:T(8,128)(2,1)S(1)} %pad_maximum_fusion.refs_2_), channel_id=1, source_target_pairs={{0,16},{4,20},{8,24},{12,28},{16,0},{20,4},{24,8},{28,12},{32,48},... | collective-permute-start | bytes 1572872 | tf_op jit(solution)/shard_map/ppermute | solution.py:17
  15.7 0.0 collective-permute-done.refs_3_.refs_2_
  15.8 3.3 %collective-permute-start.3 = (bf16[1024,256]{1,0:T(8,128)(2,1)S(1)}, bf16[1024,256]{1,0:T(8,128)(2,1)}, u32[]{:S(2)}, u32[]{:S(2)}) collective-permute-start(bf16[1024,256]{1,0:T(8,128)(2,1)S(1)} %pad_maximum_fusion.refs_2_), channel_id=1, source_target_pairs={{0,64},{4,68},{8,72},{12,76},{16,80},{20,84},{24,88},{28,92},{32,9... | collective-permute-start | bytes 1572872 | tf_op jit(solution)/shard_map/ppermute | solution.py:17
  19.1 2.7 %collective-permute-done.4.refs_7_ = bf16[1024,256]{1,0:T(8,128)(2,1)S(1)} collective-permute-done((bf16[1024,256]{1,0:T(8,128)(2,1)S(1)}, bf16[1024,256]{1,0:T(8,128)(2,1)S(1)}, u32[]{:S(2)}, u32[]{:S(2)}) %collective-permute-start.4) | collective-permute-done | bytes 524320 | tf_op jit(solution)/shard_map/ppermute | solution.py:17
  21.8 4.3 %collective-permute-start.6 = (bf16[1024,256]{1,0:T(8,128)(2,1)S(1)}, bf16[1024,256]{1,0:T(8,128)(2,1)S(1)}, u32[]{:S(2)}, u32[]{:S(2)}) collective-permute-start(bf16[1024,256]{1,0:T(8,128)(2,1)S(1)} %pad_maximum_fusion.refs_2_), channel_id=1, source_target_pairs={{0,256},{4,260},{8,264},{12,268},{16,272},{20,276},{24,280},{28,28... | collective-permute-start | bytes 1572872 | tf_op jit(solution)/shard_map/ppermute | solution.py:17
  26.1 0.0 copy-start
  26.1 1.0 pad_maximum_fusion.1
  27.2 7.7 %collective-permute-start.7 = (bf16[512,256]{1,0:T(8,128)(2,1)S(1)}, bf16[512,256]{1,0:T(8,128)(2,1)S(1)}, u32[]{:S(2)}, u32[]{:S(2)}) collective-permute-start(bf16[512,256]{1,0:T(8,128)(2,1)S(1)} %get-tuple-element.41), channel_id=1, source_target_pairs={{0,32},{4,36},{8,40},{12,44},{16,48},{20,52},{24,56},{28,60},{32,0... | collective-permute-start | bytes 786440 | tf_op jit(solution)/shard_map/ppermute | solution.py:17
  34.9 0.0 copy-start.2
  34.9 0.0 collective-permute-done.1.refs_4_
  34.9 3.0 %collective-permute-start.5 = (bf16[512,256]{1,0:T(8,128)(2,1)S(1)}, bf16[512,256]{1,0:T(8,128)(2,1)S(1)}, u32[]{:S(2)}, u32[]{:S(2)}) collective-permute-start(bf16[512,256]{1,0:T(8,128)(2,1)S(1)} %get-tuple-element.25), channel_id=1, source_target_pairs={{4,8},{8,4},{12,16},{16,12},{20,24},{24,20},{28,32},{32,28},{36,40... | collective-permute-start | bytes 786440 | tf_op jit(solution)/shard_map/ppermute | solution.py:27
  37.9 12.5 %collective-permute-done.2.refs_5_ = bf16[1024,256]{1,0:T(8,128)(2,1)S(1)} collective-permute-done((bf16[1024,256]{1,0:T(8,128)(2,1)S(1)}, bf16[1024,256]{1,0:T(8,128)(2,1)S(1)}, u32[]{:S(2)}, u32[]{:S(2)}) %collective-permute-start.2) | collective-permute-done | bytes 524320 | tf_op jit(solution)/shard_map/ppermute | solution.py:17
  50.4 6.7 %collective-permute-start.11 = (bf16[512,256]{1,0:T(8,128)(2,1)S(1)}, bf16[512,256]{1,0:T(8,128)(2,1)S(1)}, u32[]{:S(2)}, u32[]{:S(2)}) collective-permute-start(bf16[512,256]{1,0:T(8,128)(2,1)S(1)} %get-tuple-element.35), channel_id=1, source_target_pairs={{0,32},{4,36},{8,40},{12,44},{16,48},{20,52},{24,56},{28,60},{32,0... | collective-permute-start | bytes 786440 | tf_op jit(solution)/shard_map/ppermute | solution.py:17
  57.1 0.0 collective-permute-done.3.refs_6_
  57.2 0.0 copy-done
  57.2 0.0 copy-done.2
  57.2 5.2 %early1.1 = (f32[1024,128]{1,0:T(8,128)S(1)}, f32[1024,128]{1,0:T(8,128)S(1)}, f32[1024,128]{1,0:T(8,128)S(1)}) custom-call(s32[256]{0:T(256)S(1)} %copy-done.2, bf16[512,256]{1,0:T(8,128)(2,1)S(1)} %copy-done, bf16[1024,256]{1,0:T(8,128)(2,1)S(1)} %pad_maximum_fusion.refs_2_, bf16[1024,256]{1,0:T(8,128)(2,1)S(1)} %collective-permute-done.refs_3_.refs_2_, ...), custom_call_target="tpu_custom_call" | custom-call | flops 1048576 | bytes 16384 | tf_op jit(solution)/shard_map/early1/pallas_call | solution.py:166
  62.3 0.0 copy-start.1
  62.3 5.2 %early0.1 = (f32[1024,128]{1,0:T(8,128)S(1)}, f32[1024,128]{1,0:T(8,128)S(1)}, f32[1024,128]{1,0:T(8,128)S(1)}) custom-call(s32[256]{0:T(256)S(1)} %copy-done.2, bf16[512,256]{1,0:T(8,128)(2,1)S(1)} %copy-done, bf16[1024,256]{1,0:T(8,128)(2,1)S(1)} %pad_maximum_fusion.refs_2_, bf16[1024,256]{1,0:T(8,128)(2,1)S(1)} %collective-permute-done.refs_3_.refs_2_, ...), custom_call_target="tpu_custom_call" | custom-call | flops 1048576 | bytes 16384 | tf_op jit(solution)/shard_map/early0/pallas_call | solution.py:166
  67.6 0.0 collective-permute-done.7.refs_5_
  67.6 0.0 collective-permute-done.5.refs_3_
  67.6 0.0 collective-permute-done.6.refs_4_
  67.6 0.0 copy-done.1
  67.6 2.9 %late0.1 = (bf16[256,256]{1,0:T(8,128)(2,1)S(1)}, bf16[256,256]{1,0:T(8,128)(2,1)S(1)}, bf16[256,256]{1,0:T(8,128)(2,1)S(1)}, bf16[256,256]{1,0:T(8,128)(2,1)S(1)}) custom-call(s32[256]{0:T(256)S(1)} %copy-done.2, bf16[512,256]{1,0:T(8,128)(2,1)S(1)} %copy-done, bf16[1024,256]{1,0:T(8,128)(2,1)S(1)} %collective-permute-done.refs_3_.refs_2_, ...), custom_call_target="tpu_custom_call" | custom-call | flops 1048576 | bytes 16384 | tf_op jit(solution)/shard_map/late0/pallas_call | solution.py:166
  70.5 10.9 %collective-permute-start.10 = (bf16[256,256]{1,0:T(8,128)(2,1)S(1)}, bf16[256,256]{1,0:T(8,128)(2,1)S(1)}, u32[]{:S(2)}, u32[]{:S(2)}) collective-permute-start(bf16[256,256]{1,0:T(8,128)(2,1)S(1)} %get-tuple-element.33), channel_id=1, source_target_pairs={{0,3},{1,0},{2,1},{3,2},{4,7},{5,4},{6,5},{7,6},{8,11},{9,8},{10,9... | collective-permute-start | bytes 393224 | tf_op jit(solution)/shard_map/ppermute | solution.py:233
  81.4 1.9 %collective-permute-start.8 = (bf16[256,256]{1,0:T(8,128)(2,1)S(1)}, bf16[256,256]{1,0:T(8,128)(2,1)S(1)}, u32[]{:S(2)}, u32[]{:S(2)}) collective-permute-start(bf16[256,256]{1,0:T(8,128)(2,1)S(1)} %get-tuple-element.31), channel_id=1, source_target_pairs={{0,1},{1,2},{2,3},{3,0},{4,5},{5,6},{6,7},{7,4},{8,9},{9,10},{10,1... | collective-permute-start | bytes 393224 | tf_op jit(solution)/shard_map/ppermute | solution.py:233
  83.4 4.8 %collective-permute-start.9 = (bf16[256,256]{1,0:T(8,128)(2,1)S(1)}, bf16[256,256]{1,0:T(8,128)(2,1)S(1)}, u32[]{:S(2)}, u32[]{:S(2)}) collective-permute-start(bf16[256,256]{1,0:T(8,128)(2,1)S(1)} %get-tuple-element.32), channel_id=1, source_target_pairs={{0,2},{1,3},{2,0},{3,1},{4,6},{5,7},{6,4},{7,5},{8,10},{9,11},{10,... | collective-permute-start | bytes 393224 | tf_op jit(solution)/shard_map/ppermute | solution.py:233
  88.2 0.0 collective-permute-done.11.refs_5_
  88.2 3.7 %late1.1 = bf16[4,256,256]{2,1,0:T(8,128)(2,1)} custom-call(s32[256]{0:T(256)S(1)} %copy-done.2, bf16[512,256]{1,0:T(8,128)(2,1)S(1)} %copy-done, bf16[1024,256]{1,0:T(8,128)(2,1)S(1)} %collective-permute-done.refs_3_.refs_2_, bf16[512,256]{1,0:T(8,128)(2,1)S(1)} %collective-permute-done.5.refs_3_, bf16[1024,256]{1,0:T(8,128)(2,1)S(1)} %collective-permute-done.6.refs_4_, ...), custom_call_target="tpu_custom_call" | custom-call | flops 1048576 | bytes 16384 | tf_op jit(solution)/shard_map/late1/pallas_call | solution.py:166
  91.9 0.0 collective-permute-done.10
  91.9 3.9 %collective-permute-done.8 = bf16[256,256]{1,0:T(8,128)(2,1)S(1)} collective-permute-done((bf16[256,256]{1,0:T(8,128)(2,1)S(1)}, bf16[256,256]{1,0:T(8,128)(2,1)S(1)}, u32[]{:S(2)}, u32[]{:S(2)}) %collective-permute-start.8) | collective-permute-done | bytes 131104 | tf_op jit(solution)/shard_map/ppermute | solution.py:233
  95.8 0.0 collective-permute-done.9
  95.8 5.6 %all-to-all-start = ((bf16[4,256,256]{2,1,0:T(8,128)(2,1)}), bf16[4,256,256]{2,1,0:T(8,128)(2,1)S(1)}, u32[]{:S(2)}, u32[]{:S(2)}) async-start(bf16[4,256,256]{2,1,0:T(8,128)(2,1)} %late1.1), calls=%async_computation | async-start | bytes 1048576 | tf_op jit(solution)/shard_map/all_to_all | solution.py:237
  101.4 0.1 add_convert_fusion
  101.4 15.0 %all-to-all-done = bf16[4,256,256]{2,1,0:T(8,128)(2,1)S(1)} async-done(((bf16[4,256,256]{2,1,0:T(8,128)(2,1)}), bf16[4,256,256]{2,1,0:T(8,128)(2,1)S(1)}, u32[]{:S(2)}, u32[]{:S(2)}) %all-to-all-start) | async-done | bytes 524320 | tf_op jit(solution)/shard_map/all_to_all | solution.py:237
  116.5 0.1 reduce_sum.12
  116.6 0.7 pad_maximum_fusion.3
  (1 shorter events, 0.0 us)
Async XLA Ops:
  1.1 0.7 copy-start.3
  1.8 14.0 %collective-permute-start = (bf16[1024,256]{1,0:T(8,128)(2,1)S(1)}, bf16[1024,256]{1,0:T(8,128)(2,1)S(1)}, u32[]{:S(2)}, u32[]{:S(2)}) collective-permute-start(bf16[1024,256]{1,0:T(8,128)(2,1)S(1)} %pad_maximum_fusion.refs_2_), channel_id=1, source_target_pairs={{0,4},{4,0},{8,12},{12,8},{16,20},{20,16},{24,28},{28,24},{32,36},... | collective-permute-start | bytes 1572872 | tf_op jit(solution)/shard_map/ppermute | solution.py:17
  3.7 18.1 %collective-permute-start.4 = (bf16[1024,256]{1,0:T(8,128)(2,1)S(1)}, bf16[1024,256]{1,0:T(8,128)(2,1)S(1)}, u32[]{:S(2)}, u32[]{:S(2)}) collective-permute-start(bf16[1024,256]{1,0:T(8,128)(2,1)S(1)} %pad_maximum_fusion.refs_2_), channel_id=1, source_target_pairs={{0,128},{4,132},{8,136},{12,140},{16,144},{20,148},{24,152},{28,15... | collective-permute-start | bytes 1572872 | tf_op jit(solution)/shard_map/ppermute | solution.py:17
  7.7 27.2 %collective-permute-start.1 = (bf16[1024,256]{1,0:T(8,128)(2,1)S(1)}, bf16[1024,256]{1,0:T(8,128)(2,1)S(1)}, u32[]{:S(2)}, u32[]{:S(2)}) collective-permute-start(bf16[1024,256]{1,0:T(8,128)(2,1)S(1)} %pad_maximum_fusion.refs_2_), channel_id=1, source_target_pairs={{0,8},{4,12},{8,0},{12,4},{16,24},{20,28},{24,16},{28,20},{32,40},... | collective-permute-start | bytes 1572872 | tf_op jit(solution)/shard_map/ppermute | solution.py:17
  11.2 39.2 %collective-permute-start.2 = (bf16[1024,256]{1,0:T(8,128)(2,1)S(1)}, bf16[1024,256]{1,0:T(8,128)(2,1)S(1)}, u32[]{:S(2)}, u32[]{:S(2)}) collective-permute-start(bf16[1024,256]{1,0:T(8,128)(2,1)S(1)} %pad_maximum_fusion.refs_2_), channel_id=1, source_target_pairs={{0,16},{4,20},{8,24},{12,28},{16,0},{20,4},{24,8},{28,12},{32,48},... | collective-permute-start | bytes 1572872 | tf_op jit(solution)/shard_map/ppermute | solution.py:17
  15.8 41.4 %collective-permute-start.3 = (bf16[1024,256]{1,0:T(8,128)(2,1)S(1)}, bf16[1024,256]{1,0:T(8,128)(2,1)}, u32[]{:S(2)}, u32[]{:S(2)}) collective-permute-start(bf16[1024,256]{1,0:T(8,128)(2,1)S(1)} %pad_maximum_fusion.refs_2_), channel_id=1, source_target_pairs={{0,64},{4,68},{8,72},{12,76},{16,80},{20,84},{24,88},{28,92},{32,9... | collective-permute-start | bytes 1572872 | tf_op jit(solution)/shard_map/ppermute | solution.py:17
  21.8 45.8 %collective-permute-start.6 = (bf16[1024,256]{1,0:T(8,128)(2,1)S(1)}, bf16[1024,256]{1,0:T(8,128)(2,1)S(1)}, u32[]{:S(2)}, u32[]{:S(2)}) collective-permute-start(bf16[1024,256]{1,0:T(8,128)(2,1)S(1)} %pad_maximum_fusion.refs_2_), channel_id=1, source_target_pairs={{0,256},{4,260},{8,264},{12,268},{16,272},{20,276},{24,280},{28,28... | collective-permute-start | bytes 1572872 | tf_op jit(solution)/shard_map/ppermute | solution.py:17
  26.1 31.1 %copy-start = (bf16[512,256]{1,0:T(8,128)(2,1)S(1)}, bf16[512,256]{1,0:T(8,128)(2,1)}, u32[]{:S(2)}) copy-start(bf16[512,256]{1,0:T(8,128)(2,1)} %refs_1_.5) | copy-start | bytes 786436
  27.2 40.4 %collective-permute-start.7 = (bf16[512,256]{1,0:T(8,128)(2,1)S(1)}, bf16[512,256]{1,0:T(8,128)(2,1)S(1)}, u32[]{:S(2)}, u32[]{:S(2)}) collective-permute-start(bf16[512,256]{1,0:T(8,128)(2,1)S(1)} %get-tuple-element.41), channel_id=1, source_target_pairs={{0,32},{4,36},{8,40},{12,44},{16,48},{20,52},{24,56},{28,60},{32,0... | collective-permute-start | bytes 786440 | tf_op jit(solution)/shard_map/ppermute | solution.py:17
  34.9 22.3 %copy-start.2 = (s32[256]{0:T(256)S(1)}, s32[256]{0:T(256)}, u32[]{:S(2)}) copy-start(s32[256]{0:T(256)} %refs_0_.7) | copy-start | bytes 3076
  34.9 32.6 %collective-permute-start.5 = (bf16[512,256]{1,0:T(8,128)(2,1)S(1)}, bf16[512,256]{1,0:T(8,128)(2,1)S(1)}, u32[]{:S(2)}, u32[]{:S(2)}) collective-permute-start(bf16[512,256]{1,0:T(8,128)(2,1)S(1)} %get-tuple-element.25), channel_id=1, source_target_pairs={{4,8},{8,4},{12,16},{16,12},{20,24},{24,20},{28,32},{32,28},{36,40... | collective-permute-start | bytes 786440 | tf_op jit(solution)/shard_map/ppermute | solution.py:27
  50.4 37.8 %collective-permute-start.11 = (bf16[512,256]{1,0:T(8,128)(2,1)S(1)}, bf16[512,256]{1,0:T(8,128)(2,1)S(1)}, u32[]{:S(2)}, u32[]{:S(2)}) collective-permute-start(bf16[512,256]{1,0:T(8,128)(2,1)S(1)} %get-tuple-element.35), channel_id=1, source_target_pairs={{0,32},{4,36},{8,40},{12,44},{16,48},{20,52},{24,56},{28,60},{32,0... | collective-permute-start | bytes 786440 | tf_op jit(solution)/shard_map/ppermute | solution.py:17
  62.3 5.3 %copy-start.1 = (bf16[256,1024]{1,0:T(8,128)(2,1)S(1)}, bf16[256,1024]{1,0:T(8,128)(2,1)}, u32[]{:S(2)}) copy-start(bf16[256,1024]{1,0:T(8,128)(2,1)} %refs_9_.3) | copy-start | bytes 1572868
  70.5 21.4 %collective-permute-start.10 = (bf16[256,256]{1,0:T(8,128)(2,1)S(1)}, bf16[256,256]{1,0:T(8,128)(2,1)S(1)}, u32[]{:S(2)}, u32[]{:S(2)}) collective-permute-start(bf16[256,256]{1,0:T(8,128)(2,1)S(1)} %get-tuple-element.33), channel_id=1, source_target_pairs={{0,3},{1,0},{2,1},{3,2},{4,7},{5,4},{6,5},{7,6},{8,11},{9,8},{10,9... | collective-permute-start | bytes 393224 | tf_op jit(solution)/shard_map/ppermute | solution.py:233
  81.4 14.3 %collective-permute-start.8 = (bf16[256,256]{1,0:T(8,128)(2,1)S(1)}, bf16[256,256]{1,0:T(8,128)(2,1)S(1)}, u32[]{:S(2)}, u32[]{:S(2)}) collective-permute-start(bf16[256,256]{1,0:T(8,128)(2,1)S(1)} %get-tuple-element.31), channel_id=1, source_target_pairs={{0,1},{1,2},{2,3},{3,0},{4,5},{5,6},{6,7},{7,4},{8,9},{9,10},{10,1... | collective-permute-start | bytes 393224 | tf_op jit(solution)/shard_map/ppermute | solution.py:233
  83.4 12.4 %collective-permute-start.9 = (bf16[256,256]{1,0:T(8,128)(2,1)S(1)}, bf16[256,256]{1,0:T(8,128)(2,1)S(1)}, u32[]{:S(2)}, u32[]{:S(2)}) collective-permute-start(bf16[256,256]{1,0:T(8,128)(2,1)S(1)} %get-tuple-element.32), channel_id=1, source_target_pairs={{0,2},{1,3},{2,0},{3,1},{4,6},{5,7},{6,4},{7,5},{8,10},{9,11},{10,... | collective-permute-start | bytes 393224 | tf_op jit(solution)/shard_map/ppermute | solution.py:233
  95.8 20.7 %all-to-all-start = ((bf16[4,256,256]{2,1,0:T(8,128)(2,1)}), bf16[4,256,256]{2,1,0:T(8,128)(2,1)S(1)}, u32[]{:S(2)}, u32[]{:S(2)}) async-start(bf16[4,256,256]{2,1,0:T(8,128)(2,1)} %late1.1), calls=%async_computation | async-start | bytes 1048576 | tf_op jit(solution)/shard_map/all_to_all | solution.py:237

commit v4 on v2

v4 whole, which is shorter than its diff:
```python
import math

import jax
import jax.numpy as jnp
from jax import lax
from jax.experimental import pallas as pl
from jax.experimental.pallas import tpu as pltpu
from jax.sharding import PartitionSpec as P

HD = 64
BLOCK = 256
PAIR = 2 * BLOCK
MASKED = -1e30
COST = 4


def flat_exchange(value, axis, mask):
    pairs = [(source, source ^ mask) for source in range(lax.axis_size(axis))]
    return lax.ppermute(value, axis, pairs)


def halo_exchange(value, axis):
    count = lax.axis_size(axis)
    pairs = []
    for source in range(count):
        target = source + 1 if source % 2 else source - 1
        if 0 <= target < count:
            pairs.append((source, target))
    return lax.ppermute(value, axis, pairs)


def crosswise(value, axis, bits):
    mask = sum(1 << bit for bit in bits)
    groups = []
    for base in range(lax.axis_size(axis)):
        if base & mask == 0:
            groups.append([base | (i << bits[0]) for i in range(1 << len(bits))])
    return lax.all_gather(value, axis, axis_index_groups=groups)


def after(value, *others):
    return lax.optimization_barrier((value, *others))[0]


def stacked_heads(q, heads):
    lane = lax.broadcasted_iota(jnp.int32, q.shape, 1)
    zero = jnp.zeros_like(q)
    return jnp.concatenate(
        [jnp.where((lane >= h * HD) & (lane < (h + 1) * HD), q, zero) for h in range(heads)], axis=0
    )


def fold(pieces, q, scores, scale, heads, before):
    qs = stacked_heads(q, heads)
    half = qs.shape[0] // 2
    part = None
    for at, (keys, _, bias) in enumerate(pieces):
        s = lax.dot_general(qs, keys(), (((1,), (1,)), ((), ())), preferred_element_type=jnp.float32)
        scores[at] = s
        top = jnp.maximum(s[:, :128], s[:, 128:]) + bias
        part = top if part is None else jnp.maximum(part, top)
    total, acc_low, acc_high = None, None, None
    if before is None:
        m = jnp.max(part, axis=1, keepdims=True)
    else:
        m0, l0, acc0 = before()
        m = jnp.max(jnp.maximum(part, m0), axis=1, keepdims=True)
        shrink = jnp.exp2((m0 - m) * scale)
        total = l0 * shrink
        acc_low = acc0[:half] * shrink[:half]
        acc_high = acc0[half:] * shrink[half:]
    for at, (_, values, bias) in enumerate(pieces):
        p = jnp.exp2((scores[at] - (m - bias)) * scale)
        add = p[:, :128] + p[:, 128:]
        total = add if total is None else total + add
        w = p.astype(jnp.bfloat16)
        v = values()
        low = jnp.dot(w[:half], v[:, :128], preferred_element_type=jnp.float32)
        high = jnp.dot(w[half:], v[:, 128:], preferred_element_type=jnp.float32)
        acc_low = low if acc_low is None else acc_low + low
        acc_high = high if acc_high is None else acc_high + high
    return m, total, jnp.concatenate([acc_low, acc_high], axis=0)


def bias_of(keep_ref, block, count):
    safe = jnp.clip(block, 0, count - 1)
    ok = (block >= 0) & (block < count) & (keep_ref[safe] == 1)
    return jnp.where(ok, 0.0, MASKED)


def attend_kernel(scale, heads, local, plan, arrays, stateful, finish, keep_ref, q_ref, *refs):
    sources, refs = refs[:arrays], refs[arrays:]
    state, w_hbm = None, None
    if stateful:
        state, refs = refs[0], refs[1:]
    if finish:
        w_hbm, out_ref, *refs = refs
    else:
        state_out, *refs = refs
    scores, held, q_held, extra, sems = refs
    count = keep_ref.shape[0]
    rank = lax.axis_index("seq")
    block = rank * 2 + local
    q_copy = pltpu.make_async_copy(q_ref.at[pl.ds(local * BLOCK, BLOCK)], q_held, sems.at[len(plan)])
    q_copy.start()
    copies, biases = [], []
    for at, (what, array, start, number) in enumerate(plan):
        rows = pl.ds(start, PAIR)
        bias = 0.0
        if what == "near":
            mine = lax.rem(rank, 2) == local
            kept = pltpu.make_async_copy(sources[array[1]], held.at[at], sems.at[at])
            shared = pltpu.make_async_copy(sources[array[0]].at[rows], held.at[at], sems.at[at])
            pl.when(mine)(kept.start)
            pl.when(jnp.logical_not(mine))(shared.start)
            copies.append(kept)
            bias = bias_of(keep_ref, block + number, count)
        else:
            source = sources[array]
            if what == "across":
                crossed, level = number
                place = lax.rem(rank >> level, source.shape[0]) ^ crossed
                source = source.at[place]
                number = crossed << (level + 1)
            copies.append(pltpu.make_async_copy(source.at[rows], held.at[at], sems.at[at]))
            copies[-1].start()
            if what != "self":
                bias = bias_of(keep_ref, block ^ number, count)
        biases.append(bias)
    if stateful:
        state_copy = pltpu.make_async_copy(state, extra, sems.at[len(plan) + 1])
        state_copy.start()

    def keys_of(at):
        copies[at].wait()
        return held[at, :BLOCK]

    def before():
        state_copy.wait()
        return extra[0], extra[1], extra[2]

    pieces = [
        (lambda at=at: keys_of(at), lambda at=at: held[at, BLOCK:], biases[at]) for at in range(len(plan))
    ]
    q_copy.wait()
    m, total, acc = fold(pieces, q_held[...], scores, scale, heads, before if stateful else None)
    if not finish:
        extra[0] = jnp.broadcast_to(m, extra.shape[1:])
        extra[1] = total
        extra[2] = acc
        out_copy = pltpu.make_async_copy(extra, state_out, sems.at[len(plan) + 1])
        out_copy.start()
        out_copy.wait()
        return
    mixed = acc / jnp.sum(total, axis=1, keepdims=True)
    lane = lax.broadcasted_iota(jnp.int32, (BLOCK, 128), 1)
    joined = []
    for pair in range(2):
        first = mixed[2 * pair * BLOCK : (2 * pair + 1) * BLOCK]
        second = mixed[(2 * pair + 1) * BLOCK : (2 * pair + 2) * BLOCK]
        joined.append(jnp.where(lane < HD, first, second))
    attended = jnp.concatenate(joined, axis=1).astype(jnp.bfloat16)
    columns = out_ref.shape[2]
    for group in range(out_ref.shape[0]):
        w = w_hbm[:, group * columns : (group + 1) * columns]
        out_ref[group] = jnp.dot(attended, w, preferred_element_type=jnp.float32).astype(out_ref.dtype)


def attend(name, block_keep, queries, local, sources, plan, state=None, w_out=None):
    width = queries.shape[1]
    heads = width // HD
    stacked = heads * BLOCK
    scale = 1.0 / math.sqrt(HD) * math.log2(math.e)
    vmem = pl.BlockSpec(memory_space=pltpu.VMEM)
    smem = pl.BlockSpec(memory_space=pltpu.SMEM)
    hbm = pl.BlockSpec(memory_space=pltpu.HBM)
    finish = w_out is not None
    if finish:
        groups = lax.axis_size("head")
        shape = jax.ShapeDtypeStruct((groups, BLOCK, w_out.shape[1] // groups), jnp.bfloat16)
    else:
        shape = pltpu.HBM((3, stacked, 128), jnp.float32)
    far = [queries, *sources] if state is None else [queries, *sources, state]
    given = [block_keep, *(pltpu.with_memory_space_constraint(x, pltpu.HBM) for x in far)]
    specs = [smem] + [hbm] * len(far)
    if finish:
        given, specs = given + [w_out], specs + [vmem]
    return pl.pallas_call(
        lambda *refs: attend_kernel(
            scale, heads, local, plan, len(sources), state is not None, finish, *refs
        ),
        out_shape=shape,
        in_specs=specs,
        out_specs=vmem if finish else hbm,
        scratch_shapes=[
            pltpu.VMEM((len(plan), stacked, BLOCK), jnp.float32),
            pltpu.VMEM((len(plan), PAIR, width), jnp.bfloat16),
            pltpu.VMEM((BLOCK, width), jnp.bfloat16),
            pltpu.VMEM((3, stacked, 128), jnp.float32),
            pltpu.SemaphoreType.DMA((len(plan) + 2,)),
        ],
        compiler_params=pltpu.CompilerParams(vmem_limit_bytes=(2 * len(plan) + 12) << 20),
        cost_estimate=pl.CostEstimate(
            flops=len(plan) * 4 * stacked * BLOCK * width * COST,
            transcendentals=len(plan) * stacked * BLOCK,
            bytes_accessed=len(plan) * 2 * BLOCK * width * 2,
        ),
        name=name,
    )(*given)


def per_device(queries, keys, values, block_keep, w_out):
    parts = [
        jnp.concatenate([keys[at : at + BLOCK], values[at : at + BLOCK]], axis=0) for at in (0, BLOCK)
    ]
    packed = jnp.concatenate(parts, axis=0)
    side = lax.rem(lax.axis_index("seq"), 2)
    edge = jnp.where(side == 1, parts[1], parts[0])
    xs = crosswise(packed, "seq", (4, 5))
    y2a = flat_exchange(parts[0], "seq", 1 << 2)
    y2b = flat_exchange(after(parts[1], y2a), "seq", 1 << 2)
    y4a = flat_exchange(y2a, "seq", (1 << 2) | (1 << 3))
    y4b = flat_exchange(y2b, "seq", (1 << 2) | (1 << 3))
    core = flat_exchange(packed, "seq", 1)
    y1 = flat_exchange(packed, "seq", 1 << 1)
    z1 = flat_exchange(after(packed, core), "seq", 1 << 6)
    halo = halo_exchange(after(edge, y2a), "seq")
    y2, y4 = [y2a, y2b], [y4a, y4b]

    def early(local, queries):
        here, there = PAIR * local, PAIR * (1 - local)
        plan = [
            ("self", 0, here, 0),
            ("xor", 0, there, 1),
            ("xor", 1, here, 2),
            ("xor", 2, here, 4),
        ]
        return attend(f"early{local}", block_keep, queries, local, [packed, core, y1], plan)

    def late(local, state, queries):
        here, there = PAIR * local, PAIR * (1 - local)
        plan = [
            ("near", (0, 1), there, 2 * local - 1),
            ("xor", 2, here, 128),
            ("across", 3, here, (1, 4)),
            ("across", 3, here, (2, 4)),
            ("xor", 4, 0, 8),
            ("xor", 5, 0, 16),
        ]
        sources = [core, halo, z1, xs, y2[local], y4[local]]
        return attend(
            f"late{local}", block_keep, queries, local, sources, plan, state=state, w_out=w_out
        )

    state0 = early(0, queries)
    state1 = early(1, queries)
    shares0 = late(0, state0, after(queries, state1))
    out0 = lax.psum_scatter(shares0, "head", scatter_dimension=0, tiled=False)
    shares1 = late(1, state1, after(queries, shares0))
    spread = lax.all_to_all(shares1, "head", 0, 0, tiled=False)
    out1 = jnp.sum(spread.astype(jnp.float32), axis=0).astype(jnp.bfloat16)
    return jnp.concatenate([out0, out1], axis=0)


def solution(mesh):
    placed = (P("seq", "head"), P("seq", "head"), P("seq", "head"), P(), P("head", None))
    return jax.shard_map(
        per_device, mesh=mesh, in_specs=placed, out_specs=P("seq", "head"), check_vma=False
    )
```

time: 120 us -> 126 us (1.050)
  the two profiles are of different devices: /device:TPU:4 before, /device:TPU:56 now
where the time goes in v4:
time: 126 us; the launch traced here: 125 us
  blocking collectives  31.7 us (25%)
  starting transfers between devices  30.8 us (24%)
  Pallas kernels  25 us (20%)
  waiting for transfers between devices  17.4 us (14%)
  between operations  13.7 us (11%)
  local copies, waits for them, and re-layouts  4.18 us (3%)
  other arithmetic  2.63 us (2%)
    all_to_all x1, blocking collectives, per_device(): spread = lax.all_to_all(shares1, 'head', 0, 0, tiled=False)  31.7 us
    ppermute x7, starting transfers between devices, flat_exchange(): return lax.ppermute(value, axis, pairs)  26.2 us
    pallas_call x4, Pallas kernels, attend(): pl.pallas_call(lambda *refs: attend_kernel(scale, heads, local, plan, len...  25 us
    ppermute x7, waiting for transfers between devices, flat_exchange(): return lax.ppermute(value, axis, pairs)  13.5 us
    ppermute x1, starting transfers between devices, halo_exchange(): return lax.ppermute(value, axis, pairs)  4.59 us
    reduce_scatter x1, waiting for transfers between devices, per_device(): out0 = lax.psum_scatter(shares0, 'head', scatter_dimension=0, tiled=False)  3.88 us
    unnamed x22, local copies, waits for them, and re-layouts  3.05 us
  transfers between devices with their start and end apart: 10, of which 2 were waited for; matrix products, arithmetic and copies ran while one was open for 0% of the time, Pallas kernels for 20%

profile of v4, /device:TPU:56, one launch (start us, length us, event | category | flops | bytes accessed | tf_op | source)
XLA Modules:
  0.0 125.4 jit_solution(10480808300250180901)
XLA Ops:
  6.5 0.0 all-gather.3.cloned.1.call-start
  6.5 1.1 fusion
  7.7 0.0 copy-start.1
  7.7 0.8 pad_maximum_fusion.refs_2_
  8.5 0.0 all-gather.3.cloned.1.call-update
  8.5 0.0 reduce-scatter.2.cloned.1.call-start
  8.6 2.1 %collective-permute-start = (bf16[1024,256]{1,0:T(8,128)(2,1)}, bf16[1024,256]{1,0:T(8,128)(2,1)S(1)}, u32[]{:S(2)}, u32[]{:S(2)}) collective-permute-start(bf16[1024,256]{1,0:T(8,128)(2,1)} %pad_maximum_fusion.refs_2_), channel_id=1, source_target_pairs={{0,4},{4,0},{8,12},{12,8},{16,20},{20,16},{24,28},{28,24},{32,36},... | collective-permute-start | bytes 1572872 | tf_op jit(solution)/shard_map/ppermute | solution.py:19
  10.6 3.3 %collective-permute-start.1 = (bf16[1024,256]{1,0:T(8,128)(2,1)}, bf16[1024,256]{1,0:T(8,128)(2,1)S(1)}, u32[]{:S(2)}, u32[]{:S(2)}) collective-permute-start(bf16[1024,256]{1,0:T(8,128)(2,1)} %pad_maximum_fusion.refs_2_), channel_id=1, source_target_pairs={{0,8},{4,12},{8,0},{12,4},{16,24},{20,28},{24,16},{28,20},{32,40},... | collective-permute-start | bytes 1572872 | tf_op jit(solution)/shard_map/ppermute | solution.py:19
  13.9 0.1 pad_maximum_fusion.1
  14.0 4.0 %collective-permute-start.2 = (bf16[512,256]{1,0:T(8,128)(2,1)S(1)}, bf16[512,256]{1,0:T(8,128)(2,1)S(1)}, u32[]{:S(2)}, u32[]{:S(2)}) collective-permute-start(bf16[512,256]{1,0:T(8,128)(2,1)S(1)} %get-tuple-element.17), channel_id=1, source_target_pairs={{0,16},{4,20},{8,24},{12,28},{16,0},{20,4},{24,8},{28,12},{32,48},... | collective-permute-start | bytes 786440 | tf_op jit(solution)/shard_map/ppermute | solution.py:19
  18.1 13.5 %collective-permute-done.2.refs_6_ = bf16[512,256]{1,0:T(8,128)(2,1)S(1)} collective-permute-done((bf16[512,256]{1,0:T(8,128)(2,1)S(1)}, bf16[512,256]{1,0:T(8,128)(2,1)S(1)}, u32[]{:S(2)}, u32[]{:S(2)}) %collective-permute-start.2) | collective-permute-done | bytes 262176 | tf_op jit(solution)/shard_map/ppermute | solution.py:19
  31.6 4.6 %collective-permute-start.3 = (bf16[512,256]{1,0:T(8,128)(2,1)S(1)}, bf16[512,256]{1,0:T(8,128)(2,1)S(1)}, u32[]{:S(2)}, u32[]{:S(2)}) collective-permute-start(bf16[512,256]{1,0:T(8,128)(2,1)S(1)} %get-tuple-element.11), channel_id=1, source_target_pairs={{4,8},{8,4},{12,16},{16,12},{20,24},{24,20},{28,32},{32,28},{36,40... | collective-permute-start | bytes 786440 | tf_op jit(solution)/shard_map/ppermute | solution.py:29
  36.2 2.6 %collective-permute-start.6 = (bf16[512,256]{1,0:T(8,128)(2,1)S(1)}, bf16[512,256]{1,0:T(8,128)(2,1)S(1)}, u32[]{:S(2)}, u32[]{:S(2)}) collective-permute-start(bf16[512,256]{1,0:T(8,128)(2,1)S(1)} %get-tuple-element.14), channel_id=1, source_target_pairs={{0,16},{4,20},{8,24},{12,28},{16,0},{20,4},{24,8},{28,12},{32,48},... | collective-permute-start | bytes 786440 | tf_op jit(solution)/shard_map/ppermute | solution.py:19
  38.8 7.1 %collective-permute-start.5 = (bf16[512,256]{1,0:T(8,128)(2,1)S(1)}, bf16[512,256]{1,0:T(8,128)(2,1)S(1)}, u32[]{:S(2)}, u32[]{:S(2)}) collective-permute-start(bf16[512,256]{1,0:T(8,128)(2,1)S(1)} %collective-permute-done.2.refs_6_), channel_id=1, source_target_pairs={{0,48},{4,52},{8,56},{12,60},{16,32},{20,36},{24,40},{28,44},{32,1... | collective-permute-start | bytes 786440 | tf_op jit(solution)/shard_map/ppermute | solution.py:19
  45.9 0.0 collective-permute-done.refs_3_.refs_2_
  45.9 0.0 copy-done.2
  45.9 0.0 copy-start.3
  45.9 1.9 %collective-permute-start.4 = (bf16[1024,256]{1,0:T(8,128)(2,1)S(1)}, bf16[1024,256]{1,0:T(8,128)(2,1)S(1)}, u32[]{:S(2)}, u32[]{:S(2)}) collective-permute-start(bf16[1024,256]{1,0:T(8,128)(2,1)S(1)} %copy-done.2), channel_id=1, source_target_pairs={{0,256},{4,260},{8,264},{12,268},{16,272},{20,276},{24,280},{28,28... | collective-permute-start | bytes 1572872 | tf_op jit(solution)/shard_map/ppermute | solution.py:19
  47.8 0.0 collective-permute-done.1.refs_4_
  47.8 0.0 copy-done.3
  47.8 0.0 copy-start.4
  47.8 0.8 copy-done.4
  48.6 0.0 copy-done.1
  48.6 5.6 %early1.1.refs_8_ = f32[3,1024,128]{2,1,0:T(8,128)} custom-call(s32[256]{0:T(256)S(1)} %copy-done.1, bf16[512,256]{1,0:T(8,128)(2,1)} %refs_1_.5, bf16[1024,256]{1,0:T(8,128)(2,1)} %pad_maximum_fusion.refs_2_, bf16[1024,256]{1,0:T(8,128)(2,1)} %copy-done.3, bf16[1024,256]{1,0:T(8,128)(2,1)} %copy-done.4), custom_call_target="tpu_custom_call" | custom-call | flops 4294967296 | bytes 1048576 | tf_op jit(solution)/shard_map/early1/pallas_call | solution.py:188
  54.3 0.0 copy-done.8
  54.3 0.0 copy-start
  54.3 0.0 collective-permute-done.6.refs_6_
  54.3 0.0 copy-start.7
  54.3 5.2 %collective-permute-start.7 = (bf16[512,256]{1,0:T(8,128)(2,1)S(1)}, bf16[512,256]{1,0:T(8,128)(2,1)S(1)}, u32[]{:S(2)}, u32[]{:S(2)}) collective-permute-start(bf16[512,256]{1,0:T(8,128)(2,1)S(1)} %collective-permute-done.6.refs_6_), channel_id=1, source_target_pairs={{0,48},{4,52},{8,56},{12,60},{16,32},{20,36},{24,40},{28,44},{32,1... | collective-permute-start | bytes 786440 | tf_op jit(solution)/shard_map/ppermute | solution.py:19
  59.6 5.6 %early0.1.refs_8_ = f32[3,1024,128]{2,1,0:T(8,128)} custom-call(s32[256]{0:T(256)S(1)} %copy-done.1, bf16[512,256]{1,0:T(8,128)(2,1)} %refs_1_.5, bf16[1024,256]{1,0:T(8,128)(2,1)} %pad_maximum_fusion.refs_2_, bf16[1024,256]{1,0:T(8,128)(2,1)} %copy-done.3, bf16[1024,256]{1,0:T(8,128)(2,1)} %copy-done.4), custom_call_target="tpu_custom_call" | custom-call | flops 4294967296 | bytes 1048576 | tf_op jit(solution)/shard_map/early0/pallas_call | solution.py:188
  65.2 0.0 copy-done.7
  65.2 0.0 collective-permute-done.3.refs_3_
  65.2 0.0 copy-start.6
  65.2 0.0 collective-permute-done.5.refs_7_
  65.3 0.0 copy-start.10
  65.3 0.7 copy-done.10
  66.0 0.0 collective-permute-done.4.refs_4_
  66.0 0.0 copy-done.6
  66.0 0.8 copy-done.5
  66.8 7.3 %late0.1 = bf16[4,256,256]{2,1,0:T(8,128)(2,1)} custom-call(s32[256]{0:T(256)S(1)} %copy-done.1, bf16[512,256]{1,0:T(8,128)(2,1)} %refs_1_.5, bf16[1024,256]{1,0:T(8,128)(2,1)} %copy-done.3, bf16[512,256]{1,0:T(8,128)(2,1)} %copy-done.6, bf16[1024,256]{1,0:T(8,128)(2,1)} %copy-done.5, bf16[4,1024,256]{2,1,0:T(8,128)(2,1)} %bitcast.3, ...), custom_call_target="tpu_custom_call" | custom-call | flops 6442450944 | bytes 1572864 | tf_op jit(solution)/shard_map/late0/pallas_call | solution.py:188
  74.1 0.0 reduce-scatter.2.cloned.1.call-update
  74.1 0.0 collective-permute-done.7.refs_7_
  74.1 0.7 copy-done.9
  74.8 6.5 %late1.1 = bf16[4,256,256]{2,1,0:T(8,128)(2,1)S(1)} custom-call(s32[256]{0:T(256)S(1)} %copy-done.1, bf16[512,256]{1,0:T(8,128)(2,1)} %refs_1_.5, bf16[1024,256]{1,0:T(8,128)(2,1)} %copy-done.3, bf16[512,256]{1,0:T(8,128)(2,1)} %copy-done.6, bf16[1024,256]{1,0:T(8,128)(2,1)} %copy-done.5, bf16[4,1024,256]{2,1,0:T(8,128)(2,1)} %bitcast.4, ...), custom_call_target="tpu_custom_call" | custom-call | flops 6442450944 | bytes 1572864 | tf_op jit(solution)/shard_map/late1/pallas_call | solution.py:188
  81.3 31.7 %all_to_all.5 = bf16[4,256,256]{2,1,0:T(8,128)(2,1)S(1)} all-to-all(bf16[4,256,256]{2,1,0:T(8,128)(2,1)S(1)} %late1.1), channel_id=1, replica_groups=mesh['seq'=128,'head'=4] {'head'}, dimensions={0} | all-to-all | bytes 1048576 | tf_op jit(solution)/shard_map/all_to_all | solution.py:260
  113.0 0.1 reduce_sum.12
  113.1 3.9 %reduce-scatter.2.cloned.1.call-done = bf16[1,256,256]{2,1,0:T(8,128)(2,1)} async-done(((bf16[4,256,256]{2,1,0:T(8,128)(2,1)}), bf16[1,256,256]{2,1,0:T(8,128)(2,1)}) %reduce-scatter.2.cloned.1.call-update) | async-done | bytes 131088 | tf_op jit(solution)/shard_map/reduce_scatter | solution.py:258
  117.0 1.6 %pad_maximum_fusion.3 = bf16[512,256]{1,0:T(8,128)(2,1)} fusion(bf16[256,256]{1,0:T(8,128)(2,1)S(1)} %reduce_sum.12, bf16[256,256]{1,0:T(8,128)(2,1)} %bitcast.2), kind=kLoop, calls=%fused_computation.3 | loop fusion | flops 524288 | bytes 524288 | tf_op jit(solution)/shard_map/concatenate | solution.py:262
  (6 shorter events, 0.0 us)
Async XLA Ops:
  6.5 59.5 %all-gather.3.cloned.1.call-start = ((), (), s32[]{:S(2)}) async-start(), calls=%async_computation.3 | async-start | bytes 2621440 | tf_op jit(solution)/shard_map/all_gather | solution.py:38
  7.7 41.0 %copy-start.1 = (s32[256]{0:T(256)S(1)}, s32[256]{0:T(256)}, u32[]{:S(2)}) copy-start(s32[256]{0:T(256)} %refs_0_.7) | copy-start | bytes 3076
  8.5 37.4 %copy-start.2 = (bf16[1024,256]{1,0:T(8,128)(2,1)S(1)}, bf16[1024,256]{1,0:T(8,128)(2,1)}, u32[]{:S(2)}) copy-start(bf16[1024,256]{1,0:T(8,128)(2,1)} %pad_maximum_fusion.refs_2_) | copy-start | bytes 1572868
  8.5 108.4 %reduce-scatter.2.cloned.1.call-start = ((), (), s32[]{:S(2)}) async-start(), calls=%async_computation.2 | async-start | bytes 655360 | tf_op jit(solution)/shard_map/reduce_scatter | solution.py:258
  8.6 37.3 %collective-permute-start = (bf16[1024,256]{1,0:T(8,128)(2,1)}, bf16[1024,256]{1,0:T(8,128)(2,1)S(1)}, u32[]{:S(2)}, u32[]{:S(2)}) collective-permute-start(bf16[1024,256]{1,0:T(8,128)(2,1)} %pad_maximum_fusion.refs_2_), channel_id=1, source_target_pairs={{0,4},{4,0},{8,12},{12,8},{16,20},{20,16},{24,28},{28,24},{32,36},... | collective-permute-start | bytes 1572872 | tf_op jit(solution)/shard_map/ppermute | solution.py:19
  10.6 37.2 %collective-permute-start.1 = (bf16[1024,256]{1,0:T(8,128)(2,1)}, bf16[1024,256]{1,0:T(8,128)(2,1)S(1)}, u32[]{:S(2)}, u32[]{:S(2)}) collective-permute-start(bf16[1024,256]{1,0:T(8,128)(2,1)} %pad_maximum_fusion.refs_2_), channel_id=1, source_target_pairs={{0,8},{4,12},{8,0},{12,4},{16,24},{20,28},{24,16},{28,20},{32,40},... | collective-permute-start | bytes 1572872 | tf_op jit(solution)/shard_map/ppermute | solution.py:19
  14.0 17.5 %collective-permute-start.2 = (bf16[512,256]{1,0:T(8,128)(2,1)S(1)}, bf16[512,256]{1,0:T(8,128)(2,1)S(1)}, u32[]{:S(2)}, u32[]{:S(2)}) collective-permute-start(bf16[512,256]{1,0:T(8,128)(2,1)S(1)} %get-tuple-element.17), channel_id=1, source_target_pairs={{0,16},{4,20},{8,24},{12,28},{16,0},{20,4},{24,8},{28,12},{32,48},... | collective-permute-start | bytes 786440 | tf_op jit(solution)/shard_map/ppermute | solution.py:19
  31.6 22.7 %copy-start.8 = (bf16[512,256]{1,0:T(8,128)(2,1)}, bf16[512,256]{1,0:T(8,128)(2,1)S(1)}, u32[]{:S(2)}) copy-start(bf16[512,256]{1,0:T(8,128)(2,1)S(1)} %collective-permute-done.2.refs_6_) | copy-start | bytes 786436
  31.6 33.7 %collective-permute-start.3 = (bf16[512,256]{1,0:T(8,128)(2,1)S(1)}, bf16[512,256]{1,0:T(8,128)(2,1)S(1)}, u32[]{:S(2)}, u32[]{:S(2)}) collective-permute-start(bf16[512,256]{1,0:T(8,128)(2,1)S(1)} %get-tuple-element.11), channel_id=1, source_target_pairs={{4,8},{8,4},{12,16},{16,12},{20,24},{24,20},{28,32},{32,28},{36,40... | collective-permute-start | bytes 786440 | tf_op jit(solution)/shard_map/ppermute | solution.py:29
  36.2 18.1 %collective-permute-start.6 = (bf16[512,256]{1,0:T(8,128)(2,1)S(1)}, bf16[512,256]{1,0:T(8,128)(2,1)S(1)}, u32[]{:S(2)}, u32[]{:S(2)}) collective-permute-start(bf16[512,256]{1,0:T(8,128)(2,1)S(1)} %get-tuple-element.14), channel_id=1, source_target_pairs={{0,16},{4,20},{8,24},{12,28},{16,0},{20,4},{24,8},{28,12},{32,48},... | collective-permute-start | bytes 786440 | tf_op jit(solution)/shard_map/ppermute | solution.py:19
  38.8 26.5 %collective-permute-start.5 = (bf16[512,256]{1,0:T(8,128)(2,1)S(1)}, bf16[512,256]{1,0:T(8,128)(2,1)S(1)}, u32[]{:S(2)}, u32[]{:S(2)}) collective-permute-start(bf16[512,256]{1,0:T(8,128)(2,1)S(1)} %collective-permute-done.2.refs_6_), channel_id=1, source_target_pairs={{0,48},{4,52},{8,56},{12,60},{16,32},{20,36},{24,40},{28,44},{32,1... | collective-permute-start | bytes 786440 | tf_op jit(solution)/shard_map/ppermute | solution.py:19
  45.9 2.0 %copy-start.3 = (bf16[1024,256]{1,0:T(8,128)(2,1)}, bf16[1024,256]{1,0:T(8,128)(2,1)S(1)}, u32[]{:S(2)}) copy-start(bf16[1024,256]{1,0:T(8,128)(2,1)S(1)} %collective-permute-done.refs_3_.refs_2_) | copy-start | bytes 1572868
  45.9 20.1 %collective-permute-start.4 = (bf16[1024,256]{1,0:T(8,128)(2,1)S(1)}, bf16[1024,256]{1,0:T(8,128)(2,1)S(1)}, u32[]{:S(2)}, u32[]{:S(2)}) collective-permute-start(bf16[1024,256]{1,0:T(8,128)(2,1)S(1)} %copy-done.2), channel_id=1, source_target_pairs={{0,256},{4,260},{8,264},{12,268},{16,272},{20,276},{24,280},{28,28... | collective-permute-start | bytes 1572872 | tf_op jit(solution)/shard_map/ppermute | solution.py:19
  47.8 0.8 copy-start.4
  54.3 12.5 %copy-start = (bf16[256,1024]{1,0:T(8,128)(2,1)S(1)}, bf16[256,1024]{1,0:T(8,128)(2,1)}, u32[]{:S(2)}) copy-start(bf16[256,1024]{1,0:T(8,128)(2,1)} %refs_9_.3) | copy-start | bytes 1572868
  54.3 10.9 %copy-start.7 = (bf16[512,256]{1,0:T(8,128)(2,1)}, bf16[512,256]{1,0:T(8,128)(2,1)S(1)}, u32[]{:S(2)}) copy-start(bf16[512,256]{1,0:T(8,128)(2,1)S(1)} %collective-permute-done.6.refs_6_) | copy-start | bytes 786436
  54.3 19.8 %collective-permute-start.7 = (bf16[512,256]{1,0:T(8,128)(2,1)S(1)}, bf16[512,256]{1,0:T(8,128)(2,1)S(1)}, u32[]{:S(2)}, u32[]{:S(2)}) collective-permute-start(bf16[512,256]{1,0:T(8,128)(2,1)S(1)} %collective-permute-done.6.refs_6_), channel_id=1, source_target_pairs={{0,48},{4,52},{8,56},{12,60},{16,32},{20,36},{24,40},{28,44},{32,1... | collective-permute-start | bytes 786440 | tf_op jit(solution)/shard_map/ppermute | solution.py:19
  65.2 0.8 copy-start.6
  65.3 0.7 copy-start.10
  66.0 0.8 copy-start.5
  74.1 0.7 copy-start.9
Sparse Core Ops, SparseCore 0:
  9.5 42.0 all-gather.2
  74.2 42.6 reduce-scatter.1

commit v5 on v3

--- a/solution.py
+++ b/solution.py
@@ -10,6 +10,7 @@
 HD = 64
 BLOCK = 256
 MASKED = -1e30
+COST = 4
 
 
 def flat_exchange(value, axis, mask):
@@ -173,7 +174,11 @@
             pltpu.VMEM((2 * BLOCK, width), jnp.bfloat16),
         ],
         compiler_params=pltpu.CompilerParams(vmem_limit_bytes=(len(plan) + 7) << 20),
-        cost_estimate=pl.CostEstimate(flops=1 << 20, transcendentals=0, bytes_accessed=1 << 14),
+        cost_estimate=pl.CostEstimate(
+            flops=len(plan) * 4 * stacked * BLOCK * width * COST,
+            transcendentals=len(plan) * stacked * BLOCK,
+            bytes_accessed=len(plan) * 2 * BLOCK * width * 2,
+        ),
         name=name,
     )(*given)
 
@@ -202,17 +207,21 @@
             ("xor", 0, there, 1),
             ("xor", 1, here, 2),
             ("xor", 2, here, 4),
-            ("xor", 3, here, 8),
-            ("xor", 4, here, 32),
-            ("xor", 5, here, 64),
+            ("xor", 3, here, 32),
+            ("xor", 4, here, 64),
         ]
-        sources = [packed, core, y1, y2, x1, x2]
+        sources = [packed, core, y1, x1, x2]
         return attend(f"early{local}", block_keep, queries, local, sources, plan)
 
     def late(local, y4, state, queries, rotated):
         here, there = 2 * BLOCK * local, 2 * BLOCK * (1 - local)
-        plan = [("near", (0, 1), there, 2 * local - 1), ("xor", 2, here, 128), ("xor", 3, 0, 16)]
-        sources = [core, halo, z1, y4]
+        plan = [
+            ("near", (0, 1), there, 2 * local - 1),
+            ("xor", 2, here, 128),
+            ("xor", 3, here, 8),
+            ("xor", 4, 0, 16),
+        ]
+        sources = [core, halo, z1, y2, y4]
         return attend(
             f"late{local}",
             block_keep,

time: 118 us -> 117 us (level)
  the two profiles are of different devices: /device:TPU:2 before, /device:TPU:72 now
where the time goes in v5:
time: 117 us
  starting transfers between devices  53.6 us (46%)
  waiting for transfers between devices  47.4 us (41%)
  Pallas kernels  11.8 us (10%)
  other arithmetic  1.95 us (2%)
  local copies, waits for them, and re-layouts  1.8 us (2%)
    ppermute x8, starting transfers between devices, flat_exchange(): return lax.ppermute(value, axis, pairs)  31.5 us
    ppermute x8, waiting for transfers between devices, flat_exchange(): return lax.ppermute(value, axis, pairs)  22.3 us
    ppermute x3, starting transfers between devices, per_device(): lax.ppermute(piece, 'head', [(h, (h + hop + 1) % groups) for h in range(g...  16.8 us
    all_to_all x1, waiting for transfers between devices, per_device(): spread = lax.all_to_all(after(shares, *moved), 'head', 0, 0, tiled=False)  16.7 us
    pallas_call x4, Pallas kernels, attend(): pl.pallas_call(lambda *refs: attend_kernel(scale, heads, local, plan, sta...  11.8 us
    ppermute x3, waiting for transfers between devices, per_device(): lax.ppermute(piece, 'head', [(h, (h + hop + 1) % groups) for h in range(g...  8.35 us
    all_to_all x1, starting transfers between devices, per_device(): spread = lax.all_to_all(after(shares, *moved), 'head', 0, 0, tiled=False)  3.47 us
  transfers between devices with their start and end apart: 13, of which 4 were waited for; matrix products, arithmetic and copies ran while one was open for 1% of the time, Pallas kernels for 10%

profile of v5, /device:TPU:72, one launch (start us, length us, event | category | flops | bytes accessed | tf_op | source)
XLA Modules:
  0.0 116.8 jit_solution(4186681966783281647)
XLA Ops:
  0.0 1.1 fusion
  1.1 0.0 copy-start.3
  1.1 0.6 copy-done.3
  1.8 1.9 %collective-permute-start = (bf16[1024,256]{1,0:T(8,128)(2,1)S(1)}, bf16[1024,256]{1,0:T(8,128)(2,1)S(1)}, u32[]{:S(2)}, u32[]{:S(2)}) collective-permute-start(bf16[1024,256]{1,0:T(8,128)(2,1)S(1)} %pad_maximum_fusion.refs_2_), channel_id=1, source_target_pairs={{0,4},{4,0},{8,12},{12,8},{16,20},{20,16},{24,28},{28,24},{32,36},... | collective-permute-start | bytes 1572872 | tf_op jit(solution)/shard_map/ppermute | solution.py:18
  3.8 4.9 %collective-permute-start.3 = (bf16[1024,256]{1,0:T(8,128)(2,1)S(1)}, bf16[1024,256]{1,0:T(8,128)(2,1)S(1)}, u32[]{:S(2)}, u32[]{:S(2)}) collective-permute-start(bf16[1024,256]{1,0:T(8,128)(2,1)S(1)} %pad_maximum_fusion.refs_2_), channel_id=1, source_target_pairs={{0,128},{4,132},{8,136},{12,140},{16,144},{20,148},{24,152},{28,15... | collective-permute-start | bytes 1572872 | tf_op jit(solution)/shard_map/ppermute | solution.py:18
  8.7 2.4 %collective-permute-start.1 = (bf16[1024,256]{1,0:T(8,128)(2,1)S(1)}, bf16[1024,256]{1,0:T(8,128)(2,1)S(1)}, u32[]{:S(2)}, u32[]{:S(2)}) collective-permute-start(bf16[1024,256]{1,0:T(8,128)(2,1)S(1)} %pad_maximum_fusion.refs_2_), channel_id=1, source_target_pairs={{0,8},{4,12},{8,0},{12,4},{16,24},{20,28},{24,16},{28,20},{32,40},... | collective-permute-start | bytes 1572872 | tf_op jit(solution)/shard_map/ppermute | solution.py:18
  11.1 0.0 collective-permute-done.refs_3_.refs_2_
  11.1 2.5 %collective-permute-start.2 = (bf16[1024,256]{1,0:T(8,128)(2,1)S(1)}, bf16[1024,256]{1,0:T(8,128)(2,1)S(1)}, u32[]{:S(2)}, u32[]{:S(2)}) collective-permute-start(bf16[1024,256]{1,0:T(8,128)(2,1)S(1)} %pad_maximum_fusion.refs_2_), channel_id=1, source_target_pairs={{0,64},{4,68},{8,72},{12,76},{16,80},{20,84},{24,88},{28,92},{32,9... | collective-permute-start | bytes 1572872 | tf_op jit(solution)/shard_map/ppermute | solution.py:18
  13.6 4.5 %collective-permute-start.6 = (bf16[1024,256]{1,0:T(8,128)(2,1)S(1)}, bf16[1024,256]{1,0:T(8,128)(2,1)S(1)}, u32[]{:S(2)}, u32[]{:S(2)}) collective-permute-start(bf16[1024,256]{1,0:T(8,128)(2,1)S(1)} %pad_maximum_fusion.refs_2_), channel_id=1, source_target_pairs={{0,16},{4,20},{8,24},{12,28},{16,0},{20,4},{24,8},{28,12},{32,48},... | collective-permute-start | bytes 1572872 | tf_op jit(solution)/shard_map/ppermute | solution.py:18
  18.1 0.0 copy-start.1
  18.1 1.0 pad_maximum_fusion.1
  19.1 5.9 %collective-permute-start.7 = (bf16[512,256]{1,0:T(8,128)(2,1)S(1)}, bf16[512,256]{1,0:T(8,128)(2,1)S(1)}, u32[]{:S(2)}, u32[]{:S(2)}) collective-permute-start(bf16[512,256]{1,0:T(8,128)(2,1)S(1)} %get-tuple-element.41), channel_id=1, source_target_pairs={{0,32},{4,36},{8,40},{12,44},{16,48},{20,52},{24,56},{28,60},{32,0... | collective-permute-start | bytes 786440 | tf_op jit(solution)/shard_map/ppermute | solution.py:18
  25.1 0.0 copy-start.2
  25.1 0.0 collective-permute-done.3.refs_6_
  25.1 1.9 %collective-permute-start.4 = (bf16[512,256]{1,0:T(8,128)(2,1)S(1)}, bf16[512,256]{1,0:T(8,128)(2,1)S(1)}, u32[]{:S(2)}, u32[]{:S(2)}) collective-permute-start(bf16[512,256]{1,0:T(8,128)(2,1)S(1)} %get-tuple-element.25), channel_id=1, source_target_pairs={{4,8},{8,4},{12,16},{16,12},{20,24},{24,20},{28,32},{32,28},{36,40... | collective-permute-start | bytes 786440 | tf_op jit(solution)/shard_map/ppermute | solution.py:28
  27.0 3.2 %collective-permute-done.1.refs_4_ = bf16[1024,256]{1,0:T(8,128)(2,1)S(1)} collective-permute-done((bf16[1024,256]{1,0:T(8,128)(2,1)S(1)}, bf16[1024,256]{1,0:T(8,128)(2,1)S(1)}, u32[]{:S(2)}, u32[]{:S(2)}) %collective-permute-start.1) | collective-permute-done | bytes 524320 | tf_op jit(solution)/shard_map/ppermute | solution.py:18
  30.3 2.8 %collective-permute-start.5 = (bf16[1024,256]{1,0:T(8,128)(2,1)S(1)}, bf16[1024,256]{1,0:T(8,128)(2,1)S(1)}, u32[]{:S(2)}, u32[]{:S(2)}) collective-permute-start(bf16[1024,256]{1,0:T(8,128)(2,1)S(1)} %pad_maximum_fusion.refs_2_), channel_id=1, source_target_pairs={{0,256},{4,260},{8,264},{12,268},{16,272},{20,276},{24,280},{28,28... | collective-permute-start | bytes 1572872 | tf_op jit(solution)/shard_map/ppermute | solution.py:18
  33.1 0.0 collective-permute-done.2.refs_5_
  33.1 6.5 %collective-permute-start.11 = (bf16[512,256]{1,0:T(8,128)(2,1)S(1)}, bf16[512,256]{1,0:T(8,128)(2,1)S(1)}, u32[]{:S(2)}, u32[]{:S(2)}) collective-permute-start(bf16[512,256]{1,0:T(8,128)(2,1)S(1)} %get-tuple-element.35), channel_id=1, source_target_pairs={{0,32},{4,36},{8,40},{12,44},{16,48},{20,52},{24,56},{28,60},{32,0... | collective-permute-start | bytes 786440 | tf_op jit(solution)/shard_map/ppermute | solution.py:18
  39.6 0.0 copy-done.1
  39.6 0.0 copy-done.2
  39.7 2.7 %early0.1 = (f32[1024,128]{1,0:T(8,128)S(1)}, f32[1024,128]{1,0:T(8,128)S(1)}, f32[1024,128]{1,0:T(8,128)S(1)}) custom-call(s32[256]{0:T(256)S(1)} %copy-done.2, bf16[512,256]{1,0:T(8,128)(2,1)S(1)} %copy-done.1, bf16[1024,256]{1,0:T(8,128)(2,1)S(1)} %pad_maximum_fusion.refs_2_, bf16[1024,256]{1,0:T(8,128)(2,1)S(1)} %collective-permute-done.refs_3_.refs_2_, ...), custom_call_target="tpu_custom_call" | custom-call | flops 6442450944 | bytes 1572864 | tf_op jit(solution)/shard_map/early0/pallas_call | solution.py:167
  42.3 0.0 copy-start
  42.4 2.7 %early1.1 = (f32[1024,128]{1,0:T(8,128)S(1)}, f32[1024,128]{1,0:T(8,128)S(1)}, f32[1024,128]{1,0:T(8,128)S(1)}) custom-call(s32[256]{0:T(256)S(1)} %copy-done.2, bf16[512,256]{1,0:T(8,128)(2,1)S(1)} %copy-done.1, bf16[1024,256]{1,0:T(8,128)(2,1)S(1)} %pad_maximum_fusion.refs_2_, bf16[1024,256]{1,0:T(8,128)(2,1)S(1)} %collective-permute-done.refs_3_.refs_2_, ...), custom_call_target="tpu_custom_call" | custom-call | flops 6442450944 | bytes 1572864 | tf_op jit(solution)/shard_map/early1/pallas_call | solution.py:167
  45.0 0.0 collective-permute-done.7.refs_6_
  45.0 19.1 %collective-permute-done.6.refs_5_ = bf16[1024,256]{1,0:T(8,128)(2,1)S(1)} collective-permute-done((bf16[1024,256]{1,0:T(8,128)(2,1)S(1)}, bf16[1024,256]{1,0:T(8,128)(2,1)S(1)}, u32[]{:S(2)}, u32[]{:S(2)}) %collective-permute-start.6) | collective-permute-done | bytes 524320 | tf_op jit(solution)/shard_map/ppermute | solution.py:18
  64.1 0.0 collective-permute-done.4.refs_3_
  64.1 0.0 collective-permute-done.5.refs_4_
  64.1 0.0 copy-done
  64.1 2.8 %late0.1 = (bf16[256,256]{1,0:T(8,128)(2,1)S(1)}, bf16[256,256]{1,0:T(8,128)(2,1)S(1)}, bf16[256,256]{1,0:T(8,128)(2,1)S(1)}, bf16[256,256]{1,0:T(8,128)(2,1)S(1)}) custom-call(s32[256]{0:T(256)S(1)} %copy-done.2, bf16[512,256]{1,0:T(8,128)(2,1)S(1)} %copy-done.1, bf16[1024,256]{1,0:T(8,128)(2,1)S(1)} %collective-permute-done.refs_3_.refs_2_, ...), custom_call_target="tpu_custom_call" | custom-call | flops 4294967296 | bytes 1048576 | tf_op jit(solution)/shard_map/late0/pallas_call | solution.py:167
  67.0 10.0 %collective-permute-start.10 = (bf16[256,256]{1,0:T(8,128)(2,1)S(1)}, bf16[256,256]{1,0:T(8,128)(2,1)S(1)}, u32[]{:S(2)}, u32[]{:S(2)}) collective-permute-start(bf16[256,256]{1,0:T(8,128)(2,1)S(1)} %get-tuple-element.33), channel_id=1, source_target_pairs={{0,3},{1,0},{2,1},{3,2},{4,7},{5,4},{6,5},{7,6},{8,11},{9,8},{10,9... | collective-permute-start | bytes 393224 | tf_op jit(solution)/shard_map/ppermute | solution.py:242
  77.0 1.9 %collective-permute-start.8 = (bf16[256,256]{1,0:T(8,128)(2,1)S(1)}, bf16[256,256]{1,0:T(8,128)(2,1)S(1)}, u32[]{:S(2)}, u32[]{:S(2)}) collective-permute-start(bf16[256,256]{1,0:T(8,128)(2,1)S(1)} %get-tuple-element.31), channel_id=1, source_target_pairs={{0,1},{1,2},{2,3},{3,0},{4,5},{5,6},{6,7},{7,4},{8,9},{9,10},{10,1... | collective-permute-start | bytes 393224 | tf_op jit(solution)/shard_map/ppermute | solution.py:242
  79.0 4.8 %collective-permute-start.9 = (bf16[256,256]{1,0:T(8,128)(2,1)S(1)}, bf16[256,256]{1,0:T(8,128)(2,1)S(1)}, u32[]{:S(2)}, u32[]{:S(2)}) collective-permute-start(bf16[256,256]{1,0:T(8,128)(2,1)S(1)} %get-tuple-element.32), channel_id=1, source_target_pairs={{0,2},{1,3},{2,0},{3,1},{4,6},{5,7},{6,4},{7,5},{8,10},{9,11},{10,... | collective-permute-start | bytes 393224 | tf_op jit(solution)/shard_map/ppermute | solution.py:242
  83.8 0.0 collective-permute-done.11.refs_6_
  83.8 3.6 %late1.1 = bf16[4,256,256]{2,1,0:T(8,128)(2,1)} custom-call(s32[256]{0:T(256)S(1)} %copy-done.2, bf16[512,256]{1,0:T(8,128)(2,1)S(1)} %copy-done.1, bf16[1024,256]{1,0:T(8,128)(2,1)S(1)} %collective-permute-done.refs_3_.refs_2_, bf16[512,256]{1,0:T(8,128)(2,1)S(1)} %collective-permute-done.4.refs_3_, bf16[1024,256]{1,0:T(8,128)(2,1)S(1)} %collective-permute-done.5.refs_4_, ...), custom_call_target="tpu_custom_call" | custom-call | flops 4294967296 | bytes 1048576 | tf_op jit(solution)/shard_map/late1/pallas_call | solution.py:167
  87.4 0.0 collective-permute-done.10
  87.4 8.3 %collective-permute-done.8 = bf16[256,256]{1,0:T(8,128)(2,1)S(1)} collective-permute-done((bf16[256,256]{1,0:T(8,128)(2,1)S(1)}, bf16[256,256]{1,0:T(8,128)(2,1)S(1)}, u32[]{:S(2)}, u32[]{:S(2)}) %collective-permute-start.8) | collective-permute-done | bytes 131104 | tf_op jit(solution)/shard_map/ppermute | solution.py:242
  95.8 0.0 collective-permute-done.9
  95.8 3.5 %all-to-all-start = ((bf16[4,256,256]{2,1,0:T(8,128)(2,1)}), bf16[4,256,256]{2,1,0:T(8,128)(2,1)S(1)}, u32[]{:S(2)}, u32[]{:S(2)}) async-start(bf16[4,256,256]{2,1,0:T(8,128)(2,1)} %late1.1), calls=%async_computation | async-start | bytes 1048576 | tf_op jit(solution)/shard_map/all_to_all | solution.py:246
  99.2 0.1 add_convert_fusion
  99.3 16.7 %all-to-all-done = bf16[4,256,256]{2,1,0:T(8,128)(2,1)S(1)} async-done(((bf16[4,256,256]{2,1,0:T(8,128)(2,1)}), bf16[4,256,256]{2,1,0:T(8,128)(2,1)S(1)}, u32[]{:S(2)}, u32[]{:S(2)}) %all-to-all-start) | async-done | bytes 524320 | tf_op jit(solution)/shard_map/all_to_all | solution.py:246
  116.0 0.1 reduce_sum.12
  116.1 0.7 pad_maximum_fusion.3
  (1 shorter events, 0.0 us)
Async XLA Ops:
  1.1 0.7 copy-start.3
  1.8 9.2 %collective-permute-start = (bf16[1024,256]{1,0:T(8,128)(2,1)S(1)}, bf16[1024,256]{1,0:T(8,128)(2,1)S(1)}, u32[]{:S(2)}, u32[]{:S(2)}) collective-permute-start(bf16[1024,256]{1,0:T(8,128)(2,1)S(1)} %pad_maximum_fusion.refs_2_), channel_id=1, source_target_pairs={{0,4},{4,0},{8,12},{12,8},{16,20},{20,16},{24,28},{28,24},{32,36},... | collective-permute-start | bytes 1572872 | tf_op jit(solution)/shard_map/ppermute | solution.py:18
  3.8 21.4 %collective-permute-start.3 = (bf16[1024,256]{1,0:T(8,128)(2,1)S(1)}, bf16[1024,256]{1,0:T(8,128)(2,1)S(1)}, u32[]{:S(2)}, u32[]{:S(2)}) collective-permute-start(bf16[1024,256]{1,0:T(8,128)(2,1)S(1)} %pad_maximum_fusion.refs_2_), channel_id=1, source_target_pairs={{0,128},{4,132},{8,136},{12,140},{16,144},{20,148},{24,152},{28,15... | collective-permute-start | bytes 1572872 | tf_op jit(solution)/shard_map/ppermute | solution.py:18
  8.7 21.6 %collective-permute-start.1 = (bf16[1024,256]{1,0:T(8,128)(2,1)S(1)}, bf16[1024,256]{1,0:T(8,128)(2,1)S(1)}, u32[]{:S(2)}, u32[]{:S(2)}) collective-permute-start(bf16[1024,256]{1,0:T(8,128)(2,1)S(1)} %pad_maximum_fusion.refs_2_), channel_id=1, source_target_pairs={{0,8},{4,12},{8,0},{12,4},{16,24},{20,28},{24,16},{28,20},{32,40},... | collective-permute-start | bytes 1572872 | tf_op jit(solution)/shard_map/ppermute | solution.py:18
  11.1 22.0 %collective-permute-start.2 = (bf16[1024,256]{1,0:T(8,128)(2,1)S(1)}, bf16[1024,256]{1,0:T(8,128)(2,1)S(1)}, u32[]{:S(2)}, u32[]{:S(2)}) collective-permute-start(bf16[1024,256]{1,0:T(8,128)(2,1)S(1)} %pad_maximum_fusion.refs_2_), channel_id=1, source_target_pairs={{0,64},{4,68},{8,72},{12,76},{16,80},{20,84},{24,88},{28,92},{32,9... | collective-permute-start | bytes 1572872 | tf_op jit(solution)/shard_map/ppermute | solution.py:18
  13.6 50.5 %collective-permute-start.6 = (bf16[1024,256]{1,0:T(8,128)(2,1)S(1)}, bf16[1024,256]{1,0:T(8,128)(2,1)S(1)}, u32[]{:S(2)}, u32[]{:S(2)}) collective-permute-start(bf16[1024,256]{1,0:T(8,128)(2,1)S(1)} %pad_maximum_fusion.refs_2_), channel_id=1, source_target_pairs={{0,16},{4,20},{8,24},{12,28},{16,0},{20,4},{24,8},{28,12},{32,48},... | collective-permute-start | bytes 1572872 | tf_op jit(solution)/shard_map/ppermute | solution.py:18
  18.1 21.5 %copy-start.1 = (bf16[512,256]{1,0:T(8,128)(2,1)S(1)}, bf16[512,256]{1,0:T(8,128)(2,1)}, u32[]{:S(2)}) copy-start(bf16[512,256]{1,0:T(8,128)(2,1)} %refs_1_.5) | copy-start | bytes 786436
  19.1 25.9 %collective-permute-start.7 = (bf16[512,256]{1,0:T(8,128)(2,1)S(1)}, bf16[512,256]{1,0:T(8,128)(2,1)S(1)}, u32[]{:S(2)}, u32[]{:S(2)}) collective-permute-start(bf16[512,256]{1,0:T(8,128)(2,1)S(1)} %get-tuple-element.41), channel_id=1, source_target_pairs={{0,32},{4,36},{8,40},{12,44},{16,48},{20,52},{24,56},{28,60},{32,0... | collective-permute-start | bytes 786440 | tf_op jit(solution)/shard_map/ppermute | solution.py:18
  25.1 14.6 %copy-start.2 = (s32[256]{0:T(256)S(1)}, s32[256]{0:T(256)}, u32[]{:S(2)}) copy-start(s32[256]{0:T(256)} %refs_0_.7) | copy-start | bytes 3076
  25.1 39.0 %collective-permute-start.4 = (bf16[512,256]{1,0:T(8,128)(2,1)S(1)}, bf16[512,256]{1,0:T(8,128)(2,1)S(1)}, u32[]{:S(2)}, u32[]{:S(2)}) collective-permute-start(bf16[512,256]{1,0:T(8,128)(2,1)S(1)} %get-tuple-element.25), channel_id=1, source_target_pairs={{4,8},{8,4},{12,16},{16,12},{20,24},{24,20},{28,32},{32,28},{36,40... | collective-permute-start | bytes 786440 | tf_op jit(solution)/shard_map/ppermute | solution.py:28
  30.3 33.8 %collective-permute-start.5 = (bf16[1024,256]{1,0:T(8,128)(2,1)S(1)}, bf16[1024,256]{1,0:T(8,128)(2,1)S(1)}, u32[]{:S(2)}, u32[]{:S(2)}) collective-permute-start(bf16[1024,256]{1,0:T(8,128)(2,1)S(1)} %pad_maximum_fusion.refs_2_), channel_id=1, source_target_pairs={{0,256},{4,260},{8,264},{12,268},{16,272},{20,276},{24,280},{28,28... | collective-permute-start | bytes 1572872 | tf_op jit(solution)/shard_map/ppermute | solution.py:18
  33.1 50.7 %collective-permute-start.11 = (bf16[512,256]{1,0:T(8,128)(2,1)S(1)}, bf16[512,256]{1,0:T(8,128)(2,1)S(1)}, u32[]{:S(2)}, u32[]{:S(2)}) collective-permute-start(bf16[512,256]{1,0:T(8,128)(2,1)S(1)} %get-tuple-element.35), channel_id=1, source_target_pairs={{0,32},{4,36},{8,40},{12,44},{16,48},{20,52},{24,56},{28,60},{32,0... | collective-permute-start | bytes 786440 | tf_op jit(solution)/shard_map/ppermute | solution.py:18
  42.3 21.8 %copy-start = (bf16[256,1024]{1,0:T(8,128)(2,1)S(1)}, bf16[256,1024]{1,0:T(8,128)(2,1)}, u32[]{:S(2)}) copy-start(bf16[256,1024]{1,0:T(8,128)(2,1)} %refs_10_.3) | copy-start | bytes 1572868
  67.0 20.4 %collective-permute-start.10 = (bf16[256,256]{1,0:T(8,128)(2,1)S(1)}, bf16[256,256]{1,0:T(8,128)(2,1)S(1)}, u32[]{:S(2)}, u32[]{:S(2)}) collective-permute-start(bf16[256,256]{1,0:T(8,128)(2,1)S(1)} %get-tuple-element.33), channel_id=1, source_target_pairs={{0,3},{1,0},{2,1},{3,2},{4,7},{5,4},{6,5},{7,6},{8,11},{9,8},{10,9... | collective-permute-start | bytes 393224 | tf_op jit(solution)/shard_map/ppermute | solution.py:242
  77.0 18.7 %collective-permute-start.8 = (bf16[256,256]{1,0:T(8,128)(2,1)S(1)}, bf16[256,256]{1,0:T(8,128)(2,1)S(1)}, u32[]{:S(2)}, u32[]{:S(2)}) collective-permute-start(bf16[256,256]{1,0:T(8,128)(2,1)S(1)} %get-tuple-element.31), channel_id=1, source_target_pairs={{0,1},{1,2},{2,3},{3,0},{4,5},{5,6},{6,7},{7,4},{8,9},{9,10},{10,1... | collective-permute-start | bytes 393224 | tf_op jit(solution)/shard_map/ppermute | solution.py:242
  79.0 16.8 %collective-permute-start.9 = (bf16[256,256]{1,0:T(8,128)(2,1)S(1)}, bf16[256,256]{1,0:T(8,128)(2,1)S(1)}, u32[]{:S(2)}, u32[]{:S(2)}) collective-permute-start(bf16[256,256]{1,0:T(8,128)(2,1)S(1)} %get-tuple-element.32), channel_id=1, source_target_pairs={{0,2},{1,3},{2,0},{3,1},{4,6},{5,7},{6,4},{7,5},{8,10},{9,11},{10,... | collective-permute-start | bytes 393224 | tf_op jit(solution)/shard_map/ppermute | solution.py:242
  95.8 20.3 %all-to-all-start = ((bf16[4,256,256]{2,1,0:T(8,128)(2,1)}), bf16[4,256,256]{2,1,0:T(8,128)(2,1)S(1)}, u32[]{:S(2)}, u32[]{:S(2)}) async-start(bf16[4,256,256]{2,1,0:T(8,128)(2,1)} %late1.1), calls=%async_computation | async-start | bytes 1048576 | tf_op jit(solution)/shard_map/all_to_all | solution.py:246

commit v6 on v5

--- a/solution.py
+++ b/solution.py
@@ -190,59 +190,82 @@
     packed = jnp.concatenate(parts, axis=0)
     side = lax.rem(lax.axis_index("seq"), 2)
     edge = jnp.where(side == 1, parts[1], parts[0])
+    y4a = flat_exchange(parts[0], "seq", 1 << 3)
     y2 = flat_exchange(packed, "seq", 1 << 2)
-    y4a = flat_exchange(parts[0], "seq", 1 << 3)
     y1 = flat_exchange(packed, "seq", 1 << 1)
     core = flat_exchange(packed, "seq", 1)
-    x2 = flat_exchange(packed, "seq", 1 << 5)
     x1 = flat_exchange(after(packed, core), "seq", 1 << 4)
-    z1 = flat_exchange(after(packed, x2), "seq", 1 << 6)
-    halo = halo_exchange(after(edge, core), "seq")
-    y4b = flat_exchange(after(parts[1], y1), "seq", 1 << 3)
-
-    def early(local, queries):
-        here, there = 2 * BLOCK * local, 2 * BLOCK * (1 - local)
-        plan = [
-            ("self", 0, here, 0),
-            ("xor", 0, there, 1),
-            ("xor", 1, here, 2),
-            ("xor", 2, here, 4),
-            ("xor", 3, here, 32),
-            ("xor", 4, here, 64),
-        ]
-        sources = [packed, core, y1, x1, x2]
-        return attend(f"early{local}", block_keep, queries, local, sources, plan)
-
-    def late(local, y4, state, queries, rotated):
-        here, there = 2 * BLOCK * local, 2 * BLOCK * (1 - local)
-        plan = [
-            ("near", (0, 1), there, 2 * local - 1),
-            ("xor", 2, here, 128),
-            ("xor", 3, here, 8),
-            ("xor", 4, 0, 16),
-        ]
-        sources = [core, halo, z1, y2, y4]
-        return attend(
-            f"late{local}",
-            block_keep,
-            queries,
-            local,
-            sources,
-            plan,
-            state=state,
-            w_out=w_out,
-            rotated=rotated,
-        )
-
-    state0 = early(0, queries)
-    state1 = early(1, queries)
-    mine, *pieces = late(0, y4a, state0, after(queries, state1[0]), True)
+    x2 = flat_exchange(after(packed, core), "seq", 1 << 5)
+    z1 = flat_exchange(after(packed, y1), "seq", 1 << 6)
+    halo = halo_exchange(after(edge, x1), "seq")
+    y4b = flat_exchange(after(parts[1], x1), "seq", 1 << 3)
+
+    state0 = attend(
+        "early0",
+        block_keep,
+        queries,
+        0,
+        [packed, core],
+        [
+            ("self", 0, 0, 0),
+            ("xor", 0, 512, 1),
+            ("xor", 1, 0, 2),
+        ],
+    )
+    state1 = attend(
+        "early1",
+        block_keep,
+        queries,
+        1,
+        [packed, core],
+        [
+            ("self", 0, 512, 0),
+            ("xor", 0, 0, 1),
+            ("xor", 1, 512, 2),
+        ],
+    )
+    mine, *pieces = attend(
+        "late0",
+        block_keep,
+        after(queries, state1[0]),
+        0,
+        [core, halo, z1, y1, y2, x1, x2, y4a],
+        [
+            ("near", (0, 1), 512, -1),
+            ("xor", 2, 0, 128),
+            ("xor", 3, 0, 4),
+            ("xor", 4, 0, 8),
+            ("xor", 5, 0, 32),
+            ("xor", 6, 0, 64),
+            ("xor", 7, 0, 16),
+        ],
+        state=state0,
+        w_out=w_out,
+        rotated=True,
+    )
     groups = 1 + len(pieces)
     moved = [
         lax.ppermute(piece, "head", [(h, (h + hop + 1) % groups) for h in range(groups)])
         for hop, piece in enumerate(pieces)
     ]
-    shares = late(1, y4b, state1, after(queries, mine), False)
+    shares = attend(
+        "late1",
+        block_keep,
+        after(queries, mine),
+        1,
+        [core, halo, z1, y1, y2, x1, x2, y4b],
+        [
+            ("near", (0, 1), 0, 1),
+            ("xor", 2, 512, 128),
+            ("xor", 3, 512, 4),
+            ("xor", 4, 512, 8),
+            ("xor", 5, 512, 32),
+            ("xor", 6, 512, 64),
+            ("xor", 7, 0, 16),
+        ],
+        state=state1,
+        w_out=w_out,
+    )
     spread = lax.all_to_all(after(shares, *moved), "head", 0, 0, tiled=False)
     total = mine.astype(jnp.float32)
     for piece in moved:

time: 117 us -> 114 us (0.974)
  the two profiles are of different devices: /device:TPU:72 before, /device:TPU:48 now
where the time goes in v6:
time: 114 us
  starting transfers between devices  52.5 us (46%)
  waiting for transfers between devices  41.7 us (37%)
  Pallas kernels  17.4 us (15%)
  local copies, waits for them, and re-layouts  1.15 us (1%)
    ppermute x8, starting transfers between devices, flat_exchange(): return lax.ppermute(value, axis, pairs)  27.7 us
    ppermute x3, starting transfers between devices, per_device(): lax.ppermute(piece, 'head', [(h, (h + hop + 1) % groups) for h in range(g...  17.7 us
    pallas_call x4, Pallas kernels, attend(): pl.pallas_call(lambda *refs: attend_kernel(scale, heads, local, plan, sta...  17.4 us
    ppermute x1, waiting for transfers between devices, halo_exchange(): return lax.ppermute(value, axis, pairs)  15.2 us
    all_to_all x1, waiting for transfers between devices, per_device(): spread = lax.all_to_all(after(shares, *moved), 'head', 0, 0, tiled=False)  11.5 us
    ppermute x8, waiting for transfers between devices, flat_exchange(): return lax.ppermute(value, axis, pairs)  10.7 us
    all_to_all x1, starting transfers between devices, per_device(): spread = lax.all_to_all(after(shares, *moved), 'head', 0, 0, tiled=False)  4.95 us
    ppermute x3, waiting for transfers between devices, per_device(): lax.ppermute(piece, 'head', [(h, (h + hop + 1) % groups) for h in range(g...  4.3 us
  transfers between devices with their start and end apart: 13, of which 5 were waited for; matrix products, arithmetic and copies ran while one was open for 0% of the time, Pallas kernels for 15%

profile of v6, /device:TPU:48, one launch (start us, length us, event | category | flops | bytes accessed | tf_op | source)
XLA Modules:
  0.0 113.9 jit_solution(8792358879316429502)
XLA Ops:
  0.0 1.1 fusion
  1.2 1.9 %collective-permute-start = (bf16[1024,256]{1,0:T(8,128)(2,1)S(1)}, bf16[1024,256]{1,0:T(8,128)(2,1)S(1)}, u32[]{:S(2)}, u32[]{:S(2)}) collective-permute-start(bf16[1024,256]{1,0:T(8,128)(2,1)S(1)} %pad_maximum_fusion.refs_2_), channel_id=1, source_target_pairs={{0,4},{4,0},{8,12},{12,8},{16,20},{20,16},{24,28},{28,24},{32,36},... | collective-permute-start | bytes 1572872 | tf_op jit(solution)/shard_map/ppermute | solution.py:18
  3.1 2.6 %collective-permute-start.3 = (bf16[1024,256]{1,0:T(8,128)(2,1)S(1)}, bf16[1024,256]{1,0:T(8,128)(2,1)S(1)}, u32[]{:S(2)}, u32[]{:S(2)}) collective-permute-start(bf16[1024,256]{1,0:T(8,128)(2,1)S(1)} %pad_maximum_fusion.refs_2_), channel_id=1, source_target_pairs={{0,8},{4,12},{8,0},{12,4},{16,24},{20,28},{24,16},{28,20},{32,40},... | collective-permute-start | bytes 1572872 | tf_op jit(solution)/shard_map/ppermute | solution.py:18
  5.7 0.0 collective-permute-done.refs_3_.refs_2_
  5.7 3.4 %collective-permute-start.1 = (bf16[1024,256]{1,0:T(8,128)(2,1)S(1)}, bf16[1024,256]{1,0:T(8,128)(2,1)S(1)}, u32[]{:S(2)}, u32[]{:S(2)}) collective-permute-start(bf16[1024,256]{1,0:T(8,128)(2,1)S(1)} %pad_maximum_fusion.refs_2_), channel_id=1, source_target_pairs={{0,64},{4,68},{8,72},{12,76},{16,80},{20,84},{24,88},{28,92},{32,9... | collective-permute-start | bytes 1572872 | tf_op jit(solution)/shard_map/ppermute | solution.py:18
  9.1 4.0 %collective-permute-start.5 = (bf16[1024,256]{1,0:T(8,128)(2,1)S(1)}, bf16[1024,256]{1,0:T(8,128)(2,1)S(1)}, u32[]{:S(2)}, u32[]{:S(2)}) collective-permute-start(bf16[1024,256]{1,0:T(8,128)(2,1)S(1)} %pad_maximum_fusion.refs_2_), channel_id=1, source_target_pairs={{0,16},{4,20},{8,24},{12,28},{16,0},{20,4},{24,8},{28,12},{32,48},... | collective-permute-start | bytes 1572872 | tf_op jit(solution)/shard_map/ppermute | solution.py:18
  13.2 0.0 copy-start.1
  13.2 0.1 pad_maximum_fusion.1
  13.3 0.0 copy-start.2
  13.3 5.2 %collective-permute-start.7 = (bf16[512,256]{1,0:T(8,128)(2,1)S(1)}, bf16[512,256]{1,0:T(8,128)(2,1)S(1)}, u32[]{:S(2)}, u32[]{:S(2)}) collective-permute-start(bf16[512,256]{1,0:T(8,128)(2,1)S(1)} %get-tuple-element.41), channel_id=1, source_target_pairs={{0,32},{4,36},{8,40},{12,44},{16,48},{20,52},{24,56},{28,60},{32,0... | collective-permute-start | bytes 786440 | tf_op jit(solution)/shard_map/ppermute | solution.py:18
  18.6 2.3 %collective-permute-start.6 = (bf16[1024,256]{1,0:T(8,128)(2,1)S(1)}, bf16[1024,256]{1,0:T(8,128)(2,1)S(1)}, u32[]{:S(2)}, u32[]{:S(2)}) collective-permute-start(bf16[1024,256]{1,0:T(8,128)(2,1)S(1)} %pad_maximum_fusion.refs_2_), channel_id=1, source_target_pairs={{0,128},{4,132},{8,136},{12,140},{16,144},{20,148},{24,152},{28,15... | collective-permute-start | bytes 1572872 | tf_op jit(solution)/shard_map/ppermute | solution.py:18
  20.9 2.9 %collective-permute-done.3.refs_5_ = bf16[1024,256]{1,0:T(8,128)(2,1)S(1)} collective-permute-done((bf16[1024,256]{1,0:T(8,128)(2,1)S(1)}, bf16[1024,256]{1,0:T(8,128)(2,1)S(1)}, u32[]{:S(2)}, u32[]{:S(2)}) %collective-permute-start.3) | collective-permute-done | bytes 524320 | tf_op jit(solution)/shard_map/ppermute | solution.py:18
  23.8 4.3 %collective-permute-start.4 = (bf16[1024,256]{1,0:T(8,128)(2,1)S(1)}, bf16[1024,256]{1,0:T(8,128)(2,1)S(1)}, u32[]{:S(2)}, u32[]{:S(2)}) collective-permute-start(bf16[1024,256]{1,0:T(8,128)(2,1)S(1)} %pad_maximum_fusion.refs_2_), channel_id=1, source_target_pairs={{0,256},{4,260},{8,264},{12,268},{16,272},{20,276},{24,280},{28,28... | collective-permute-start | bytes 1572872 | tf_op jit(solution)/shard_map/ppermute | solution.py:18
  28.0 0.0 copy-done.1
  28.0 0.0 copy-done.2
  28.1 2.5 %early1.1 = (f32[1024,128]{1,0:T(8,128)S(1)}, f32[1024,128]{1,0:T(8,128)S(1)}, f32[1024,128]{1,0:T(8,128)S(1)}) custom-call(s32[256]{0:T(256)S(1)} %copy-done.2, bf16[512,256]{1,0:T(8,128)(2,1)S(1)} %copy-done.1, bf16[1024,256]{1,0:T(8,128)(2,1)S(1)} %pad_maximum_fusion.refs_2_, bf16[1024,256]{1,0:T(8,128)(2,1)S(1)} %collective-permute-done.refs_3_.refs_2_), custom_call_target="tpu_custom_call" | custom-call | flops 3221225472 | bytes 786432 | tf_op jit(solution)/shard_map/early1/pallas_call | solution.py:167
  30.6 0.0 collective-permute-done.1.refs_7_
  30.6 0.0 copy-start
  30.6 2.1 %collective-permute-start.2 = (bf16[512,256]{1,0:T(8,128)(2,1)S(1)}, bf16[512,256]{1,0:T(8,128)(2,1)S(1)}, u32[]{:S(2)}, u32[]{:S(2)}) collective-permute-start(bf16[512,256]{1,0:T(8,128)(2,1)S(1)} %get-tuple-element.25), channel_id=1, source_target_pairs={{4,8},{8,4},{12,16},{16,12},{20,24},{24,20},{28,32},{32,28},{36,40... | collective-permute-start | bytes 786440 | tf_op jit(solution)/shard_map/ppermute | solution.py:28
  32.7 2.5 %early0.1 = (f32[1024,128]{1,0:T(8,128)S(1)}, f32[1024,128]{1,0:T(8,128)S(1)}, f32[1024,128]{1,0:T(8,128)S(1)}) custom-call(s32[256]{0:T(256)S(1)} %copy-done.2, bf16[512,256]{1,0:T(8,128)(2,1)S(1)} %copy-done.1, bf16[1024,256]{1,0:T(8,128)(2,1)S(1)} %pad_maximum_fusion.refs_2_, bf16[1024,256]{1,0:T(8,128)(2,1)S(1)} %collective-permute-done.refs_3_.refs_2_), custom_call_target="tpu_custom_call" | custom-call | flops 3221225472 | bytes 786432 | tf_op jit(solution)/shard_map/early0/pallas_call | solution.py:167
  35.2 0.0 collective-permute-done.7.refs_9_
  35.2 4.0 %collective-permute-start.11 = (bf16[512,256]{1,0:T(8,128)(2,1)S(1)}, bf16[512,256]{1,0:T(8,128)(2,1)S(1)}, u32[]{:S(2)}, u32[]{:S(2)}) collective-permute-start(bf16[512,256]{1,0:T(8,128)(2,1)S(1)} %get-tuple-element.35), channel_id=1, source_target_pairs={{0,32},{4,36},{8,40},{12,44},{16,48},{20,52},{24,56},{28,60},{32,0... | collective-permute-start | bytes 786440 | tf_op jit(solution)/shard_map/ppermute | solution.py:18
  39.2 7.8 %collective-permute-done.5.refs_6_ = bf16[1024,256]{1,0:T(8,128)(2,1)S(1)} collective-permute-done((bf16[1024,256]{1,0:T(8,128)(2,1)S(1)}, bf16[1024,256]{1,0:T(8,128)(2,1)S(1)}, u32[]{:S(2)}, u32[]{:S(2)}) %collective-permute-start.5) | collective-permute-done | bytes 524320 | tf_op jit(solution)/shard_map/ppermute | solution.py:18
  47.0 0.0 collective-permute-done.4.refs_4_
  47.0 0.0 collective-permute-done.6.refs_8_
  47.0 15.2 %collective-permute-done.2.refs_3_ = bf16[512,256]{1,0:T(8,128)(2,1)S(1)} collective-permute-done((bf16[512,256]{1,0:T(8,128)(2,1)S(1)}, bf16[512,256]{1,0:T(8,128)(2,1)S(1)}, u32[]{:S(2)}, u32[]{:S(2)}) %collective-permute-start.2) | collective-permute-done | bytes 262176 | tf_op jit(solution)/shard_map/ppermute | solution.py:28
  62.2 0.0 copy-done
  62.2 5.7 %late0.1 = (bf16[256,256]{1,0:T(8,128)(2,1)S(1)}, bf16[256,256]{1,0:T(8,128)(2,1)S(1)}, bf16[256,256]{1,0:T(8,128)(2,1)S(1)}, bf16[256,256]{1,0:T(8,128)(2,1)S(1)}) custom-call(s32[256]{0:T(256)S(1)} %copy-done.2, bf16[512,256]{1,0:T(8,128)(2,1)S(1)} %copy-done.1, bf16[1024,256]{1,0:T(8,128)(2,1)S(1)} %collective-permute-done.refs_3_.refs_2_, ...), custom_call_target="tpu_custom_call" | custom-call | flops 7516192768 | bytes 1835008 | tf_op jit(solution)/shard_map/late0/pallas_call | solution.py:167
  67.9 5.0 %collective-permute-start.8 = (bf16[256,256]{1,0:T(8,128)(2,1)S(1)}, bf16[256,256]{1,0:T(8,128)(2,1)S(1)}, u32[]{:S(2)}, u32[]{:S(2)}) collective-permute-start(bf16[256,256]{1,0:T(8,128)(2,1)S(1)} %get-tuple-element.31), channel_id=1, source_target_pairs={{0,1},{1,2},{2,3},{3,0},{4,5},{5,6},{6,7},{7,4},{8,9},{9,10},{10,1... | collective-permute-start | bytes 393224 | tf_op jit(solution)/shard_map/ppermute | solution.py:248
  72.8 9.1 %collective-permute-start.9 = (bf16[256,256]{1,0:T(8,128)(2,1)S(1)}, bf16[256,256]{1,0:T(8,128)(2,1)S(1)}, u32[]{:S(2)}, u32[]{:S(2)}) collective-permute-start(bf16[256,256]{1,0:T(8,128)(2,1)S(1)} %get-tuple-element.32), channel_id=1, source_target_pairs={{0,2},{1,3},{2,0},{3,1},{4,6},{5,7},{6,4},{7,5},{8,10},{9,11},{10,... | collective-permute-start | bytes 393224 | tf_op jit(solution)/shard_map/ppermute | solution.py:248
  81.9 3.7 %collective-permute-start.10 = (bf16[256,256]{1,0:T(8,128)(2,1)S(1)}, bf16[256,256]{1,0:T(8,128)(2,1)S(1)}, u32[]{:S(2)}, u32[]{:S(2)}) collective-permute-start(bf16[256,256]{1,0:T(8,128)(2,1)S(1)} %get-tuple-element.33), channel_id=1, source_target_pairs={{0,3},{1,0},{2,1},{3,2},{4,7},{5,4},{6,5},{7,6},{8,11},{9,8},{10,9... | collective-permute-start | bytes 393224 | tf_op jit(solution)/shard_map/ppermute | solution.py:248
  85.6 0.0 collective-permute-done.11.refs_9_
  85.6 6.7 %late1.1 = bf16[4,256,256]{2,1,0:T(8,128)(2,1)} custom-call(s32[256]{0:T(256)S(1)} %copy-done.2, bf16[512,256]{1,0:T(8,128)(2,1)S(1)} %copy-done.1, bf16[1024,256]{1,0:T(8,128)(2,1)S(1)} %collective-permute-done.refs_3_.refs_2_, bf16[512,256]{1,0:T(8,128)(2,1)S(1)} %collective-permute-done.2.refs_3_, bf16[1024,256]{1,0:T(8,128)(2,1)S(1)} %collective-permute-done.4.refs_4_, ...), custom_call_target="tpu_custom_call" | custom-call | flops 7516192768 | bytes 1835008 | tf_op jit(solution)/shard_map/late1/pallas_call | solution.py:167
  92.3 0.0 collective-permute-done.8
  92.3 0.0 collective-permute-done.9
  92.3 4.3 %collective-permute-done.10 = bf16[256,256]{1,0:T(8,128)(2,1)S(1)} collective-permute-done((bf16[256,256]{1,0:T(8,128)(2,1)S(1)}, bf16[256,256]{1,0:T(8,128)(2,1)S(1)}, u32[]{:S(2)}, u32[]{:S(2)}) %collective-permute-start.10) | collective-permute-done | bytes 131104 | tf_op jit(solution)/shard_map/ppermute | solution.py:248
  96.6 4.9 %all-to-all-start = ((bf16[4,256,256]{2,1,0:T(8,128)(2,1)}), bf16[4,256,256]{2,1,0:T(8,128)(2,1)S(1)}, u32[]{:S(2)}, u32[]{:S(2)}) async-start(bf16[4,256,256]{2,1,0:T(8,128)(2,1)} %late1.1), calls=%async_computation | async-start | bytes 1048576 | tf_op jit(solution)/shard_map/all_to_all | solution.py:269
  101.5 0.1 add_convert_fusion
  101.6 11.5 %all-to-all-done = bf16[4,256,256]{2,1,0:T(8,128)(2,1)S(1)} async-done(((bf16[4,256,256]{2,1,0:T(8,128)(2,1)}), bf16[4,256,256]{2,1,0:T(8,128)(2,1)S(1)}, u32[]{:S(2)}, u32[]{:S(2)}) %all-to-all-start) | async-done | bytes 524320 | tf_op jit(solution)/shard_map/all_to_all | solution.py:269
  113.1 0.1 reduce_sum.12
  113.2 0.7 pad_maximum_fusion.3
  (1 shorter events, 0.0 us)
Async XLA Ops:
  1.2 4.5 %collective-permute-start = (bf16[1024,256]{1,0:T(8,128)(2,1)S(1)}, bf16[1024,256]{1,0:T(8,128)(2,1)S(1)}, u32[]{:S(2)}, u32[]{:S(2)}) collective-permute-start(bf16[1024,256]{1,0:T(8,128)(2,1)S(1)} %pad_maximum_fusion.refs_2_), channel_id=1, source_target_pairs={{0,4},{4,0},{8,12},{12,8},{16,20},{20,16},{24,28},{28,24},{32,36},... | collective-permute-start | bytes 1572872 | tf_op jit(solution)/shard_map/ppermute | solution.py:18
  3.1 20.7 %collective-permute-start.3 = (bf16[1024,256]{1,0:T(8,128)(2,1)S(1)}, bf16[1024,256]{1,0:T(8,128)(2,1)S(1)}, u32[]{:S(2)}, u32[]{:S(2)}) collective-permute-start(bf16[1024,256]{1,0:T(8,128)(2,1)S(1)} %pad_maximum_fusion.refs_2_), channel_id=1, source_target_pairs={{0,8},{4,12},{8,0},{12,4},{16,24},{20,28},{24,16},{28,20},{32,40},... | collective-permute-start | bytes 1572872 | tf_op jit(solution)/shard_map/ppermute | solution.py:18
  5.7 24.9 %collective-permute-start.1 = (bf16[1024,256]{1,0:T(8,128)(2,1)S(1)}, bf16[1024,256]{1,0:T(8,128)(2,1)S(1)}, u32[]{:S(2)}, u32[]{:S(2)}) collective-permute-start(bf16[1024,256]{1,0:T(8,128)(2,1)S(1)} %pad_maximum_fusion.refs_2_), channel_id=1, source_target_pairs={{0,64},{4,68},{8,72},{12,76},{16,80},{20,84},{24,88},{28,92},{32,9... | collective-permute-start | bytes 1572872 | tf_op jit(solution)/shard_map/ppermute | solution.py:18
  9.1 37.9 %collective-permute-start.5 = (bf16[1024,256]{1,0:T(8,128)(2,1)S(1)}, bf16[1024,256]{1,0:T(8,128)(2,1)S(1)}, u32[]{:S(2)}, u32[]{:S(2)}) collective-permute-start(bf16[1024,256]{1,0:T(8,128)(2,1)S(1)} %pad_maximum_fusion.refs_2_), channel_id=1, source_target_pairs={{0,16},{4,20},{8,24},{12,28},{16,0},{20,4},{24,8},{28,12},{32,48},... | collective-permute-start | bytes 1572872 | tf_op jit(solution)/shard_map/ppermute | solution.py:18
  13.2 14.9 %copy-start.1 = (bf16[512,256]{1,0:T(8,128)(2,1)S(1)}, bf16[512,256]{1,0:T(8,128)(2,1)}, u32[]{:S(2)}) copy-start(bf16[512,256]{1,0:T(8,128)(2,1)} %refs_1_.5) | copy-start | bytes 786436
  13.3 14.8 %copy-start.2 = (s32[256]{0:T(256)S(1)}, s32[256]{0:T(256)}, u32[]{:S(2)}) copy-start(s32[256]{0:T(256)} %refs_0_.7) | copy-start | bytes 3076
  13.3 21.9 %collective-permute-start.7 = (bf16[512,256]{1,0:T(8,128)(2,1)S(1)}, bf16[512,256]{1,0:T(8,128)(2,1)S(1)}, u32[]{:S(2)}, u32[]{:S(2)}) collective-permute-start(bf16[512,256]{1,0:T(8,128)(2,1)S(1)} %get-tuple-element.41), channel_id=1, source_target_pairs={{0,32},{4,36},{8,40},{12,44},{16,48},{20,52},{24,56},{28,60},{32,0... | collective-permute-start | bytes 786440 | tf_op jit(solution)/shard_map/ppermute | solution.py:18
  18.6 28.4 %collective-permute-start.6 = (bf16[1024,256]{1,0:T(8,128)(2,1)S(1)}, bf16[1024,256]{1,0:T(8,128)(2,1)S(1)}, u32[]{:S(2)}, u32[]{:S(2)}) collective-permute-start(bf16[1024,256]{1,0:T(8,128)(2,1)S(1)} %pad_maximum_fusion.refs_2_), channel_id=1, source_target_pairs={{0,128},{4,132},{8,136},{12,140},{16,144},{20,148},{24,152},{28,15... | collective-permute-start | bytes 1572872 | tf_op jit(solution)/shard_map/ppermute | solution.py:18
  23.8 23.2 %collective-permute-start.4 = (bf16[1024,256]{1,0:T(8,128)(2,1)S(1)}, bf16[1024,256]{1,0:T(8,128)(2,1)S(1)}, u32[]{:S(2)}, u32[]{:S(2)}) collective-permute-start(bf16[1024,256]{1,0:T(8,128)(2,1)S(1)} %pad_maximum_fusion.refs_2_), channel_id=1, source_target_pairs={{0,256},{4,260},{8,264},{12,268},{16,272},{20,276},{24,280},{28,28... | collective-permute-start | bytes 1572872 | tf_op jit(solution)/shard_map/ppermute | solution.py:18
  30.6 31.6 %copy-start = (bf16[256,1024]{1,0:T(8,128)(2,1)S(1)}, bf16[256,1024]{1,0:T(8,128)(2,1)}, u32[]{:S(2)}) copy-start(bf16[256,1024]{1,0:T(8,128)(2,1)} %refs_13_.3) | copy-start | bytes 1572868
  30.6 31.6 %collective-permute-start.2 = (bf16[512,256]{1,0:T(8,128)(2,1)S(1)}, bf16[512,256]{1,0:T(8,128)(2,1)S(1)}, u32[]{:S(2)}, u32[]{:S(2)}) collective-permute-start(bf16[512,256]{1,0:T(8,128)(2,1)S(1)} %get-tuple-element.25), channel_id=1, source_target_pairs={{4,8},{8,4},{12,16},{16,12},{20,24},{24,20},{28,32},{32,28},{36,40... | collective-permute-start | bytes 786440 | tf_op jit(solution)/shard_map/ppermute | solution.py:28
  35.2 50.4 %collective-permute-start.11 = (bf16[512,256]{1,0:T(8,128)(2,1)S(1)}, bf16[512,256]{1,0:T(8,128)(2,1)S(1)}, u32[]{:S(2)}, u32[]{:S(2)}) collective-permute-start(bf16[512,256]{1,0:T(8,128)(2,1)S(1)} %get-tuple-element.35), channel_id=1, source_target_pairs={{0,32},{4,36},{8,40},{12,44},{16,48},{20,52},{24,56},{28,60},{32,0... | collective-permute-start | bytes 786440 | tf_op jit(solution)/shard_map/ppermute | solution.py:18
  67.9 24.4 %collective-permute-start.8 = (bf16[256,256]{1,0:T(8,128)(2,1)S(1)}, bf16[256,256]{1,0:T(8,128)(2,1)S(1)}, u32[]{:S(2)}, u32[]{:S(2)}) collective-permute-start(bf16[256,256]{1,0:T(8,128)(2,1)S(1)} %get-tuple-element.31), channel_id=1, source_target_pairs={{0,1},{1,2},{2,3},{3,0},{4,5},{5,6},{6,7},{7,4},{8,9},{9,10},{10,1... | collective-permute-start | bytes 393224 | tf_op jit(solution)/shard_map/ppermute | solution.py:248
  72.8 19.5 %collective-permute-start.9 = (bf16[256,256]{1,0:T(8,128)(2,1)S(1)}, bf16[256,256]{1,0:T(8,128)(2,1)S(1)}, u32[]{:S(2)}, u32[]{:S(2)}) collective-permute-start(bf16[256,256]{1,0:T(8,128)(2,1)S(1)} %get-tuple-element.32), channel_id=1, source_target_pairs={{0,2},{1,3},{2,0},{3,1},{4,6},{5,7},{6,4},{7,5},{8,10},{9,11},{10,... | collective-permute-start | bytes 393224 | tf_op jit(solution)/shard_map/ppermute | solution.py:248
  81.9 14.6 %collective-permute-start.10 = (bf16[256,256]{1,0:T(8,128)(2,1)S(1)}, bf16[256,256]{1,0:T(8,128)(2,1)S(1)}, u32[]{:S(2)}, u32[]{:S(2)}) collective-permute-start(bf16[256,256]{1,0:T(8,128)(2,1)S(1)} %get-tuple-element.33), channel_id=1, source_target_pairs={{0,3},{1,0},{2,1},{3,2},{4,7},{5,4},{6,5},{7,6},{8,11},{9,8},{10,9... | collective-permute-start | bytes 393224 | tf_op jit(solution)/shard_map/ppermute | solution.py:248
  96.6 16.5 %all-to-all-start = ((bf16[4,256,256]{2,1,0:T(8,128)(2,1)}), bf16[4,256,256]{2,1,0:T(8,128)(2,1)S(1)}, u32[]{:S(2)}, u32[]{:S(2)}) async-start(bf16[4,256,256]{2,1,0:T(8,128)(2,1)} %late1.1), calls=%async_computation | async-start | bytes 1048576 | tf_op jit(solution)/shard_map/all_to_all | solution.py:269

commit v7 on v6

--- a/solution.py
+++ b/solution.py
@@ -190,14 +190,14 @@
     packed = jnp.concatenate(parts, axis=0)
     side = lax.rem(lax.axis_index("seq"), 2)
     edge = jnp.where(side == 1, parts[1], parts[0])
+    core = flat_exchange(packed, "seq", 1)
+    halo = halo_exchange(edge, "seq")
     y4a = flat_exchange(parts[0], "seq", 1 << 3)
     y2 = flat_exchange(packed, "seq", 1 << 2)
     y1 = flat_exchange(packed, "seq", 1 << 1)
-    core = flat_exchange(packed, "seq", 1)
     x1 = flat_exchange(after(packed, core), "seq", 1 << 4)
     x2 = flat_exchange(after(packed, core), "seq", 1 << 5)
     z1 = flat_exchange(after(packed, y1), "seq", 1 << 6)
-    halo = halo_exchange(after(edge, x1), "seq")
     y4b = flat_exchange(after(parts[1], x1), "seq", 1 << 3)
 
     state0 = attend(
@@ -205,11 +205,12 @@
         block_keep,
         queries,
         0,
-        [packed, core],
+        [packed, core, halo],
         [
             ("self", 0, 0, 0),
             ("xor", 0, 512, 1),
             ("xor", 1, 0, 2),
+            ("near", (1, 2), 512, -1),
         ],
     )
     state1 = attend(
@@ -217,11 +218,12 @@
         block_keep,
         queries,
         1,
-        [packed, core],
+        [packed, core, halo],
         [
             ("self", 0, 512, 0),
             ("xor", 0, 0, 1),
             ("xor", 1, 512, 2),
+            ("near", (1, 2), 0, 1),
         ],
     )
     mine, *pieces = attend(
@@ -229,15 +231,14 @@
         block_keep,
         after(queries, state1[0]),
         0,
-        [core, halo, z1, y1, y2, x1, x2, y4a],
-        [
-            ("near", (0, 1), 512, -1),
-            ("xor", 2, 0, 128),
-            ("xor", 3, 0, 4),
-            ("xor", 4, 0, 8),
-            ("xor", 5, 0, 32),
-            ("xor", 6, 0, 64),
-            ("xor", 7, 0, 16),
+        [z1, y1, y2, x1, x2, y4a],
+        [
+            ("xor", 0, 0, 128),
+            ("xor", 1, 0, 4),
+            ("xor", 2, 0, 8),
+            ("xor", 3, 0, 32),
+            ("xor", 4, 0, 64),
+            ("xor", 5, 0, 16),
         ],
         state=state0,
         w_out=w_out,
@@ -253,15 +254,14 @@
         block_keep,
         after(queries, mine),
         1,
-        [core, halo, z1, y1, y2, x1, x2, y4b],
-        [
-            ("near", (0, 1), 0, 1),
-            ("xor", 2, 512, 128),
-            ("xor", 3, 512, 4),
-            ("xor", 4, 512, 8),
-            ("xor", 5, 512, 32),
-            ("xor", 6, 512, 64),
-            ("xor", 7, 0, 16),
+        [z1, y1, y2, x1, x2, y4b],
+        [
+            ("xor", 0, 512, 128),
+            ("xor", 1, 512, 4),
+            ("xor", 2, 512, 8),
+            ("xor", 3, 512, 32),
+            ("xor", 4, 512, 64),
+            ("xor", 5, 0, 16),
         ],
         state=state1,
         w_out=w_out,

time: 114 us -> 112 us (0.982)
  the two profiles are of different devices: /device:TPU:48 before, /device:TPU:100 now
where the time goes in v7:
time: 112 us; the launch traced here: 111 us
  waiting for transfers between devices  50.4 us (45%)
  starting transfers between devices  45.8 us (41%)
  Pallas kernels  12.9 us (12%)
  local copies, waits for them, and re-layouts  1.15 us (1%)
    ppermute x8, waiting for transfers between devices, flat_exchange(): return lax.ppermute(value, axis, pairs)  28 us
    ppermute x8, starting transfers between devices, flat_exchange(): return lax.ppermute(value, axis, pairs)  23.6 us
    ppermute x3, starting transfers between devices, per_device(): lax.ppermute(piece, 'head', [(h, (h + hop + 1) % groups) for h in range(g...  16.8 us
    all_to_all x1, waiting for transfers between devices, per_device(): spread = lax.all_to_all(after(shares, *moved), 'head', 0, 0, tiled=False)  16.4 us
    pallas_call x4, Pallas kernels, attend(): pl.pallas_call(lambda *refs: attend_kernel(scale, heads, local, plan, sta...  12.9 us
    ppermute x3, waiting for transfers between devices, per_device(): lax.ppermute(piece, 'head', [(h, (h + hop + 1) % groups) for h in range(g...  5.97 us
    all_to_all x1, starting transfers between devices, per_device(): spread = lax.all_to_all(after(shares, *moved), 'head', 0, 0, tiled=False)  3.54 us
  transfers between devices with their start and end apart: 13, of which 5 were waited for; matrix products, arithmetic and copies ran while one was open for 0% of the time, Pallas kernels for 12%

profile of v7, /device:TPU:100, one launch (start us, length us, event | category | flops | bytes accessed | tf_op | source)
XLA Modules:
  0.0 111.4 jit_solution(9102471690169934454)
XLA Ops:
  0.0 1.1 %fusion = (bf16[256,256]{1,0:T(8,128)(2,1)S(1)}, bf16[256,256]{1,0:T(8,128)(2,1)S(1)}, bf16[256,256]{1,0:T(8,128)(2,1)S(1)}, bf16[256,256]{1,0:T(8,128)(2,1)S(1)}) fusion(bf16[512,256]{1,0:T(8,128)(2,1)} %param.6, bf16[512,256]{1,0:T(8,128)(2,1)} %param.7), kind=kLoop, calls=%fused_computation.6 | loop fusion | bytes 1048576 | tf_op jit(solution)/shard_map/slice | solution.py:188
  1.2 1.9 %collective-permute-start = (bf16[1024,256]{1,0:T(8,128)(2,1)S(1)}, bf16[1024,256]{1,0:T(8,128)(2,1)S(1)}, u32[]{:S(2)}, u32[]{:S(2)}) collective-permute-start(bf16[1024,256]{1,0:T(8,128)(2,1)S(1)} %pad_maximum_fusion.refs_2_), channel_id=1, source_target_pairs={{0,4},{4,0},{8,12},{12,8},{16,20},{20,16},{24,28},{28,24},{32,36},... | collective-permute-start | bytes 1572872 | tf_op jit(solution)/shard_map/ppermute | solution.py:18
  3.1 2.6 %collective-permute-start.2 = (bf16[1024,256]{1,0:T(8,128)(2,1)S(1)}, bf16[1024,256]{1,0:T(8,128)(2,1)S(1)}, u32[]{:S(2)}, u32[]{:S(2)}) collective-permute-start(bf16[1024,256]{1,0:T(8,128)(2,1)S(1)} %pad_maximum_fusion.refs_2_), channel_id=1, source_target_pairs={{0,8},{4,12},{8,0},{12,4},{16,24},{20,28},{24,16},{28,20},{32,40},... | collective-permute-start | bytes 1572872 | tf_op jit(solution)/shard_map/ppermute | solution.py:18
  5.7 0.0 copy-start.1
  5.7 0.1 pad_maximum_fusion.1
  5.8 0.0 copy-start.2
  5.8 2.0 %collective-permute-start.1 = (bf16[512,256]{1,0:T(8,128)(2,1)S(1)}, bf16[512,256]{1,0:T(8,128)(2,1)S(1)}, u32[]{:S(2)}, u32[]{:S(2)}) collective-permute-start(bf16[512,256]{1,0:T(8,128)(2,1)S(1)} %get-tuple-element.38), channel_id=1, source_target_pairs={{4,8},{8,4},{12,16},{16,12},{20,24},{24,20},{28,32},{32,28},{36,40... | collective-permute-start | bytes 786440 | tf_op jit(solution)/shard_map/ppermute | solution.py:28
  7.8 4.5 %collective-permute-start.4 = (bf16[1024,256]{1,0:T(8,128)(2,1)S(1)}, bf16[1024,256]{1,0:T(8,128)(2,1)S(1)}, u32[]{:S(2)}, u32[]{:S(2)}) collective-permute-start(bf16[1024,256]{1,0:T(8,128)(2,1)S(1)} %pad_maximum_fusion.refs_2_), channel_id=1, source_target_pairs={{0,16},{4,20},{8,24},{12,28},{16,0},{20,4},{24,8},{28,12},{32,48},... | collective-permute-start | bytes 1572872 | tf_op jit(solution)/shard_map/ppermute | solution.py:18
  12.3 3.3 %collective-permute-start.7 = (bf16[512,256]{1,0:T(8,128)(2,1)S(1)}, bf16[512,256]{1,0:T(8,128)(2,1)S(1)}, u32[]{:S(2)}, u32[]{:S(2)}) collective-permute-start(bf16[512,256]{1,0:T(8,128)(2,1)S(1)} %get-tuple-element.39), channel_id=1, source_target_pairs={{0,32},{4,36},{8,40},{12,44},{16,48},{20,52},{24,56},{28,60},{32,0... | collective-permute-start | bytes 786440 | tf_op jit(solution)/shard_map/ppermute | solution.py:18
  15.6 0.0 collective-permute-done.refs_3_
  15.6 3.4 %collective-permute-start.5 = (bf16[1024,256]{1,0:T(8,128)(2,1)S(1)}, bf16[1024,256]{1,0:T(8,128)(2,1)S(1)}, u32[]{:S(2)}, u32[]{:S(2)}) collective-permute-start(bf16[1024,256]{1,0:T(8,128)(2,1)S(1)} %pad_maximum_fusion.refs_2_), channel_id=1, source_target_pairs={{0,64},{4,68},{8,72},{12,76},{16,80},{20,84},{24,88},{28,92},{32,9... | collective-permute-start | bytes 1572872 | tf_op jit(solution)/shard_map/ppermute | solution.py:18
  19.1 8.4 %collective-permute-done.2.refs_3_ = bf16[1024,256]{1,0:T(8,128)(2,1)S(1)} collective-permute-done((bf16[1024,256]{1,0:T(8,128)(2,1)S(1)}, bf16[1024,256]{1,0:T(8,128)(2,1)S(1)}, u32[]{:S(2)}, u32[]{:S(2)}) %collective-permute-start.2) | collective-permute-done | bytes 524320 | tf_op jit(solution)/shard_map/ppermute | solution.py:18
  27.4 2.4 %collective-permute-start.6 = (bf16[1024,256]{1,0:T(8,128)(2,1)S(1)}, bf16[1024,256]{1,0:T(8,128)(2,1)S(1)}, u32[]{:S(2)}, u32[]{:S(2)}) collective-permute-start(bf16[1024,256]{1,0:T(8,128)(2,1)S(1)} %pad_maximum_fusion.refs_2_), channel_id=1, source_target_pairs={{0,128},{4,132},{8,136},{12,140},{16,144},{20,148},{24,152},{28,15... | collective-permute-start | bytes 1572872 | tf_op jit(solution)/shard_map/ppermute | solution.py:18
  29.8 0.0 collective-permute-done.1.refs_4_
  29.9 1.9 %collective-permute-start.3 = (bf16[1024,256]{1,0:T(8,128)(2,1)S(1)}, bf16[1024,256]{1,0:T(8,128)(2,1)S(1)}, u32[]{:S(2)}, u32[]{:S(2)}) collective-permute-start(bf16[1024,256]{1,0:T(8,128)(2,1)S(1)} %pad_maximum_fusion.refs_2_), channel_id=1, source_target_pairs={{0,256},{4,260},{8,264},{12,268},{16,272},{20,276},{24,280},{28,28... | collective-permute-start | bytes 1572872 | tf_op jit(solution)/shard_map/ppermute | solution.py:18
  31.8 0.0 copy-done.1
  31.8 0.0 copy-done.2
  31.8 2.4 %early1.1 = (f32[1024,128]{1,0:T(8,128)S(1)}, f32[1024,128]{1,0:T(8,128)S(1)}, f32[1024,128]{1,0:T(8,128)S(1)}) custom-call(s32[256]{0:T(256)S(1)} %copy-done.2, bf16[512,256]{1,0:T(8,128)(2,1)S(1)} %copy-done.1, bf16[1024,256]{1,0:T(8,128)(2,1)S(1)} %pad_maximum_fusion.refs_2_, bf16[1024,256]{1,0:T(8,128)(2,1)S(1)} %collective-permute-done.refs_3_, ...), custom_call_target="tpu_custom_call" | custom-call | flops 4294967296 | bytes 1048576 | tf_op jit(solution)/shard_map/early1/pallas_call | solution.py:167
  34.2 0.0 copy-start
  34.2 2.4 %early0.1 = (f32[1024,128]{1,0:T(8,128)S(1)}, f32[1024,128]{1,0:T(8,128)S(1)}, f32[1024,128]{1,0:T(8,128)S(1)}) custom-call(s32[256]{0:T(256)S(1)} %copy-done.2, bf16[512,256]{1,0:T(8,128)(2,1)S(1)} %copy-done.1, bf16[1024,256]{1,0:T(8,128)(2,1)S(1)} %pad_maximum_fusion.refs_2_, bf16[1024,256]{1,0:T(8,128)(2,1)S(1)} %collective-permute-done.refs_3_, ...), custom_call_target="tpu_custom_call" | custom-call | flops 4294967296 | bytes 1048576 | tf_op jit(solution)/shard_map/early0/pallas_call | solution.py:167
  36.6 0.0 collective-permute-done.5.refs_5_
  36.6 3.5 %collective-permute-start.11 = (bf16[512,256]{1,0:T(8,128)(2,1)S(1)}, bf16[512,256]{1,0:T(8,128)(2,1)S(1)}, u32[]{:S(2)}, u32[]{:S(2)}) collective-permute-start(bf16[512,256]{1,0:T(8,128)(2,1)S(1)} %get-tuple-element.33), channel_id=1, source_target_pairs={{0,32},{4,36},{8,40},{12,44},{16,48},{20,52},{24,56},{28,60},{32,0... | collective-permute-start | bytes 786440 | tf_op jit(solution)/shard_map/ppermute | solution.py:18
  40.1 1.8 %collective-permute-done.7.refs_7_ = bf16[512,256]{1,0:T(8,128)(2,1)S(1)} collective-permute-done((bf16[512,256]{1,0:T(8,128)(2,1)S(1)}, bf16[512,256]{1,0:T(8,128)(2,1)S(1)}, u32[]{:S(2)}, u32[]{:S(2)}) %collective-permute-start.7) | collective-permute-done | bytes 262176 | tf_op jit(solution)/shard_map/ppermute | solution.py:18
  42.0 17.7 %collective-permute-done.4.refs_4_ = bf16[1024,256]{1,0:T(8,128)(2,1)S(1)} collective-permute-done((bf16[1024,256]{1,0:T(8,128)(2,1)S(1)}, bf16[1024,256]{1,0:T(8,128)(2,1)S(1)}, u32[]{:S(2)}, u32[]{:S(2)}) %collective-permute-start.4) | collective-permute-done | bytes 524320 | tf_op jit(solution)/shard_map/ppermute | solution.py:18
  59.7 0.0 collective-permute-done.6.refs_6_
  59.7 0.0 collective-permute-done.3.refs_2_
  59.7 0.0 copy-done
  59.7 3.6 %late0.1 = (bf16[256,256]{1,0:T(8,128)(2,1)S(1)}, bf16[256,256]{1,0:T(8,128)(2,1)S(1)}, bf16[256,256]{1,0:T(8,128)(2,1)S(1)}, bf16[256,256]{1,0:T(8,128)(2,1)S(1)}) custom-call(s32[256]{0:T(256)S(1)} %copy-done.2, bf16[512,256]{1,0:T(8,128)(2,1)S(1)} %copy-done.1, bf16[1024,256]{1,0:T(8,128)(2,1)S(1)} %collective-permute-done.3.refs_2_, ...), custom_call_target="tpu_custom_call" | custom-call | flops 6442450944 | bytes 1572864 | tf_op jit(solution)/shard_map/late0/pallas_call | solution.py:167
  63.4 10.0 %collective-permute-start.10 = (bf16[256,256]{1,0:T(8,128)(2,1)S(1)}, bf16[256,256]{1,0:T(8,128)(2,1)S(1)}, u32[]{:S(2)}, u32[]{:S(2)}) collective-permute-start(bf16[256,256]{1,0:T(8,128)(2,1)S(1)} %get-tuple-element.31), channel_id=1, source_target_pairs={{0,3},{1,0},{2,1},{3,2},{4,7},{5,4},{6,5},{7,6},{8,11},{9,8},{10,9... | collective-permute-start | bytes 393224 | tf_op jit(solution)/shard_map/ppermute | solution.py:249
  73.4 1.9 %collective-permute-start.8 = (bf16[256,256]{1,0:T(8,128)(2,1)S(1)}, bf16[256,256]{1,0:T(8,128)(2,1)S(1)}, u32[]{:S(2)}, u32[]{:S(2)}) collective-permute-start(bf16[256,256]{1,0:T(8,128)(2,1)S(1)} %get-tuple-element.29), channel_id=1, source_target_pairs={{0,1},{1,2},{2,3},{3,0},{4,5},{5,6},{6,7},{7,4},{8,9},{9,10},{10,1... | collective-permute-start | bytes 393224 | tf_op jit(solution)/shard_map/ppermute | solution.py:249
  75.3 4.8 %collective-permute-start.9 = (bf16[256,256]{1,0:T(8,128)(2,1)S(1)}, bf16[256,256]{1,0:T(8,128)(2,1)S(1)}, u32[]{:S(2)}, u32[]{:S(2)}) collective-permute-start(bf16[256,256]{1,0:T(8,128)(2,1)S(1)} %get-tuple-element.30), channel_id=1, source_target_pairs={{0,2},{1,3},{2,0},{3,1},{4,6},{5,7},{6,4},{7,5},{8,10},{9,11},{10,... | collective-permute-start | bytes 393224 | tf_op jit(solution)/shard_map/ppermute | solution.py:249
  80.1 0.0 collective-permute-done.11.refs_7_
  80.1 4.5 %late1.1 = bf16[4,256,256]{2,1,0:T(8,128)(2,1)} custom-call(s32[256]{0:T(256)S(1)} %copy-done.2, bf16[512,256]{1,0:T(8,128)(2,1)S(1)} %copy-done.1, bf16[1024,256]{1,0:T(8,128)(2,1)S(1)} %collective-permute-done.3.refs_2_, bf16[1024,256]{1,0:T(8,128)(2,1)S(1)} %collective-permute-done.2.refs_3_, bf16[1024,256]{1,0:T(8,128)(2,1)S(1)} %collective-permute-done.4.refs_4_, ...), custom_call_target="tpu_custom_call" | custom-call | flops 6442450944 | bytes 1572864 | tf_op jit(solution)/shard_map/late1/pallas_call | solution.py:167
  84.6 0.0 collective-permute-done.10
  84.6 6.0 %collective-permute-done.8 = bf16[256,256]{1,0:T(8,128)(2,1)S(1)} collective-permute-done((bf16[256,256]{1,0:T(8,128)(2,1)S(1)}, bf16[256,256]{1,0:T(8,128)(2,1)S(1)}, u32[]{:S(2)}, u32[]{:S(2)}) %collective-permute-start.8) | collective-permute-done | bytes 131104 | tf_op jit(solution)/shard_map/ppermute | solution.py:249
  90.6 0.0 collective-permute-done.9
  90.6 3.5 %all-to-all-start = ((bf16[4,256,256]{2,1,0:T(8,128)(2,1)}), bf16[4,256,256]{2,1,0:T(8,128)(2,1)S(1)}, u32[]{:S(2)}, u32[]{:S(2)}) async-start(bf16[4,256,256]{2,1,0:T(8,128)(2,1)} %late1.1), calls=%async_computation | async-start | bytes 1048576 | tf_op jit(solution)/shard_map/all_to_all | solution.py:269
  94.1 0.1 add_convert_fusion
  94.2 16.4 %all-to-all-done = bf16[4,256,256]{2,1,0:T(8,128)(2,1)S(1)} async-done(((bf16[4,256,256]{2,1,0:T(8,128)(2,1)}), bf16[4,256,256]{2,1,0:T(8,128)(2,1)S(1)}, u32[]{:S(2)}, u32[]{:S(2)}) %all-to-all-start) | async-done | bytes 524320 | tf_op jit(solution)/shard_map/all_to_all | solution.py:269
  110.6 0.1 reduce_sum.12
  110.7 0.7 pad_maximum_fusion.3
  (1 shorter events, 0.0 us)
Async XLA Ops:
  1.2 14.5 %collective-permute-start = (bf16[1024,256]{1,0:T(8,128)(2,1)S(1)}, bf16[1024,256]{1,0:T(8,128)(2,1)S(1)}, u32[]{:S(2)}, u32[]{:S(2)}) collective-permute-start(bf16[1024,256]{1,0:T(8,128)(2,1)S(1)} %pad_maximum_fusion.refs_2_), channel_id=1, source_target_pairs={{0,4},{4,0},{8,12},{12,8},{16,20},{20,16},{24,28},{28,24},{32,36},... | collective-permute-start | bytes 1572872 | tf_op jit(solution)/shard_map/ppermute | solution.py:18
  3.1 24.3 %collective-permute-start.2 = (bf16[1024,256]{1,0:T(8,128)(2,1)S(1)}, bf16[1024,256]{1,0:T(8,128)(2,1)S(1)}, u32[]{:S(2)}, u32[]{:S(2)}) collective-permute-start(bf16[1024,256]{1,0:T(8,128)(2,1)S(1)} %pad_maximum_fusion.refs_2_), channel_id=1, source_target_pairs={{0,8},{4,12},{8,0},{12,4},{16,24},{20,28},{24,16},{28,20},{32,40},... | collective-permute-start | bytes 1572872 | tf_op jit(solution)/shard_map/ppermute | solution.py:18
  5.7 26.1 %copy-start.1 = (bf16[512,256]{1,0:T(8,128)(2,1)S(1)}, bf16[512,256]{1,0:T(8,128)(2,1)}, u32[]{:S(2)}) copy-start(bf16[512,256]{1,0:T(8,128)(2,1)} %refs_1_.5) | copy-start | bytes 786436
  5.8 26.0 %copy-start.2 = (s32[256]{0:T(256)S(1)}, s32[256]{0:T(256)}, u32[]{:S(2)}) copy-start(s32[256]{0:T(256)} %refs_0_.7) | copy-start | bytes 3076
  5.8 24.0 %collective-permute-start.1 = (bf16[512,256]{1,0:T(8,128)(2,1)S(1)}, bf16[512,256]{1,0:T(8,128)(2,1)S(1)}, u32[]{:S(2)}, u32[]{:S(2)}) collective-permute-start(bf16[512,256]{1,0:T(8,128)(2,1)S(1)} %get-tuple-element.38), channel_id=1, source_target_pairs={{4,8},{8,4},{12,16},{16,12},{20,24},{24,20},{28,32},{32,28},{36,40... | collective-permute-start | bytes 786440 | tf_op jit(solution)/shard_map/ppermute | solution.py:28
  7.8 51.9 %collective-permute-start.4 = (bf16[1024,256]{1,0:T(8,128)(2,1)S(1)}, bf16[1024,256]{1,0:T(8,128)(2,1)S(1)}, u32[]{:S(2)}, u32[]{:S(2)}) collective-permute-start(bf16[1024,256]{1,0:T(8,128)(2,1)S(1)} %pad_maximum_fusion.refs_2_), channel_id=1, source_target_pairs={{0,16},{4,20},{8,24},{12,28},{16,0},{20,4},{24,8},{28,12},{32,48},... | collective-permute-start | bytes 1572872 | tf_op jit(solution)/shard_map/ppermute | solution.py:18
  12.3 29.7 %collective-permute-start.7 = (bf16[512,256]{1,0:T(8,128)(2,1)S(1)}, bf16[512,256]{1,0:T(8,128)(2,1)S(1)}, u32[]{:S(2)}, u32[]{:S(2)}) collective-permute-start(bf16[512,256]{1,0:T(8,128)(2,1)S(1)} %get-tuple-element.39), channel_id=1, source_target_pairs={{0,32},{4,36},{8,40},{12,44},{16,48},{20,52},{24,56},{28,60},{32,0... | collective-permute-start | bytes 786440 | tf_op jit(solution)/shard_map/ppermute | solution.py:18
  15.6 21.0 %collective-permute-start.5 = (bf16[1024,256]{1,0:T(8,128)(2,1)S(1)}, bf16[1024,256]{1,0:T(8,128)(2,1)S(1)}, u32[]{:S(2)}, u32[]{:S(2)}) collective-permute-start(bf16[1024,256]{1,0:T(8,128)(2,1)S(1)} %pad_maximum_fusion.refs_2_), channel_id=1, source_target_pairs={{0,64},{4,68},{8,72},{12,76},{16,80},{20,84},{24,88},{28,92},{32,9... | collective-permute-start | bytes 1572872 | tf_op jit(solution)/shard_map/ppermute | solution.py:18
  27.4 32.3 %collective-permute-start.6 = (bf16[1024,256]{1,0:T(8,128)(2,1)S(1)}, bf16[1024,256]{1,0:T(8,128)(2,1)S(1)}, u32[]{:S(2)}, u32[]{:S(2)}) collective-permute-start(bf16[1024,256]{1,0:T(8,128)(2,1)S(1)} %pad_maximum_fusion.refs_2_), channel_id=1, source_target_pairs={{0,128},{4,132},{8,136},{12,140},{16,144},{20,148},{24,152},{28,15... | collective-permute-start | bytes 1572872 | tf_op jit(solution)/shard_map/ppermute | solution.py:18
  29.9 29.8 %collective-permute-start.3 = (bf16[1024,256]{1,0:T(8,128)(2,1)S(1)}, bf16[1024,256]{1,0:T(8,128)(2,1)S(1)}, u32[]{:S(2)}, u32[]{:S(2)}) collective-permute-start(bf16[1024,256]{1,0:T(8,128)(2,1)S(1)} %pad_maximum_fusion.refs_2_), channel_id=1, source_target_pairs={{0,256},{4,260},{8,264},{12,268},{16,272},{20,276},{24,280},{28,28... | collective-permute-start | bytes 1572872 | tf_op jit(solution)/shard_map/ppermute | solution.py:18
  34.2 25.5 %copy-start = (bf16[256,1024]{1,0:T(8,128)(2,1)S(1)}, bf16[256,1024]{1,0:T(8,128)(2,1)}, u32[]{:S(2)}) copy-start(bf16[256,1024]{1,0:T(8,128)(2,1)} %refs_11_.3) | copy-start | bytes 1572868
  36.6 43.5 %collective-permute-start.11 = (bf16[512,256]{1,0:T(8,128)(2,1)S(1)}, bf16[512,256]{1,0:T(8,128)(2,1)S(1)}, u32[]{:S(2)}, u32[]{:S(2)}) collective-permute-start(bf16[512,256]{1,0:T(8,128)(2,1)S(1)} %get-tuple-element.33), channel_id=1, source_target_pairs={{0,32},{4,36},{8,40},{12,44},{16,48},{20,52},{24,56},{28,60},{32,0... | collective-permute-start | bytes 786440 | tf_op jit(solution)/shard_map/ppermute | solution.py:18
  63.4 21.2 %collective-permute-start.10 = (bf16[256,256]{1,0:T(8,128)(2,1)S(1)}, bf16[256,256]{1,0:T(8,128)(2,1)S(1)}, u32[]{:S(2)}, u32[]{:S(2)}) collective-permute-start(bf16[256,256]{1,0:T(8,128)(2,1)S(1)} %get-tuple-element.31), channel_id=1, source_target_pairs={{0,3},{1,0},{2,1},{3,2},{4,7},{5,4},{6,5},{7,6},{8,11},{9,8},{10,9... | collective-permute-start | bytes 393224 | tf_op jit(solution)/shard_map/ppermute | solution.py:249
  73.4 17.2 %collective-permute-start.8 = (bf16[256,256]{1,0:T(8,128)(2,1)S(1)}, bf16[256,256]{1,0:T(8,128)(2,1)S(1)}, u32[]{:S(2)}, u32[]{:S(2)}) collective-permute-start(bf16[256,256]{1,0:T(8,128)(2,1)S(1)} %get-tuple-element.29), channel_id=1, source_target_pairs={{0,1},{1,2},{2,3},{3,0},{4,5},{5,6},{6,7},{7,4},{8,9},{9,10},{10,1... | collective-permute-start | bytes 393224 | tf_op jit(solution)/shard_map/ppermute | solution.py:249
  75.3 15.2 %collective-permute-start.9 = (bf16[256,256]{1,0:T(8,128)(2,1)S(1)}, bf16[256,256]{1,0:T(8,128)(2,1)S(1)}, u32[]{:S(2)}, u32[]{:S(2)}) collective-permute-start(bf16[256,256]{1,0:T(8,128)(2,1)S(1)} %get-tuple-element.30), channel_id=1, source_target_pairs={{0,2},{1,3},{2,0},{3,1},{4,6},{5,7},{6,4},{7,5},{8,10},{9,11},{10,... | collective-permute-start | bytes 393224 | tf_op jit(solution)/shard_map/ppermute | solution.py:249
  90.6 20.0 %all-to-all-start = ((bf16[4,256,256]{2,1,0:T(8,128)(2,1)}), bf16[4,256,256]{2,1,0:T(8,128)(2,1)S(1)}, u32[]{:S(2)}, u32[]{:S(2)}) async-start(bf16[4,256,256]{2,1,0:T(8,128)(2,1)} %late1.1), calls=%async_computation | async-start | bytes 1048576 | tf_op jit(solution)/shard_map/all_to_all | solution.py:269

commit v8 on v7

--- a/solution.py
+++ b/solution.py
@@ -193,12 +193,13 @@
     core = flat_exchange(packed, "seq", 1)
     halo = halo_exchange(edge, "seq")
     y4a = flat_exchange(parts[0], "seq", 1 << 3)
-    y2 = flat_exchange(packed, "seq", 1 << 2)
+    y2a = flat_exchange(parts[0], "seq", 1 << 2)
     y1 = flat_exchange(packed, "seq", 1 << 1)
     x1 = flat_exchange(after(packed, core), "seq", 1 << 4)
-    x2 = flat_exchange(after(packed, core), "seq", 1 << 5)
-    z1 = flat_exchange(after(packed, y1), "seq", 1 << 6)
-    y4b = flat_exchange(after(parts[1], x1), "seq", 1 << 3)
+    x2 = flat_exchange(after(packed, x1), "seq", 1 << 5)
+    z1 = flat_exchange(after(packed, x1), "seq", 1 << 6)
+    y2b = flat_exchange(after(parts[1], y2a), "seq", 1 << 2)
+    y4b = flat_exchange(after(parts[1], y2a), "seq", 1 << 3)
 
     state0 = attend(
         "early0",
@@ -231,13 +232,13 @@
         block_keep,
         after(queries, state1[0]),
         0,
-        [z1, y1, y2, x1, x2, y4a],
+        [z1, y1, x1, x2, y2a, y4a],
         [
             ("xor", 0, 0, 128),
             ("xor", 1, 0, 4),
-            ("xor", 2, 0, 8),
-            ("xor", 3, 0, 32),
-            ("xor", 4, 0, 64),
+            ("xor", 2, 0, 32),
+            ("xor", 3, 0, 64),
+            ("xor", 4, 0, 8),
             ("xor", 5, 0, 16),
         ],
         state=state0,
@@ -254,13 +255,13 @@
         block_keep,
         after(queries, mine),
         1,
-        [z1, y1, y2, x1, x2, y4b],
+        [z1, y1, x1, x2, y2b, y4b],
         [
             ("xor", 0, 512, 128),
             ("xor", 1, 512, 4),
-            ("xor", 2, 512, 8),
-            ("xor", 3, 512, 32),
-            ("xor", 4, 512, 64),
+            ("xor", 2, 512, 32),
+            ("xor", 3, 512, 64),
+            ("xor", 4, 0, 8),
             ("xor", 5, 0, 16),
         ],
         state=state1,

time: 112 us -> 110 us (0.982)
  the two profiles are of different devices: /device:TPU:100 before, /device:TPU:56 now
where the time goes in v8:
time: 110 us; the launch traced here: 109 us
  starting transfers between devices  57.6 us (52%)
  waiting for transfers between devices  36.1 us (33%)
  Pallas kernels  12.8 us (12%)
  local copies, waits for them, and re-layouts  1.15 us (1%)
    ppermute x9, starting transfers between devices, flat_exchange(): return lax.ppermute(value, axis, pairs)  32.2 us
    ppermute x9, waiting for transfers between devices, flat_exchange(): return lax.ppermute(value, axis, pairs)  17.9 us
    ppermute x3, starting transfers between devices, per_device(): lax.ppermute(piece, 'head', [(h, (h + hop + 1) % groups) for h in range(g...  17.6 us
    all_to_all x1, waiting for transfers between devices, per_device(): spread = lax.all_to_all(after(shares, *moved), 'head', 0, 0, tiled=False)  13.6 us
    pallas_call x4, Pallas kernels, attend(): pl.pallas_call(lambda *refs: attend_kernel(scale, heads, local, plan, sta...  12.8 us
    all_to_all x1, starting transfers between devices, per_device(): spread = lax.all_to_all(after(shares, *moved), 'head', 0, 0, tiled=False)  5.34 us
    ppermute x3, waiting for transfers between devices, per_device(): lax.ppermute(piece, 'head', [(h, (h + hop + 1) % groups) for h in range(g...  4.58 us
    ppermute x1, starting transfers between devices, halo_exchange(): return lax.ppermute(value, axis, pairs)  2.44 us
  transfers between devices with their start and end apart: 14, of which 5 were waited for; matrix products, arithmetic and copies ran while one was open for 0% of the time, Pallas kernels for 12%

profile of v8, /device:TPU:56, one launch (start us, length us, event | category | flops | bytes accessed | tf_op | source)
XLA Modules:
  0.0 108.9 jit_solution(17145939733443927723)
XLA Ops:
  0.0 1.1 %fusion = (bf16[256,256]{1,0:T(8,128)(2,1)S(1)}, bf16[256,256]{1,0:T(8,128)(2,1)S(1)}, bf16[256,256]{1,0:T(8,128)(2,1)S(1)}, bf16[256,256]{1,0:T(8,128)(2,1)S(1)}) fusion(bf16[512,256]{1,0:T(8,128)(2,1)} %param.6, bf16[512,256]{1,0:T(8,128)(2,1)} %param.7), kind=kLoop, calls=%fused_computation.6 | loop fusion | bytes 1048576 | tf_op jit(solution)/shard_map/slice | solution.py:188
  1.2 1.9 %collective-permute-start = (bf16[1024,256]{1,0:T(8,128)(2,1)S(1)}, bf16[1024,256]{1,0:T(8,128)(2,1)S(1)}, u32[]{:S(2)}, u32[]{:S(2)}) collective-permute-start(bf16[1024,256]{1,0:T(8,128)(2,1)S(1)} %pad_maximum_fusion.refs_2_), channel_id=1, source_target_pairs={{0,4},{4,0},{8,12},{12,8},{16,20},{20,16},{24,28},{28,24},{32,36},... | collective-permute-start | bytes 1572872 | tf_op jit(solution)/shard_map/ppermute | solution.py:18
  3.1 1.9 %collective-permute-done.refs_3_ = bf16[1024,256]{1,0:T(8,128)(2,1)S(1)} collective-permute-done((bf16[1024,256]{1,0:T(8,128)(2,1)S(1)}, bf16[1024,256]{1,0:T(8,128)(2,1)S(1)}, u32[]{:S(2)}, u32[]{:S(2)}) %collective-permute-start) | collective-permute-done | bytes 524320 | tf_op jit(solution)/shard_map/ppermute | solution.py:18
  5.0 3.4 %collective-permute-start.2 = (bf16[1024,256]{1,0:T(8,128)(2,1)S(1)}, bf16[1024,256]{1,0:T(8,128)(2,1)S(1)}, u32[]{:S(2)}, u32[]{:S(2)}) collective-permute-start(bf16[1024,256]{1,0:T(8,128)(2,1)S(1)} %pad_maximum_fusion.refs_2_), channel_id=1, source_target_pairs={{0,64},{4,68},{8,72},{12,76},{16,80},{20,84},{24,88},{28,92},{32,9... | collective-permute-start | bytes 1572872 | tf_op jit(solution)/shard_map/ppermute | solution.py:18
  8.4 0.0 copy-start.1
  8.4 0.1 pad_maximum_fusion.1
  8.5 4.0 %collective-permute-start.6 = (bf16[512,256]{1,0:T(8,128)(2,1)S(1)}, bf16[512,256]{1,0:T(8,128)(2,1)S(1)}, u32[]{:S(2)}, u32[]{:S(2)}) collective-permute-start(bf16[512,256]{1,0:T(8,128)(2,1)S(1)} %get-tuple-element.39), channel_id=1, source_target_pairs={{0,16},{4,20},{8,24},{12,28},{16,0},{20,4},{24,8},{28,12},{32,48},... | collective-permute-start | bytes 786440 | tf_op jit(solution)/shard_map/ppermute | solution.py:18
  12.5 0.0 copy-start.2
  12.6 2.4 %collective-permute-start.1 = (bf16[512,256]{1,0:T(8,128)(2,1)S(1)}, bf16[512,256]{1,0:T(8,128)(2,1)S(1)}, u32[]{:S(2)}, u32[]{:S(2)}) collective-permute-start(bf16[512,256]{1,0:T(8,128)(2,1)S(1)} %get-tuple-element.38), channel_id=1, source_target_pairs={{4,8},{8,4},{12,16},{16,12},{20,24},{24,20},{28,32},{32,28},{36,40... | collective-permute-start | bytes 786440 | tf_op jit(solution)/shard_map/ppermute | solution.py:28
  15.0 6.2 %collective-permute-start.7 = (bf16[512,256]{1,0:T(8,128)(2,1)S(1)}, bf16[512,256]{1,0:T(8,128)(2,1)S(1)}, u32[]{:S(2)}, u32[]{:S(2)}) collective-permute-start(bf16[512,256]{1,0:T(8,128)(2,1)S(1)} %get-tuple-element.39), channel_id=1, source_target_pairs={{0,32},{4,36},{8,40},{12,44},{16,48},{20,52},{24,56},{28,60},{32,0... | collective-permute-start | bytes 786440 | tf_op jit(solution)/shard_map/ppermute | solution.py:18
  21.2 2.5 %collective-permute-start.4 = (bf16[1024,256]{1,0:T(8,128)(2,1)S(1)}, bf16[1024,256]{1,0:T(8,128)(2,1)S(1)}, u32[]{:S(2)}, u32[]{:S(2)}) collective-permute-start(bf16[1024,256]{1,0:T(8,128)(2,1)S(1)} %pad_maximum_fusion.refs_2_), channel_id=1, source_target_pairs={{0,8},{4,12},{8,0},{12,4},{16,24},{20,28},{24,16},{28,20},{32,40},... | collective-permute-start | bytes 1572872 | tf_op jit(solution)/shard_map/ppermute | solution.py:18
  23.7 8.4 %collective-permute-done.6.refs_6_ = bf16[512,256]{1,0:T(8,128)(2,1)S(1)} collective-permute-done((bf16[512,256]{1,0:T(8,128)(2,1)S(1)}, bf16[512,256]{1,0:T(8,128)(2,1)S(1)}, u32[]{:S(2)}, u32[]{:S(2)}) %collective-permute-start.6) | collective-permute-done | bytes 262176 | tf_op jit(solution)/shard_map/ppermute | solution.py:18
  32.1 1.9 %collective-permute-start.11 = (bf16[512,256]{1,0:T(8,128)(2,1)S(1)}, bf16[512,256]{1,0:T(8,128)(2,1)S(1)}, u32[]{:S(2)}, u32[]{:S(2)}) collective-permute-start(bf16[512,256]{1,0:T(8,128)(2,1)S(1)} %get-tuple-element.33), channel_id=1, source_target_pairs={{0,16},{4,20},{8,24},{12,28},{16,0},{20,4},{24,8},{28,12},{32,48},... | collective-permute-start | bytes 786440 | tf_op jit(solution)/shard_map/ppermute | solution.py:18
  34.0 0.0 collective-permute-done.2.refs_4_
  34.0 3.9 %collective-permute-start.3 = (bf16[1024,256]{1,0:T(8,128)(2,1)S(1)}, bf16[1024,256]{1,0:T(8,128)(2,1)S(1)}, u32[]{:S(2)}, u32[]{:S(2)}) collective-permute-start(bf16[1024,256]{1,0:T(8,128)(2,1)S(1)} %pad_maximum_fusion.refs_2_), channel_id=1, source_target_pairs={{0,256},{4,260},{8,264},{12,268},{16,272},{20,276},{24,280},{28,28... | collective-permute-start | bytes 1572872 | tf_op jit(solution)/shard_map/ppermute | solution.py:18
  37.9 0.0 collective-permute-done.1.refs_4_
  37.9 4.6 %collective-permute-start.5 = (bf16[1024,256]{1,0:T(8,128)(2,1)S(1)}, bf16[1024,256]{1,0:T(8,128)(2,1)S(1)}, u32[]{:S(2)}, u32[]{:S(2)}) collective-permute-start(bf16[1024,256]{1,0:T(8,128)(2,1)S(1)} %pad_maximum_fusion.refs_2_), channel_id=1, source_target_pairs={{0,128},{4,132},{8,136},{12,140},{16,144},{20,148},{24,152},{28,15... | collective-permute-start | bytes 1572872 | tf_op jit(solution)/shard_map/ppermute | solution.py:18
  42.6 0.0 copy-done.1
  42.6 0.0 copy-done.2
  42.6 2.4 %early1.1 = (f32[1024,128]{1,0:T(8,128)S(1)}, f32[1024,128]{1,0:T(8,128)S(1)}, f32[1024,128]{1,0:T(8,128)S(1)}) custom-call(s32[256]{0:T(256)S(1)} %copy-done.2, bf16[512,256]{1,0:T(8,128)(2,1)S(1)} %copy-done.1, bf16[1024,256]{1,0:T(8,128)(2,1)S(1)} %pad_maximum_fusion.refs_2_, bf16[1024,256]{1,0:T(8,128)(2,1)S(1)} %collective-permute-done.refs_3_, ...), custom_call_target="tpu_custom_call" | custom-call | flops 4294967296 | bytes 1048576 | tf_op jit(solution)/shard_map/early1/pallas_call | solution.py:167
  45.0 0.0 copy-start
  45.0 2.4 %early0.1 = (f32[1024,128]{1,0:T(8,128)S(1)}, f32[1024,128]{1,0:T(8,128)S(1)}, f32[1024,128]{1,0:T(8,128)S(1)}) custom-call(s32[256]{0:T(256)S(1)} %copy-done.2, bf16[512,256]{1,0:T(8,128)(2,1)S(1)} %copy-done.1, bf16[1024,256]{1,0:T(8,128)(2,1)S(1)} %pad_maximum_fusion.refs_2_, bf16[1024,256]{1,0:T(8,128)(2,1)S(1)} %collective-permute-done.refs_3_, ...), custom_call_target="tpu_custom_call" | custom-call | flops 4294967296 | bytes 1048576 | tf_op jit(solution)/shard_map/early0/pallas_call | solution.py:167
  47.4 0.0 collective-permute-done.7.refs_7_
  47.4 3.7 %collective-permute-start.12 = (bf16[512,256]{1,0:T(8,128)(2,1)S(1)}, bf16[512,256]{1,0:T(8,128)(2,1)S(1)}, u32[]{:S(2)}, u32[]{:S(2)}) collective-permute-start(bf16[512,256]{1,0:T(8,128)(2,1)S(1)} %get-tuple-element.33), channel_id=1, source_target_pairs={{0,32},{4,36},{8,40},{12,44},{16,48},{20,52},{24,56},{28,60},{32,0... | collective-permute-start | bytes 786440 | tf_op jit(solution)/shard_map/ppermute | solution.py:18
  51.2 7.6 %collective-permute-done.4.refs_3_ = bf16[1024,256]{1,0:T(8,128)(2,1)S(1)} collective-permute-done((bf16[1024,256]{1,0:T(8,128)(2,1)S(1)}, bf16[1024,256]{1,0:T(8,128)(2,1)S(1)}, u32[]{:S(2)}, u32[]{:S(2)}) %collective-permute-start.4) | collective-permute-done | bytes 524320 | tf_op jit(solution)/shard_map/ppermute | solution.py:18
  58.8 0.0 collective-permute-done.3.refs_2_
  58.8 0.0 collective-permute-done.5.refs_5_
  58.8 0.0 copy-done
  58.8 3.6 %late0.1 = (bf16[256,256]{1,0:T(8,128)(2,1)S(1)}, bf16[256,256]{1,0:T(8,128)(2,1)S(1)}, bf16[256,256]{1,0:T(8,128)(2,1)S(1)}, bf16[256,256]{1,0:T(8,128)(2,1)S(1)}) custom-call(s32[256]{0:T(256)S(1)} %copy-done.2, bf16[512,256]{1,0:T(8,128)(2,1)S(1)} %copy-done.1, bf16[1024,256]{1,0:T(8,128)(2,1)S(1)} %collective-permute-done.3.refs_2_, ...), custom_call_target="tpu_custom_call" | custom-call | flops 6442450944 | bytes 1572864 | tf_op jit(solution)/shard_map/late0/pallas_call | solution.py:167
  62.4 10.9 %collective-permute-start.10 = (bf16[256,256]{1,0:T(8,128)(2,1)S(1)}, bf16[256,256]{1,0:T(8,128)(2,1)S(1)}, u32[]{:S(2)}, u32[]{:S(2)}) collective-permute-start(bf16[256,256]{1,0:T(8,128)(2,1)S(1)} %get-tuple-element.31), channel_id=1, source_target_pairs={{0,3},{1,0},{2,1},{3,2},{4,7},{5,4},{6,5},{7,6},{8,11},{9,8},{10,9... | collective-permute-start | bytes 393224 | tf_op jit(solution)/shard_map/ppermute | solution.py:250
  73.3 1.9 %collective-permute-start.8 = (bf16[256,256]{1,0:T(8,128)(2,1)S(1)}, bf16[256,256]{1,0:T(8,128)(2,1)S(1)}, u32[]{:S(2)}, u32[]{:S(2)}) collective-permute-start(bf16[256,256]{1,0:T(8,128)(2,1)S(1)} %get-tuple-element.29), channel_id=1, source_target_pairs={{0,1},{1,2},{2,3},{3,0},{4,5},{5,6},{6,7},{7,4},{8,9},{9,10},{10,1... | collective-permute-start | bytes 393224 | tf_op jit(solution)/shard_map/ppermute | solution.py:250
  75.3 4.8 %collective-permute-start.9 = (bf16[256,256]{1,0:T(8,128)(2,1)S(1)}, bf16[256,256]{1,0:T(8,128)(2,1)S(1)}, u32[]{:S(2)}, u32[]{:S(2)}) collective-permute-start(bf16[256,256]{1,0:T(8,128)(2,1)S(1)} %get-tuple-element.30), channel_id=1, source_target_pairs={{0,2},{1,3},{2,0},{3,1},{4,6},{5,7},{6,4},{7,5},{8,10},{9,11},{10,... | collective-permute-start | bytes 393224 | tf_op jit(solution)/shard_map/ppermute | solution.py:250
  80.1 0.0 collective-permute-done.11.refs_6_
  80.1 0.0 collective-permute-done.12.refs_7_
  80.1 4.4 %late1.1 = bf16[4,256,256]{2,1,0:T(8,128)(2,1)} custom-call(s32[256]{0:T(256)S(1)} %copy-done.2, bf16[512,256]{1,0:T(8,128)(2,1)S(1)} %copy-done.1, bf16[1024,256]{1,0:T(8,128)(2,1)S(1)} %collective-permute-done.3.refs_2_, bf16[1024,256]{1,0:T(8,128)(2,1)S(1)} %collective-permute-done.4.refs_3_, bf16[1024,256]{1,0:T(8,128)(2,1)S(1)} %collective-permute-done.2.refs_4_, ...), custom_call_target="tpu_custom_call" | custom-call | flops 6442450944 | bytes 1572864 | tf_op jit(solution)/shard_map/late1/pallas_call | solution.py:167
  84.5 0.0 collective-permute-done.10
  84.5 4.6 %collective-permute-done.8 = bf16[256,256]{1,0:T(8,128)(2,1)S(1)} collective-permute-done((bf16[256,256]{1,0:T(8,128)(2,1)S(1)}, bf16[256,256]{1,0:T(8,128)(2,1)S(1)}, u32[]{:S(2)}, u32[]{:S(2)}) %collective-permute-start.8) | collective-permute-done | bytes 131104 | tf_op jit(solution)/shard_map/ppermute | solution.py:250
  89.1 0.0 collective-permute-done.9
  89.1 5.3 %all-to-all-start = ((bf16[4,256,256]{2,1,0:T(8,128)(2,1)}), bf16[4,256,256]{2,1,0:T(8,128)(2,1)S(1)}, u32[]{:S(2)}, u32[]{:S(2)}) async-start(bf16[4,256,256]{2,1,0:T(8,128)(2,1)} %late1.1), calls=%async_computation | async-start | bytes 1048576 | tf_op jit(solution)/shard_map/all_to_all | solution.py:270
  94.4 0.1 add_convert_fusion
  94.5 13.6 %all-to-all-done = bf16[4,256,256]{2,1,0:T(8,128)(2,1)S(1)} async-done(((bf16[4,256,256]{2,1,0:T(8,128)(2,1)}), bf16[4,256,256]{2,1,0:T(8,128)(2,1)S(1)}, u32[]{:S(2)}, u32[]{:S(2)}) %all-to-all-start) | async-done | bytes 524320 | tf_op jit(solution)/shard_map/all_to_all | solution.py:270
  108.1 0.1 reduce_sum.12
  108.2 0.7 pad_maximum_fusion.3
  (1 shorter events, 0.0 us)
Async XLA Ops:
  1.2 3.8 %collective-permute-start = (bf16[1024,256]{1,0:T(8,128)(2,1)S(1)}, bf16[1024,256]{1,0:T(8,128)(2,1)S(1)}, u32[]{:S(2)}, u32[]{:S(2)}) collective-permute-start(bf16[1024,256]{1,0:T(8,128)(2,1)S(1)} %pad_maximum_fusion.refs_2_), channel_id=1, source_target_pairs={{0,4},{4,0},{8,12},{12,8},{16,20},{20,16},{24,28},{28,24},{32,36},... | collective-permute-start | bytes 1572872 | tf_op jit(solution)/shard_map/ppermute | solution.py:18
  5.0 29.1 %collective-permute-start.2 = (bf16[1024,256]{1,0:T(8,128)(2,1)S(1)}, bf16[1024,256]{1,0:T(8,128)(2,1)S(1)}, u32[]{:S(2)}, u32[]{:S(2)}) collective-permute-start(bf16[1024,256]{1,0:T(8,128)(2,1)S(1)} %pad_maximum_fusion.refs_2_), channel_id=1, source_target_pairs={{0,64},{4,68},{8,72},{12,76},{16,80},{20,84},{24,88},{28,92},{32,9... | collective-permute-start | bytes 1572872 | tf_op jit(solution)/shard_map/ppermute | solution.py:18
  8.4 34.2 %copy-start.1 = (bf16[512,256]{1,0:T(8,128)(2,1)S(1)}, bf16[512,256]{1,0:T(8,128)(2,1)}, u32[]{:S(2)}) copy-start(bf16[512,256]{1,0:T(8,128)(2,1)} %refs_1_.5) | copy-start | bytes 786436
  8.5 23.6 %collective-permute-start.6 = (bf16[512,256]{1,0:T(8,128)(2,1)S(1)}, bf16[512,256]{1,0:T(8,128)(2,1)S(1)}, u32[]{:S(2)}, u32[]{:S(2)}) collective-permute-start(bf16[512,256]{1,0:T(8,128)(2,1)S(1)} %get-tuple-element.39), channel_id=1, source_target_pairs={{0,16},{4,20},{8,24},{12,28},{16,0},{20,4},{24,8},{28,12},{32,48},... | collective-permute-start | bytes 786440 | tf_op jit(solution)/shard_map/ppermute | solution.py:18
  12.5 30.1 %copy-start.2 = (s32[256]{0:T(256)S(1)}, s32[256]{0:T(256)}, u32[]{:S(2)}) copy-start(s32[256]{0:T(256)} %refs_0_.7) | copy-start | bytes 3076
  12.6 25.4 %collective-permute-start.1 = (bf16[512,256]{1,0:T(8,128)(2,1)S(1)}, bf16[512,256]{1,0:T(8,128)(2,1)S(1)}, u32[]{:S(2)}, u32[]{:S(2)}) collective-permute-start(bf16[512,256]{1,0:T(8,128)(2,1)S(1)} %get-tuple-element.38), channel_id=1, source_target_pairs={{4,8},{8,4},{12,16},{16,12},{20,24},{24,20},{28,32},{32,28},{36,40... | collective-permute-start | bytes 786440 | tf_op jit(solution)/shard_map/ppermute | solution.py:28
  15.0 32.4 %collective-permute-start.7 = (bf16[512,256]{1,0:T(8,128)(2,1)S(1)}, bf16[512,256]{1,0:T(8,128)(2,1)S(1)}, u32[]{:S(2)}, u32[]{:S(2)}) collective-permute-start(bf16[512,256]{1,0:T(8,128)(2,1)S(1)} %get-tuple-element.39), channel_id=1, source_target_pairs={{0,32},{4,36},{8,40},{12,44},{16,48},{20,52},{24,56},{28,60},{32,0... | collective-permute-start | bytes 786440 | tf_op jit(solution)/shard_map/ppermute | solution.py:18
  21.2 37.6 %collective-permute-start.4 = (bf16[1024,256]{1,0:T(8,128)(2,1)S(1)}, bf16[1024,256]{1,0:T(8,128)(2,1)S(1)}, u32[]{:S(2)}, u32[]{:S(2)}) collective-permute-start(bf16[1024,256]{1,0:T(8,128)(2,1)S(1)} %pad_maximum_fusion.refs_2_), channel_id=1, source_target_pairs={{0,8},{4,12},{8,0},{12,4},{16,24},{20,28},{24,16},{28,20},{32,40},... | collective-permute-start | bytes 1572872 | tf_op jit(solution)/shard_map/ppermute | solution.py:18
  32.1 47.9 %collective-permute-start.11 = (bf16[512,256]{1,0:T(8,128)(2,1)S(1)}, bf16[512,256]{1,0:T(8,128)(2,1)S(1)}, u32[]{:S(2)}, u32[]{:S(2)}) collective-permute-start(bf16[512,256]{1,0:T(8,128)(2,1)S(1)} %get-tuple-element.33), channel_id=1, source_target_pairs={{0,16},{4,20},{8,24},{12,28},{16,0},{20,4},{24,8},{28,12},{32,48},... | collective-permute-start | bytes 786440 | tf_op jit(solution)/shard_map/ppermute | solution.py:18
  34.0 24.7 %collective-permute-start.3 = (bf16[1024,256]{1,0:T(8,128)(2,1)S(1)}, bf16[1024,256]{1,0:T(8,128)(2,1)S(1)}, u32[]{:S(2)}, u32[]{:S(2)}) collective-permute-start(bf16[1024,256]{1,0:T(8,128)(2,1)S(1)} %pad_maximum_fusion.refs_2_), channel_id=1, source_target_pairs={{0,256},{4,260},{8,264},{12,268},{16,272},{20,276},{24,280},{28,28... | collective-permute-start | bytes 1572872 | tf_op jit(solution)/shard_map/ppermute | solution.py:18
  37.9 20.8 %collective-permute-start.5 = (bf16[1024,256]{1,0:T(8,128)(2,1)S(1)}, bf16[1024,256]{1,0:T(8,128)(2,1)S(1)}, u32[]{:S(2)}, u32[]{:S(2)}) collective-permute-start(bf16[1024,256]{1,0:T(8,128)(2,1)S(1)} %pad_maximum_fusion.refs_2_), channel_id=1, source_target_pairs={{0,128},{4,132},{8,136},{12,140},{16,144},{20,148},{24,152},{28,15... | collective-permute-start | bytes 1572872 | tf_op jit(solution)/shard_map/ppermute | solution.py:18
  45.0 13.8 %copy-start = (bf16[256,1024]{1,0:T(8,128)(2,1)S(1)}, bf16[256,1024]{1,0:T(8,128)(2,1)}, u32[]{:S(2)}) copy-start(bf16[256,1024]{1,0:T(8,128)(2,1)} %refs_11_.3) | copy-start | bytes 1572868
  47.4 32.6 %collective-permute-start.12 = (bf16[512,256]{1,0:T(8,128)(2,1)S(1)}, bf16[512,256]{1,0:T(8,128)(2,1)S(1)}, u32[]{:S(2)}, u32[]{:S(2)}) collective-permute-start(bf16[512,256]{1,0:T(8,128)(2,1)S(1)} %get-tuple-element.33), channel_id=1, source_target_pairs={{0,32},{4,36},{8,40},{12,44},{16,48},{20,52},{24,56},{28,60},{32,0... | collective-permute-start | bytes 786440 | tf_op jit(solution)/shard_map/ppermute | solution.py:18
  62.4 22.1 %collective-permute-start.10 = (bf16[256,256]{1,0:T(8,128)(2,1)S(1)}, bf16[256,256]{1,0:T(8,128)(2,1)S(1)}, u32[]{:S(2)}, u32[]{:S(2)}) collective-permute-start(bf16[256,256]{1,0:T(8,128)(2,1)S(1)} %get-tuple-element.31), channel_id=1, source_target_pairs={{0,3},{1,0},{2,1},{3,2},{4,7},{5,4},{6,5},{7,6},{8,11},{9,8},{10,9... | collective-permute-start | bytes 393224 | tf_op jit(solution)/shard_map/ppermute | solution.py:250
  73.3 15.7 %collective-permute-start.8 = (bf16[256,256]{1,0:T(8,128)(2,1)S(1)}, bf16[256,256]{1,0:T(8,128)(2,1)S(1)}, u32[]{:S(2)}, u32[]{:S(2)}) collective-permute-start(bf16[256,256]{1,0:T(8,128)(2,1)S(1)} %get-tuple-element.29), channel_id=1, source_target_pairs={{0,1},{1,2},{2,3},{3,0},{4,5},{5,6},{6,7},{7,4},{8,9},{9,10},{10,1... | collective-permute-start | bytes 393224 | tf_op jit(solution)/shard_map/ppermute | solution.py:250
  75.3 13.8 %collective-permute-start.9 = (bf16[256,256]{1,0:T(8,128)(2,1)S(1)}, bf16[256,256]{1,0:T(8,128)(2,1)S(1)}, u32[]{:S(2)}, u32[]{:S(2)}) collective-permute-start(bf16[256,256]{1,0:T(8,128)(2,1)S(1)} %get-tuple-element.30), channel_id=1, source_target_pairs={{0,2},{1,3},{2,0},{3,1},{4,6},{5,7},{6,4},{7,5},{8,10},{9,11},{10,... | collective-permute-start | bytes 393224 | tf_op jit(solution)/shard_map/ppermute | solution.py:250
  89.1 19.0 %all-to-all-start = ((bf16[4,256,256]{2,1,0:T(8,128)(2,1)}), bf16[4,256,256]{2,1,0:T(8,128)(2,1)S(1)}, u32[]{:S(2)}, u32[]{:S(2)}) async-start(bf16[4,256,256]{2,1,0:T(8,128)(2,1)} %late1.1), calls=%async_computation | async-start | bytes 1048576 | tf_op jit(solution)/shard_map/all_to_all | solution.py:270

commit v9 on v8

--- a/solution.py
+++ b/solution.py
@@ -196,10 +196,10 @@
     y2a = flat_exchange(parts[0], "seq", 1 << 2)
     y1 = flat_exchange(packed, "seq", 1 << 1)
     x1 = flat_exchange(after(packed, core), "seq", 1 << 4)
-    x2 = flat_exchange(after(packed, x1), "seq", 1 << 5)
-    z1 = flat_exchange(after(packed, x1), "seq", 1 << 6)
-    y2b = flat_exchange(after(parts[1], y2a), "seq", 1 << 2)
-    y4b = flat_exchange(after(parts[1], y2a), "seq", 1 << 3)
+    x2 = flat_exchange(after(packed, halo), "seq", 1 << 5)
+    z1 = flat_exchange(after(packed, y1), "seq", 1 << 6)
+    y2b = flat_exchange(after(parts[1], x1), "seq", 1 << 2)
+    y4b = flat_exchange(after(parts[1], x1), "seq", 1 << 3)
 
     state0 = attend(
         "early0",

time: 110 us -> 109 us (level); the launches traced: 109 us -> 107 us
  waiting for transfers between devices: 36.1 us -> 28.9 us
  starting transfers between devices: 57.6 us -> 62.3 us
    ppermute x9, waiting for transfers between devices: 17.9 us -> 1.73 us  [flat_exchange(): return lax.ppermute(value, axis, pairs)]
    ppermute x1, waiting for transfers between devices: 0.01 us -> 11.5 us  [halo_exchange(): return lax.ppermute(value, axis, pairs)]
    ppermute x9, starting transfers between devices: 32.2 us -> 38.9 us  [flat_exchange(): return lax.ppermute(value, axis, pairs)]
    all_to_all x1, waiting for transfers between devices: 13.6 us -> 11.8 us  [per_device(): spread = lax.all_to_all(after(shares, *moved), 'head', 0, 0, tiled=False)]
    all_to_all x1, starting transfers between devices: 5.34 us -> 4.16 us  [per_device(): spread = lax.all_to_all(after(shares, *moved), 'head', 0, 0, tiled=False)]
  transfers between devices with their start and end apart: 14 -> 14, of which waited for: 5 -> 4; matrix products, arithmetic and copies ran while one was open for 0% -> 0% of each run, Pallas kernels for 12% -> 12%
where the time goes in v9:
time: 109 us; the launch traced here: 107 us
  starting transfers between devices  62.3 us (57%)
  waiting for transfers between devices  28.9 us (27%)
  Pallas kernels  12.9 us (12%)
  local copies, waits for them, and re-layouts  1.15 us (1%)
    ppermute x9, starting transfers between devices, flat_exchange(): return lax.ppermute(value, axis, pairs)  38.9 us
    ppermute x3, starting transfers between devices, per_device(): lax.ppermute(piece, 'head', [(h, (h + hop + 1) % groups) for h in range(g...  16.9 us
    pallas_call x4, Pallas kernels, attend(): pl.pallas_call(lambda *refs: attend_kernel(scale, heads, local, plan, sta...  12.9 us
    all_to_all x1, waiting for transfers between devices, per_device(): spread = lax.all_to_all(after(shares, *moved), 'head', 0, 0, tiled=False)  11.8 us
    ppermute x1, waiting for transfers between devices, halo_exchange(): return lax.ppermute(value, axis, pairs)  11.5 us
    all_to_all x1, starting transfers between devices, per_device(): spread = lax.all_to_all(after(shares, *moved), 'head', 0, 0, tiled=False)  4.16 us
    ppermute x3, waiting for transfers between devices, per_device(): lax.ppermute(piece, 'head', [(h, (h + hop + 1) % groups) for h in range(g...  3.89 us
    ppermute x1, starting transfers between devices, halo_exchange(): return lax.ppermute(value, axis, pairs)  2.41 us
  transfers between devices with their start and end apart: 14, of which 4 were waited for; matrix products, arithmetic and copies ran while one was open for 0% of the time, Pallas kernels for 12%

profile of v9, /device:TPU:56, one launch (start us, length us, event | category | flops | bytes accessed | tf_op | source)
XLA Modules:
  0.0 106.5 jit_solution(16581611575862623247)
XLA Ops:
  0.0 1.1 %fusion = (bf16[256,256]{1,0:T(8,128)(2,1)S(1)}, bf16[256,256]{1,0:T(8,128)(2,1)S(1)}, bf16[256,256]{1,0:T(8,128)(2,1)S(1)}, bf16[256,256]{1,0:T(8,128)(2,1)S(1)}) fusion(bf16[512,256]{1,0:T(8,128)(2,1)} %param.6, bf16[512,256]{1,0:T(8,128)(2,1)} %param.7), kind=kLoop, calls=%fused_computation.6 | loop fusion | bytes 1048576 | tf_op jit(solution)/shard_map/slice | solution.py:188
  1.2 1.9 %collective-permute-start = (bf16[1024,256]{1,0:T(8,128)(2,1)S(1)}, bf16[1024,256]{1,0:T(8,128)(2,1)S(1)}, u32[]{:S(2)}, u32[]{:S(2)}) collective-permute-start(bf16[1024,256]{1,0:T(8,128)(2,1)S(1)} %pad_maximum_fusion.refs_2_), channel_id=1, source_target_pairs={{0,4},{4,0},{8,12},{12,8},{16,20},{20,16},{24,28},{28,24},{32,36},... | collective-permute-start | bytes 1572872 | tf_op jit(solution)/shard_map/ppermute | solution.py:18
  3.1 3.3 %collective-permute-start.2 = (bf16[1024,256]{1,0:T(8,128)(2,1)S(1)}, bf16[1024,256]{1,0:T(8,128)(2,1)S(1)}, u32[]{:S(2)}, u32[]{:S(2)}) collective-permute-start(bf16[1024,256]{1,0:T(8,128)(2,1)S(1)} %pad_maximum_fusion.refs_2_), channel_id=1, source_target_pairs={{0,8},{4,12},{8,0},{12,4},{16,24},{20,28},{24,16},{28,20},{32,40},... | collective-permute-start | bytes 1572872 | tf_op jit(solution)/shard_map/ppermute | solution.py:18
  6.4 0.0 copy-start.1
  6.4 0.1 pad_maximum_fusion.1
  6.5 0.0 copy-start.2
  6.5 2.4 %collective-permute-start.1 = (bf16[512,256]{1,0:T(8,128)(2,1)S(1)}, bf16[512,256]{1,0:T(8,128)(2,1)S(1)}, u32[]{:S(2)}, u32[]{:S(2)}) collective-permute-start(bf16[512,256]{1,0:T(8,128)(2,1)S(1)} %get-tuple-element.40), channel_id=1, source_target_pairs={{4,8},{8,4},{12,16},{16,12},{20,24},{24,20},{28,32},{32,28},{36,40... | collective-permute-start | bytes 786440 | tf_op jit(solution)/shard_map/ppermute | solution.py:28
  8.9 4.0 %collective-permute-start.6 = (bf16[512,256]{1,0:T(8,128)(2,1)S(1)}, bf16[512,256]{1,0:T(8,128)(2,1)S(1)}, u32[]{:S(2)}, u32[]{:S(2)}) collective-permute-start(bf16[512,256]{1,0:T(8,128)(2,1)S(1)} %get-tuple-element.41), channel_id=1, source_target_pairs={{0,16},{4,20},{8,24},{12,28},{16,0},{20,4},{24,8},{28,12},{32,48},... | collective-permute-start | bytes 786440 | tf_op jit(solution)/shard_map/ppermute | solution.py:18
  13.0 7.0 %collective-permute-start.7 = (bf16[512,256]{1,0:T(8,128)(2,1)S(1)}, bf16[512,256]{1,0:T(8,128)(2,1)S(1)}, u32[]{:S(2)}, u32[]{:S(2)}) collective-permute-start(bf16[512,256]{1,0:T(8,128)(2,1)S(1)} %get-tuple-element.41), channel_id=1, source_target_pairs={{0,32},{4,36},{8,40},{12,44},{16,48},{20,52},{24,56},{28,60},{32,0... | collective-permute-start | bytes 786440 | tf_op jit(solution)/shard_map/ppermute | solution.py:18
  20.0 11.5 %collective-permute-done.1.refs_4_ = bf16[512,256]{1,0:T(8,128)(2,1)S(1)} collective-permute-done((bf16[512,256]{1,0:T(8,128)(2,1)S(1)}, bf16[512,256]{1,0:T(8,128)(2,1)S(1)}, u32[]{:S(2)}, u32[]{:S(2)}) %collective-permute-start.1) | collective-permute-done | bytes 262176 | tf_op jit(solution)/shard_map/ppermute | solution.py:28
  31.5 5.6 %collective-permute-start.5 = (bf16[1024,256]{1,0:T(8,128)(2,1)S(1)}, bf16[1024,256]{1,0:T(8,128)(2,1)S(1)}, u32[]{:S(2)}, u32[]{:S(2)}) collective-permute-start(bf16[1024,256]{1,0:T(8,128)(2,1)S(1)} %pad_maximum_fusion.refs_2_), channel_id=1, source_target_pairs={{0,128},{4,132},{8,136},{12,140},{16,144},{20,148},{24,152},{28,15... | collective-permute-start | bytes 1572872 | tf_op jit(solution)/shard_map/ppermute | solution.py:18
  37.0 0.0 collective-permute-done.refs_3_
  37.0 2.5 %collective-permute-start.4 = (bf16[1024,256]{1,0:T(8,128)(2,1)S(1)}, bf16[1024,256]{1,0:T(8,128)(2,1)S(1)}, u32[]{:S(2)}, u32[]{:S(2)}) collective-permute-start(bf16[1024,256]{1,0:T(8,128)(2,1)S(1)} %pad_maximum_fusion.refs_2_), channel_id=1, source_target_pairs={{0,64},{4,68},{8,72},{12,76},{16,80},{20,84},{24,88},{28,92},{32,9... | collective-permute-start | bytes 1572872 | tf_op jit(solution)/shard_map/ppermute | solution.py:18
  39.6 0.0 collective-permute-done.2.refs_3_
  39.6 4.3 %collective-permute-start.3 = (bf16[1024,256]{1,0:T(8,128)(2,1)S(1)}, bf16[1024,256]{1,0:T(8,128)(2,1)S(1)}, u32[]{:S(2)}, u32[]{:S(2)}) collective-permute-start(bf16[1024,256]{1,0:T(8,128)(2,1)S(1)} %pad_maximum_fusion.refs_2_), channel_id=1, source_target_pairs={{0,256},{4,260},{8,264},{12,268},{16,272},{20,276},{24,280},{28,28... | collective-permute-start | bytes 1572872 | tf_op jit(solution)/shard_map/ppermute | solution.py:18
  43.9 0.0 copy-done.1
  43.9 0.0 copy-done.2
  43.9 2.4 %early1.1 = (f32[1024,128]{1,0:T(8,128)S(1)}, f32[1024,128]{1,0:T(8,128)S(1)}, f32[1024,128]{1,0:T(8,128)S(1)}) custom-call(s32[256]{0:T(256)S(1)} %copy-done.2, bf16[512,256]{1,0:T(8,128)(2,1)S(1)} %copy-done.1, bf16[1024,256]{1,0:T(8,128)(2,1)S(1)} %pad_maximum_fusion.refs_2_, bf16[1024,256]{1,0:T(8,128)(2,1)S(1)} %collective-permute-done.refs_3_, ...), custom_call_target="tpu_custom_call" | custom-call | flops 4294967296 | bytes 1048576 | tf_op jit(solution)/shard_map/early1/pallas_call | solution.py:167
  46.3 0.0 copy-start
  46.3 2.4 %early0.1 = (f32[1024,128]{1,0:T(8,128)S(1)}, f32[1024,128]{1,0:T(8,128)S(1)}, f32[1024,128]{1,0:T(8,128)S(1)}) custom-call(s32[256]{0:T(256)S(1)} %copy-done.2, bf16[512,256]{1,0:T(8,128)(2,1)S(1)} %copy-done.1, bf16[1024,256]{1,0:T(8,128)(2,1)S(1)} %pad_maximum_fusion.refs_2_, bf16[1024,256]{1,0:T(8,128)(2,1)S(1)} %collective-permute-done.refs_3_, ...), custom_call_target="tpu_custom_call" | custom-call | flops 4294967296 | bytes 1048576 | tf_op jit(solution)/shard_map/early0/pallas_call | solution.py:167
  48.7 1.7 %collective-permute-done.4.refs_4_ = bf16[1024,256]{1,0:T(8,128)(2,1)S(1)} collective-permute-done((bf16[1024,256]{1,0:T(8,128)(2,1)S(1)}, bf16[1024,256]{1,0:T(8,128)(2,1)S(1)}, u32[]{:S(2)}, u32[]{:S(2)}) %collective-permute-start.4) | collective-permute-done | bytes 524320 | tf_op jit(solution)/shard_map/ppermute | solution.py:18
  50.4 4.0 %collective-permute-start.11 = (bf16[512,256]{1,0:T(8,128)(2,1)S(1)}, bf16[512,256]{1,0:T(8,128)(2,1)S(1)}, u32[]{:S(2)}, u32[]{:S(2)}) collective-permute-start(bf16[512,256]{1,0:T(8,128)(2,1)S(1)} %get-tuple-element.35), channel_id=1, source_target_pairs={{0,16},{4,20},{8,24},{12,28},{16,0},{20,4},{24,8},{28,12},{32,48},... | collective-permute-start | bytes 786440 | tf_op jit(solution)/shard_map/ppermute | solution.py:18
  54.4 0.0 collective-permute-done.6.refs_6_
  54.4 6.3 %collective-permute-start.12 = (bf16[512,256]{1,0:T(8,128)(2,1)S(1)}, bf16[512,256]{1,0:T(8,128)(2,1)S(1)}, u32[]{:S(2)}, u32[]{:S(2)}) collective-permute-start(bf16[512,256]{1,0:T(8,128)(2,1)S(1)} %get-tuple-element.35), channel_id=1, source_target_pairs={{0,32},{4,36},{8,40},{12,44},{16,48},{20,52},{24,56},{28,60},{32,0... | collective-permute-start | bytes 786440 | tf_op jit(solution)/shard_map/ppermute | solution.py:18
  60.7 0.0 collective-permute-done.7.refs_7_
  60.7 0.0 collective-permute-done.5.refs_5_
  60.7 0.0 collective-permute-done.3.refs_2_
  60.7 0.0 copy-done
  60.7 3.6 %late0.1 = (bf16[256,256]{1,0:T(8,128)(2,1)S(1)}, bf16[256,256]{1,0:T(8,128)(2,1)S(1)}, bf16[256,256]{1,0:T(8,128)(2,1)S(1)}, bf16[256,256]{1,0:T(8,128)(2,1)S(1)}) custom-call(s32[256]{0:T(256)S(1)} %copy-done.2, bf16[512,256]{1,0:T(8,128)(2,1)S(1)} %copy-done.1, bf16[1024,256]{1,0:T(8,128)(2,1)S(1)} %collective-permute-done.3.refs_2_, ...), custom_call_target="tpu_custom_call" | custom-call | flops 6442450944 | bytes 1572864 | tf_op jit(solution)/shard_map/late0/pallas_call | solution.py:167
  64.4 10.2 %collective-permute-start.10 = (bf16[256,256]{1,0:T(8,128)(2,1)S(1)}, bf16[256,256]{1,0:T(8,128)(2,1)S(1)}, u32[]{:S(2)}, u32[]{:S(2)}) collective-permute-start(bf16[256,256]{1,0:T(8,128)(2,1)S(1)} %get-tuple-element.33), channel_id=1, source_target_pairs={{0,3},{1,0},{2,1},{3,2},{4,7},{5,4},{6,5},{7,6},{8,11},{9,8},{10,9... | collective-permute-start | bytes 393224 | tf_op jit(solution)/shard_map/ppermute | solution.py:250
  74.6 1.9 %collective-permute-start.8 = (bf16[256,256]{1,0:T(8,128)(2,1)S(1)}, bf16[256,256]{1,0:T(8,128)(2,1)S(1)}, u32[]{:S(2)}, u32[]{:S(2)}) collective-permute-start(bf16[256,256]{1,0:T(8,128)(2,1)S(1)} %get-tuple-element.31), channel_id=1, source_target_pairs={{0,1},{1,2},{2,3},{3,0},{4,5},{5,6},{6,7},{7,4},{8,9},{9,10},{10,1... | collective-permute-start | bytes 393224 | tf_op jit(solution)/shard_map/ppermute | solution.py:250
  76.5 4.8 %collective-permute-start.9 = (bf16[256,256]{1,0:T(8,128)(2,1)S(1)}, bf16[256,256]{1,0:T(8,128)(2,1)S(1)}, u32[]{:S(2)}, u32[]{:S(2)}) collective-permute-start(bf16[256,256]{1,0:T(8,128)(2,1)S(1)} %get-tuple-element.32), channel_id=1, source_target_pairs={{0,2},{1,3},{2,0},{3,1},{4,6},{5,7},{6,4},{7,5},{8,10},{9,11},{10,... | collective-permute-start | bytes 393224 | tf_op jit(solution)/shard_map/ppermute | solution.py:250
  81.3 0.0 collective-permute-done.11.refs_6_
  81.3 0.0 collective-permute-done.12.refs_7_
  81.3 4.4 %late1.1 = bf16[4,256,256]{2,1,0:T(8,128)(2,1)} custom-call(s32[256]{0:T(256)S(1)} %copy-done.2, bf16[512,256]{1,0:T(8,128)(2,1)S(1)} %copy-done.1, bf16[1024,256]{1,0:T(8,128)(2,1)S(1)} %collective-permute-done.3.refs_2_, bf16[1024,256]{1,0:T(8,128)(2,1)S(1)} %collective-permute-done.2.refs_3_, bf16[1024,256]{1,0:T(8,128)(2,1)S(1)} %collective-permute-done.4.refs_4_, ...), custom_call_target="tpu_custom_call" | custom-call | flops 6442450944 | bytes 1572864 | tf_op jit(solution)/shard_map/late1/pallas_call | solution.py:167
  85.8 0.0 collective-permute-done.10
  85.8 0.0 collective-permute-done.8
  85.8 3.9 %collective-permute-done.9 = bf16[256,256]{1,0:T(8,128)(2,1)S(1)} collective-permute-done((bf16[256,256]{1,0:T(8,128)(2,1)S(1)}, bf16[256,256]{1,0:T(8,128)(2,1)S(1)}, u32[]{:S(2)}, u32[]{:S(2)}) %collective-permute-start.9) | collective-permute-done | bytes 131104 | tf_op jit(solution)/shard_map/ppermute | solution.py:250
  89.7 4.2 %all-to-all-start = ((bf16[4,256,256]{2,1,0:T(8,128)(2,1)}), bf16[4,256,256]{2,1,0:T(8,128)(2,1)S(1)}, u32[]{:S(2)}, u32[]{:S(2)}) async-start(bf16[4,256,256]{2,1,0:T(8,128)(2,1)} %late1.1), calls=%async_computation | async-start | bytes 1048576 | tf_op jit(solution)/shard_map/all_to_all | solution.py:270
  93.8 0.1 add_convert_fusion
  93.9 11.8 %all-to-all-done = bf16[4,256,256]{2,1,0:T(8,128)(2,1)S(1)} async-done(((bf16[4,256,256]{2,1,0:T(8,128)(2,1)}), bf16[4,256,256]{2,1,0:T(8,128)(2,1)S(1)}, u32[]{:S(2)}, u32[]{:S(2)}) %all-to-all-start) | async-done | bytes 524320 | tf_op jit(solution)/shard_map/all_to_all | solution.py:270
  105.7 0.1 reduce_sum.12
  105.8 0.7 pad_maximum_fusion.3
  (1 shorter events, 0.0 us)
Async XLA Ops:
  1.2 35.9 %collective-permute-start = (bf16[1024,256]{1,0:T(8,128)(2,1)S(1)}, bf16[1024,256]{1,0:T(8,128)(2,1)S(1)}, u32[]{:S(2)}, u32[]{:S(2)}) collective-permute-start(bf16[1024,256]{1,0:T(8,128)(2,1)S(1)} %pad_maximum_fusion.refs_2_), channel_id=1, source_target_pairs={{0,4},{4,0},{8,12},{12,8},{16,20},{20,16},{24,28},{28,24},{32,36},... | collective-permute-start | bytes 1572872 | tf_op jit(solution)/shard_map/ppermute | solution.py:18
  3.1 36.5 %collective-permute-start.2 = (bf16[1024,256]{1,0:T(8,128)(2,1)S(1)}, bf16[1024,256]{1,0:T(8,128)(2,1)S(1)}, u32[]{:S(2)}, u32[]{:S(2)}) collective-permute-start(bf16[1024,256]{1,0:T(8,128)(2,1)S(1)} %pad_maximum_fusion.refs_2_), channel_id=1, source_target_pairs={{0,8},{4,12},{8,0},{12,4},{16,24},{20,28},{24,16},{28,20},{32,40},... | collective-permute-start | bytes 1572872 | tf_op jit(solution)/shard_map/ppermute | solution.py:18
  6.4 37.5 %copy-start.1 = (bf16[512,256]{1,0:T(8,128)(2,1)S(1)}, bf16[512,256]{1,0:T(8,128)(2,1)}, u32[]{:S(2)}) copy-start(bf16[512,256]{1,0:T(8,128)(2,1)} %refs_1_.5) | copy-start | bytes 786436
  6.5 37.4 %copy-start.2 = (s32[256]{0:T(256)S(1)}, s32[256]{0:T(256)}, u32[]{:S(2)}) copy-start(s32[256]{0:T(256)} %refs_0_.7) | copy-start | bytes 3076
  6.5 25.0 %collective-permute-start.1 = (bf16[512,256]{1,0:T(8,128)(2,1)S(1)}, bf16[512,256]{1,0:T(8,128)(2,1)S(1)}, u32[]{:S(2)}, u32[]{:S(2)}) collective-permute-start(bf16[512,256]{1,0:T(8,128)(2,1)S(1)} %get-tuple-element.40), channel_id=1, source_target_pairs={{4,8},{8,4},{12,16},{16,12},{20,24},{24,20},{28,32},{32,28},{36,40... | collective-permute-start | bytes 786440 | tf_op jit(solution)/shard_map/ppermute | solution.py:28
  8.9 45.5 %collective-permute-start.6 = (bf16[512,256]{1,0:T(8,128)(2,1)S(1)}, bf16[512,256]{1,0:T(8,128)(2,1)S(1)}, u32[]{:S(2)}, u32[]{:S(2)}) collective-permute-start(bf16[512,256]{1,0:T(8,128)(2,1)S(1)} %get-tuple-element.41), channel_id=1, source_target_pairs={{0,16},{4,20},{8,24},{12,28},{16,0},{20,4},{24,8},{28,12},{32,48},... | collective-permute-start | bytes 786440 | tf_op jit(solution)/shard_map/ppermute | solution.py:18
  13.0 47.7 %collective-permute-start.7 = (bf16[512,256]{1,0:T(8,128)(2,1)S(1)}, bf16[512,256]{1,0:T(8,128)(2,1)S(1)}, u32[]{:S(2)}, u32[]{:S(2)}) collective-permute-start(bf16[512,256]{1,0:T(8,128)(2,1)S(1)} %get-tuple-element.41), channel_id=1, source_target_pairs={{0,32},{4,36},{8,40},{12,44},{16,48},{20,52},{24,56},{28,60},{32,0... | collective-permute-start | bytes 786440 | tf_op jit(solution)/shard_map/ppermute | solution.py:18
  31.5 29.3 %collective-permute-start.5 = (bf16[1024,256]{1,0:T(8,128)(2,1)S(1)}, bf16[1024,256]{1,0:T(8,128)(2,1)S(1)}, u32[]{:S(2)}, u32[]{:S(2)}) collective-permute-start(bf16[1024,256]{1,0:T(8,128)(2,1)S(1)} %pad_maximum_fusion.refs_2_), channel_id=1, source_target_pairs={{0,128},{4,132},{8,136},{12,140},{16,144},{20,148},{24,152},{28,15... | collective-permute-start | bytes 1572872 | tf_op jit(solution)/shard_map/ppermute | solution.py:18
  37.0 13.3 %collective-permute-start.4 = (bf16[1024,256]{1,0:T(8,128)(2,1)S(1)}, bf16[1024,256]{1,0:T(8,128)(2,1)S(1)}, u32[]{:S(2)}, u32[]{:S(2)}) collective-permute-start(bf16[1024,256]{1,0:T(8,128)(2,1)S(1)} %pad_maximum_fusion.refs_2_), channel_id=1, source_target_pairs={{0,64},{4,68},{8,72},{12,76},{16,80},{20,84},{24,88},{28,92},{32,9... | collective-permute-start | bytes 1572872 | tf_op jit(solution)/shard_map/ppermute | solution.py:18
  39.6 21.2 %collective-permute-start.3 = (bf16[1024,256]{1,0:T(8,128)(2,1)S(1)}, bf16[1024,256]{1,0:T(8,128)(2,1)S(1)}, u32[]{:S(2)}, u32[]{:S(2)}) collective-permute-start(bf16[1024,256]{1,0:T(8,128)(2,1)S(1)} %pad_maximum_fusion.refs_2_), channel_id=1, source_target_pairs={{0,256},{4,260},{8,264},{12,268},{16,272},{20,276},{24,280},{28,28... | collective-permute-start | bytes 1572872 | tf_op jit(solution)/shard_map/ppermute | solution.py:18
  46.3 14.5 %copy-start = (bf16[256,1024]{1,0:T(8,128)(2,1)S(1)}, bf16[256,1024]{1,0:T(8,128)(2,1)}, u32[]{:S(2)}) copy-start(bf16[256,1024]{1,0:T(8,128)(2,1)} %refs_11_.3) | copy-start | bytes 1572868
  50.4 30.9 %collective-permute-start.11 = (bf16[512,256]{1,0:T(8,128)(2,1)S(1)}, bf16[512,256]{1,0:T(8,128)(2,1)S(1)}, u32[]{:S(2)}, u32[]{:S(2)}) collective-permute-start(bf16[512,256]{1,0:T(8,128)(2,1)S(1)} %get-tuple-element.35), channel_id=1, source_target_pairs={{0,16},{4,20},{8,24},{12,28},{16,0},{20,4},{24,8},{28,12},{32,48},... | collective-permute-start | bytes 786440 | tf_op jit(solution)/shard_map/ppermute | solution.py:18
  54.4 26.9 %collective-permute-start.12 = (bf16[512,256]{1,0:T(8,128)(2,1)S(1)}, bf16[512,256]{1,0:T(8,128)(2,1)S(1)}, u32[]{:S(2)}, u32[]{:S(2)}) collective-permute-start(bf16[512,256]{1,0:T(8,128)(2,1)S(1)} %get-tuple-element.35), channel_id=1, source_target_pairs={{0,32},{4,36},{8,40},{12,44},{16,48},{20,52},{24,56},{28,60},{32,0... | collective-permute-start | bytes 786440 | tf_op jit(solution)/shard_map/ppermute | solution.py:18
  64.4 21.4 %collective-permute-start.10 = (bf16[256,256]{1,0:T(8,128)(2,1)S(1)}, bf16[256,256]{1,0:T(8,128)(2,1)S(1)}, u32[]{:S(2)}, u32[]{:S(2)}) collective-permute-start(bf16[256,256]{1,0:T(8,128)(2,1)S(1)} %get-tuple-element.33), channel_id=1, source_target_pairs={{0,3},{1,0},{2,1},{3,2},{4,7},{5,4},{6,5},{7,6},{8,11},{9,8},{10,9... | collective-permute-start | bytes 393224 | tf_op jit(solution)/shard_map/ppermute | solution.py:250
  74.6 11.2 %collective-permute-start.8 = (bf16[256,256]{1,0:T(8,128)(2,1)S(1)}, bf16[256,256]{1,0:T(8,128)(2,1)S(1)}, u32[]{:S(2)}, u32[]{:S(2)}) collective-permute-start(bf16[256,256]{1,0:T(8,128)(2,1)S(1)} %get-tuple-element.31), channel_id=1, source_target_pairs={{0,1},{1,2},{2,3},{3,0},{4,5},{5,6},{6,7},{7,4},{8,9},{9,10},{10,1... | collective-permute-start | bytes 393224 | tf_op jit(solution)/shard_map/ppermute | solution.py:250
  76.5 13.2 %collective-permute-start.9 = (bf16[256,256]{1,0:T(8,128)(2,1)S(1)}, bf16[256,256]{1,0:T(8,128)(2,1)S(1)}, u32[]{:S(2)}, u32[]{:S(2)}) collective-permute-start(bf16[256,256]{1,0:T(8,128)(2,1)S(1)} %get-tuple-element.32), channel_id=1, source_target_pairs={{0,2},{1,3},{2,0},{3,1},{4,6},{5,7},{6,4},{7,5},{8,10},{9,11},{10,... | collective-permute-start | bytes 393224 | tf_op jit(solution)/shard_map/ppermute | solution.py:250
  89.7 16.0 %all-to-all-start = ((bf16[4,256,256]{2,1,0:T(8,128)(2,1)}), bf16[4,256,256]{2,1,0:T(8,128)(2,1)S(1)}, u32[]{:S(2)}, u32[]{:S(2)}) async-start(bf16[4,256,256]{2,1,0:T(8,128)(2,1)} %late1.1), calls=%async_computation | async-start | bytes 1048576 | tf_op jit(solution)/shard_map/all_to_all | solution.py:270

commit v10 on v9

--- a/solution.py
+++ b/solution.py
@@ -194,7 +194,7 @@
     halo = halo_exchange(edge, "seq")
     y4a = flat_exchange(parts[0], "seq", 1 << 3)
     y2a = flat_exchange(parts[0], "seq", 1 << 2)
-    y1 = flat_exchange(packed, "seq", 1 << 1)
+    y1 = flat_exchange(after(packed, halo), "seq", 1 << 1)
     x1 = flat_exchange(after(packed, core), "seq", 1 << 4)
     x2 = flat_exchange(after(packed, halo), "seq", 1 << 5)
     z1 = flat_exchange(after(packed, y1), "seq", 1 << 6)

time: 109 us -> 111 us (1.018)
  the two profiles are of different devices: /device:TPU:56 before, /device:TPU:2 now
where the time goes in v10:
time: 111 us; the launch traced here: 110 us
  starting transfers between devices  59.9 us (54%)
  waiting for transfers between devices  34.8 us (31%)
  Pallas kernels  12.9 us (12%)
  local copies, waits for them, and re-layouts  1.15 us (1%)
    ppermute x9, starting transfers between devices, flat_exchange(): return lax.ppermute(value, axis, pairs)  30.9 us
    ppermute x3, starting transfers between devices, per_device(): lax.ppermute(piece, 'head', [(h, (h + hop + 1) % groups) for h in range(g...  17.7 us
    all_to_all x1, waiting for transfers between devices, per_device(): spread = lax.all_to_all(after(shares, *moved), 'head', 0, 0, tiled=False)  15.6 us
    pallas_call x4, Pallas kernels, attend(): pl.pallas_call(lambda *refs: attend_kernel(scale, heads, local, plan, sta...  12.9 us
    ppermute x9, waiting for transfers between devices, flat_exchange(): return lax.ppermute(value, axis, pairs)  12.8 us
    all_to_all x1, starting transfers between devices, per_device(): spread = lax.all_to_all(after(shares, *moved), 'head', 0, 0, tiled=False)  6.5 us
    ppermute x1, starting transfers between devices, halo_exchange(): return lax.ppermute(value, axis, pairs)  4.92 us
    ppermute x3, waiting for transfers between devices, per_device(): lax.ppermute(piece, 'head', [(h, (h + hop + 1) % groups) for h in range(g...  3.43 us
  transfers between devices with their start and end apart: 14, of which 5 were waited for; matrix products, arithmetic and copies ran while one was open for 0% of the time, Pallas kernels for 12%

profile of v10, /device:TPU:2, one launch (start us, length us, event | category | flops | bytes accessed | tf_op | source)
XLA Modules:
  0.0 110.0 jit_solution(15487772519553162878)
XLA Ops:
  0.0 1.1 %fusion = (bf16[256,256]{1,0:T(8,128)(2,1)S(1)}, bf16[256,256]{1,0:T(8,128)(2,1)S(1)}, bf16[256,256]{1,0:T(8,128)(2,1)S(1)}, bf16[256,256]{1,0:T(8,128)(2,1)S(1)}) fusion(bf16[512,256]{1,0:T(8,128)(2,1)} %param.6, bf16[512,256]{1,0:T(8,128)(2,1)} %param.7), kind=kLoop, calls=%fused_computation.6 | loop fusion | bytes 1048576 | tf_op jit(solution)/shard_map/slice | solution.py:188
  1.1 0.1 pad_maximum_fusion.1
  1.2 0.0 copy-start.1
  1.2 4.9 %collective-permute-start.1 = (bf16[512,256]{1,0:T(8,128)(2,1)S(1)}, bf16[512,256]{1,0:T(8,128)(2,1)S(1)}, u32[]{:S(2)}, u32[]{:S(2)}) collective-permute-start(bf16[512,256]{1,0:T(8,128)(2,1)S(1)} %get-tuple-element.40), channel_id=1, source_target_pairs={{4,8},{8,4},{12,16},{16,12},{20,24},{24,20},{28,32},{32,28},{36,40... | collective-permute-start | bytes 786440 | tf_op jit(solution)/shard_map/ppermute | solution.py:28
  6.2 0.0 copy-start.2
  6.2 1.9 %collective-permute-start = (bf16[1024,256]{1,0:T(8,128)(2,1)S(1)}, bf16[1024,256]{1,0:T(8,128)(2,1)S(1)}, u32[]{:S(2)}, u32[]{:S(2)}) collective-permute-start(bf16[1024,256]{1,0:T(8,128)(2,1)S(1)} %pad_maximum_fusion.refs_2_), channel_id=1, source_target_pairs={{0,4},{4,0},{8,12},{12,8},{16,20},{20,16},{24,28},{28,24},{32,36},... | collective-permute-start | bytes 1572872 | tf_op jit(solution)/shard_map/ppermute | solution.py:18
  8.2 3.0 %collective-permute-done.1.refs_4_ = bf16[512,256]{1,0:T(8,128)(2,1)S(1)} collective-permute-done((bf16[512,256]{1,0:T(8,128)(2,1)S(1)}, bf16[512,256]{1,0:T(8,128)(2,1)S(1)}, u32[]{:S(2)}, u32[]{:S(2)}) %collective-permute-start.1) | collective-permute-done | bytes 262176 | tf_op jit(solution)/shard_map/ppermute | solution.py:28
  11.2 1.9 %collective-permute-start.2 = (bf16[1024,256]{1,0:T(8,128)(2,1)S(1)}, bf16[1024,256]{1,0:T(8,128)(2,1)S(1)}, u32[]{:S(2)}, u32[]{:S(2)}) collective-permute-start(bf16[1024,256]{1,0:T(8,128)(2,1)S(1)} %pad_maximum_fusion.refs_2_), channel_id=1, source_target_pairs={{0,8},{4,12},{8,0},{12,4},{16,24},{20,28},{24,16},{28,20},{32,40},... | collective-permute-start | bytes 1572872 | tf_op jit(solution)/shard_map/ppermute | solution.py:18
  13.1 4.0 %collective-permute-start.6 = (bf16[512,256]{1,0:T(8,128)(2,1)S(1)}, bf16[512,256]{1,0:T(8,128)(2,1)S(1)}, u32[]{:S(2)}, u32[]{:S(2)}) collective-permute-start(bf16[512,256]{1,0:T(8,128)(2,1)S(1)} %get-tuple-element.41), channel_id=1, source_target_pairs={{0,16},{4,20},{8,24},{12,28},{16,0},{20,4},{24,8},{28,12},{32,48},... | collective-permute-start | bytes 786440 | tf_op jit(solution)/shard_map/ppermute | solution.py:18
  17.1 5.0 %collective-permute-start.7 = (bf16[512,256]{1,0:T(8,128)(2,1)S(1)}, bf16[512,256]{1,0:T(8,128)(2,1)S(1)}, u32[]{:S(2)}, u32[]{:S(2)}) collective-permute-start(bf16[512,256]{1,0:T(8,128)(2,1)S(1)} %get-tuple-element.41), channel_id=1, source_target_pairs={{0,32},{4,36},{8,40},{12,44},{16,48},{20,52},{24,56},{28,60},{32,0... | collective-permute-start | bytes 786440 | tf_op jit(solution)/shard_map/ppermute | solution.py:18
  22.1 4.0 %collective-permute-start.5 = (bf16[1024,256]{1,0:T(8,128)(2,1)S(1)}, bf16[1024,256]{1,0:T(8,128)(2,1)S(1)}, u32[]{:S(2)}, u32[]{:S(2)}) collective-permute-start(bf16[1024,256]{1,0:T(8,128)(2,1)S(1)} %pad_maximum_fusion.refs_2_), channel_id=1, source_target_pairs={{0,128},{4,132},{8,136},{12,140},{16,144},{20,148},{24,152},{28,15... | collective-permute-start | bytes 1572872 | tf_op jit(solution)/shard_map/ppermute | solution.py:18
  26.1 0.0 collective-permute-done.refs_3_
  26.2 3.3 %collective-permute-start.4 = (bf16[1024,256]{1,0:T(8,128)(2,1)S(1)}, bf16[1024,256]{1,0:T(8,128)(2,1)S(1)}, u32[]{:S(2)}, u32[]{:S(2)}) collective-permute-start(bf16[1024,256]{1,0:T(8,128)(2,1)S(1)} %pad_maximum_fusion.refs_2_), channel_id=1, source_target_pairs={{0,64},{4,68},{8,72},{12,76},{16,80},{20,84},{24,88},{28,92},{32,9... | collective-permute-start | bytes 1572872 | tf_op jit(solution)/shard_map/ppermute | solution.py:18
  29.5 4.0 %collective-permute-done.2.refs_3_ = bf16[1024,256]{1,0:T(8,128)(2,1)S(1)} collective-permute-done((bf16[1024,256]{1,0:T(8,128)(2,1)S(1)}, bf16[1024,256]{1,0:T(8,128)(2,1)S(1)}, u32[]{:S(2)}, u32[]{:S(2)}) %collective-permute-start.2) | collective-permute-done | bytes 524320 | tf_op jit(solution)/shard_map/ppermute | solution.py:18
  33.5 4.3 %collective-permute-start.3 = (bf16[1024,256]{1,0:T(8,128)(2,1)S(1)}, bf16[1024,256]{1,0:T(8,128)(2,1)S(1)}, u32[]{:S(2)}, u32[]{:S(2)}) collective-permute-start(bf16[1024,256]{1,0:T(8,128)(2,1)S(1)} %pad_maximum_fusion.refs_2_), channel_id=1, source_target_pairs={{0,256},{4,260},{8,264},{12,268},{16,272},{20,276},{24,280},{28,28... | collective-permute-start | bytes 1572872 | tf_op jit(solution)/shard_map/ppermute | solution.py:18
  37.8 0.0 copy-done.1
  37.8 0.0 copy-done.2
  37.8 2.4 %early1.1 = (f32[1024,128]{1,0:T(8,128)S(1)}, f32[1024,128]{1,0:T(8,128)S(1)}, f32[1024,128]{1,0:T(8,128)S(1)}) custom-call(s32[256]{0:T(256)S(1)} %copy-done.2, bf16[512,256]{1,0:T(8,128)(2,1)S(1)} %copy-done.1, bf16[1024,256]{1,0:T(8,128)(2,1)S(1)} %pad_maximum_fusion.refs_2_, bf16[1024,256]{1,0:T(8,128)(2,1)S(1)} %collective-permute-done.refs_3_, ...), custom_call_target="tpu_custom_call" | custom-call | flops 4294967296 | bytes 1048576 | tf_op jit(solution)/shard_map/early1/pallas_call | solution.py:167
  40.2 0.0 copy-start
  40.2 2.4 %early0.1 = (f32[1024,128]{1,0:T(8,128)S(1)}, f32[1024,128]{1,0:T(8,128)S(1)}, f32[1024,128]{1,0:T(8,128)S(1)}) custom-call(s32[256]{0:T(256)S(1)} %copy-done.2, bf16[512,256]{1,0:T(8,128)(2,1)S(1)} %copy-done.1, bf16[1024,256]{1,0:T(8,128)(2,1)S(1)} %pad_maximum_fusion.refs_2_, bf16[1024,256]{1,0:T(8,128)(2,1)S(1)} %collective-permute-done.refs_3_, ...), custom_call_target="tpu_custom_call" | custom-call | flops 4294967296 | bytes 1048576 | tf_op jit(solution)/shard_map/early0/pallas_call | solution.py:167
  42.6 8.8 %collective-permute-done.4.refs_4_ = bf16[1024,256]{1,0:T(8,128)(2,1)S(1)} collective-permute-done((bf16[1024,256]{1,0:T(8,128)(2,1)S(1)}, bf16[1024,256]{1,0:T(8,128)(2,1)S(1)}, u32[]{:S(2)}, u32[]{:S(2)}) %collective-permute-start.4) | collective-permute-done | bytes 524320 | tf_op jit(solution)/shard_map/ppermute | solution.py:18
  51.4 2.7 %collective-permute-start.11 = (bf16[512,256]{1,0:T(8,128)(2,1)S(1)}, bf16[512,256]{1,0:T(8,128)(2,1)S(1)}, u32[]{:S(2)}, u32[]{:S(2)}) collective-permute-start(bf16[512,256]{1,0:T(8,128)(2,1)S(1)} %get-tuple-element.35), channel_id=1, source_target_pairs={{0,16},{4,20},{8,24},{12,28},{16,0},{20,4},{24,8},{28,12},{32,48},... | collective-permute-start | bytes 786440 | tf_op jit(solution)/shard_map/ppermute | solution.py:18
  54.1 0.0 collective-permute-done.6.refs_6_
  54.1 3.7 %collective-permute-start.12 = (bf16[512,256]{1,0:T(8,128)(2,1)S(1)}, bf16[512,256]{1,0:T(8,128)(2,1)S(1)}, u32[]{:S(2)}, u32[]{:S(2)}) collective-permute-start(bf16[512,256]{1,0:T(8,128)(2,1)S(1)} %get-tuple-element.35), channel_id=1, source_target_pairs={{0,32},{4,36},{8,40},{12,44},{16,48},{20,52},{24,56},{28,60},{32,0... | collective-permute-start | bytes 786440 | tf_op jit(solution)/shard_map/ppermute | solution.py:18
  57.9 0.0 collective-permute-done.7.refs_7_
  57.9 0.0 collective-permute-done.5.refs_5_
  57.9 0.0 collective-permute-done.3.refs_2_
  57.9 0.0 copy-done
  57.9 3.6 %late0.1 = (bf16[256,256]{1,0:T(8,128)(2,1)S(1)}, bf16[256,256]{1,0:T(8,128)(2,1)S(1)}, bf16[256,256]{1,0:T(8,128)(2,1)S(1)}, bf16[256,256]{1,0:T(8,128)(2,1)S(1)}) custom-call(s32[256]{0:T(256)S(1)} %copy-done.2, bf16[512,256]{1,0:T(8,128)(2,1)S(1)} %copy-done.1, bf16[1024,256]{1,0:T(8,128)(2,1)S(1)} %collective-permute-done.3.refs_2_, ...), custom_call_target="tpu_custom_call" | custom-call | flops 6442450944 | bytes 1572864 | tf_op jit(solution)/shard_map/late0/pallas_call | solution.py:167
  61.5 10.9 %collective-permute-start.10 = (bf16[256,256]{1,0:T(8,128)(2,1)S(1)}, bf16[256,256]{1,0:T(8,128)(2,1)S(1)}, u32[]{:S(2)}, u32[]{:S(2)}) collective-permute-start(bf16[256,256]{1,0:T(8,128)(2,1)S(1)} %get-tuple-element.33), channel_id=1, source_target_pairs={{0,3},{1,0},{2,1},{3,2},{4,7},{5,4},{6,5},{7,6},{8,11},{9,8},{10,9... | collective-permute-start | bytes 393224 | tf_op jit(solution)/shard_map/ppermute | solution.py:250
  72.5 1.9 %collective-permute-start.8 = (bf16[256,256]{1,0:T(8,128)(2,1)S(1)}, bf16[256,256]{1,0:T(8,128)(2,1)S(1)}, u32[]{:S(2)}, u32[]{:S(2)}) collective-permute-start(bf16[256,256]{1,0:T(8,128)(2,1)S(1)} %get-tuple-element.31), channel_id=1, source_target_pairs={{0,1},{1,2},{2,3},{3,0},{4,5},{5,6},{6,7},{7,4},{8,9},{9,10},{10,1... | collective-permute-start | bytes 393224 | tf_op jit(solution)/shard_map/ppermute | solution.py:250
  74.4 4.8 %collective-permute-start.9 = (bf16[256,256]{1,0:T(8,128)(2,1)S(1)}, bf16[256,256]{1,0:T(8,128)(2,1)S(1)}, u32[]{:S(2)}, u32[]{:S(2)}) collective-permute-start(bf16[256,256]{1,0:T(8,128)(2,1)S(1)} %get-tuple-element.32), channel_id=1, source_target_pairs={{0,2},{1,3},{2,0},{3,1},{4,6},{5,7},{6,4},{7,5},{8,10},{9,11},{10,... | collective-permute-start | bytes 393224 | tf_op jit(solution)/shard_map/ppermute | solution.py:250
  79.2 0.0 collective-permute-done.11.refs_6_
  79.2 0.0 collective-permute-done.12.refs_7_
  79.2 4.4 %late1.1 = bf16[4,256,256]{2,1,0:T(8,128)(2,1)} custom-call(s32[256]{0:T(256)S(1)} %copy-done.2, bf16[512,256]{1,0:T(8,128)(2,1)S(1)} %copy-done.1, bf16[1024,256]{1,0:T(8,128)(2,1)S(1)} %collective-permute-done.3.refs_2_, bf16[1024,256]{1,0:T(8,128)(2,1)S(1)} %collective-permute-done.2.refs_3_, bf16[1024,256]{1,0:T(8,128)(2,1)S(1)} %collective-permute-done.4.refs_4_, ...), custom_call_target="tpu_custom_call" | custom-call | flops 6442450944 | bytes 1572864 | tf_op jit(solution)/shard_map/late1/pallas_call | solution.py:167
  83.7 0.0 collective-permute-done.10
  83.7 3.4 %collective-permute-done.8 = bf16[256,256]{1,0:T(8,128)(2,1)S(1)} collective-permute-done((bf16[256,256]{1,0:T(8,128)(2,1)S(1)}, bf16[256,256]{1,0:T(8,128)(2,1)S(1)}, u32[]{:S(2)}, u32[]{:S(2)}) %collective-permute-start.8) | collective-permute-done | bytes 131104 | tf_op jit(solution)/shard_map/ppermute | solution.py:250
  87.1 0.0 collective-permute-done.9
  87.1 6.5 %all-to-all-start = ((bf16[4,256,256]{2,1,0:T(8,128)(2,1)}), bf16[4,256,256]{2,1,0:T(8,128)(2,1)S(1)}, u32[]{:S(2)}, u32[]{:S(2)}) async-start(bf16[4,256,256]{2,1,0:T(8,128)(2,1)} %late1.1), calls=%async_computation | async-start | bytes 1048576 | tf_op jit(solution)/shard_map/all_to_all | solution.py:270
  93.6 0.1 add_convert_fusion
  93.7 15.6 %all-to-all-done = bf16[4,256,256]{2,1,0:T(8,128)(2,1)S(1)} async-done(((bf16[4,256,256]{2,1,0:T(8,128)(2,1)}), bf16[4,256,256]{2,1,0:T(8,128)(2,1)S(1)}, u32[]{:S(2)}, u32[]{:S(2)}) %all-to-all-start) | async-done | bytes 524320 | tf_op jit(solution)/shard_map/all_to_all | solution.py:270
  109.2 0.1 reduce_sum.12
  109.3 0.7 pad_maximum_fusion.3
  (1 shorter events, 0.0 us)
Async XLA Ops:
  1.2 36.6 %copy-start.1 = (bf16[512,256]{1,0:T(8,128)(2,1)S(1)}, bf16[512,256]{1,0:T(8,128)(2,1)}, u32[]{:S(2)}) copy-start(bf16[512,256]{1,0:T(8,128)(2,1)} %refs_1_.5) | copy-start | bytes 786436
  1.2 9.9 %collective-permute-start.1 = (bf16[512,256]{1,0:T(8,128)(2,1)S(1)}, bf16[512,256]{1,0:T(8,128)(2,1)S(1)}, u32[]{:S(2)}, u32[]{:S(2)}) collective-permute-start(bf16[512,256]{1,0:T(8,128)(2,1)S(1)} %get-tuple-element.40), channel_id=1, source_target_pairs={{4,8},{8,4},{12,16},{16,12},{20,24},{24,20},{28,32},{32,28},{36,40... | collective-permute-start | bytes 786440 | tf_op jit(solution)/shard_map/ppermute | solution.py:28
  6.2 31.6 %copy-start.2 = (s32[256]{0:T(256)S(1)}, s32[256]{0:T(256)}, u32[]{:S(2)}) copy-start(s32[256]{0:T(256)} %refs_0_.7) | copy-start | bytes 3076
  6.2 19.9 %collective-permute-start = (bf16[1024,256]{1,0:T(8,128)(2,1)S(1)}, bf16[1024,256]{1,0:T(8,128)(2,1)S(1)}, u32[]{:S(2)}, u32[]{:S(2)}) collective-permute-start(bf16[1024,256]{1,0:T(8,128)(2,1)S(1)} %pad_maximum_fusion.refs_2_), channel_id=1, source_target_pairs={{0,4},{4,0},{8,12},{12,8},{16,20},{20,16},{24,28},{28,24},{32,36},... | collective-permute-start | bytes 1572872 | tf_op jit(solution)/shard_map/ppermute | solution.py:18
  11.2 22.3 %collective-permute-start.2 = (bf16[1024,256]{1,0:T(8,128)(2,1)S(1)}, bf16[1024,256]{1,0:T(8,128)(2,1)S(1)}, u32[]{:S(2)}, u32[]{:S(2)}) collective-permute-start(bf16[1024,256]{1,0:T(8,128)(2,1)S(1)} %pad_maximum_fusion.refs_2_), channel_id=1, source_target_pairs={{0,8},{4,12},{8,0},{12,4},{16,24},{20,28},{24,16},{28,20},{32,40},... | collective-permute-start | bytes 1572872 | tf_op jit(solution)/shard_map/ppermute | solution.py:18
  13.1 41.0 %collective-permute-start.6 = (bf16[512,256]{1,0:T(8,128)(2,1)S(1)}, bf16[512,256]{1,0:T(8,128)(2,1)S(1)}, u32[]{:S(2)}, u32[]{:S(2)}) collective-permute-start(bf16[512,256]{1,0:T(8,128)(2,1)S(1)} %get-tuple-element.41), channel_id=1, source_target_pairs={{0,16},{4,20},{8,24},{12,28},{16,0},{20,4},{24,8},{28,12},{32,48},... | collective-permute-start | bytes 786440 | tf_op jit(solution)/shard_map/ppermute | solution.py:18
  17.1 40.8 %collective-permute-start.7 = (bf16[512,256]{1,0:T(8,128)(2,1)S(1)}, bf16[512,256]{1,0:T(8,128)(2,1)S(1)}, u32[]{:S(2)}, u32[]{:S(2)}) collective-permute-start(bf16[512,256]{1,0:T(8,128)(2,1)S(1)} %get-tuple-element.41), channel_id=1, source_target_pairs={{0,32},{4,36},{8,40},{12,44},{16,48},{20,52},{24,56},{28,60},{32,0... | collective-permute-start | bytes 786440 | tf_op jit(solution)/shard_map/ppermute | solution.py:18
  22.1 35.8 %collective-permute-start.5 = (bf16[1024,256]{1,0:T(8,128)(2,1)S(1)}, bf16[1024,256]{1,0:T(8,128)(2,1)S(1)}, u32[]{:S(2)}, u32[]{:S(2)}) collective-permute-start(bf16[1024,256]{1,0:T(8,128)(2,1)S(1)} %pad_maximum_fusion.refs_2_), channel_id=1, source_target_pairs={{0,128},{4,132},{8,136},{12,140},{16,144},{20,148},{24,152},{28,15... | collective-permute-start | bytes 1572872 | tf_op jit(solution)/shard_map/ppermute | solution.py:18
  26.2 25.3 %collective-permute-start.4 = (bf16[1024,256]{1,0:T(8,128)(2,1)S(1)}, bf16[1024,256]{1,0:T(8,128)(2,1)S(1)}, u32[]{:S(2)}, u32[]{:S(2)}) collective-permute-start(bf16[1024,256]{1,0:T(8,128)(2,1)S(1)} %pad_maximum_fusion.refs_2_), channel_id=1, source_target_pairs={{0,64},{4,68},{8,72},{12,76},{16,80},{20,84},{24,88},{28,92},{32,9... | collective-permute-start | bytes 1572872 | tf_op jit(solution)/shard_map/ppermute | solution.py:18
  33.5 24.4 %collective-permute-start.3 = (bf16[1024,256]{1,0:T(8,128)(2,1)S(1)}, bf16[1024,256]{1,0:T(8,128)(2,1)S(1)}, u32[]{:S(2)}, u32[]{:S(2)}) collective-permute-start(bf16[1024,256]{1,0:T(8,128)(2,1)S(1)} %pad_maximum_fusion.refs_2_), channel_id=1, source_target_pairs={{0,256},{4,260},{8,264},{12,268},{16,272},{20,276},{24,280},{28,28... | collective-permute-start | bytes 1572872 | tf_op jit(solution)/shard_map/ppermute | solution.py:18
  40.2 17.7 %copy-start = (bf16[256,1024]{1,0:T(8,128)(2,1)S(1)}, bf16[256,1024]{1,0:T(8,128)(2,1)}, u32[]{:S(2)}) copy-start(bf16[256,1024]{1,0:T(8,128)(2,1)} %refs_11_.3) | copy-start | bytes 1572868
  51.4 27.8 %collective-permute-start.11 = (bf16[512,256]{1,0:T(8,128)(2,1)S(1)}, bf16[512,256]{1,0:T(8,128)(2,1)S(1)}, u32[]{:S(2)}, u32[]{:S(2)}) collective-permute-start(bf16[512,256]{1,0:T(8,128)(2,1)S(1)} %get-tuple-element.35), channel_id=1, source_target_pairs={{0,16},{4,20},{8,24},{12,28},{16,0},{20,4},{24,8},{28,12},{32,48},... | collective-permute-start | bytes 786440 | tf_op jit(solution)/shard_map/ppermute | solution.py:18
  54.1 25.1 %collective-permute-start.12 = (bf16[512,256]{1,0:T(8,128)(2,1)S(1)}, bf16[512,256]{1,0:T(8,128)(2,1)S(1)}, u32[]{:S(2)}, u32[]{:S(2)}) collective-permute-start(bf16[512,256]{1,0:T(8,128)(2,1)S(1)} %get-tuple-element.35), channel_id=1, source_target_pairs={{0,32},{4,36},{8,40},{12,44},{16,48},{20,52},{24,56},{28,60},{32,0... | collective-permute-start | bytes 786440 | tf_op jit(solution)/shard_map/ppermute | solution.py:18
  61.5 22.1 %collective-permute-start.10 = (bf16[256,256]{1,0:T(8,128)(2,1)S(1)}, bf16[256,256]{1,0:T(8,128)(2,1)S(1)}, u32[]{:S(2)}, u32[]{:S(2)}) collective-permute-start(bf16[256,256]{1,0:T(8,128)(2,1)S(1)} %get-tuple-element.33), channel_id=1, source_target_pairs={{0,3},{1,0},{2,1},{3,2},{4,7},{5,4},{6,5},{7,6},{8,11},{9,8},{10,9... | collective-permute-start | bytes 393224 | tf_op jit(solution)/shard_map/ppermute | solution.py:250
  72.5 14.6 %collective-permute-start.8 = (bf16[256,256]{1,0:T(8,128)(2,1)S(1)}, bf16[256,256]{1,0:T(8,128)(2,1)S(1)}, u32[]{:S(2)}, u32[]{:S(2)}) collective-permute-start(bf16[256,256]{1,0:T(8,128)(2,1)S(1)} %get-tuple-element.31), channel_id=1, source_target_pairs={{0,1},{1,2},{2,3},{3,0},{4,5},{5,6},{6,7},{7,4},{8,9},{9,10},{10,1... | collective-permute-start | bytes 393224 | tf_op jit(solution)/shard_map/ppermute | solution.py:250
  74.4 12.7 %collective-permute-start.9 = (bf16[256,256]{1,0:T(8,128)(2,1)S(1)}, bf16[256,256]{1,0:T(8,128)(2,1)S(1)}, u32[]{:S(2)}, u32[]{:S(2)}) collective-permute-start(bf16[256,256]{1,0:T(8,128)(2,1)S(1)} %get-tuple-element.32), channel_id=1, source_target_pairs={{0,2},{1,3},{2,0},{3,1},{4,6},{5,7},{6,4},{7,5},{8,10},{9,11},{10,... | collective-permute-start | bytes 393224 | tf_op jit(solution)/shard_map/ppermute | solution.py:250
  87.1 22.1 %all-to-all-start = ((bf16[4,256,256]{2,1,0:T(8,128)(2,1)}), bf16[4,256,256]{2,1,0:T(8,128)(2,1)S(1)}, u32[]{:S(2)}, u32[]{:S(2)}) async-start(bf16[4,256,256]{2,1,0:T(8,128)(2,1)} %late1.1), calls=%async_computation | async-start | bytes 1048576 | tf_op jit(solution)/shard_map/all_to_all | solution.py:270

commit v11 on v10

--- a/solution.py
+++ b/solution.py
@@ -195,11 +195,11 @@
     y4a = flat_exchange(parts[0], "seq", 1 << 3)
     y2a = flat_exchange(parts[0], "seq", 1 << 2)
     y1 = flat_exchange(after(packed, halo), "seq", 1 << 1)
-    x1 = flat_exchange(after(packed, core), "seq", 1 << 4)
+    x1 = flat_exchange(after(packed, halo), "seq", 1 << 4)
     x2 = flat_exchange(after(packed, halo), "seq", 1 << 5)
     z1 = flat_exchange(after(packed, y1), "seq", 1 << 6)
-    y2b = flat_exchange(after(parts[1], x1), "seq", 1 << 2)
-    y4b = flat_exchange(after(parts[1], x1), "seq", 1 << 3)
+    y2b = flat_exchange(after(parts[1], y1), "seq", 1 << 2)
+    y4b = flat_exchange(after(parts[1], y1), "seq", 1 << 3)
 
     state0 = attend(
         "early0",

time: 111 us -> 109 us (0.982)
  the two profiles are of different devices: /device:TPU:2 before, /device:TPU:88 now
where the time goes in v11:
time: 109 us; the launch traced here: 108 us
  starting transfers between devices  57.2 us (52%)
  waiting for transfers between devices  35.9 us (33%)
  Pallas kernels  12.9 us (12%)
  local copies, waits for them, and re-layouts  1.15 us (1%)
    ppermute x9, starting transfers between devices, flat_exchange(): return lax.ppermute(value, axis, pairs)  34.9 us
    ppermute x3, starting transfers between devices, per_device(): lax.ppermute(piece, 'head', [(h, (h + hop + 1) % groups) for h in range(g...  16.8 us
    all_to_all x1, waiting for transfers between devices, per_device(): spread = lax.all_to_all(after(shares, *moved), 'head', 0, 0, tiled=False)  16.4 us
    pallas_call x4, Pallas kernels, attend(): pl.pallas_call(lambda *refs: attend_kernel(scale, heads, local, plan, sta...  12.9 us
    ppermute x3, waiting for transfers between devices, per_device(): lax.ppermute(piece, 'head', [(h, (h + hop + 1) % groups) for h in range(g...  7.25 us
    ppermute x9, waiting for transfers between devices, flat_exchange(): return lax.ppermute(value, axis, pairs)  6.53 us
    ppermute x1, waiting for transfers between devices, halo_exchange(): return lax.ppermute(value, axis, pairs)  5.71 us
    all_to_all x1, starting transfers between devices, per_device(): spread = lax.all_to_all(after(shares, *moved), 'head', 0, 0, tiled=False)  3.47 us
  transfers between devices with their start and end apart: 14, of which 6 were waited for; matrix products, arithmetic and copies ran while one was open for 0% of the time, Pallas kernels for 12%

profile of v11, /device:TPU:88, one launch (start us, length us, event | category | flops | bytes accessed | tf_op | source)
XLA Modules:
  0.0 108.4 jit_solution(2579452463182768527)
XLA Ops:
  0.0 1.1 %fusion = (bf16[256,256]{1,0:T(8,128)(2,1)S(1)}, bf16[256,256]{1,0:T(8,128)(2,1)S(1)}, bf16[256,256]{1,0:T(8,128)(2,1)S(1)}, bf16[256,256]{1,0:T(8,128)(2,1)S(1)}) fusion(bf16[512,256]{1,0:T(8,128)(2,1)} %param.6, bf16[512,256]{1,0:T(8,128)(2,1)} %param.7), kind=kLoop, calls=%fused_computation.6 | loop fusion | bytes 1048576 | tf_op jit(solution)/shard_map/slice | solution.py:188
  1.1 0.1 pad_maximum_fusion.1
  1.2 0.0 copy-start.1
  1.2 2.1 %collective-permute-start.1 = (bf16[512,256]{1,0:T(8,128)(2,1)S(1)}, bf16[512,256]{1,0:T(8,128)(2,1)S(1)}, u32[]{:S(2)}, u32[]{:S(2)}) collective-permute-start(bf16[512,256]{1,0:T(8,128)(2,1)S(1)} %get-tuple-element.38), channel_id=1, source_target_pairs={{4,8},{8,4},{12,16},{16,12},{20,24},{24,20},{28,32},{32,28},{36,40... | collective-permute-start | bytes 786440 | tf_op jit(solution)/shard_map/ppermute | solution.py:28
  3.4 0.0 copy-start.2
  3.4 5.7 %collective-permute-done.1.refs_4_ = bf16[512,256]{1,0:T(8,128)(2,1)S(1)} collective-permute-done((bf16[512,256]{1,0:T(8,128)(2,1)S(1)}, bf16[512,256]{1,0:T(8,128)(2,1)S(1)}, u32[]{:S(2)}, u32[]{:S(2)}) %collective-permute-start.1) | collective-permute-done | bytes 262176 | tf_op jit(solution)/shard_map/ppermute | solution.py:28
  9.1 2.3 %collective-permute-start.2 = (bf16[1024,256]{1,0:T(8,128)(2,1)S(1)}, bf16[1024,256]{1,0:T(8,128)(2,1)S(1)}, u32[]{:S(2)}, u32[]{:S(2)}) collective-permute-start(bf16[1024,256]{1,0:T(8,128)(2,1)S(1)} %pad_maximum_fusion.refs_2_), channel_id=1, source_target_pairs={{0,8},{4,12},{8,0},{12,4},{16,24},{20,28},{24,16},{28,20},{32,40},... | collective-permute-start | bytes 1572872 | tf_op jit(solution)/shard_map/ppermute | solution.py:18
  11.4 2.6 %collective-permute-start = (bf16[1024,256]{1,0:T(8,128)(2,1)S(1)}, bf16[1024,256]{1,0:T(8,128)(2,1)S(1)}, u32[]{:S(2)}, u32[]{:S(2)}) collective-permute-start(bf16[1024,256]{1,0:T(8,128)(2,1)S(1)} %pad_maximum_fusion.refs_2_), channel_id=1, source_target_pairs={{0,4},{4,0},{8,12},{12,8},{16,20},{20,16},{24,28},{28,24},{32,36},... | collective-permute-start | bytes 1572872 | tf_op jit(solution)/shard_map/ppermute | solution.py:18
  14.1 5.7 %collective-permute-start.6 = (bf16[512,256]{1,0:T(8,128)(2,1)S(1)}, bf16[512,256]{1,0:T(8,128)(2,1)S(1)}, u32[]{:S(2)}, u32[]{:S(2)}) collective-permute-start(bf16[512,256]{1,0:T(8,128)(2,1)S(1)} %get-tuple-element.39), channel_id=1, source_target_pairs={{0,16},{4,20},{8,24},{12,28},{16,0},{20,4},{24,8},{28,12},{32,48},... | collective-permute-start | bytes 786440 | tf_op jit(solution)/shard_map/ppermute | solution.py:18
  19.8 4.7 %collective-permute-start.7 = (bf16[512,256]{1,0:T(8,128)(2,1)S(1)}, bf16[512,256]{1,0:T(8,128)(2,1)S(1)}, u32[]{:S(2)}, u32[]{:S(2)}) collective-permute-start(bf16[512,256]{1,0:T(8,128)(2,1)S(1)} %get-tuple-element.39), channel_id=1, source_target_pairs={{0,32},{4,36},{8,40},{12,44},{16,48},{20,52},{24,56},{28,60},{32,0... | collective-permute-start | bytes 786440 | tf_op jit(solution)/shard_map/ppermute | solution.py:18
  24.6 3.4 %collective-permute-start.4 = (bf16[1024,256]{1,0:T(8,128)(2,1)S(1)}, bf16[1024,256]{1,0:T(8,128)(2,1)S(1)}, u32[]{:S(2)}, u32[]{:S(2)}) collective-permute-start(bf16[1024,256]{1,0:T(8,128)(2,1)S(1)} %pad_maximum_fusion.refs_2_), channel_id=1, source_target_pairs={{0,64},{4,68},{8,72},{12,76},{16,80},{20,84},{24,88},{28,92},{32,9... | collective-permute-start | bytes 1572872 | tf_op jit(solution)/shard_map/ppermute | solution.py:18
  28.0 3.4 %collective-permute-done.2.refs_3_ = bf16[1024,256]{1,0:T(8,128)(2,1)S(1)} collective-permute-done((bf16[1024,256]{1,0:T(8,128)(2,1)S(1)}, bf16[1024,256]{1,0:T(8,128)(2,1)S(1)}, u32[]{:S(2)}, u32[]{:S(2)}) %collective-permute-start.2) | collective-permute-done | bytes 524320 | tf_op jit(solution)/shard_map/ppermute | solution.py:18
  31.4 7.8 %collective-permute-start.5 = (bf16[1024,256]{1,0:T(8,128)(2,1)S(1)}, bf16[1024,256]{1,0:T(8,128)(2,1)S(1)}, u32[]{:S(2)}, u32[]{:S(2)}) collective-permute-start(bf16[1024,256]{1,0:T(8,128)(2,1)S(1)} %pad_maximum_fusion.refs_2_), channel_id=1, source_target_pairs={{0,128},{4,132},{8,136},{12,140},{16,144},{20,148},{24,152},{28,15... | collective-permute-start | bytes 1572872 | tf_op jit(solution)/shard_map/ppermute | solution.py:18
  39.1 0.0 collective-permute-done.refs_3_
  39.2 1.9 %collective-permute-start.3 = (bf16[1024,256]{1,0:T(8,128)(2,1)S(1)}, bf16[1024,256]{1,0:T(8,128)(2,1)S(1)}, u32[]{:S(2)}, u32[]{:S(2)}) collective-permute-start(bf16[1024,256]{1,0:T(8,128)(2,1)S(1)} %pad_maximum_fusion.refs_2_), channel_id=1, source_target_pairs={{0,256},{4,260},{8,264},{12,268},{16,272},{20,276},{24,280},{28,28... | collective-permute-start | bytes 1572872 | tf_op jit(solution)/shard_map/ppermute | solution.py:18
  41.1 0.0 copy-done.1
  41.1 0.0 copy-done.2
  41.1 2.4 %early1.1 = (f32[1024,128]{1,0:T(8,128)S(1)}, f32[1024,128]{1,0:T(8,128)S(1)}, f32[1024,128]{1,0:T(8,128)S(1)}) custom-call(s32[256]{0:T(256)S(1)} %copy-done.2, bf16[512,256]{1,0:T(8,128)(2,1)S(1)} %copy-done.1, bf16[1024,256]{1,0:T(8,128)(2,1)S(1)} %pad_maximum_fusion.refs_2_, bf16[1024,256]{1,0:T(8,128)(2,1)S(1)} %collective-permute-done.refs_3_, ...), custom_call_target="tpu_custom_call" | custom-call | flops 4294967296 | bytes 1048576 | tf_op jit(solution)/shard_map/early1/pallas_call | solution.py:167
  43.5 0.0 copy-start
  43.5 2.4 %early0.1 = (f32[1024,128]{1,0:T(8,128)S(1)}, f32[1024,128]{1,0:T(8,128)S(1)}, f32[1024,128]{1,0:T(8,128)S(1)}) custom-call(s32[256]{0:T(256)S(1)} %copy-done.2, bf16[512,256]{1,0:T(8,128)(2,1)S(1)} %copy-done.1, bf16[1024,256]{1,0:T(8,128)(2,1)S(1)} %pad_maximum_fusion.refs_2_, bf16[1024,256]{1,0:T(8,128)(2,1)S(1)} %collective-permute-done.refs_3_, ...), custom_call_target="tpu_custom_call" | custom-call | flops 4294967296 | bytes 1048576 | tf_op jit(solution)/shard_map/early0/pallas_call | solution.py:167
  45.9 0.0 collective-permute-done.6.refs_6_
  45.9 1.9 %collective-permute-start.11 = (bf16[512,256]{1,0:T(8,128)(2,1)S(1)}, bf16[512,256]{1,0:T(8,128)(2,1)S(1)}, u32[]{:S(2)}, u32[]{:S(2)}) collective-permute-start(bf16[512,256]{1,0:T(8,128)(2,1)S(1)} %get-tuple-element.33), channel_id=1, source_target_pairs={{0,16},{4,20},{8,24},{12,28},{16,0},{20,4},{24,8},{28,12},{32,48},... | collective-permute-start | bytes 786440 | tf_op jit(solution)/shard_map/ppermute | solution.py:18
  47.9 0.0 collective-permute-done.7.refs_7_
  47.9 4.5 %collective-permute-start.12 = (bf16[512,256]{1,0:T(8,128)(2,1)S(1)}, bf16[512,256]{1,0:T(8,128)(2,1)S(1)}, u32[]{:S(2)}, u32[]{:S(2)}) collective-permute-start(bf16[512,256]{1,0:T(8,128)(2,1)S(1)} %get-tuple-element.33), channel_id=1, source_target_pairs={{0,32},{4,36},{8,40},{12,44},{16,48},{20,52},{24,56},{28,60},{32,0... | collective-permute-start | bytes 786440 | tf_op jit(solution)/shard_map/ppermute | solution.py:18
  52.3 0.0 collective-permute-done.4.refs_4_
  52.3 1.3 %collective-permute-done.5.refs_5_ = bf16[1024,256]{1,0:T(8,128)(2,1)S(1)} collective-permute-done((bf16[1024,256]{1,0:T(8,128)(2,1)S(1)}, bf16[1024,256]{1,0:T(8,128)(2,1)S(1)}, u32[]{:S(2)}, u32[]{:S(2)}) %collective-permute-start.5) | collective-permute-done | bytes 524320 | tf_op jit(solution)/shard_map/ppermute | solution.py:18
  53.6 1.8 %collective-permute-done.3.refs_2_ = bf16[1024,256]{1,0:T(8,128)(2,1)S(1)} collective-permute-done((bf16[1024,256]{1,0:T(8,128)(2,1)S(1)}, bf16[1024,256]{1,0:T(8,128)(2,1)S(1)}, u32[]{:S(2)}, u32[]{:S(2)}) %collective-permute-start.3) | collective-permute-done | bytes 524320 | tf_op jit(solution)/shard_map/ppermute | solution.py:18
  55.4 0.0 copy-done
  55.5 3.6 %late0.1 = (bf16[256,256]{1,0:T(8,128)(2,1)S(1)}, bf16[256,256]{1,0:T(8,128)(2,1)S(1)}, bf16[256,256]{1,0:T(8,128)(2,1)S(1)}, bf16[256,256]{1,0:T(8,128)(2,1)S(1)}) custom-call(s32[256]{0:T(256)S(1)} %copy-done.2, bf16[512,256]{1,0:T(8,128)(2,1)S(1)} %copy-done.1, bf16[1024,256]{1,0:T(8,128)(2,1)S(1)} %collective-permute-done.3.refs_2_, ...), custom_call_target="tpu_custom_call" | custom-call | flops 6442450944 | bytes 1572864 | tf_op jit(solution)/shard_map/late0/pallas_call | solution.py:167
  59.1 10.0 %collective-permute-start.10 = (bf16[256,256]{1,0:T(8,128)(2,1)S(1)}, bf16[256,256]{1,0:T(8,128)(2,1)S(1)}, u32[]{:S(2)}, u32[]{:S(2)}) collective-permute-start(bf16[256,256]{1,0:T(8,128)(2,1)S(1)} %get-tuple-element.31), channel_id=1, source_target_pairs={{0,3},{1,0},{2,1},{3,2},{4,7},{5,4},{6,5},{7,6},{8,11},{9,8},{10,9... | collective-permute-start | bytes 393224 | tf_op jit(solution)/shard_map/ppermute | solution.py:250
  69.1 1.9 %collective-permute-start.8 = (bf16[256,256]{1,0:T(8,128)(2,1)S(1)}, bf16[256,256]{1,0:T(8,128)(2,1)S(1)}, u32[]{:S(2)}, u32[]{:S(2)}) collective-permute-start(bf16[256,256]{1,0:T(8,128)(2,1)S(1)} %get-tuple-element.29), channel_id=1, source_target_pairs={{0,1},{1,2},{2,3},{3,0},{4,5},{5,6},{6,7},{7,4},{8,9},{9,10},{10,1... | collective-permute-start | bytes 393224 | tf_op jit(solution)/shard_map/ppermute | solution.py:250
  71.1 4.8 %collective-permute-start.9 = (bf16[256,256]{1,0:T(8,128)(2,1)S(1)}, bf16[256,256]{1,0:T(8,128)(2,1)S(1)}, u32[]{:S(2)}, u32[]{:S(2)}) collective-permute-start(bf16[256,256]{1,0:T(8,128)(2,1)S(1)} %get-tuple-element.30), channel_id=1, source_target_pairs={{0,2},{1,3},{2,0},{3,1},{4,6},{5,7},{6,4},{7,5},{8,10},{9,11},{10,... | collective-permute-start | bytes 393224 | tf_op jit(solution)/shard_map/ppermute | solution.py:250
  75.9 0.0 collective-permute-done.11.refs_6_
  75.9 0.0 collective-permute-done.12.refs_7_
  75.9 4.4 %late1.1 = bf16[4,256,256]{2,1,0:T(8,128)(2,1)} custom-call(s32[256]{0:T(256)S(1)} %copy-done.2, bf16[512,256]{1,0:T(8,128)(2,1)S(1)} %copy-done.1, bf16[1024,256]{1,0:T(8,128)(2,1)S(1)} %collective-permute-done.3.refs_2_, bf16[1024,256]{1,0:T(8,128)(2,1)S(1)} %collective-permute-done.2.refs_3_, bf16[1024,256]{1,0:T(8,128)(2,1)S(1)} %collective-permute-done.4.refs_4_, ...), custom_call_target="tpu_custom_call" | custom-call | flops 6442450944 | bytes 1572864 | tf_op jit(solution)/shard_map/late1/pallas_call | solution.py:167
  80.3 0.0 collective-permute-done.10
  80.3 7.2 %collective-permute-done.8 = bf16[256,256]{1,0:T(8,128)(2,1)S(1)} collective-permute-done((bf16[256,256]{1,0:T(8,128)(2,1)S(1)}, bf16[256,256]{1,0:T(8,128)(2,1)S(1)}, u32[]{:S(2)}, u32[]{:S(2)}) %collective-permute-start.8) | collective-permute-done | bytes 131104 | tf_op jit(solution)/shard_map/ppermute | solution.py:250
  87.6 0.0 collective-permute-done.9
  87.6 3.5 %all-to-all-start = ((bf16[4,256,256]{2,1,0:T(8,128)(2,1)}), bf16[4,256,256]{2,1,0:T(8,128)(2,1)S(1)}, u32[]{:S(2)}, u32[]{:S(2)}) async-start(bf16[4,256,256]{2,1,0:T(8,128)(2,1)} %late1.1), calls=%async_computation | async-start | bytes 1048576 | tf_op jit(solution)/shard_map/all_to_all | solution.py:270
  91.1 0.1 add_convert_fusion
  91.1 16.4 %all-to-all-done = bf16[4,256,256]{2,1,0:T(8,128)(2,1)S(1)} async-done(((bf16[4,256,256]{2,1,0:T(8,128)(2,1)}), bf16[4,256,256]{2,1,0:T(8,128)(2,1)S(1)}, u32[]{:S(2)}, u32[]{:S(2)}) %all-to-all-start) | async-done | bytes 524320 | tf_op jit(solution)/shard_map/all_to_all | solution.py:270
  107.6 0.1 reduce_sum.12
  107.6 0.7 pad_maximum_fusion.3
  (1 shorter events, 0.0 us)
Async XLA Ops:
  1.2 39.8 %copy-start.1 = (bf16[512,256]{1,0:T(8,128)(2,1)S(1)}, bf16[512,256]{1,0:T(8,128)(2,1)}, u32[]{:S(2)}) copy-start(bf16[512,256]{1,0:T(8,128)(2,1)} %refs_1_.5) | copy-start | bytes 786436
  1.2 7.8 %collective-permute-start.1 = (bf16[512,256]{1,0:T(8,128)(2,1)S(1)}, bf16[512,256]{1,0:T(8,128)(2,1)S(1)}, u32[]{:S(2)}, u32[]{:S(2)}) collective-permute-start(bf16[512,256]{1,0:T(8,128)(2,1)S(1)} %get-tuple-element.38), channel_id=1, source_target_pairs={{4,8},{8,4},{12,16},{16,12},{20,24},{24,20},{28,32},{32,28},{36,40... | collective-permute-start | bytes 786440 | tf_op jit(solution)/shard_map/ppermute | solution.py:28
  3.4 37.7 %copy-start.2 = (s32[256]{0:T(256)S(1)}, s32[256]{0:T(256)}, u32[]{:S(2)}) copy-start(s32[256]{0:T(256)} %refs_0_.7) | copy-start | bytes 3076
  9.1 22.3 %collective-permute-start.2 = (bf16[1024,256]{1,0:T(8,128)(2,1)S(1)}, bf16[1024,256]{1,0:T(8,128)(2,1)S(1)}, u32[]{:S(2)}, u32[]{:S(2)}) collective-permute-start(bf16[1024,256]{1,0:T(8,128)(2,1)S(1)} %pad_maximum_fusion.refs_2_), channel_id=1, source_target_pairs={{0,8},{4,12},{8,0},{12,4},{16,24},{20,28},{24,16},{28,20},{32,40},... | collective-permute-start | bytes 1572872 | tf_op jit(solution)/shard_map/ppermute | solution.py:18
  11.4 27.7 %collective-permute-start = (bf16[1024,256]{1,0:T(8,128)(2,1)S(1)}, bf16[1024,256]{1,0:T(8,128)(2,1)S(1)}, u32[]{:S(2)}, u32[]{:S(2)}) collective-permute-start(bf16[1024,256]{1,0:T(8,128)(2,1)S(1)} %pad_maximum_fusion.refs_2_), channel_id=1, source_target_pairs={{0,4},{4,0},{8,12},{12,8},{16,20},{20,16},{24,28},{28,24},{32,36},... | collective-permute-start | bytes 1572872 | tf_op jit(solution)/shard_map/ppermute | solution.py:18
  14.1 31.9 %collective-permute-start.6 = (bf16[512,256]{1,0:T(8,128)(2,1)S(1)}, bf16[512,256]{1,0:T(8,128)(2,1)S(1)}, u32[]{:S(2)}, u32[]{:S(2)}) collective-permute-start(bf16[512,256]{1,0:T(8,128)(2,1)S(1)} %get-tuple-element.39), channel_id=1, source_target_pairs={{0,16},{4,20},{8,24},{12,28},{16,0},{20,4},{24,8},{28,12},{32,48},... | collective-permute-start | bytes 786440 | tf_op jit(solution)/shard_map/ppermute | solution.py:18
  19.8 28.0 %collective-permute-start.7 = (bf16[512,256]{1,0:T(8,128)(2,1)S(1)}, bf16[512,256]{1,0:T(8,128)(2,1)S(1)}, u32[]{:S(2)}, u32[]{:S(2)}) collective-permute-start(bf16[512,256]{1,0:T(8,128)(2,1)S(1)} %get-tuple-element.39), channel_id=1, source_target_pairs={{0,32},{4,36},{8,40},{12,44},{16,48},{20,52},{24,56},{28,60},{32,0... | collective-permute-start | bytes 786440 | tf_op jit(solution)/shard_map/ppermute | solution.py:18
  24.6 27.8 %collective-permute-start.4 = (bf16[1024,256]{1,0:T(8,128)(2,1)S(1)}, bf16[1024,256]{1,0:T(8,128)(2,1)S(1)}, u32[]{:S(2)}, u32[]{:S(2)}) collective-permute-start(bf16[1024,256]{1,0:T(8,128)(2,1)S(1)} %pad_maximum_fusion.refs_2_), channel_id=1, source_target_pairs={{0,64},{4,68},{8,72},{12,76},{16,80},{20,84},{24,88},{28,92},{32,9... | collective-permute-start | bytes 1572872 | tf_op jit(solution)/shard_map/ppermute | solution.py:18
  31.4 22.3 %collective-permute-start.5 = (bf16[1024,256]{1,0:T(8,128)(2,1)S(1)}, bf16[1024,256]{1,0:T(8,128)(2,1)S(1)}, u32[]{:S(2)}, u32[]{:S(2)}) collective-permute-start(bf16[1024,256]{1,0:T(8,128)(2,1)S(1)} %pad_maximum_fusion.refs_2_), channel_id=1, source_target_pairs={{0,128},{4,132},{8,136},{12,140},{16,144},{20,148},{24,152},{28,15... | collective-permute-start | bytes 1572872 | tf_op jit(solution)/shard_map/ppermute | solution.py:18
  39.2 16.3 %collective-permute-start.3 = (bf16[1024,256]{1,0:T(8,128)(2,1)S(1)}, bf16[1024,256]{1,0:T(8,128)(2,1)S(1)}, u32[]{:S(2)}, u32[]{:S(2)}) collective-permute-start(bf16[1024,256]{1,0:T(8,128)(2,1)S(1)} %pad_maximum_fusion.refs_2_), channel_id=1, source_target_pairs={{0,256},{4,260},{8,264},{12,268},{16,272},{20,276},{24,280},{28,28... | collective-permute-start | bytes 1572872 | tf_op jit(solution)/shard_map/ppermute | solution.py:18
  43.5 11.9 %copy-start = (bf16[256,1024]{1,0:T(8,128)(2,1)S(1)}, bf16[256,1024]{1,0:T(8,128)(2,1)}, u32[]{:S(2)}) copy-start(bf16[256,1024]{1,0:T(8,128)(2,1)} %refs_11_.3) | copy-start | bytes 1572868
  45.9 29.9 %collective-permute-start.11 = (bf16[512,256]{1,0:T(8,128)(2,1)S(1)}, bf16[512,256]{1,0:T(8,128)(2,1)S(1)}, u32[]{:S(2)}, u32[]{:S(2)}) collective-permute-start(bf16[512,256]{1,0:T(8,128)(2,1)S(1)} %get-tuple-element.33), channel_id=1, source_target_pairs={{0,16},{4,20},{8,24},{12,28},{16,0},{20,4},{24,8},{28,12},{32,48},... | collective-permute-start | bytes 786440 | tf_op jit(solution)/shard_map/ppermute | solution.py:18
  47.9 28.0 %collective-permute-start.12 = (bf16[512,256]{1,0:T(8,128)(2,1)S(1)}, bf16[512,256]{1,0:T(8,128)(2,1)S(1)}, u32[]{:S(2)}, u32[]{:S(2)}) collective-permute-start(bf16[512,256]{1,0:T(8,128)(2,1)S(1)} %get-tuple-element.33), channel_id=1, source_target_pairs={{0,32},{4,36},{8,40},{12,44},{16,48},{20,52},{24,56},{28,60},{32,0... | collective-permute-start | bytes 786440 | tf_op jit(solution)/shard_map/ppermute | solution.py:18
  59.1 21.2 %collective-permute-start.10 = (bf16[256,256]{1,0:T(8,128)(2,1)S(1)}, bf16[256,256]{1,0:T(8,128)(2,1)S(1)}, u32[]{:S(2)}, u32[]{:S(2)}) collective-permute-start(bf16[256,256]{1,0:T(8,128)(2,1)S(1)} %get-tuple-element.31), channel_id=1, source_target_pairs={{0,3},{1,0},{2,1},{3,2},{4,7},{5,4},{6,5},{7,6},{8,11},{9,8},{10,9... | collective-permute-start | bytes 393224 | tf_op jit(solution)/shard_map/ppermute | solution.py:250
  69.1 18.4 %collective-permute-start.8 = (bf16[256,256]{1,0:T(8,128)(2,1)S(1)}, bf16[256,256]{1,0:T(8,128)(2,1)S(1)}, u32[]{:S(2)}, u32[]{:S(2)}) collective-permute-start(bf16[256,256]{1,0:T(8,128)(2,1)S(1)} %get-tuple-element.29), channel_id=1, source_target_pairs={{0,1},{1,2},{2,3},{3,0},{4,5},{5,6},{6,7},{7,4},{8,9},{9,10},{10,1... | collective-permute-start | bytes 393224 | tf_op jit(solution)/shard_map/ppermute | solution.py:250
  71.1 16.5 %collective-permute-start.9 = (bf16[256,256]{1,0:T(8,128)(2,1)S(1)}, bf16[256,256]{1,0:T(8,128)(2,1)S(1)}, u32[]{:S(2)}, u32[]{:S(2)}) collective-permute-start(bf16[256,256]{1,0:T(8,128)(2,1)S(1)} %get-tuple-element.30), channel_id=1, source_target_pairs={{0,2},{1,3},{2,0},{3,1},{4,6},{5,7},{6,4},{7,5},{8,10},{9,11},{10,... | collective-permute-start | bytes 393224 | tf_op jit(solution)/shard_map/ppermute | solution.py:250
  87.6 20.0 %all-to-all-start = ((bf16[4,256,256]{2,1,0:T(8,128)(2,1)}), bf16[4,256,256]{2,1,0:T(8,128)(2,1)S(1)}, u32[]{:S(2)}, u32[]{:S(2)}) async-start(bf16[4,256,256]{2,1,0:T(8,128)(2,1)} %late1.1), calls=%async_computation | async-start | bytes 1048576 | tf_op jit(solution)/shard_map/all_to_all | solution.py:270

commit v12 on v11

--- a/solution.py
+++ b/solution.py
@@ -227,7 +227,7 @@
             ("near", (1, 2), 0, 1),
         ],
     )
-    mine, *pieces = attend(
+    first = attend(
         "late0",
         block_keep,
         after(queries, state1[0]),
@@ -243,17 +243,12 @@
         ],
         state=state0,
         w_out=w_out,
-        rotated=True,
-    )
-    groups = 1 + len(pieces)
-    moved = [
-        lax.ppermute(piece, "head", [(h, (h + hop + 1) % groups) for h in range(groups)])
-        for hop, piece in enumerate(pieces)
-    ]
+    )
+    spread = [lax.all_to_all(first, "head", 0, 0, tiled=False)]
     shares = attend(
         "late1",
         block_keep,
-        after(queries, mine),
+        after(queries, first),
         1,
         [z1, y1, x1, x2, y2b, y4b],
         [
@@ -267,12 +262,9 @@
         state=state1,
         w_out=w_out,
     )
-    spread = lax.all_to_all(after(shares, *moved), "head", 0, 0, tiled=False)
-    total = mine.astype(jnp.float32)
-    for piece in moved:
-        total = total + piece.astype(jnp.float32)
-    outs = [total, jnp.sum(spread.astype(jnp.float32), axis=0)]
-    return jnp.concatenate([out.astype(jnp.bfloat16) for out in outs], axis=0)
+    spread.append(lax.all_to_all(after(shares, spread[0]), "head", 0, 0, tiled=False))
+    outs = [jnp.sum(piece.astype(jnp.float32), axis=0).astype(jnp.bfloat16) for piece in spread]
+    return jnp.concatenate(outs, axis=0)
 
 
 def solution(mesh):

time: 109 us -> 111 us (1.018)
  the two profiles are of different devices: /device:TPU:88 before, /device:TPU:56 now
where the time goes in v12:
time: 111 us; the launch traced here: 110 us
  starting transfers between devices  53.5 us (48%)
  waiting for transfers between devices  35 us (32%)
  Pallas kernels  13.5 us (12%)
  local copies, waits for them, and re-layouts  5.07 us (5%)
  other arithmetic  2.77 us (2%)
    ppermute x9, starting transfers between devices, flat_exchange(): return lax.ppermute(value, axis, pairs)  36.4 us
    all_to_all x1, waiting for transfers between devices, per_device(): lax.all_to_all(after(shares, spread[0]), 'head', 0, 0, tiled=False)  16.4 us
    pallas_call x4, Pallas kernels, attend(): pl.pallas_call(lambda *refs: attend_kernel(scale, heads, local, plan, sta...  13.5 us
    all_to_all x1, starting transfers between devices, per_device(): spread = [lax.all_to_all(first, 'head', 0, 0, tiled=False)]  9.4 us
    ppermute x9, waiting for transfers between devices, flat_exchange(): return lax.ppermute(value, axis, pairs)  9.14 us
    ppermute x1, waiting for transfers between devices, halo_exchange(): return lax.ppermute(value, axis, pairs)  4.93 us
    all_to_all x1, starting transfers between devices, per_device(): lax.all_to_all(after(shares, spread[0]), 'head', 0, 0, tiled=False)  4.87 us
    all_to_all x1, waiting for transfers between devices, per_device(): spread = [lax.all_to_all(first, 'head', 0, 0, tiled=False)]  4.53 us
  transfers between devices with their start and end apart: 12, of which 5 were waited for; matrix products, arithmetic and copies ran while one was open for 1% of the time, Pallas kernels for 12%

profile of v12, /device:TPU:56, one launch (start us, length us, event | category | flops | bytes accessed | tf_op | source)
XLA Modules:
  0.0 110.0 jit_solution(11136284304017436176)
XLA Ops:
  0.0 1.1 %fusion = (bf16[256,256]{1,0:T(8,128)(2,1)S(1)}, bf16[256,256]{1,0:T(8,128)(2,1)S(1)}, bf16[256,256]{1,0:T(8,128)(2,1)S(1)}, bf16[256,256]{1,0:T(8,128)(2,1)S(1)}) fusion(bf16[512,256]{1,0:T(8,128)(2,1)} %param.6, bf16[512,256]{1,0:T(8,128)(2,1)} %param.7), kind=kLoop, calls=%fused_computation.5 | loop fusion | bytes 1048576 | tf_op jit(solution)/shard_map/slice | solution.py:188
  1.1 0.8 pad_maximum_fusion.1
  1.9 0.0 copy-start.1
  1.9 2.8 %collective-permute-start.1 = (bf16[512,256]{1,0:T(8,128)(2,1)S(1)}, bf16[512,256]{1,0:T(8,128)(2,1)S(1)}, u32[]{:S(2)}, u32[]{:S(2)}) collective-permute-start(bf16[512,256]{1,0:T(8,128)(2,1)S(1)} %get-tuple-element.30), channel_id=1, source_target_pairs={{4,8},{8,4},{12,16},{16,12},{20,24},{24,20},{28,32},{32,28},{36,40... | collective-permute-start | bytes 786440 | tf_op jit(solution)/shard_map/ppermute | solution.py:28
  4.8 0.0 copy-start.2
  4.8 4.9 %collective-permute-done.1.refs_4_ = bf16[512,256]{1,0:T(8,128)(2,1)S(1)} collective-permute-done((bf16[512,256]{1,0:T(8,128)(2,1)S(1)}, bf16[512,256]{1,0:T(8,128)(2,1)S(1)}, u32[]{:S(2)}, u32[]{:S(2)}) %collective-permute-start.1) | collective-permute-done | bytes 262176 | tf_op jit(solution)/shard_map/ppermute | solution.py:28
  9.7 3.2 %collective-permute-start.2 = (bf16[1024,256]{1,0:T(8,128)(2,1)S(1)}, bf16[1024,256]{1,0:T(8,128)(2,1)S(1)}, u32[]{:S(2)}, u32[]{:S(2)}) collective-permute-start(bf16[1024,256]{1,0:T(8,128)(2,1)S(1)} %pad_maximum_fusion.refs_2_), channel_id=1, source_target_pairs={{0,8},{4,12},{8,0},{12,4},{16,24},{20,28},{24,16},{28,20},{32,40},... | collective-permute-start | bytes 1572872 | tf_op jit(solution)/shard_map/ppermute | solution.py:18
  13.0 2.5 %collective-permute-start = (bf16[1024,256]{1,0:T(8,128)(2,1)S(1)}, bf16[1024,256]{1,0:T(8,128)(2,1)S(1)}, u32[]{:S(2)}, u32[]{:S(2)}) collective-permute-start(bf16[1024,256]{1,0:T(8,128)(2,1)S(1)} %pad_maximum_fusion.refs_2_), channel_id=1, source_target_pairs={{0,4},{4,0},{8,12},{12,8},{16,20},{20,16},{24,28},{28,24},{32,36},... | collective-permute-start | bytes 1572872 | tf_op jit(solution)/shard_map/ppermute | solution.py:18
  15.5 4.7 %collective-permute-start.6 = (bf16[512,256]{1,0:T(8,128)(2,1)S(1)}, bf16[512,256]{1,0:T(8,128)(2,1)S(1)}, u32[]{:S(2)}, u32[]{:S(2)}) collective-permute-start(bf16[512,256]{1,0:T(8,128)(2,1)S(1)} %get-tuple-element.31), channel_id=1, source_target_pairs={{0,16},{4,20},{8,24},{12,28},{16,0},{20,4},{24,8},{28,12},{32,48},... | collective-permute-start | bytes 786440 | tf_op jit(solution)/shard_map/ppermute | solution.py:18
  20.2 1.9 %collective-permute-start.7 = (bf16[512,256]{1,0:T(8,128)(2,1)S(1)}, bf16[512,256]{1,0:T(8,128)(2,1)S(1)}, u32[]{:S(2)}, u32[]{:S(2)}) collective-permute-start(bf16[512,256]{1,0:T(8,128)(2,1)S(1)} %get-tuple-element.31), channel_id=1, source_target_pairs={{0,32},{4,36},{8,40},{12,44},{16,48},{20,52},{24,56},{28,60},{32,0... | collective-permute-start | bytes 786440 | tf_op jit(solution)/shard_map/ppermute | solution.py:18
  22.1 4.4 %collective-permute-start.4 = (bf16[1024,256]{1,0:T(8,128)(2,1)S(1)}, bf16[1024,256]{1,0:T(8,128)(2,1)S(1)}, u32[]{:S(2)}, u32[]{:S(2)}) collective-permute-start(bf16[1024,256]{1,0:T(8,128)(2,1)S(1)} %pad_maximum_fusion.refs_2_), channel_id=1, source_target_pairs={{0,64},{4,68},{8,72},{12,76},{16,80},{20,84},{24,88},{28,92},{32,9... | collective-permute-start | bytes 1572872 | tf_op jit(solution)/shard_map/ppermute | solution.py:18
  26.5 4.6 %collective-permute-done.2.refs_3_ = bf16[1024,256]{1,0:T(8,128)(2,1)S(1)} collective-permute-done((bf16[1024,256]{1,0:T(8,128)(2,1)S(1)}, bf16[1024,256]{1,0:T(8,128)(2,1)S(1)}, u32[]{:S(2)}, u32[]{:S(2)}) %collective-permute-start.2) | collective-permute-done | bytes 524320 | tf_op jit(solution)/shard_map/ppermute | solution.py:18
  31.1 4.9 %collective-permute-start.5 = (bf16[1024,256]{1,0:T(8,128)(2,1)S(1)}, bf16[1024,256]{1,0:T(8,128)(2,1)S(1)}, u32[]{:S(2)}, u32[]{:S(2)}) collective-permute-start(bf16[1024,256]{1,0:T(8,128)(2,1)S(1)} %pad_maximum_fusion.refs_2_), channel_id=1, source_target_pairs={{0,128},{4,132},{8,136},{12,140},{16,144},{20,148},{24,152},{28,15... | collective-permute-start | bytes 1572872 | tf_op jit(solution)/shard_map/ppermute | solution.py:18
  36.0 0.0 collective-permute-done.refs_3_
  36.0 4.3 %collective-permute-start.3 = (bf16[1024,256]{1,0:T(8,128)(2,1)S(1)}, bf16[1024,256]{1,0:T(8,128)(2,1)S(1)}, u32[]{:S(2)}, u32[]{:S(2)}) collective-permute-start(bf16[1024,256]{1,0:T(8,128)(2,1)S(1)} %pad_maximum_fusion.refs_2_), channel_id=1, source_target_pairs={{0,256},{4,260},{8,264},{12,268},{16,272},{20,276},{24,280},{28,28... | collective-permute-start | bytes 1572872 | tf_op jit(solution)/shard_map/ppermute | solution.py:18
  40.3 0.0 copy-done.1
  40.3 0.0 copy-done.2
  40.3 2.4 %early1.1 = (f32[1024,128]{1,0:T(8,128)S(1)}, f32[1024,128]{1,0:T(8,128)S(1)}, f32[1024,128]{1,0:T(8,128)S(1)}) custom-call(s32[256]{0:T(256)S(1)} %copy-done.2, bf16[512,256]{1,0:T(8,128)(2,1)S(1)} %copy-done.1, bf16[1024,256]{1,0:T(8,128)(2,1)S(1)} %pad_maximum_fusion.refs_2_, bf16[1024,256]{1,0:T(8,128)(2,1)S(1)} %collective-permute-done.refs_3_, ...), custom_call_target="tpu_custom_call" | custom-call | flops 4294967296 | bytes 1048576 | tf_op jit(solution)/shard_map/early1/pallas_call | solution.py:167
  42.7 0.0 copy-start.7
  42.7 0.8 copy-done.7
  43.5 0.0 copy-start.3
  43.5 0.0 copy-start.5
  43.5 0.0 copy-start
  43.5 2.4 %early0.1 = (f32[1024,128]{1,0:T(8,128)S(1)}, f32[1024,128]{1,0:T(8,128)S(1)}, f32[1024,128]{1,0:T(8,128)S(1)}) custom-call(s32[256]{0:T(256)S(1)} %copy-done.2, bf16[512,256]{1,0:T(8,128)(2,1)S(1)} %copy-done.1, bf16[1024,256]{1,0:T(8,128)(2,1)S(1)} %pad_maximum_fusion.refs_2_, bf16[1024,256]{1,0:T(8,128)(2,1)S(1)} %collective-permute-done.refs_3_, ...), custom_call_target="tpu_custom_call" | custom-call | flops 4294967296 | bytes 1048576 | tf_op jit(solution)/shard_map/early0/pallas_call | solution.py:167
  45.9 0.0 copy-done.3
  45.9 0.0 copy-done.5
  45.9 0.0 collective-permute-done.6.refs_6_
  46.0 5.2 %collective-permute-start.8 = (bf16[512,256]{1,0:T(8,128)(2,1)}, bf16[512,256]{1,0:T(8,128)(2,1)S(1)}, u32[]{:S(2)}, u32[]{:S(2)}) collective-permute-start(bf16[512,256]{1,0:T(8,128)(2,1)} %get-tuple-element.25), channel_id=1, source_target_pairs={{0,16},{4,20},{8,24},{12,28},{16,0},{20,4},{24,8},{28,12},{32,48},... | collective-permute-start | bytes 786440 | tf_op jit(solution)/shard_map/ppermute | solution.py:18
  51.1 0.0 collective-permute-done.7.refs_7_
  51.1 5.3 %collective-permute-start.9 = (bf16[512,256]{1,0:T(8,128)(2,1)}, bf16[512,256]{1,0:T(8,128)(2,1)S(1)}, u32[]{:S(2)}, u32[]{:S(2)}) collective-permute-start(bf16[512,256]{1,0:T(8,128)(2,1)} %get-tuple-element.25), channel_id=1, source_target_pairs={{0,32},{4,36},{8,40},{12,44},{16,48},{20,52},{24,56},{28,60},{32,0... | collective-permute-start | bytes 786440 | tf_op jit(solution)/shard_map/ppermute | solution.py:18
  56.4 0.0 collective-permute-done.4.refs_4_
  56.4 0.0 collective-permute-done.5.refs_5_
  56.5 0.0 collective-permute-done.3.refs_2_
  56.5 0.0 copy-done
  56.5 4.4 %late0.1 = bf16[4,256,256]{2,1,0:T(8,128)(2,1)} custom-call(s32[256]{0:T(256)S(1)} %copy-done.2, bf16[512,256]{1,0:T(8,128)(2,1)S(1)} %copy-done.1, bf16[1024,256]{1,0:T(8,128)(2,1)S(1)} %collective-permute-done.3.refs_2_, bf16[1024,256]{1,0:T(8,128)(2,1)S(1)} %collective-permute-done.2.refs_3_, bf16[1024,256]{1,0:T(8,128)(2,1)S(1)} %collective-permute-done.4.refs_4_, ...), custom_call_target="tpu_custom_call" | custom-call | flops 6442450944 | bytes 1572864 | tf_op jit(solution)/shard_map/late0/pallas_call | solution.py:167
  60.9 9.4 %all-to-all-start = ((bf16[4,256,256]{2,1,0:T(8,128)(2,1)}), bf16[4,256,256]{2,1,0:T(8,128)(2,1)}, u32[]{:S(2)}, u32[]{:S(2)}) async-start(bf16[4,256,256]{2,1,0:T(8,128)(2,1)} %late0.1), calls=%async_computation | async-start | bytes 1048576 | tf_op jit(solution)/shard_map/all_to_all | solution.py:247
  70.3 4.6 %collective-permute-done.8.refs_6_ = bf16[512,256]{1,0:T(8,128)(2,1)S(1)} collective-permute-done((bf16[512,256]{1,0:T(8,128)(2,1)}, bf16[512,256]{1,0:T(8,128)(2,1)S(1)}, u32[]{:S(2)}, u32[]{:S(2)}) %collective-permute-start.8) | collective-permute-done | bytes 262176 | tf_op jit(solution)/shard_map/ppermute | solution.py:18
  74.8 0.0 collective-permute-done.9.refs_7_
  74.8 1.0 copy-done.4
  75.9 1.0 copy-done.6
  76.9 1.0 copy-done.8
  78.0 4.4 %late1.1 = bf16[4,256,256]{2,1,0:T(8,128)(2,1)} custom-call(s32[256]{0:T(256)S(1)} %copy-done.2, bf16[512,256]{1,0:T(8,128)(2,1)S(1)} %copy-done.1, bf16[1024,256]{1,0:T(8,128)(2,1)S(1)} %collective-permute-done.3.refs_2_, bf16[1024,256]{1,0:T(8,128)(2,1)S(1)} %collective-permute-done.2.refs_3_, bf16[1024,256]{1,0:T(8,128)(2,1)S(1)} %collective-permute-done.4.refs_4_, ...), custom_call_target="tpu_custom_call" | custom-call | flops 6442450944 | bytes 1572864 | tf_op jit(solution)/shard_map/late1/pallas_call | solution.py:167
  82.3 4.5 %all-to-all-done = bf16[4,256,256]{2,1,0:T(8,128)(2,1)} async-done(((bf16[4,256,256]{2,1,0:T(8,128)(2,1)}), bf16[4,256,256]{2,1,0:T(8,128)(2,1)}, u32[]{:S(2)}, u32[]{:S(2)}) %all-to-all-start) | async-done | bytes 524320 | tf_op jit(solution)/shard_map/all_to_all | solution.py:247
  86.9 4.9 %all-to-all-start.1 = ((bf16[4,256,256]{2,1,0:T(8,128)(2,1)}), bf16[4,256,256]{2,1,0:T(8,128)(2,1)S(1)}, u32[]{:S(2)}, u32[]{:S(2)}) async-start(bf16[4,256,256]{2,1,0:T(8,128)(2,1)} %late1.1), calls=%async_computation.1 | async-start | bytes 1048576 | tf_op jit(solution)/shard_map/all_to_all | solution.py:265
  91.7 1.1 %reduce_sum.24 = bf16[256,256]{1,0:T(8,128)(2,1)S(1)} reduce(bf16[4,256,256]{2,1,0:T(8,128)(2,1)} %all-to-all-done, bf16[]{:T(256)} %constant.15.clone.1), dimensions={0}, to_apply=%region_0.1 | reduce | flops 196608 | bytes 655362 | tf_op jit(solution)/shard_map/reduce_sum | solution.py:266
  92.9 16.4 %all-to-all-done.1 = bf16[4,256,256]{2,1,0:T(8,128)(2,1)S(1)} async-done(((bf16[4,256,256]{2,1,0:T(8,128)(2,1)}), bf16[4,256,256]{2,1,0:T(8,128)(2,1)S(1)}, u32[]{:S(2)}, u32[]{:S(2)}) %all-to-all-start.1) | async-done | bytes 524320 | tf_op jit(solution)/shard_map/all_to_all | solution.py:265
  109.2 0.1 reduce_sum.25
  109.3 0.7 pad_maximum_fusion.3
  (4 shorter events, 0.0 us)
Async XLA Ops:
  1.9 38.4 %copy-start.1 = (bf16[512,256]{1,0:T(8,128)(2,1)S(1)}, bf16[512,256]{1,0:T(8,128)(2,1)}, u32[]{:S(2)}) copy-start(bf16[512,256]{1,0:T(8,128)(2,1)} %refs_1_.5) | copy-start | bytes 786436
  1.9 7.8 %collective-permute-start.1 = (bf16[512,256]{1,0:T(8,128)(2,1)S(1)}, bf16[512,256]{1,0:T(8,128)(2,1)S(1)}, u32[]{:S(2)}, u32[]{:S(2)}) collective-permute-start(bf16[512,256]{1,0:T(8,128)(2,1)S(1)} %get-tuple-element.30), channel_id=1, source_target_pairs={{4,8},{8,4},{12,16},{16,12},{20,24},{24,20},{28,32},{32,28},{36,40... | collective-permute-start | bytes 786440 | tf_op jit(solution)/shard_map/ppermute | solution.py:28
  4.8 35.5 %copy-start.2 = (s32[256]{0:T(256)S(1)}, s32[256]{0:T(256)}, u32[]{:S(2)}) copy-start(s32[256]{0:T(256)} %refs_0_.7) | copy-start | bytes 3076
  9.7 21.3 %collective-permute-start.2 = (bf16[1024,256]{1,0:T(8,128)(2,1)S(1)}, bf16[1024,256]{1,0:T(8,128)(2,1)S(1)}, u32[]{:S(2)}, u32[]{:S(2)}) collective-permute-start(bf16[1024,256]{1,0:T(8,128)(2,1)S(1)} %pad_maximum_fusion.refs_2_), channel_id=1, source_target_pairs={{0,8},{4,12},{8,0},{12,4},{16,24},{20,28},{24,16},{28,20},{32,40},... | collective-permute-start | bytes 1572872 | tf_op jit(solution)/shard_map/ppermute | solution.py:18
  13.0 23.0 %collective-permute-start = (bf16[1024,256]{1,0:T(8,128)(2,1)S(1)}, bf16[1024,256]{1,0:T(8,128)(2,1)S(1)}, u32[]{:S(2)}, u32[]{:S(2)}) collective-permute-start(bf16[1024,256]{1,0:T(8,128)(2,1)S(1)} %pad_maximum_fusion.refs_2_), channel_id=1, source_target_pairs={{0,4},{4,0},{8,12},{12,8},{16,20},{20,16},{24,28},{28,24},{32,36},... | collective-permute-start | bytes 1572872 | tf_op jit(solution)/shard_map/ppermute | solution.py:18
  15.5 30.4 %collective-permute-start.6 = (bf16[512,256]{1,0:T(8,128)(2,1)S(1)}, bf16[512,256]{1,0:T(8,128)(2,1)S(1)}, u32[]{:S(2)}, u32[]{:S(2)}) collective-permute-start(bf16[512,256]{1,0:T(8,128)(2,1)S(1)} %get-tuple-element.31), channel_id=1, source_target_pairs={{0,16},{4,20},{8,24},{12,28},{16,0},{20,4},{24,8},{28,12},{32,48},... | collective-permute-start | bytes 786440 | tf_op jit(solution)/shard_map/ppermute | solution.py:18
  20.2 30.9 %collective-permute-start.7 = (bf16[512,256]{1,0:T(8,128)(2,1)S(1)}, bf16[512,256]{1,0:T(8,128)(2,1)S(1)}, u32[]{:S(2)}, u32[]{:S(2)}) collective-permute-start(bf16[512,256]{1,0:T(8,128)(2,1)S(1)} %get-tuple-element.31), channel_id=1, source_target_pairs={{0,32},{4,36},{8,40},{12,44},{16,48},{20,52},{24,56},{28,60},{32,0... | collective-permute-start | bytes 786440 | tf_op jit(solution)/shard_map/ppermute | solution.py:18
  22.1 34.3 %collective-permute-start.4 = (bf16[1024,256]{1,0:T(8,128)(2,1)S(1)}, bf16[1024,256]{1,0:T(8,128)(2,1)S(1)}, u32[]{:S(2)}, u32[]{:S(2)}) collective-permute-start(bf16[1024,256]{1,0:T(8,128)(2,1)S(1)} %pad_maximum_fusion.refs_2_), channel_id=1, source_target_pairs={{0,64},{4,68},{8,72},{12,76},{16,80},{20,84},{24,88},{28,92},{32,9... | collective-permute-start | bytes 1572872 | tf_op jit(solution)/shard_map/ppermute | solution.py:18
  31.1 25.4 %collective-permute-start.5 = (bf16[1024,256]{1,0:T(8,128)(2,1)S(1)}, bf16[1024,256]{1,0:T(8,128)(2,1)S(1)}, u32[]{:S(2)}, u32[]{:S(2)}) collective-permute-start(bf16[1024,256]{1,0:T(8,128)(2,1)S(1)} %pad_maximum_fusion.refs_2_), channel_id=1, source_target_pairs={{0,128},{4,132},{8,136},{12,140},{16,144},{20,148},{24,152},{28,15... | collective-permute-start | bytes 1572872 | tf_op jit(solution)/shard_map/ppermute | solution.py:18
  36.0 20.4 %collective-permute-start.3 = (bf16[1024,256]{1,0:T(8,128)(2,1)S(1)}, bf16[1024,256]{1,0:T(8,128)(2,1)S(1)}, u32[]{:S(2)}, u32[]{:S(2)}) collective-permute-start(bf16[1024,256]{1,0:T(8,128)(2,1)S(1)} %pad_maximum_fusion.refs_2_), channel_id=1, source_target_pairs={{0,256},{4,260},{8,264},{12,268},{16,272},{20,276},{24,280},{28,28... | collective-permute-start | bytes 1572872 | tf_op jit(solution)/shard_map/ppermute | solution.py:18
  42.7 0.8 copy-start.7
  43.5 2.4 %copy-start.3 = (f32[1024,128]{1,0:T(8,128)}, f32[1024,128]{1,0:T(8,128)S(1)}, u32[]{:S(2)}) copy-start(f32[1024,128]{1,0:T(8,128)S(1)} %get-tuple-element.17.refs_8_) | copy-start | bytes 1572868
  43.5 2.4 %copy-start.5 = (f32[1024,128]{1,0:T(8,128)}, f32[1024,128]{1,0:T(8,128)S(1)}, u32[]{:S(2)}) copy-start(f32[1024,128]{1,0:T(8,128)S(1)} %get-tuple-element.26.refs_9_) | copy-start | bytes 1572868
  43.5 12.9 %copy-start = (bf16[256,1024]{1,0:T(8,128)(2,1)S(1)}, bf16[256,1024]{1,0:T(8,128)(2,1)}, u32[]{:S(2)}) copy-start(bf16[256,1024]{1,0:T(8,128)(2,1)} %refs_11_.3) | copy-start | bytes 1572868
  46.0 28.9 %collective-permute-start.8 = (bf16[512,256]{1,0:T(8,128)(2,1)}, bf16[512,256]{1,0:T(8,128)(2,1)S(1)}, u32[]{:S(2)}, u32[]{:S(2)}) collective-permute-start(bf16[512,256]{1,0:T(8,128)(2,1)} %get-tuple-element.25), channel_id=1, source_target_pairs={{0,16},{4,20},{8,24},{12,28},{16,0},{20,4},{24,8},{28,12},{32,48},... | collective-permute-start | bytes 786440 | tf_op jit(solution)/shard_map/ppermute | solution.py:18
  51.1 23.7 %collective-permute-start.9 = (bf16[512,256]{1,0:T(8,128)(2,1)}, bf16[512,256]{1,0:T(8,128)(2,1)S(1)}, u32[]{:S(2)}, u32[]{:S(2)}) collective-permute-start(bf16[512,256]{1,0:T(8,128)(2,1)} %get-tuple-element.25), channel_id=1, source_target_pairs={{0,32},{4,36},{8,40},{12,44},{16,48},{20,52},{24,56},{28,60},{32,0... | collective-permute-start | bytes 786440 | tf_op jit(solution)/shard_map/ppermute | solution.py:18
  60.9 26.0 %all-to-all-start = ((bf16[4,256,256]{2,1,0:T(8,128)(2,1)}), bf16[4,256,256]{2,1,0:T(8,128)(2,1)}, u32[]{:S(2)}, u32[]{:S(2)}) async-start(bf16[4,256,256]{2,1,0:T(8,128)(2,1)} %late0.1), calls=%async_computation | async-start | bytes 1048576 | tf_op jit(solution)/shard_map/all_to_all | solution.py:247
  74.8 1.0 copy-start.4
  75.9 1.0 copy-start.6
  76.9 1.0 copy-start.8
  86.9 22.4 %all-to-all-start.1 = ((bf16[4,256,256]{2,1,0:T(8,128)(2,1)}), bf16[4,256,256]{2,1,0:T(8,128)(2,1)S(1)}, u32[]{:S(2)}, u32[]{:S(2)}) async-start(bf16[4,256,256]{2,1,0:T(8,128)(2,1)} %late1.1), calls=%async_computation.1 | async-start | bytes 1048576 | tf_op jit(solution)/shard_map/all_to_all | solution.py:265

commit v13 on v9

--- a/solution.py
+++ b/solution.py
@@ -196,7 +196,7 @@
     y2a = flat_exchange(parts[0], "seq", 1 << 2)
     y1 = flat_exchange(packed, "seq", 1 << 1)
     x1 = flat_exchange(after(packed, core), "seq", 1 << 4)
-    x2 = flat_exchange(after(packed, halo), "seq", 1 << 5)
+    x2 = flat_exchange(after(packed, core), "seq", 1 << 5)
     z1 = flat_exchange(after(packed, y1), "seq", 1 << 6)
     y2b = flat_exchange(after(parts[1], x1), "seq", 1 << 2)
     y4b = flat_exchange(after(parts[1], x1), "seq", 1 << 3)

time: 109 us -> 102 us (0.936)
  the two profiles are of different devices: /device:TPU:56 before, /device:TPU:64 now
where the time goes in v13:
time: 102 us
  starting transfers between devices  58.8 us (58%)
  waiting for transfers between devices  27.6 us (27%)
  Pallas kernels  12.9 us (13%)
  local copies, waits for them, and re-layouts  1.15 us (1%)
    ppermute x9, starting transfers between devices, flat_exchange(): return lax.ppermute(value, axis, pairs)  32.3 us
    ppermute x3, starting transfers between devices, per_device(): lax.ppermute(piece, 'head', [(h, (h + hop + 1) % groups) for h in range(g...  16.8 us
    all_to_all x1, waiting for transfers between devices, per_device(): spread = lax.all_to_all(after(shares, *moved), 'head', 0, 0, tiled=False)  16.6 us
    pallas_call x4, Pallas kernels, attend(): pl.pallas_call(lambda *refs: attend_kernel(scale, heads, local, plan, sta...  12.9 us
    ppermute x3, waiting for transfers between devices, per_device(): lax.ppermute(piece, 'head', [(h, (h + hop + 1) % groups) for h in range(g...  7.62 us
    ppermute x1, starting transfers between devices, halo_exchange(): return lax.ppermute(value, axis, pairs)  6.26 us
    all_to_all x1, starting transfers between devices, per_device(): spread = lax.all_to_all(after(shares, *moved), 'head', 0, 0, tiled=False)  3.47 us
    ppermute x9, waiting for transfers between devices, flat_exchange(): return lax.ppermute(value, axis, pairs)  3.44 us
  transfers between devices with their start and end apart: 14, of which 4 were waited for; matrix products, arithmetic and copies ran while one was open for 0% of the time, Pallas kernels for 13%

profile of v13, /device:TPU:64, one launch (start us, length us, event | category | flops | bytes accessed | tf_op | source)
XLA Modules:
  0.0 101.7 jit_solution(2417332402474516635)
XLA Ops:
  0.0 1.1 %fusion = (bf16[256,256]{1,0:T(8,128)(2,1)S(1)}, bf16[256,256]{1,0:T(8,128)(2,1)S(1)}, bf16[256,256]{1,0:T(8,128)(2,1)S(1)}, bf16[256,256]{1,0:T(8,128)(2,1)S(1)}) fusion(bf16[512,256]{1,0:T(8,128)(2,1)} %param.6, bf16[512,256]{1,0:T(8,128)(2,1)} %param.7), kind=kLoop, calls=%fused_computation.6 | loop fusion | bytes 1048576 | tf_op jit(solution)/shard_map/slice | solution.py:188
  1.2 1.9 %collective-permute-start = (bf16[1024,256]{1,0:T(8,128)(2,1)S(1)}, bf16[1024,256]{1,0:T(8,128)(2,1)S(1)}, u32[]{:S(2)}, u32[]{:S(2)}) collective-permute-start(bf16[1024,256]{1,0:T(8,128)(2,1)S(1)} %pad_maximum_fusion.refs_2_), channel_id=1, source_target_pairs={{0,4},{4,0},{8,12},{12,8},{16,20},{20,16},{24,28},{28,24},{32,36},... | collective-permute-start | bytes 1572872 | tf_op jit(solution)/shard_map/ppermute | solution.py:18
  3.1 3.5 %collective-permute-start.2 = (bf16[1024,256]{1,0:T(8,128)(2,1)S(1)}, bf16[1024,256]{1,0:T(8,128)(2,1)S(1)}, u32[]{:S(2)}, u32[]{:S(2)}) collective-permute-start(bf16[1024,256]{1,0:T(8,128)(2,1)S(1)} %pad_maximum_fusion.refs_2_), channel_id=1, source_target_pairs={{0,8},{4,12},{8,0},{12,4},{16,24},{20,28},{24,16},{28,20},{32,40},... | collective-permute-start | bytes 1572872 | tf_op jit(solution)/shard_map/ppermute | solution.py:18
  6.6 0.0 copy-start.1
  6.6 0.1 pad_maximum_fusion.1
  6.7 0.0 copy-start.2
  6.7 6.3 %collective-permute-start.1 = (bf16[512,256]{1,0:T(8,128)(2,1)S(1)}, bf16[512,256]{1,0:T(8,128)(2,1)S(1)}, u32[]{:S(2)}, u32[]{:S(2)}) collective-permute-start(bf16[512,256]{1,0:T(8,128)(2,1)S(1)} %get-tuple-element.38), channel_id=1, source_target_pairs={{4,8},{8,4},{12,16},{16,12},{20,24},{24,20},{28,32},{32,28},{36,40... | collective-permute-start | bytes 786440 | tf_op jit(solution)/shard_map/ppermute | solution.py:28
  13.0 1.9 %collective-permute-start.6 = (bf16[512,256]{1,0:T(8,128)(2,1)S(1)}, bf16[512,256]{1,0:T(8,128)(2,1)S(1)}, u32[]{:S(2)}, u32[]{:S(2)}) collective-permute-start(bf16[512,256]{1,0:T(8,128)(2,1)S(1)} %get-tuple-element.39), channel_id=1, source_target_pairs={{0,16},{4,20},{8,24},{12,28},{16,0},{20,4},{24,8},{28,12},{32,48},... | collective-permute-start | bytes 786440 | tf_op jit(solution)/shard_map/ppermute | solution.py:18
  14.9 5.1 %collective-permute-start.7 = (bf16[512,256]{1,0:T(8,128)(2,1)S(1)}, bf16[512,256]{1,0:T(8,128)(2,1)S(1)}, u32[]{:S(2)}, u32[]{:S(2)}) collective-permute-start(bf16[512,256]{1,0:T(8,128)(2,1)S(1)} %get-tuple-element.39), channel_id=1, source_target_pairs={{0,32},{4,36},{8,40},{12,44},{16,48},{20,52},{24,56},{28,60},{32,0... | collective-permute-start | bytes 786440 | tf_op jit(solution)/shard_map/ppermute | solution.py:18
  20.0 0.0 collective-permute-done.refs_3_
  20.0 3.4 %collective-permute-start.4 = (bf16[1024,256]{1,0:T(8,128)(2,1)S(1)}, bf16[1024,256]{1,0:T(8,128)(2,1)S(1)}, u32[]{:S(2)}, u32[]{:S(2)}) collective-permute-start(bf16[1024,256]{1,0:T(8,128)(2,1)S(1)} %pad_maximum_fusion.refs_2_), channel_id=1, source_target_pairs={{0,64},{4,68},{8,72},{12,76},{16,80},{20,84},{24,88},{28,92},{32,9... | collective-permute-start | bytes 1572872 | tf_op jit(solution)/shard_map/ppermute | solution.py:18
  23.5 1.9 %collective-permute-done.2.refs_3_ = bf16[1024,256]{1,0:T(8,128)(2,1)S(1)} collective-permute-done((bf16[1024,256]{1,0:T(8,128)(2,1)S(1)}, bf16[1024,256]{1,0:T(8,128)(2,1)S(1)}, u32[]{:S(2)}, u32[]{:S(2)}) %collective-permute-start.2) | collective-permute-done | bytes 524320 | tf_op jit(solution)/shard_map/ppermute | solution.py:18
  25.3 4.9 %collective-permute-start.5 = (bf16[1024,256]{1,0:T(8,128)(2,1)S(1)}, bf16[1024,256]{1,0:T(8,128)(2,1)S(1)}, u32[]{:S(2)}, u32[]{:S(2)}) collective-permute-start(bf16[1024,256]{1,0:T(8,128)(2,1)S(1)} %pad_maximum_fusion.refs_2_), channel_id=1, source_target_pairs={{0,128},{4,132},{8,136},{12,140},{16,144},{20,148},{24,152},{28,15... | collective-permute-start | bytes 1572872 | tf_op jit(solution)/shard_map/ppermute | solution.py:18
  30.3 0.0 collective-permute-done.1.refs_4_
  30.3 4.6 %collective-permute-start.3 = (bf16[1024,256]{1,0:T(8,128)(2,1)S(1)}, bf16[1024,256]{1,0:T(8,128)(2,1)S(1)}, u32[]{:S(2)}, u32[]{:S(2)}) collective-permute-start(bf16[1024,256]{1,0:T(8,128)(2,1)S(1)} %pad_maximum_fusion.refs_2_), channel_id=1, source_target_pairs={{0,256},{4,260},{8,264},{12,268},{16,272},{20,276},{24,280},{28,28... | collective-permute-start | bytes 1572872 | tf_op jit(solution)/shard_map/ppermute | solution.py:18
  34.9 0.0 copy-done.1
  34.9 0.0 copy-done.2
  34.9 2.4 %early1.1 = (f32[1024,128]{1,0:T(8,128)S(1)}, f32[1024,128]{1,0:T(8,128)S(1)}, f32[1024,128]{1,0:T(8,128)S(1)}) custom-call(s32[256]{0:T(256)S(1)} %copy-done.2, bf16[512,256]{1,0:T(8,128)(2,1)S(1)} %copy-done.1, bf16[1024,256]{1,0:T(8,128)(2,1)S(1)} %pad_maximum_fusion.refs_2_, bf16[1024,256]{1,0:T(8,128)(2,1)S(1)} %collective-permute-done.refs_3_, ...), custom_call_target="tpu_custom_call" | custom-call | flops 4294967296 | bytes 1048576 | tf_op jit(solution)/shard_map/early1/pallas_call | solution.py:167
  37.3 0.0 copy-start
  37.3 2.4 %early0.1 = (f32[1024,128]{1,0:T(8,128)S(1)}, f32[1024,128]{1,0:T(8,128)S(1)}, f32[1024,128]{1,0:T(8,128)S(1)}) custom-call(s32[256]{0:T(256)S(1)} %copy-done.2, bf16[512,256]{1,0:T(8,128)(2,1)S(1)} %copy-done.1, bf16[1024,256]{1,0:T(8,128)(2,1)S(1)} %pad_maximum_fusion.refs_2_, bf16[1024,256]{1,0:T(8,128)(2,1)S(1)} %collective-permute-done.refs_3_, ...), custom_call_target="tpu_custom_call" | custom-call | flops 4294967296 | bytes 1048576 | tf_op jit(solution)/shard_map/early0/pallas_call | solution.py:167
  39.7 0.0 collective-permute-done.4.refs_4_
  39.7 1.9 %collective-permute-start.11 = (bf16[512,256]{1,0:T(8,128)(2,1)S(1)}, bf16[512,256]{1,0:T(8,128)(2,1)S(1)}, u32[]{:S(2)}, u32[]{:S(2)}) collective-permute-start(bf16[512,256]{1,0:T(8,128)(2,1)S(1)} %get-tuple-element.33), channel_id=1, source_target_pairs={{0,16},{4,20},{8,24},{12,28},{16,0},{20,4},{24,8},{28,12},{32,48},... | collective-permute-start | bytes 786440 | tf_op jit(solution)/shard_map/ppermute | solution.py:18
  41.7 0.0 collective-permute-done.6.refs_6_
  41.7 5.0 %collective-permute-start.12 = (bf16[512,256]{1,0:T(8,128)(2,1)S(1)}, bf16[512,256]{1,0:T(8,128)(2,1)S(1)}, u32[]{:S(2)}, u32[]{:S(2)}) collective-permute-start(bf16[512,256]{1,0:T(8,128)(2,1)S(1)} %get-tuple-element.33), channel_id=1, source_target_pairs={{0,32},{4,36},{8,40},{12,44},{16,48},{20,52},{24,56},{28,60},{32,0... | collective-permute-start | bytes 786440 | tf_op jit(solution)/shard_map/ppermute | solution.py:18
  46.7 0.0 collective-permute-done.7.refs_7_
  46.7 1.5 %collective-permute-done.5.refs_5_ = bf16[1024,256]{1,0:T(8,128)(2,1)S(1)} collective-permute-done((bf16[1024,256]{1,0:T(8,128)(2,1)S(1)}, bf16[1024,256]{1,0:T(8,128)(2,1)S(1)}, u32[]{:S(2)}, u32[]{:S(2)}) %collective-permute-start.5) | collective-permute-done | bytes 524320 | tf_op jit(solution)/shard_map/ppermute | solution.py:18
  48.3 0.0 collective-permute-done.3.refs_2_
  48.3 0.0 copy-done
  48.3 3.6 %late0.1 = (bf16[256,256]{1,0:T(8,128)(2,1)S(1)}, bf16[256,256]{1,0:T(8,128)(2,1)S(1)}, bf16[256,256]{1,0:T(8,128)(2,1)S(1)}, bf16[256,256]{1,0:T(8,128)(2,1)S(1)}) custom-call(s32[256]{0:T(256)S(1)} %copy-done.2, bf16[512,256]{1,0:T(8,128)(2,1)S(1)} %copy-done.1, bf16[1024,256]{1,0:T(8,128)(2,1)S(1)} %collective-permute-done.3.refs_2_, ...), custom_call_target="tpu_custom_call" | custom-call | flops 6442450944 | bytes 1572864 | tf_op jit(solution)/shard_map/late0/pallas_call | solution.py:167
  51.9 10.0 %collective-permute-start.10 = (bf16[256,256]{1,0:T(8,128)(2,1)S(1)}, bf16[256,256]{1,0:T(8,128)(2,1)S(1)}, u32[]{:S(2)}, u32[]{:S(2)}) collective-permute-start(bf16[256,256]{1,0:T(8,128)(2,1)S(1)} %get-tuple-element.31), channel_id=1, source_target_pairs={{0,3},{1,0},{2,1},{3,2},{4,7},{5,4},{6,5},{7,6},{8,11},{9,8},{10,9... | collective-permute-start | bytes 393224 | tf_op jit(solution)/shard_map/ppermute | solution.py:250
  62.0 1.9 %collective-permute-start.8 = (bf16[256,256]{1,0:T(8,128)(2,1)S(1)}, bf16[256,256]{1,0:T(8,128)(2,1)S(1)}, u32[]{:S(2)}, u32[]{:S(2)}) collective-permute-start(bf16[256,256]{1,0:T(8,128)(2,1)S(1)} %get-tuple-element.29), channel_id=1, source_target_pairs={{0,1},{1,2},{2,3},{3,0},{4,5},{5,6},{6,7},{7,4},{8,9},{9,10},{10,1... | collective-permute-start | bytes 393224 | tf_op jit(solution)/shard_map/ppermute | solution.py:250
  63.9 4.8 %collective-permute-start.9 = (bf16[256,256]{1,0:T(8,128)(2,1)S(1)}, bf16[256,256]{1,0:T(8,128)(2,1)S(1)}, u32[]{:S(2)}, u32[]{:S(2)}) collective-permute-start(bf16[256,256]{1,0:T(8,128)(2,1)S(1)} %get-tuple-element.30), channel_id=1, source_target_pairs={{0,2},{1,3},{2,0},{3,1},{4,6},{5,7},{6,4},{7,5},{8,10},{9,11},{10,... | collective-permute-start | bytes 393224 | tf_op jit(solution)/shard_map/ppermute | solution.py:250
  68.7 0.0 collective-permute-done.11.refs_6_
  68.7 0.0 collective-permute-done.12.refs_7_
  68.7 4.4 %late1.1 = bf16[4,256,256]{2,1,0:T(8,128)(2,1)} custom-call(s32[256]{0:T(256)S(1)} %copy-done.2, bf16[512,256]{1,0:T(8,128)(2,1)S(1)} %copy-done.1, bf16[1024,256]{1,0:T(8,128)(2,1)S(1)} %collective-permute-done.3.refs_2_, bf16[1024,256]{1,0:T(8,128)(2,1)S(1)} %collective-permute-done.2.refs_3_, bf16[1024,256]{1,0:T(8,128)(2,1)S(1)} %collective-permute-done.4.refs_4_, ...), custom_call_target="tpu_custom_call" | custom-call | flops 6442450944 | bytes 1572864 | tf_op jit(solution)/shard_map/late1/pallas_call | solution.py:167
  73.2 0.0 collective-permute-done.10
  73.2 7.6 %collective-permute-done.8 = bf16[256,256]{1,0:T(8,128)(2,1)S(1)} collective-permute-done((bf16[256,256]{1,0:T(8,128)(2,1)S(1)}, bf16[256,256]{1,0:T(8,128)(2,1)S(1)}, u32[]{:S(2)}, u32[]{:S(2)}) %collective-permute-start.8) | collective-permute-done | bytes 131104 | tf_op jit(solution)/shard_map/ppermute | solution.py:250
  80.8 0.0 collective-permute-done.9
  80.8 3.5 %all-to-all-start = ((bf16[4,256,256]{2,1,0:T(8,128)(2,1)}), bf16[4,256,256]{2,1,0:T(8,128)(2,1)S(1)}, u32[]{:S(2)}, u32[]{:S(2)}) async-start(bf16[4,256,256]{2,1,0:T(8,128)(2,1)} %late1.1), calls=%async_computation | async-start | bytes 1048576 | tf_op jit(solution)/shard_map/all_to_all | solution.py:270
  84.3 0.1 add_convert_fusion
  84.3 16.6 %all-to-all-done = bf16[4,256,256]{2,1,0:T(8,128)(2,1)S(1)} async-done(((bf16[4,256,256]{2,1,0:T(8,128)(2,1)}), bf16[4,256,256]{2,1,0:T(8,128)(2,1)S(1)}, u32[]{:S(2)}, u32[]{:S(2)}) %all-to-all-start) | async-done | bytes 524320 | tf_op jit(solution)/shard_map/all_to_all | solution.py:270
  100.9 0.1 reduce_sum.12
  101.0 0.7 pad_maximum_fusion.3
  (1 shorter events, 0.0 us)
Async XLA Ops:
  1.2 18.9 %collective-permute-start = (bf16[1024,256]{1,0:T(8,128)(2,1)S(1)}, bf16[1024,256]{1,0:T(8,128)(2,1)S(1)}, u32[]{:S(2)}, u32[]{:S(2)}) collective-permute-start(bf16[1024,256]{1,0:T(8,128)(2,1)S(1)} %pad_maximum_fusion.refs_2_), channel_id=1, source_target_pairs={{0,4},{4,0},{8,12},{12,8},{16,20},{20,16},{24,28},{28,24},{32,36},... | collective-permute-start | bytes 1572872 | tf_op jit(solution)/shard_map/ppermute | solution.py:18
  3.1 22.2 %collective-permute-start.2 = (bf16[1024,256]{1,0:T(8,128)(2,1)S(1)}, bf16[1024,256]{1,0:T(8,128)(2,1)S(1)}, u32[]{:S(2)}, u32[]{:S(2)}) collective-permute-start(bf16[1024,256]{1,0:T(8,128)(2,1)S(1)} %pad_maximum_fusion.refs_2_), channel_id=1, source_target_pairs={{0,8},{4,12},{8,0},{12,4},{16,24},{20,28},{24,16},{28,20},{32,40},... | collective-permute-start | bytes 1572872 | tf_op jit(solution)/shard_map/ppermute | solution.py:18
  6.6 28.3 %copy-start.1 = (bf16[512,256]{1,0:T(8,128)(2,1)S(1)}, bf16[512,256]{1,0:T(8,128)(2,1)}, u32[]{:S(2)}) copy-start(bf16[512,256]{1,0:T(8,128)(2,1)} %refs_1_.5) | copy-start | bytes 786436
  6.7 28.2 %copy-start.2 = (s32[256]{0:T(256)S(1)}, s32[256]{0:T(256)}, u32[]{:S(2)}) copy-start(s32[256]{0:T(256)} %refs_0_.7) | copy-start | bytes 3076
  6.7 23.5 %collective-permute-start.1 = (bf16[512,256]{1,0:T(8,128)(2,1)S(1)}, bf16[512,256]{1,0:T(8,128)(2,1)S(1)}, u32[]{:S(2)}, u32[]{:S(2)}) collective-permute-start(bf16[512,256]{1,0:T(8,128)(2,1)S(1)} %get-tuple-element.38), channel_id=1, source_target_pairs={{4,8},{8,4},{12,16},{16,12},{20,24},{24,20},{28,32},{32,28},{36,40... | collective-permute-start | bytes 786440 | tf_op jit(solution)/shard_map/ppermute | solution.py:28
  13.0 28.7 %collective-permute-start.6 = (bf16[512,256]{1,0:T(8,128)(2,1)S(1)}, bf16[512,256]{1,0:T(8,128)(2,1)S(1)}, u32[]{:S(2)}, u32[]{:S(2)}) collective-permute-start(bf16[512,256]{1,0:T(8,128)(2,1)S(1)} %get-tuple-element.39), channel_id=1, source_target_pairs={{0,16},{4,20},{8,24},{12,28},{16,0},{20,4},{24,8},{28,12},{32,48},... | collective-permute-start | bytes 786440 | tf_op jit(solution)/shard_map/ppermute | solution.py:18
  14.9 31.8 %collective-permute-start.7 = (bf16[512,256]{1,0:T(8,128)(2,1)S(1)}, bf16[512,256]{1,0:T(8,128)(2,1)S(1)}, u32[]{:S(2)}, u32[]{:S(2)}) collective-permute-start(bf16[512,256]{1,0:T(8,128)(2,1)S(1)} %get-tuple-element.39), channel_id=1, source_target_pairs={{0,32},{4,36},{8,40},{12,44},{16,48},{20,52},{24,56},{28,60},{32,0... | collective-permute-start | bytes 786440 | tf_op jit(solution)/shard_map/ppermute | solution.py:18
  20.0 19.7 %collective-permute-start.4 = (bf16[1024,256]{1,0:T(8,128)(2,1)S(1)}, bf16[1024,256]{1,0:T(8,128)(2,1)S(1)}, u32[]{:S(2)}, u32[]{:S(2)}) collective-permute-start(bf16[1024,256]{1,0:T(8,128)(2,1)S(1)} %pad_maximum_fusion.refs_2_), channel_id=1, source_target_pairs={{0,64},{4,68},{8,72},{12,76},{16,80},{20,84},{24,88},{28,92},{32,9... | collective-permute-start | bytes 1572872 | tf_op jit(solution)/shard_map/ppermute | solution.py:18
  25.3 22.9 %collective-permute-start.5 = (bf16[1024,256]{1,0:T(8,128)(2,1)S(1)}, bf16[1024,256]{1,0:T(8,128)(2,1)S(1)}, u32[]{:S(2)}, u32[]{:S(2)}) collective-permute-start(bf16[1024,256]{1,0:T(8,128)(2,1)S(1)} %pad_maximum_fusion.refs_2_), channel_id=1, source_target_pairs={{0,128},{4,132},{8,136},{12,140},{16,144},{20,148},{24,152},{28,15... | collective-permute-start | bytes 1572872 | tf_op jit(solution)/shard_map/ppermute | solution.py:18
  30.3 18.0 %collective-permute-start.3 = (bf16[1024,256]{1,0:T(8,128)(2,1)S(1)}, bf16[1024,256]{1,0:T(8,128)(2,1)S(1)}, u32[]{:S(2)}, u32[]{:S(2)}) collective-permute-start(bf16[1024,256]{1,0:T(8,128)(2,1)S(1)} %pad_maximum_fusion.refs_2_), channel_id=1, source_target_pairs={{0,256},{4,260},{8,264},{12,268},{16,272},{20,276},{24,280},{28,28... | collective-permute-start | bytes 1572872 | tf_op jit(solution)/shard_map/ppermute | solution.py:18
  37.3 10.9 %copy-start = (bf16[256,1024]{1,0:T(8,128)(2,1)S(1)}, bf16[256,1024]{1,0:T(8,128)(2,1)}, u32[]{:S(2)}) copy-start(bf16[256,1024]{1,0:T(8,128)(2,1)} %refs_11_.3) | copy-start | bytes 1572868
  39.7 29.0 %collective-permute-start.11 = (bf16[512,256]{1,0:T(8,128)(2,1)S(1)}, bf16[512,256]{1,0:T(8,128)(2,1)S(1)}, u32[]{:S(2)}, u32[]{:S(2)}) collective-permute-start(bf16[512,256]{1,0:T(8,128)(2,1)S(1)} %get-tuple-element.33), channel_id=1, source_target_pairs={{0,16},{4,20},{8,24},{12,28},{16,0},{20,4},{24,8},{28,12},{32,48},... | collective-permute-start | bytes 786440 | tf_op jit(solution)/shard_map/ppermute | solution.py:18
  41.7 27.0 %collective-permute-start.12 = (bf16[512,256]{1,0:T(8,128)(2,1)S(1)}, bf16[512,256]{1,0:T(8,128)(2,1)S(1)}, u32[]{:S(2)}, u32[]{:S(2)}) collective-permute-start(bf16[512,256]{1,0:T(8,128)(2,1)S(1)} %get-tuple-element.33), channel_id=1, source_target_pairs={{0,32},{4,36},{8,40},{12,44},{16,48},{20,52},{24,56},{28,60},{32,0... | collective-permute-start | bytes 786440 | tf_op jit(solution)/shard_map/ppermute | solution.py:18
  51.9 21.2 %collective-permute-start.10 = (bf16[256,256]{1,0:T(8,128)(2,1)S(1)}, bf16[256,256]{1,0:T(8,128)(2,1)S(1)}, u32[]{:S(2)}, u32[]{:S(2)}) collective-permute-start(bf16[256,256]{1,0:T(8,128)(2,1)S(1)} %get-tuple-element.31), channel_id=1, source_target_pairs={{0,3},{1,0},{2,1},{3,2},{4,7},{5,4},{6,5},{7,6},{8,11},{9,8},{10,9... | collective-permute-start | bytes 393224 | tf_op jit(solution)/shard_map/ppermute | solution.py:250
  62.0 18.8 %collective-permute-start.8 = (bf16[256,256]{1,0:T(8,128)(2,1)S(1)}, bf16[256,256]{1,0:T(8,128)(2,1)S(1)}, u32[]{:S(2)}, u32[]{:S(2)}) collective-permute-start(bf16[256,256]{1,0:T(8,128)(2,1)S(1)} %get-tuple-element.29), channel_id=1, source_target_pairs={{0,1},{1,2},{2,3},{3,0},{4,5},{5,6},{6,7},{7,4},{8,9},{9,10},{10,1... | collective-permute-start | bytes 393224 | tf_op jit(solution)/shard_map/ppermute | solution.py:250
  63.9 16.9 %collective-permute-start.9 = (bf16[256,256]{1,0:T(8,128)(2,1)S(1)}, bf16[256,256]{1,0:T(8,128)(2,1)S(1)}, u32[]{:S(2)}, u32[]{:S(2)}) collective-permute-start(bf16[256,256]{1,0:T(8,128)(2,1)S(1)} %get-tuple-element.30), channel_id=1, source_target_pairs={{0,2},{1,3},{2,0},{3,1},{4,6},{5,7},{6,4},{7,5},{8,10},{9,11},{10,... | collective-permute-start | bytes 393224 | tf_op jit(solution)/shard_map/ppermute | solution.py:250
  80.8 20.1 %all-to-all-start = ((bf16[4,256,256]{2,1,0:T(8,128)(2,1)}), bf16[4,256,256]{2,1,0:T(8,128)(2,1)S(1)}, u32[]{:S(2)}, u32[]{:S(2)}) async-start(bf16[4,256,256]{2,1,0:T(8,128)(2,1)} %late1.1), calls=%async_computation | async-start | bytes 1048576 | tf_op jit(solution)/shard_map/all_to_all | solution.py:270
